TPU v7x, 32 devices: a whole 2x2x4 slice. The times are simulated.
32 devices in a mesh: dp: 8 (over z, y), seq: 4 (over x, core).
Axes of the slice: x: 2, y: 2, z: 4, core: 2. Of those that a mesh axis runs over, the one named last changes fastest.
Arguments:
- inputs: bfloat16 [2, 4096, 1152], P(None, ('dp', 'seq')), may hold values from -6 to 6
- cotangent: bfloat16 [2, 4096, 1152], P(None, ('dp', 'seq')), may hold values from -6 to 6
- lengths: int32 [2, 4], replicated, may hold values from 1 to 2048, 3840 in all within a row
- deal: int32 [2, 16], replicated, may hold values from 0 to 15, as said below
- w_query: bfloat16 [1152, 1024], P(('dp', 'seq')), may hold values from -0.1875 to 0.1875
- w_key: bfloat16 [1152, 256], P(('dp', 'seq')), may hold values from -0.1875 to 0.1875
- w_value: bfloat16 [1152, 256], P(('dp', 'seq')), may hold values from -0.1875 to 0.1875
- w_out: bfloat16 [1024, 1152], P(('dp', 'seq')), may hold values from -0.375 to 0.375
- w_gate: bfloat16 [1152, 6912], P(('dp', 'seq')), may hold values from -0.1875 to 0.1875
- w_up: bfloat16 [1152, 6912], P(('dp', 'seq')), may hold values from -0.1875 to 0.1875
- w_down: bfloat16 [6912, 1152], P(('dp', 'seq')), may hold values from -0.078125 to 0.078125
- gain_attn_pre: bfloat16 [1152], P(('dp', 'seq')), may hold values from 0.5 to 1.5
- gain_attn_post: bfloat16 [1152], P(('dp', 'seq')), may hold values from 0.5 to 1.5
- gain_ffw_pre: bfloat16 [1152], P(('dp', 'seq')), may hold values from 0.5 to 1.5
- gain_ffw_post: bfloat16 [1152], P(('dp', 'seq')), may hold values from 0.5 to 1.5
- gain_query: bfloat16 [256], P(('dp', 'seq')), may hold values from 0.099609375 to 1.8984375
- gain_key: bfloat16 [256], P(('dp', 'seq')), may hold values from 0.099609375 to 1.8984375
Outputs:
- output: bfloat16 [2, 4096, 1152], P(None, ('dp', 'seq'))
- input_grad: bfloat16 [2, 4096, 1152], P(None, ('dp', 'seq'))
- grad_w_query: float32 [1152, 1024], P(('dp', 'seq'))
- grad_w_key: float32 [1152, 256], P(('dp', 'seq'))
- grad_w_value: float32 [1152, 256], P(('dp', 'seq'))
- grad_w_out: float32 [1024, 1152], P(('dp', 'seq'))
- grad_w_gate: float32 [1152, 6912], P(('dp', 'seq'))
- grad_w_up: float32 [1152, 6912], P(('dp', 'seq'))
- grad_w_down: float32 [6912, 1152], P(('dp', 'seq'))
- grad_gain_attn_pre: float32 [1152], P(('dp', 'seq'))
- grad_gain_attn_post: float32 [1152], P(('dp', 'seq'))
- grad_gain_ffw_pre: float32 [1152], P(('dp', 'seq'))
- grad_gain_ffw_post: float32 [1152], P(('dp', 'seq'))
- grad_gain_query: float32 [256], P(('dp', 'seq'))
- grad_gain_key: float32 [256], P(('dp', 'seq'))
Inputs may be any that keep to these rules, and one draw needn't show every extreme that they name: Each row of deal is a permutation of the 16 stretches in which slots 2 g and 2 g + 1 hold stretches i and 15 - i for some i.
All inputs are finite; a program needn't handle non-finite values.
Results may differ from a plain program's by a relative error of at most 0.035.
Values may be sent and summed in bfloat16 or wider, within the bound.
No kernel may reach another device: no remote copies, remote signals or barrier semaphores. Data moves between devices by JAX's collectives and lax.ppermute only.
A program may use at most 320 MiB of HBM per device.

v0:
```python
import jax
import jax.numpy as jnp
from jax import lax
from jax.sharding import PartitionSpec as P

HEADS = 4
HEAD = 256
MAXLEN = 4096
MB = 2


eps = 1e-06
rope_base = 1000000.0
masked_score = -1e30


def norm_scale(values):
    return lax.rsqrt(jnp.mean(values * values, axis=-1, keepdims=True) + eps)


def norm_back(values, scale, weighted):
    return scale * weighted - values * (scale * scale * scale) * jnp.mean(
        weighted * values, axis=-1, keepdims=True
    )


def rotary_tables(positions, width):
    half_width = width // 2
    freqs = rope_base ** (-2.0 * jnp.arange(half_width, dtype=jnp.float32) / width)
    angle = positions.astype(jnp.float32)[:, None, None] * freqs
    return (jnp.cos(angle), jnp.sin(angle))


def rotate(values, cosine, sine):
    half_width = values.shape[-1] // 2
    first = values[..., :half_width]
    second = values[..., half_width:]
    return jnp.concatenate(
        [first * cosine - second * sine, second * cosine + first * sine], axis=-1
    )


def rotate_back(grads, cosine, sine):
    half_width = grads.shape[-1] // 2
    first = grads[..., :half_width]
    second = grads[..., half_width:]
    return jnp.concatenate(
        [first * cosine + second * sine, second * cosine - first * sine], axis=-1
    )


def layout(lengths, row_ids):
    ends = jnp.cumsum(lengths)
    after = row_ids[:, None] >= ends[None, :]
    segment = jnp.sum(after.astype(jnp.int32), axis=1)
    starts = jnp.max(jnp.where(after, ends[None, :], 0), axis=1)
    return (segment, row_ids - starts)


def matmul(left, right):
    return jnp.dot(left, right, preferred_element_type=jnp.float32)


def matmul_tn(left, right):
    return lax.dot_general(
        left, right, (((0,), (0,)), ((), ())), preferred_element_type=jnp.float32
    )


def matmul_nt(left, right):
    return lax.dot_general(
        left, right, (((1,), (1,)), ((), ())), preferred_element_type=jnp.float32
    )


def keep_state(state):
    return state


def gelu_product(gate_in, up_in):
    return jax.nn.gelu(gate_in, approximate=True) * up_in


def per_device(
    inputs,
    cotangent,
    lengths,
    deal,
    w_query,
    w_key,
    w_value,
    w_out,
    w_gate,
    w_up,
    w_down,
    gain_attn_pre,
    gain_attn_post,
    gain_ffw_pre,
    gain_ffw_post,
    gain_query,
    gain_key,
):
    tok_rows = inputs.shape[1]
    stretch_rows = 2 * tok_rows
    seq_count = lax.axis_size("seq")
    device_count = lax.axis_size(("dp", "seq"))
    total_rows = tok_rows * device_count
    stretch_count = deal.shape[1]
    longest = min(MAXLEN, total_rows // 2)
    window = (longest + stretch_rows - 2) // stretch_rows + 1
    scale = HEAD ** (-0.5)
    device_id = lax.axis_index("dp") * seq_count + lax.axis_index("seq")
    group_slot = lax.axis_index("dp") * (seq_count // 2)
    query_stretches = seq_count // 2
    stretch_ids = jnp.arange(stretch_count, dtype=jnp.int32)
    local_ids = jnp.arange(tok_rows, dtype=jnp.int32)
    block_ids = jnp.arange(stretch_rows, dtype=jnp.int32)
    shards = (
        w_query,
        w_key,
        w_value,
        w_out,
        w_gate,
        w_up,
        w_down,
        gain_attn_pre,
        gain_attn_post,
        gain_ffw_pre,
        gain_ffw_post,
        gain_query,
        gain_key,
    )
    outputs = []
    input_grads = []
    grad_total = None
    for micro_index in range(MB):
        seq_lengths = lengths[micro_index]
        dealt_slots = deal[micro_index]
        match = (dealt_slots[:, None] == stretch_ids[None, :]).astype(jnp.int32)
        inverse = jnp.sum(stretch_ids[:, None] * match, axis=0)
        my_rows = dealt_slots[device_id // 2] * stretch_rows + device_id % 2 * tok_rows + local_ids
        my_seg, my_pos = layout(seq_lengths, my_rows)
        valid = (my_rows < total_rows - stretch_rows)[:, None]
        full = (
            lax.all_gather(shards[0], ("dp", "seq"), axis=0, tiled=True),
            lax.all_gather(shards[1], ("dp", "seq"), axis=0, tiled=True),
            lax.all_gather(shards[2], ("dp", "seq"), axis=0, tiled=True),
            lax.all_gather(shards[3], ("dp", "seq"), axis=0, tiled=True),
            lax.all_gather(shards[4], ("dp", "seq"), axis=0, tiled=True),
            lax.all_gather(shards[5], ("dp", "seq"), axis=0, tiled=True),
            lax.all_gather(shards[6], ("dp", "seq"), axis=0, tiled=True),
            lax.all_gather(shards[7], ("dp", "seq"), axis=0, tiled=True),
            lax.all_gather(shards[8], ("dp", "seq"), axis=0, tiled=True),
            lax.all_gather(shards[9], ("dp", "seq"), axis=0, tiled=True),
            lax.all_gather(shards[10], ("dp", "seq"), axis=0, tiled=True),
            lax.all_gather(shards[11], ("dp", "seq"), axis=0, tiled=True),
            lax.all_gather(shards[12], ("dp", "seq"), axis=0, tiled=True),
        )
        (
            query_weight,
            key_weight,
            value_weight,
            out_weight,
            gate_weight,
            up_weight,
            down_weight,
            pre_attention,
            post_attention,
            pre_feed,
            post_feed,
            query_gain,
            key_gain,
        ) = full
        pre_attention = pre_attention.astype(jnp.float32)
        post_attention = post_attention.astype(jnp.float32)
        pre_feed = pre_feed.astype(jnp.float32)
        post_feed = post_feed.astype(jnp.float32)
        query_gain = query_gain.astype(jnp.float32)
        key_gain = key_gain.astype(jnp.float32)
        rows_in = inputs[micro_index].astype(jnp.float32)
        scale_one = norm_scale(rows_in)
        normed_one = (rows_in * scale_one * pre_attention).astype(jnp.bfloat16)
        query_raw = matmul(normed_one, query_weight).reshape(tok_rows, HEADS, HEAD)
        key_raw = matmul(normed_one, key_weight).reshape(tok_rows, 1, HEAD)
        value_raw = matmul(normed_one, value_weight)
        cosine, sine = rotary_tables(my_pos, HEAD)
        query_scale = norm_scale(query_raw)
        query_rot = rotate(query_raw * query_scale * query_gain, cosine, sine).astype(jnp.bfloat16)
        key_scale = norm_scale(key_raw)
        key_rot = rotate(key_raw * key_scale * key_gain, cosine, sine).astype(jnp.bfloat16)
        value_low = value_raw.astype(jnp.bfloat16)
        query_heads = lax.all_to_all(query_rot, "seq", split_axis=1, concat_axis=0, tiled=True)[
            :, 0, :
        ]
        keys_all = lax.all_gather(
            jnp.concatenate([key_rot[:, 0, :], value_low], axis=1),
            ("dp", "seq"),
            axis=0,
            tiled=True,
        )

        def key_block(query_stretch, offset):
            source_stretch = query_stretch - offset
            slot = inverse[jnp.maximum(source_stretch, 0)]
            block = lax.dynamic_slice_in_dim(keys_all, slot * stretch_rows, stretch_rows, 0)
            return (block, source_stretch * stretch_rows + block_ids)

        def allowed_mask(query_ids, query_seg, key_ids):
            key_seg, key_pos = layout(seq_lengths, key_ids)
            return (
                (key_ids[None, :] >= 0)
                & (key_ids[None, :] <= query_ids[:, None])
                & (key_seg[None, :] == query_seg[:, None])
            )

        def scores_of(query_block, block, mask):
            raw = matmul_nt(query_block, block[:, :HEAD]) * scale
            return jnp.where(mask, raw, masked_score)

        saved = []
        contexts = []
        for part_index in range(query_stretches):
            query_stretch = dealt_slots[group_slot + part_index]
            query_ids = query_stretch * stretch_rows + block_ids
            query_seg, query_pos = layout(seq_lengths, query_ids)
            query_block = query_heads[part_index * stretch_rows : (part_index + 1) * stretch_rows]

            def max_step(offset, carry):
                block, key_ids = key_block(query_stretch, offset)
                mask = allowed_mask(query_ids, query_seg, key_ids)

                def max_update(state):
                    scores = scores_of(query_block, block, mask)
                    new_max = jnp.maximum(state[0], jnp.max(scores, axis=1))
                    terms = jnp.where(mask, jnp.exp(scores - new_max[:, None]), 0.0)
                    return (
                        new_max,
                        state[1] * jnp.exp(state[0] - new_max) + jnp.sum(terms, axis=1),
                    )

                return lax.cond(jnp.any(mask), max_update, keep_state, carry)

            run_max, run_sum = lax.fori_loop(
                0,
                window,
                max_step,
                (
                    jnp.full((stretch_rows,), masked_score, jnp.float32),
                    jnp.zeros((stretch_rows,), jnp.float32),
                ),
            )
            log_total = run_max + jnp.log(run_sum)

            def value_step(offset, carry):
                block, key_ids = key_block(query_stretch, offset)
                mask = allowed_mask(query_ids, query_seg, key_ids)

                def value_update(state):
                    probs = jnp.where(
                        mask, jnp.exp(scores_of(query_block, block, mask) - log_total[:, None]), 0.0
                    )
                    return state + matmul(probs.astype(jnp.bfloat16), block[:, HEAD:])

                return lax.cond(jnp.any(mask), value_update, keep_state, carry)

            contexts.append(
                lax.fori_loop(0, window, value_step, jnp.zeros((stretch_rows, HEAD), jnp.float32))
            )
            saved.append((query_stretch, query_ids, query_seg, query_block, log_total))
        context_low = jnp.concatenate(contexts, axis=0).astype(jnp.bfloat16)[:, None, :]
        context_rows = lax.all_to_all(
            context_low, "seq", split_axis=0, concat_axis=1, tiled=True
        ).reshape(tok_rows, HEADS * HEAD)
        attended = matmul(context_rows, out_weight)
        scale_two = norm_scale(attended)
        hidden_res = rows_in + attended * scale_two * post_attention
        scale_three = norm_scale(hidden_res)
        normed_two = (hidden_res * scale_three * pre_feed).astype(jnp.bfloat16)
        gate_raw = matmul(normed_two, gate_weight)
        up_raw = matmul(normed_two, up_weight)
        gated, gelu_pull = jax.vjp(gelu_product, gate_raw, up_raw)
        hidden_low = gated.astype(jnp.bfloat16)
        mixed = matmul(hidden_low, down_weight)
        scale_four = norm_scale(mixed)
        result = hidden_res + mixed * scale_four * post_feed
        outputs.append(jnp.where(valid, result, 0.0).astype(jnp.bfloat16))
        back_full = (
            lax.all_gather(shards[0], ("dp", "seq"), axis=0, tiled=True),
            lax.all_gather(shards[1], ("dp", "seq"), axis=0, tiled=True),
            lax.all_gather(shards[2], ("dp", "seq"), axis=0, tiled=True),
            lax.all_gather(shards[3], ("dp", "seq"), axis=0, tiled=True),
            lax.all_gather(shards[4], ("dp", "seq"), axis=0, tiled=True),
            lax.all_gather(shards[5], ("dp", "seq"), axis=0, tiled=True),
            lax.all_gather(shards[6], ("dp", "seq"), axis=0, tiled=True),
            lax.all_gather(shards[7], ("dp", "seq"), axis=0, tiled=True),
            lax.all_gather(shards[8], ("dp", "seq"), axis=0, tiled=True),
            lax.all_gather(shards[9], ("dp", "seq"), axis=0, tiled=True),
            lax.all_gather(shards[10], ("dp", "seq"), axis=0, tiled=True),
            lax.all_gather(shards[11], ("dp", "seq"), axis=0, tiled=True),
            lax.all_gather(shards[12], ("dp", "seq"), axis=0, tiled=True),
        )
        (
            query_weight,
            key_weight,
            value_weight,
            out_weight,
            gate_weight,
            up_weight,
            down_weight,
            pre_attention,
            post_attention,
            pre_feed,
            post_feed,
            query_gain,
            key_gain,
        ) = back_full
        pre_attention = pre_attention.astype(jnp.float32)
        post_attention = post_attention.astype(jnp.float32)
        pre_feed = pre_feed.astype(jnp.float32)
        post_feed = post_feed.astype(jnp.float32)
        query_gain = query_gain.astype(jnp.float32)
        key_gain = key_gain.astype(jnp.float32)
        upstream = jnp.where(valid, cotangent[micro_index].astype(jnp.float32), 0.0)
        grad_post_feed = jnp.sum(upstream * mixed * scale_four, axis=0)
        mixed_grad = norm_back(mixed, scale_four, post_feed * upstream).astype(jnp.bfloat16)
        grad_down = matmul_tn(hidden_low, mixed_grad)
        hidden_grad = matmul_nt(mixed_grad, down_weight)
        gate_grad, up_grad = gelu_pull(hidden_grad)
        gate_grad = gate_grad.astype(jnp.bfloat16)
        up_grad = up_grad.astype(jnp.bfloat16)
        grad_gate = matmul_tn(normed_two, gate_grad)
        grad_up = matmul_tn(normed_two, up_grad)
        normed_two_grad = matmul_nt(gate_grad, gate_weight) + matmul_nt(up_grad, up_weight)
        grad_pre_feed = jnp.sum(normed_two_grad * hidden_res * scale_three, axis=0)
        hidden_res_grad = upstream + norm_back(hidden_res, scale_three, pre_feed * normed_two_grad)
        grad_post_attention = jnp.sum(hidden_res_grad * attended * scale_two, axis=0)
        attended_grad = norm_back(attended, scale_two, post_attention * hidden_res_grad).astype(
            jnp.bfloat16
        )
        grad_out = matmul_tn(context_rows, attended_grad)
        context_grad = (
            matmul_nt(attended_grad, out_weight).astype(jnp.bfloat16).reshape(tok_rows, HEADS, HEAD)
        )
        grad_heads = lax.all_to_all(context_grad, "seq", split_axis=1, concat_axis=0, tiled=True)[
            :, 0, :
        ]
        deltas = []
        query_grads = []
        for part_index in range(query_stretches):
            query_stretch, query_ids, query_seg, query_block, log_total = saved[part_index]
            grad_block = grad_heads[part_index * stretch_rows : (part_index + 1) * stretch_rows]

            def delta_step(offset, carry):
                block, key_ids = key_block(query_stretch, offset)
                mask = allowed_mask(query_ids, query_seg, key_ids)

                def delta_update(state):
                    probs = jnp.where(
                        mask, jnp.exp(scores_of(query_block, block, mask) - log_total[:, None]), 0.0
                    )
                    dots = matmul_nt(grad_block, block[:, HEAD:])
                    return state + jnp.sum(probs * dots, axis=1)

                return lax.cond(jnp.any(mask), delta_update, keep_state, carry)

            delta = lax.fori_loop(0, window, delta_step, jnp.zeros((stretch_rows,), jnp.float32))

            def query_step(offset, carry):
                block, key_ids = key_block(query_stretch, offset)
                mask = allowed_mask(query_ids, query_seg, key_ids)

                def query_update(state):
                    probs = jnp.where(
                        mask, jnp.exp(scores_of(query_block, block, mask) - log_total[:, None]), 0.0
                    )
                    dots = matmul_nt(grad_block, block[:, HEAD:])
                    score_grad = (probs * (dots - delta[:, None])).astype(jnp.bfloat16)
                    return state + matmul(score_grad, block[:, :HEAD]) * scale

                return lax.cond(jnp.any(mask), query_update, keep_state, carry)

            query_grads.append(
                lax.fori_loop(0, window, query_step, jnp.zeros((stretch_rows, HEAD), jnp.float32))
            )
            deltas.append(delta)
        query_grad_low = jnp.concatenate(query_grads, axis=0).astype(jnp.bfloat16)[:, None, :]
        query_rot_grad = lax.all_to_all(
            query_grad_low, "seq", split_axis=0, concat_axis=1, tiled=True
        ).astype(jnp.float32)

        def one_block(block_index):
            first_row = block_index * tok_rows
            block = lax.dynamic_slice_in_dim(keys_all, first_row, tok_rows, 0)
            key_ids = (
                dealt_slots[first_row // stretch_rows] * stretch_rows
                + first_row % stretch_rows
                + local_ids
            )
            total = jnp.zeros((tok_rows, 2 * HEAD), jnp.float32)
            for part_index in range(query_stretches):
                query_stretch, query_ids, query_seg, query_block, log_total = saved[part_index]
                grad_block = grad_heads[part_index * stretch_rows : (part_index + 1) * stretch_rows]
                delta = deltas[part_index]
                mask = allowed_mask(query_ids, query_seg, key_ids)

                def one_update(state):
                    probs = jnp.where(
                        mask, jnp.exp(scores_of(query_block, block, mask) - log_total[:, None]), 0.0
                    )
                    dots = matmul_nt(grad_block, block[:, HEAD:])
                    score_grad = (probs * (dots - delta[:, None])).astype(jnp.bfloat16)
                    key_part = matmul_tn(score_grad, query_block) * scale
                    value_part = matmul_tn(probs.astype(jnp.bfloat16), grad_block)
                    return state + jnp.concatenate([key_part, value_part], axis=1)

                total = lax.cond(jnp.any(mask), one_update, keep_state, total)
            return total

        blocks = lax.map(
            one_block,
            jnp.arange(tok_rows * lax.axis_size(("dp", "seq")) // tok_rows, dtype=jnp.int32),
        )
        key_grads = lax.psum_scatter(
            blocks.reshape(tok_rows * lax.axis_size(("dp", "seq")), 2 * HEAD),
            ("dp", "seq"),
            scatter_dimension=0,
            tiled=True,
        )
        value_grad = key_grads[:, HEAD:].astype(jnp.bfloat16)
        key_turned = rotate_back(key_grads[:, None, :HEAD], cosine, sine)
        grad_key_gain = jnp.sum(key_turned * key_raw * key_scale, axis=(0, 1))
        key_grad = norm_back(key_raw, key_scale, key_gain * key_turned)[:, 0, :].astype(
            jnp.bfloat16
        )
        query_turned = rotate_back(query_rot_grad, cosine, sine)
        grad_query_gain = jnp.sum(query_turned * query_raw * query_scale, axis=(0, 1))
        query_grad = (
            norm_back(query_raw, query_scale, query_gain * query_turned)
            .reshape(tok_rows, HEADS * HEAD)
            .astype(jnp.bfloat16)
        )
        grad_query = matmul_tn(normed_one, query_grad)
        grad_key = matmul_tn(normed_one, key_grad)
        grad_value = matmul_tn(normed_one, value_grad)
        normed_one_grad = (
            matmul_nt(query_grad, query_weight)
            + matmul_nt(key_grad, key_weight)
            + matmul_nt(value_grad, value_weight)
        )
        grad_pre_attention = jnp.sum(normed_one_grad * rows_in * scale_one, axis=0)
        rows_grad = hidden_res_grad + norm_back(rows_in, scale_one, pre_attention * normed_one_grad)
        input_grads.append(rows_grad.astype(jnp.bfloat16))
        summed = (
            lax.psum_scatter(grad_query, ("dp", "seq"), scatter_dimension=0, tiled=True),
            lax.psum_scatter(grad_key, ("dp", "seq"), scatter_dimension=0, tiled=True),
            lax.psum_scatter(grad_value, ("dp", "seq"), scatter_dimension=0, tiled=True),
            lax.psum_scatter(grad_out, ("dp", "seq"), scatter_dimension=0, tiled=True),
            lax.psum_scatter(grad_gate, ("dp", "seq"), scatter_dimension=0, tiled=True),
            lax.psum_scatter(grad_up, ("dp", "seq"), scatter_dimension=0, tiled=True),
            lax.psum_scatter(grad_down, ("dp", "seq"), scatter_dimension=0, tiled=True),
            lax.psum_scatter(grad_pre_attention, ("dp", "seq"), scatter_dimension=0, tiled=True),
            lax.psum_scatter(grad_post_attention, ("dp", "seq"), scatter_dimension=0, tiled=True),
            lax.psum_scatter(grad_pre_feed, ("dp", "seq"), scatter_dimension=0, tiled=True),
            lax.psum_scatter(grad_post_feed, ("dp", "seq"), scatter_dimension=0, tiled=True),
            lax.psum_scatter(grad_query_gain, ("dp", "seq"), scatter_dimension=0, tiled=True),
            lax.psum_scatter(grad_key_gain, ("dp", "seq"), scatter_dimension=0, tiled=True),
        )
        if grad_total is None:
            grad_total = summed
        else:
            grad_total = jax.tree.map(jnp.add, grad_total, summed)
    return (
        jnp.stack(outputs, axis=0),
        jnp.stack(input_grads, axis=0),
        grad_total[0],
        grad_total[1],
        grad_total[2],
        grad_total[3],
        grad_total[4],
        grad_total[5],
        grad_total[6],
        grad_total[7],
        grad_total[8],
        grad_total[9],
        grad_total[10],
        grad_total[11],
        grad_total[12],
    )


def solution(mesh):
    placed = (
        P(None, ("dp", "seq"), None),
        P(None, ("dp", "seq"), None),
        P(),
        P(),
        P(("dp", "seq"), None),
        P(("dp", "seq"), None),
        P(("dp", "seq"), None),
        P(("dp", "seq"), None),
        P(("dp", "seq"), None),
        P(("dp", "seq"), None),
        P(("dp", "seq"), None),
        P(("dp", "seq")),
        P(("dp", "seq")),
        P(("dp", "seq")),
        P(("dp", "seq")),
        P(("dp", "seq")),
        P(("dp", "seq")),
    )
    return jax.shard_map(
        per_device,
        mesh=mesh,
        in_specs=placed,
        out_specs=(
            P(None, ("dp", "seq"), None),
            P(None, ("dp", "seq"), None),
            P(("dp", "seq"), None),
            P(("dp", "seq"), None),
            P(("dp", "seq"), None),
            P(("dp", "seq"), None),
            P(("dp", "seq"), None),
            P(("dp", "seq"), None),
            P(("dp", "seq"), None),
            P(("dp", "seq")),
            P(("dp", "seq")),
            P(("dp", "seq")),
            P(("dp", "seq")),
            P(("dp", "seq")),
            P(("dp", "seq")),
        ),
        check_vma=False,
    )
```

profile of v0, /device:TPU:0, one launch (start us, length us, event | category | flops | bytes accessed | tf_op | source)
XLA Modules:
  0.0 2937.9 jit_solution(8761735474517002306)
XLA Ops:
  17.5 42.5 %all-reduce.24 = (bf16[1152]{0:T(1024)(128)(2,1)S(1)}, bf16[256]{0:T(256)(128)(2,1)S(1)}, bf16[256]{0:T(256)(128)(2,1)S(1)}, bf16[1152]{0:T(1024)(128)(2,1)S(1)}...) all-reduce(bf16[1152]{0:T(1024)(128)(2,1)S(1)} %dynamic-update-slic, ...), channel_id=1, replica_groups=mesh['dp'=8,'seq'=4] {'dp','seq'}, use_global_device_ids=true, to_apply=%add | all-reduce | flops 5120 | bytes 20480
  60.0 42.5 %all-gather = bf16[32,36,256]{2,1,0:T(8,128)(2,1)S(1)} all-gather(bf16[1,36,256]{2,1,0:T(8,128)(2,1)} %bitcast.702), channel_id=1, replica_groups=mesh['dp'=8,'seq'=4] {'dp','seq'}, dimensions={0}, use_global_device_ids=true | all-gather | bytes 608256 | tf_op jit(solution)/shard_map/all_gather | solution.py:146
  102.7 38.7 %all-gather.1 = bf16[32,36,256]{2,1,0:T(8,128)(2,1)S(1)} all-gather(bf16[1,36,256]{2,1,0:T(8,128)(2,1)} %bitcast.703), channel_id=1, replica_groups=mesh['dp'=8,'seq'=4] {'dp','seq'}, dimensions={0}, use_global_device_ids=true | all-gather | bytes 608256 | tf_op jit(solution)/shard_map/all_gather | solution.py:147
  304.4 25.3 while.326
  329.7 38.0 %while.328 = (s32[]{:T(128)}, f32[256]{0:T(256)S(1)}, f32[256]{0:T(256)S(1)}, s32[]{:T(128)}, s32[1,4]{1,0:T(1,128)S(1)}, /*index=5*/s32[256]{0:T(256)S(1)}, s32...) while((s32[]{:T(128)}, f32[256]{0:T(256)S(1)}, ...), condition=%wide.region_30.31_spmd.clone, body=%wide.region_23.0_spmd.clone.sunk | while | flops 34279688 | bytes 1005401 | solution.py:243
  367.7 25.6 while.327
  393.4 39.4 %while.329 = (s32[]{:T(128)}, f32[256,256]{1,0:T(8,128)S(1)}, s32[]{:T(128)}, s32[1,4]{1,0:T(1,128)S(1)}, s32[256]{0:T(256)S(1)}, /*index=5*/s32[16]{0:T(128)S(1...) while((s32[]{:T(128)}, f32[256,256]{1,0:T(8,128)S(1)}, ...), condition=%wide.region_36.37_spmd.clone, body=%wide.region_31.36_spmd.clone.sunk | while | flops 67833608 | bytes 1060161 | solution.py:267
  471.7 101.9 %all-gather.25.cloned.1.call-done = bf16[32,36,6912]{2,1,0:T(8,128)(2,1)} async-done(((bf16[1,36,6912]{2,1,0:T(8,128)(2,1)}), bf16[32,36,6912]{2,1,0:T(8,128)(2,1)}) %all-gather.25.cloned.1.call-update) | async-done | bytes 15925264 | tf_op jit(solution)/shard_map/all_gather | solution.py:150
  608.7 76.6 %all-gather.17.cloned.1.call-done = bf16[6912,1152]{1,0:T(8,128)(2,1)} async-done(((bf16[216,1152]{1,0:T(8,128)(2,1)}), bf16[6912,1152]{1,0:T(8,128)(2,1)}) %all-gather.17.cloned.1.call-update) | async-done | bytes 15925264 | tf_op jit(solution)/shard_map/all_gather | solution.py:151
  809.7 24.6 while.339
  863.0 208.6 %while.343 = (s32[]{:T(128)}, f32[32,128,512]{2,1,0:T(8,128)}, s32[32]{0:T(128)S(1)}, s32[16]{0:T(128)S(1)}, s32[1,4]{1,0:T(1,128)S(1)}, /*index=5*/s32[256]{0:T...) while((s32[]{:T(128)}, f32[32,128,512]{2,1,0:T(8,128)}, ...), condition=%wide.region_160.161_spmd.clone, body=%wide.region_152.160_spmd.clone.sunk | while | flops 135334176 | bytes 4863943 | solution.py:419
  1072.2 27.4 while.334
  1099.7 45.4 %while.336 = (s32[]{:T(128)}, f32[256]{0:T(256)S(1)}, s32[]{:T(128)}, s32[1,4]{1,0:T(1,128)S(1)}, s32[256]{0:T(256)S(1)}, /*index=5*/s32[16]{0:T(128)S(1)}, bf16...) while((s32[]{:T(128)}, f32[256]{0:T(256)S(1)}, ...), condition=%wide.region_102.103_spmd.clone, body=%wide.region_96.102_spmd.clone.sunk | while | flops 67833608 | bytes 1193821 | solution.py:366
  1150.1 222.8 %while.338 = (s32[]{:T(128)}, f32[32,128,512]{2,1,0:T(8,128)}, s32[32]{0:T(128)S(1)}, s32[16]{0:T(128)S(1)}, s32[1,4]{1,0:T(1,128)S(1)}, /*index=5*/s32[256]{0:T...) while((s32[]{:T(128)}, f32[32,128,512]{2,1,0:T(8,128)}, ...), condition=%wide.region_118.119_spmd.clone, body=%wide.region_110.118_spmd.clone.sunk | while | flops 135334176 | bytes 4863943 | solution.py:419
  1407.1 24.1 convolution_add_fusion.4
  1454.7 537.1 %fusion.80 = f32[40,6912]{1,0:T(8,128)} fusion(f32[1152,6912]{1,0:T(8,128)} %convolution_add_fusion.4), kind=kCustom, calls=%all-reduce-scatter.4 | all-reduce-scatter fusion | flops 8847361 | bytes 32956416
  2016.0 23.9 convolution_add_fusion.5
  2039.9 24.5 while.340
  2093.1 28.0 while.335
  2121.2 47.6 %while.337 = (s32[]{:T(128)}, f32[256,256]{1,0:T(8,128)S(1)}, s32[]{:T(128)}, s32[1,4]{1,0:T(1,128)S(1)}, s32[256]{0:T(256)S(1)}, /*index=5*/s32[16]{0:T(128)S(1...) while((s32[]{:T(128)}, f32[256,256]{1,0:T(8,128)S(1)}, ...), condition=%wide.region_108.109_spmd.clone, body=%wide.region_103.108_spmd.clone.sunk | while | flops 101584640 | bytes 1847653 | solution.py:383
  2196.1 23.8 concatenate.162
  2228.6 492.8 %fusion.477 = (f32[40,1024]{1,0:T(8,128)}, f32[40,256]{1,0:T(8,128)}, f32[40,256]{1,0:T(8,128)}, f32[40,6912]{1,0:T(8,128)}) fusion(f32[1152,1024]{1,0:T(8,128)} %convolution_add_fusion.8, f32[1152,256]{1,0:T(8,128)S(1)} %convolution_add_fusion.10, f32[1152,256]{1,0:T(8,128)} %convolution_add_fusion.9, f32[1152,6912]{1,0:T(8,128)} %convolution_add_fusion.5), kind=kCustom, calls=%all-reduce-scatter.5 | all-reduce-scatter fusion | flops 10813441 | bytes 40280064
  2770.0 36.8 %collective-permute-start.6 = (f32[40,256]{1,0:T(8,128)S(1)}, f32[40,256]{1,0:T(8,128)S(1)}, u32[]{:S(2)}, u32[]{:S(2)}) collective-permute-start(f32[40,256]{1,0:T(8,128)S(1)} %copy-done.75), channel_id=1, source_target_pairs={{0,3},{1,4},{2,5},{3,6},{4,7},{5,8},{6,9},{7,10},{8,11},{9,12},{10... | collective-permute-start | bytes 122888
  2813.0 73.7 %all-reduce.23 = (f32[1152]{0:T(1024)S(1)}, f32[1152]{0:T(1024)S(1)}, f32[1152]{0:T(1024)S(1)}, f32[1152]{0:T(1024)S(1)}, f32[256]{0:T(256)S(1)}, /*index=5*/f32[256]{0:T(256)S(1)}) all-reduce(f32[1152]{0:T(1024)S(1)} %add.1770, f32[1152]{0:T(1024)S(1)} %add.1771, ...), channel_id=24, replica_groups=mesh['dp'=8,'seq'=4] {'dp','seq'}, use_global_device_ids=true, to_apply=%region_179.180.clone | all-reduce | flops 5120 | bytes 40960
  (2359 shorter events, 1311.7 us)
Async XLA Ops:
  7.2 146.7 %all-gather.21.cloned.1.call-start = ((), (), s32[]{:S(2)}) async-start(), calls=%async_computation.19 | async-start | bytes 2703360 | tf_op jit(solution)/shard_map/all_gather | solution.py:145
  7.9 199.5 %all-gather.19.cloned.1.call-start = ((), (), s32[]{:S(2)}) async-start(), calls=%async_computation.15 | async-start | bytes 4325376 | tf_op jit(solution)/shard_map/all_gather | solution.py:195
  146.4 157.9 %all-gather.13.cloned.1.call-start = ((), (), s32[]{:S(2)}) async-start(), calls=%async_computation.12 | async-start | bytes 4325376 | tf_op jit(solution)/shard_map/all_gather | solution.py:195
  147.5 296.9 %all-gather.15.cloned.1.call-start = ((), (), s32[]{:S(2)}) async-start(), calls=%async_computation.13 | async-start | bytes 2433024 | tf_op jit(solution)/shard_map/all_gather | solution.py:148
  148.1 305.1 %all-gather.23.cloned.1.call-start = ((), (), s32[]{:S(2)}) async-start(), calls=%async_computation.20 | async-start | bytes 18247680 | tf_op jit(solution)/shard_map/all_gather | solution.py:149
  148.7 424.9 %all-gather.25.cloned.1.call-start = ((), (), s32[]{:S(2)}) async-start(), calls=%async_computation.21 | async-start | bytes 18247680 | tf_op jit(solution)/shard_map/all_gather | solution.py:150
  149.2 536.2 %all-gather.17.cloned.1.call-start = ((), (), s32[]{:S(2)}) async-start(), calls=%async_computation.14 | async-start | bytes 16422912 | tf_op jit(solution)/shard_map/all_gather | solution.py:151
  300.6 133.9 %all-to-all-start.3 = ((bf16[4,2,16384]{2,1,0:T(2,128)(2,1)}), bf16[4,2,16384]{2,1,0:T(2,128)(2,1)S(1)}, u32[]{:S(2)}, u32[]{:S(2)}) async-start(bf16[4,2,16384]{2,1,0:T(2,128)(2,1)} %reshape.1589), calls=%async_computation.3 | async-start | bytes 524288 | tf_op jit(solution)/shard_map/all_to_all | solution.py:271
  806.2 265.5 %all-to-all-start.4 = ((bf16[128,4,256]{2,0,1:T(8,128)(2,1)}), bf16[128,4,256]{2,0,1:T(8,128)(2,1)S(1)}, u32[]{:S(2)}, u32[]{:S(2)}) async-start(bf16[128,4,256]{2,0,1:T(8,128)(2,1)} %bitcast.598), calls=%async_computation.4 | async-start | bytes 524288 | tf_op jit(solution)/shard_map/all_to_all | solution.py:344
  809.6 1412.7 %reduce-scatter.19.cloned.1.call-start = ((), (), s32[]{:S(2)}) async-start(), calls=%async_computation.17 | async-start | bytes 8650752 | tf_op jit(solution)/shard_map/reduce_scatter | solution.py:423
  1071.7 1151.6 %reduce-scatter.17.cloned.1.call-start = ((), (), s32[]{:S(2)}) async-start(), calls=%async_computation.16 | async-start | bytes 8650752 | tf_op jit(solution)/shard_map/reduce_scatter | solution.py:423
  1372.9 1558.0 %reduce-scatter.21.cloned.1.call-start = ((), (), s32[]{:S(2)}) async-start(), calls=%async_computation.18 | async-start | bytes 4866048 | tf_op jit(solution)/shard_map/reduce_scatter | solution.py:457
  1392.6 1538.3 %reduce-scatter.23.cloned.1.call-start = ((), (), s32[]{:S(2)}) async-start(), calls=%async_computation.22 | async-start | bytes 32845824
  1991.7 204.3 %collective-permute-start.16 = (f32[40,6912]{1,0:T(8,128)}, f32[40,6912]{1,0:T(8,128)}, u32[]{:S(2)}, u32[]{:S(2)}) collective-permute-start(f32[40,6912]{1,0:T(8,128)} %fusion.80), channel_id=1, source_target_pairs={{0,1},{1,2},{2,3},{3,4},{4,5},{5,6},{6,7},{7,8},{8,9},{9,10},{10,1... | collective-permute-start | bytes 3317768
  1994.0 202.1 %collective-permute-start.17 = (f32[40,6912]{1,0:T(8,128)}, f32[40,6912]{1,0:T(8,128)}, u32[]{:S(2)}, u32[]{:S(2)}) collective-permute-start(f32[40,6912]{1,0:T(8,128)} %fusion.80), channel_id=1, source_target_pairs={{0,2},{1,3},{2,4},{3,5},{4,6},{5,7},{6,8},{7,9},{8,10},{9,11},{10,... | collective-permute-start | bytes 3317768
  1996.3 199.8 %collective-permute-start.18 = (f32[40,6912]{1,0:T(8,128)}, f32[40,6912]{1,0:T(8,128)}, u32[]{:S(2)}, u32[]{:S(2)}) collective-permute-start(f32[40,6912]{1,0:T(8,128)} %fusion.80), channel_id=1, source_target_pairs={{0,3},{1,4},{2,5},{3,6},{4,7},{5,8},{6,9},{7,10},{8,11},{9,12},{10... | collective-permute-start | bytes 3317768
  2000.2 195.8 %collective-permute-start.19 = (f32[4,6912]{1,0:T(4,128)}, f32[4,6912]{1,0:T(4,128)}, u32[]{:S(2)}, u32[]{:S(2)}) collective-permute-start(f32[4,6912]{1,0:T(4,128)} %slice.402), channel_id=1, source_target_pairs={{0,4},{1,5},{2,6},{3,7},{4,8},{5,9},{6,10},{7,11},{8,12},{9,13},{1... | collective-permute-start | bytes 331784
  2089.5 81.0 %all-to-all-start.7 = ((bf16[4,2,16384]{2,1,0:T(2,128)(2,1)}), bf16[4,2,16384]{2,1,0:T(2,128)(2,1)S(1)}, u32[]{:S(2)}, u32[]{:S(2)}) async-start(bf16[4,2,16384]{2,1,0:T(2,128)(2,1)} %reshape.1593), calls=%async_computation.8 | async-start | bytes 524288 | tf_op jit(solution)/shard_map/all_to_all | solution.py:387
  2724.2 41.5 %collective-permute-start.9 = (f32[40,256]{1,0:T(8,128)}, f32[40,256]{1,0:T(8,128)S(1)}, u32[]{:S(2)}, u32[]{:S(2)}) collective-permute-start(f32[40,256]{1,0:T(8,128)} %get-tuple-element.7337), channel_id=1, source_target_pairs={{0,2},{1,3},{2,4},{3,5},{4,6},{5,7},{6,8},{7,9},{8,10},{9,11},{10,... | collective-permute-start | bytes 122888
  2734.6 171.1 %collective-permute-start.12 = (f32[40,6912]{1,0:T(8,128)}, f32[40,6912]{1,0:T(8,128)}, u32[]{:S(2)}, u32[]{:S(2)}) collective-permute-start(f32[40,6912]{1,0:T(8,128)} %get-tuple-element.7338), channel_id=1, source_target_pairs={{0,1},{1,2},{2,3},{3,4},{4,5},{5,6},{6,7},{7,8},{8,9},{9,10},{10,1... | collective-permute-start | bytes 3317768
  2745.8 160.0 %collective-permute-start.13 = (f32[40,6912]{1,0:T(8,128)}, f32[40,6912]{1,0:T(8,128)}, u32[]{:S(2)}, u32[]{:S(2)}) collective-permute-start(f32[40,6912]{1,0:T(8,128)} %get-tuple-element.7338), channel_id=1, source_target_pairs={{0,2},{1,3},{2,4},{3,5},{4,6},{5,7},{6,8},{7,9},{8,10},{9,11},{10,... | collective-permute-start | bytes 3317768
  2759.2 146.6 %collective-permute-start.14 = (f32[40,6912]{1,0:T(8,128)}, f32[40,6912]{1,0:T(8,128)}, u32[]{:S(2)}, u32[]{:S(2)}) collective-permute-start(f32[40,6912]{1,0:T(8,128)} %get-tuple-element.7338), channel_id=1, source_target_pairs={{0,3},{1,4},{2,5},{3,6},{4,7},{5,8},{6,9},{7,10},{8,11},{9,12},{10... | collective-permute-start | bytes 3317768
  2770.0 120.8 %collective-permute-start.6 = (f32[40,256]{1,0:T(8,128)S(1)}, f32[40,256]{1,0:T(8,128)S(1)}, u32[]{:S(2)}, u32[]{:S(2)}) collective-permute-start(f32[40,256]{1,0:T(8,128)S(1)} %copy-done.75), channel_id=1, source_target_pairs={{0,3},{1,4},{2,5},{3,6},{4,7},{5,8},{6,9},{7,10},{8,11},{9,12},{10... | collective-permute-start | bytes 122888
  2806.8 88.1 %collective-permute-start = (f32[40,1024]{1,0:T(8,128)S(1)}, f32[40,1024]{1,0:T(8,128)S(1)}, u32[]{:S(2)}, u32[]{:S(2)}) collective-permute-start(f32[40,1024]{1,0:T(8,128)S(1)} %copy-done.60), channel_id=1, source_target_pairs={{0,1},{1,2},{2,3},{3,4},{4,5},{5,6},{6,7},{7,8},{8,9},{9,10},{10,1... | collective-permute-start | bytes 491528
  (166 other events, 6368.1 us)
Sparse Core Ops, SparseCore 0:
  10.8 60.7 all-gather.20
  146.6 60.8 all-gather.18
  210.9 60.6 all-gather.12
  274.4 55.8 all-gather.14
  333.0 120.1 all-gather.22
  456.0 117.5 all-gather.24
  576.5 108.8 all-gather.16
  1071.8 218.5 reduce-scatter.18
  1373.1 283.5 reduce-scatter.16
  1662.5 160.3 reduce-scatter.20
  1829.9 379.9 reduce-scatter.22
where the time goes:
time: 2960 us; the launch traced here: 2940 us
  blocking collectives  1230 us (42%)
  loops' own time  392 us (13%)
  matrix products  363 us (12%)
  local copies, waits for them, and re-layouts  352 us (12%)
  waiting for transfers between devices  229 us (8%)
  other arithmetic  222 us (8%)
  starting transfers between devices  132 us (4%)
    unnamed x4, blocking collectives  1150 us
    another operation x2, loops' own time, per_device(): lax.map(one_block, jnp.arange(tok_rows * lax.axis_size(('dp', 'seq')) //...  168 us
    dot_general x58, matrix products, matmul_tn(): lax.dot_general(left, right, (((0,), (0,)), ((), ())), preferred_element_...  140 us
    dot_general x80, matrix products, matmul_nt(): lax.dot_general(left, right, (((1,), (1,)), ((), ())), preferred_element_...  136 us
    unnamed x352, local copies, waits for them, and re-layouts  124 us
    unnamed x21, starting transfers between devices  103 us
    all_gather x1, waiting for transfers between devices, per_device(): lax.all_gather(shards[5], ('dp', 'seq'), axis=0, tiled=True)  102 us
    dot_general x36, matrix products, matmul(): return jnp.dot(left, right, preferred_element_type=jnp.float32)  86.7 us
  transfers between devices with their start and end apart: 39, of which 10 were waited for; matrix products, arithmetic and copies ran while one was open for 63% of the time, Pallas kernels for 0%

commit v1 on v0

v1 whole, which is shorter than its diff:
```python
import functools

import jax
import jax.numpy as jnp
from jax import lax
from jax.experimental import pallas as pl
from jax.experimental.pallas import tpu as pltpu
from jax.sharding import PartitionSpec as P

HEADS = 4
HEAD = 256
MB = 2
STRETCH = 256

eps = 1e-06
rope_base = 1000000.0
masked_score = -1e30
bf16 = jnp.bfloat16
f32 = jnp.float32
ALL = ("dp", "seq")


def norm_scale(values):
    return lax.rsqrt(jnp.mean(values * values, axis=-1, keepdims=True) + eps)


def norm_back(values, scale, weighted):
    return scale * weighted - values * (scale * scale * scale) * jnp.mean(
        weighted * values, axis=-1, keepdims=True
    )


def rotate(values, cosine, sine):
    first, second = jnp.split(values, 2, axis=-1)
    return jnp.concatenate([first * cosine - second * sine, second * cosine + first * sine], axis=-1)


def layout_start(ends, row_ids):
    after = row_ids[:, None] >= ends[None, :]
    return jnp.max(jnp.where(after, ends[None, :], 0), axis=1)


def dot(left, right, dims):
    return lax.dot_general(left, right, (dims, ((), ())), preferred_element_type=f32)


def mm(left, right):
    return dot(left, right, ((1,), (0,)))


def mm_tn(left, right):
    return dot(left, right, ((0,), (0,)))


def mm_nt(left, right):
    return dot(left, right, ((1,), (1,)))


def swap(value, axis, bit):
    size = lax.axis_size(axis)
    return lax.ppermute(value, axis, [(i, i ^ bit) for i in range(size)])


def gather_seq(rows):
    far = swap(rows, "seq", 2)
    return jnp.concatenate([rows, swap(rows, "seq", 1), far, swap(far, "seq", 1)], axis=0)


def scatter_seq(parts):
    count = parts.shape[0] // 4
    piece = [parts[i * count : (i + 1) * count] for i in range(4)]
    far = piece[2] + swap(piece[3].astype(bf16), "seq", 1).astype(f32)
    near = piece[0] + swap(piece[1].astype(bf16), "seq", 1).astype(f32)
    return near + swap(far.astype(bf16), "seq", 2).astype(f32)


def gather_dp(shard):
    return lax.all_gather(shard, "dp", axis=0, tiled=True)


def scatter_dp(total):
    return lax.psum_scatter(total.astype(bf16), "dp", scatter_dimension=0, tiled=True)


def query_vectors(meta_ref, ends_ref, micro, rows):
    lanes = lax.broadcasted_iota(jnp.int32, (1, HEADS * rows), 1)
    ids = meta_ref[micro, 0] + lanes % rows
    start = jnp.zeros_like(ids)
    for index in range(ends_ref.shape[1]):
        end = ends_ref[micro, index]
        start = jnp.where(ids >= end, end, start)
    return ids, start


def masked_of(key_stretch, ids, start):
    key = key_stretch * STRETCH + lax.broadcasted_iota(jnp.int32, (STRETCH, 1), 0)
    return (key <= ids) & (key >= start)


def attend_kernel(rows, meta_ref, ends_ref, deal_ref, q_ref, kv_ref, o_ref, lse_ref, top, total, acc):
    micro, slot = pl.program_id(0), pl.program_id(1)

    @pl.when(slot == 0)
    def _():
        top[...] = jnp.full_like(top, masked_score)
        total[...] = jnp.zeros_like(total)
        acc[...] = jnp.zeros_like(acc)

    key_stretch = deal_ref[micro, slot]

    @pl.when((key_stretch <= meta_ref[micro, 1]) & (key_stretch >= meta_ref[micro, 2]))
    def _():
        ids, start = query_vectors(meta_ref, ends_ref, micro, rows)
        block = kv_ref[...].reshape(STRETCH, 2 * HEAD)
        query = q_ref[...].reshape(HEADS * rows, HEAD)
        scores = jnp.where(masked_of(key_stretch, ids, start), mm_nt(block[:, :HEAD], query), masked_score)
        old = top[...]
        new = jnp.maximum(old, jnp.max(scores, axis=0, keepdims=True))
        keep = jnp.exp(old - new)
        terms = jnp.exp(scores - new)
        top[...] = new
        total[...] = total[...] * keep + jnp.sum(terms, axis=0, keepdims=True)
        acc[...] = acc[...] * keep + mm_tn(block[:, HEAD:], terms.astype(bf16))

    @pl.when(slot == pl.num_programs(1) - 1)
    def _():
        out = acc[...] * (1.0 / total[...])
        o_ref[...] = out.T.reshape(o_ref.shape)
        lse_ref[...] = (top[...] + jnp.log(total[...])).reshape(lse_ref.shape)


def attend_back_kernel(
    rows, meta_ref, ends_ref, deal_ref, q_ref, dc_ref, lse_ref, delta_ref, kv_ref, dq_ref, dkv_ref, acc
):
    micro, slot = pl.program_id(0), pl.program_id(1)

    @pl.when(slot == 0)
    def _():
        acc[...] = jnp.zeros_like(acc)

    key_stretch = deal_ref[micro, slot]
    active = (key_stretch <= meta_ref[micro, 1]) & (key_stretch >= meta_ref[micro, 2])

    @pl.when(active)
    def _():
        ids, start = query_vectors(meta_ref, ends_ref, micro, rows)
        block = kv_ref[...].reshape(STRETCH, 2 * HEAD)
        key, value = block[:, :HEAD], block[:, HEAD:]
        query = q_ref[...].reshape(HEADS * rows, HEAD)
        grad = dc_ref[...].reshape(HEADS * rows, HEAD)
        probs = jnp.where(
            masked_of(key_stretch, ids, start),
            jnp.exp(mm_nt(key, query) - lse_ref[...].reshape(1, HEADS * rows)),
            0.0,
        )
        score_grad = probs * (mm_nt(value, grad) - delta_ref[...].reshape(1, HEADS * rows))
        score_grad = score_grad.astype(bf16)
        acc[...] += mm_tn(key, score_grad)
        key_grad = mm(score_grad, query)
        value_grad = mm(probs.astype(bf16), grad)
        both = jnp.concatenate([key_grad, value_grad], axis=1)
        dkv_ref[...] = both.astype(bf16).reshape(dkv_ref.shape)

    @pl.when(jnp.logical_not(active))
    def _():
        dkv_ref[...] = jnp.zeros_like(dkv_ref)

    @pl.when(slot == pl.num_programs(1) - 1)
    def _():
        dq_ref[...] = (acc[...].T * HEAD**-0.5).reshape(dq_ref.shape)


def attend(meta, ends, deal, query, keys):
    rows, slots = query.shape[2], deal.shape[1]
    wide = HEADS * rows
    per_micro = pl.BlockSpec((1, HEADS, rows, HEAD), lambda b, j, *_: (b, 0, 0, 0))
    line = pl.BlockSpec((1, 1, wide), lambda b, j, *_: (b, 0, 0))
    key_spec = pl.BlockSpec((STRETCH // rows, None, rows, 2 * HEAD), lambda b, j, *_: (j, b, 0, 0))
    return pl.pallas_call(
        functools.partial(attend_kernel, rows),
        grid_spec=pltpu.PrefetchScalarGridSpec(
            num_scalar_prefetch=3,
            grid=(MB, slots),
            in_specs=[per_micro, key_spec],
            out_specs=[per_micro, line],
            scratch_shapes=[
                pltpu.VMEM((1, wide), f32),
                pltpu.VMEM((1, wide), f32),
                pltpu.VMEM((HEAD, wide), f32),
            ],
        ),
        out_shape=[
            jax.ShapeDtypeStruct(query.shape, f32),
            jax.ShapeDtypeStruct((MB, 1, wide), f32),
        ],
        name="attend",
        cost_estimate=pl.CostEstimate(
            flops=4 * MB * 9 * STRETCH * wide * HEAD, bytes_accessed=2 * keys.size, transcendentals=MB * 9 * STRETCH * wide
        ),
    )(meta, ends, deal, query, keys)


def attend_back(meta, ends, deal, query, grad, lse, delta, keys):
    rows, slots = query.shape[2], deal.shape[1]
    wide = HEADS * rows
    per_micro = pl.BlockSpec((1, HEADS, rows, HEAD), lambda b, j, *_: (b, 0, 0, 0))
    line = pl.BlockSpec((1, 1, wide), lambda b, j, *_: (b, 0, 0))
    key_spec = pl.BlockSpec((STRETCH // rows, None, rows, 2 * HEAD), lambda b, j, *_: (j, b, 0, 0))
    return pl.pallas_call(
        functools.partial(attend_back_kernel, rows),
        grid_spec=pltpu.PrefetchScalarGridSpec(
            num_scalar_prefetch=3,
            grid=(MB, slots),
            in_specs=[per_micro, per_micro, line, line, key_spec],
            out_specs=[per_micro, key_spec],
            scratch_shapes=[pltpu.VMEM((HEAD, wide), f32)],
        ),
        out_shape=[
            jax.ShapeDtypeStruct(query.shape, f32),
            jax.ShapeDtypeStruct(keys.shape, bf16),
        ],
        name="attend_back",
        cost_estimate=pl.CostEstimate(
            flops=10 * MB * 9 * STRETCH * wide * HEAD, bytes_accessed=4 * keys.size, transcendentals=MB * 9 * STRETCH * wide
        ),
    )(meta, ends, deal, query, grad, lse, delta, keys)


def per_device(
    inputs,
    cotangent,
    lengths,
    deal,
    w_query,
    w_key,
    w_value,
    w_out,
    w_gate,
    w_up,
    w_down,
    gain_attn_pre,
    gain_attn_post,
    gain_ffw_pre,
    gain_ffw_post,
    gain_query,
    gain_key,
):
    rows, width = inputs.shape[1], inputs.shape[2]
    groups, members = lax.axis_size("dp"), lax.axis_size("seq")
    devices = groups * members
    total_rows = rows * devices
    dp_id, seq_id = lax.axis_index("dp"), lax.axis_index("seq")
    device_id = dp_id * members + seq_id
    count = MB * rows
    model_rows = w_query.shape[0]
    ff_rows = w_down.shape[0]
    ff_local = groups * ff_rows
    wide_q = HEADS * HEAD
    wide_qkv = wide_q + 2 * HEAD
    gain_rows, head_rows = gain_attn_pre.shape[0], gain_query.shape[0]
    gain_sizes = [gain_rows] * 4 + [head_rows] * 2
    gain_total = sum(gain_sizes)

    gains = jnp.concatenate([gain_attn_pre, gain_attn_post, gain_ffw_pre, gain_ffw_post, gain_query, gain_key])
    gain_line = jnp.pad(gains[None, :], ((0, 0), (0, wide_qkv - gain_total)))
    attn_shard = jnp.concatenate([jnp.concatenate([w_query, w_key, w_value], axis=1), gain_line], axis=0)
    attn_all = lax.all_gather(attn_shard, ALL, axis=0, tiled=False)
    w_qkv = attn_all[:, :model_rows].reshape(devices * model_rows, wide_qkv)
    gain_all = attn_all[:, model_rows, :gain_total].astype(f32)
    full_gain, at = [], 0
    for size in gain_sizes:
        full_gain.append(gain_all[:, at : at + size].reshape(devices * size))
        at += size
    pre_attention, post_attention, pre_feed, post_feed, query_gain, key_gain = full_gain
    out_weight = lax.all_gather(w_out, ALL, axis=0, tiled=True)

    def columns_to_members(weight):
        split = weight.reshape(model_rows, groups, members, ff_rows)
        split = split.transpose(2, 0, 1, 3).reshape(members, model_rows, ff_local)
        moved = lax.all_to_all(split, "seq", split_axis=0, concat_axis=0, tiled=True)
        return gather_dp(moved.reshape(members * model_rows, ff_local))

    gate_weight = columns_to_members(w_gate)
    up_weight = columns_to_members(w_up)
    down_weight = gather_dp(w_down)

    ends = jnp.cumsum(lengths, axis=1)
    local_ids = jnp.arange(rows, dtype=jnp.int32)
    stretches = lax.dynamic_index_in_dim(deal, device_id * rows // STRETCH, 1, keepdims=False)
    first_rows = stretches * STRETCH + device_id * rows % STRETCH
    my_rows = first_rows[:, None] + local_ids[None, :]
    starts = jnp.stack([layout_start(ends[b], my_rows[b]) for b in range(MB)])
    meta = jnp.stack([first_rows, stretches, starts[:, 0] // STRETCH], axis=1)
    positions = (my_rows - starts).reshape(count)
    valid = (my_rows < total_rows - STRETCH).reshape(count, 1)
    freqs = rope_base ** (-2.0 * jnp.arange(HEAD // 2, dtype=f32) / HEAD)
    angle = positions.astype(f32)[:, None, None] * freqs
    cosine, sine = jnp.cos(angle), jnp.sin(angle)

    rows_in = inputs.reshape(count, width).astype(f32)
    scale_one = norm_scale(rows_in)
    normed_one = (rows_in * scale_one * pre_attention).astype(bf16)
    qkv = mm(normed_one, w_qkv)
    query_raw = qkv[:, :wide_q].reshape(count, HEADS, HEAD)
    key_raw = qkv[:, wide_q : wide_q + HEAD].reshape(count, 1, HEAD)
    value_low = qkv[:, wide_q + HEAD :].astype(bf16)
    query_scale = norm_scale(query_raw)
    query_rot = rotate(query_raw * query_scale * query_gain, cosine, sine).astype(bf16) * HEAD**-0.5
    key_scale = norm_scale(key_raw)
    key_rot = rotate(key_raw * key_scale * key_gain, cosine, sine).astype(bf16)

    def to_heads(values):
        return values.reshape(MB, rows, HEADS, HEAD).transpose(0, 2, 1, 3)

    def from_heads(values):
        return values.transpose(0, 2, 1, 3).reshape(count, HEADS, HEAD)

    query_heads = to_heads(query_rot.astype(bf16))
    keys_mine = jnp.concatenate([key_rot[:, 0], value_low], axis=1).reshape(MB, rows, 2 * HEAD)
    keys_all = lax.all_gather(keys_mine, ALL, axis=0, tiled=False)
    context, lse = attend(meta, ends, deal, query_heads, keys_all)
    context_rows = from_heads(context.astype(bf16)).reshape(count, wide_q)
    attended = mm(context_rows, out_weight)
    scale_two = norm_scale(attended)
    hidden_res = rows_in + attended * scale_two * post_attention
    scale_three = norm_scale(hidden_res)
    normed_two = (hidden_res * scale_three * pre_feed).astype(bf16)

    normed_group = gather_seq(normed_two)
    gate_raw = mm(normed_group, gate_weight)
    up_raw = mm(normed_group, up_weight)
    hidden_low = (jax.nn.gelu(gate_raw, approximate=True) * up_raw).astype(bf16)
    mixed = scatter_seq(mm(hidden_low, down_weight))
    scale_four = norm_scale(mixed)
    result = hidden_res + mixed * scale_four * post_feed
    output = jnp.where(valid, result, 0.0).astype(bf16)

    upstream = jnp.where(valid, cotangent.reshape(count, width).astype(f32), 0.0)
    grad_post_feed = jnp.sum(upstream * mixed * scale_four, axis=0)
    mixed_grad = norm_back(mixed, scale_four, post_feed * upstream).astype(bf16)
    mixed_group = gather_seq(mixed_grad)
    hidden_grad = mm_nt(mixed_group, down_weight)
    _, gelu_pull = jax.vjp(lambda g, u: jax.nn.gelu(g, approximate=True) * u, gate_raw, up_raw)
    gate_grad, up_grad = gelu_pull(hidden_grad)
    gate_grad, up_grad = gate_grad.astype(bf16), up_grad.astype(bf16)
    normed_two_grad = scatter_seq(mm_nt(gate_grad, gate_weight) + mm_nt(up_grad, up_weight))
    grad_down = scatter_dp(mm_tn(hidden_low, mixed_group)).astype(f32)

    def columns_home(total):
        mine = scatter_dp(total).reshape(members, model_rows, ff_local)
        moved = lax.all_to_all(mine, "seq", split_axis=0, concat_axis=0, tiled=True)
        split = moved.reshape(members, model_rows, groups, ff_rows).transpose(1, 2, 0, 3)
        return split.reshape(model_rows, devices * ff_rows).astype(f32)

    grad_gate = columns_home(mm_tn(normed_group, gate_grad))
    grad_up = columns_home(mm_tn(normed_group, up_grad))
    grad_pre_feed = jnp.sum(normed_two_grad * hidden_res * scale_three, axis=0)
    hidden_res_grad = upstream + norm_back(hidden_res, scale_three, pre_feed * normed_two_grad)

    grad_post_attention = jnp.sum(hidden_res_grad * attended * scale_two, axis=0)
    attended_grad = norm_back(attended, scale_two, post_attention * hidden_res_grad).astype(bf16)
    grad_out = lax.psum_scatter(
        mm_tn(context_rows, attended_grad).astype(bf16), ALL, scatter_dimension=0, tiled=True
    ).astype(f32)
    context_grad = to_heads(mm_nt(attended_grad, out_weight).astype(bf16))
    delta = jnp.sum(context_grad.astype(f32) * context, axis=-1).reshape(MB, 1, HEADS * rows)
    query_grads, key_parts = attend_back(
        meta, ends, deal, query_heads, context_grad, lse, delta, keys_all
    )
    key_grads = lax.psum_scatter(key_parts, ALL, scatter_dimension=0, tiled=False)
    key_grads = key_grads.reshape(count, 2 * HEAD)
    value_grad = key_grads[:, HEAD:].astype(bf16)
    key_turned = rotate(key_grads[:, None, :HEAD].astype(f32), cosine, -sine)
    grad_key_gain = jnp.sum(key_turned * key_raw * key_scale, axis=(0, 1))
    key_grad = norm_back(key_raw, key_scale, key_gain * key_turned)[:, 0, :].astype(bf16)
    query_turned = rotate(from_heads(query_grads), cosine, -sine)
    grad_query_gain = jnp.sum(query_turned * query_raw * query_scale, axis=(0, 1))
    query_grad = norm_back(query_raw, query_scale, query_gain * query_turned)
    query_grad = query_grad.reshape(count, wide_q).astype(bf16)
    qkv_grad = jnp.concatenate([query_grad, key_grad, value_grad], axis=1)
    normed_one_grad = mm_nt(qkv_grad, w_qkv)
    grad_pre_attention = jnp.sum(normed_one_grad * rows_in * scale_one, axis=0)
    rows_grad = hidden_res_grad + norm_back(rows_in, scale_one, pre_attention * normed_one_grad)
    input_grad = rows_grad.astype(bf16)
    grad_qkv = mm_tn(normed_one, qkv_grad).reshape(devices, model_rows, wide_qkv)
    gain_grads = [
        grad_pre_attention,
        grad_post_attention,
        grad_pre_feed,
        grad_post_feed,
        grad_query_gain,
        grad_key_gain,
    ]
    gain_grads = jnp.concatenate([g.reshape(devices, -1) for g in gain_grads], axis=1)
    gain_grads = jnp.pad(gain_grads, ((0, 0), (0, wide_qkv - gain_total)))[:, None, :]
    last = jnp.concatenate([grad_qkv, gain_grads], axis=1).astype(bf16)
    last = lax.psum_scatter(last, ALL, scatter_dimension=0, tiled=False).astype(f32)
    gain_out, at = [], 0
    for size in gain_sizes:
        gain_out.append(last[model_rows, at : at + size])
        at += size
    return (
        output.reshape(inputs.shape),
        input_grad.reshape(inputs.shape),
        last[:model_rows, :wide_q],
        last[:model_rows, wide_q : wide_q + HEAD],
        last[:model_rows, wide_q + HEAD :],
        grad_out,
        grad_gate,
        grad_up,
        grad_down,
        *gain_out,
    )


def solution(mesh):
    split = P(None, ALL, None)
    weight, gain = P(ALL, None), P(ALL)
    return jax.shard_map(
        per_device,
        mesh=mesh,
        in_specs=(split, split, P(), P(), *[weight] * 7, *[gain] * 6),
        out_specs=(split, split, *[weight] * 7, *[gain] * 6),
        check_vma=False,
    )
```

time: 2960 us -> 1230 us (0.42)
  blocking collectives: 1230 us -> 30.9 us
  waiting for transfers between devices: 229 us -> 916 us
  loops' own time: 392 us -> 0 us
  local copies, waits for them, and re-layouts: 352 us -> 53.8 us
  matrix products: 363 us -> 107 us
  other arithmetic: 222 us -> 39.5 us
  starting transfers between devices: 132 us -> 15.1 us
  Pallas kernels: 0 us -> 46.3 us
    unnamed x4 -> x0, blocking collectives: 1150 us -> none
    reduce_scatter x3 -> x5, waiting for transfers between devices: 0.02 us -> 468 us  [the longest x2 162 us: scatter_dp(): lax.psum_scatter(total.astype(bf16), 'dp', scatter_dimension=0, tiled=True)]
    another operation x290 -> x0, loops' own time: 392 us -> none  [the longest x2 168 us: per_device(): lax.map(one_block, jnp.arange(tok_rows * lax.axis_size(('dp', 'seq')) //...]
    dot_general x174 -> x15, matrix products: 363 us -> 107 us  [dot(): lax.dot_general(left, right, (dims, ((), ())), preferred_element_type=f32)]
    reduce_or x208 -> x0, other arithmetic: 171 us -> none  [the longest x64 54.7 us: one_block(): total = lax.cond(jnp.any(mask), one_update, keep_state, total)]
    dynamic_slice x238 -> x0, local copies, waits for them, and re-layouts: 161 us -> none  [the longest x64 58.4 us: one_block(): block = lax.dynamic_slice_in_dim(keys_all, first_row, tok_rows, 0)]
    unnamed x352 -> x126, local copies, waits for them, and re-layouts: 124 us -> 8.94 us
    unnamed x21 -> x1, starting transfers between devices: 103 us -> 0.25 us
  transfers between devices with their start and end apart: 39 -> 26, of which waited for: 10 -> 19; matrix products, arithmetic and copies ran while one was open for 63% -> 10% of each run, Pallas kernels for 0% -> 2%
where the time goes in v1:
time: 1230 us; the launch traced here: 1220 us
  waiting for transfers between devices  916 us (74%)
  matrix products  107 us (9%)
  local copies, waits for them, and re-layouts  53.8 us (4%)
  Pallas kernels  46.3 us (4%)
  other arithmetic  39.5 us (3%)
  blocking collectives  30.9 us (3%)
  between operations  15.7 us (1%)
  starting transfers between devices  15.1 us (1%)
    all_gather x3, waiting for transfers between devices, gather_dp(): return lax.all_gather(shard, 'dp', axis=0, tiled=True)  172 us
    reduce_scatter x2, waiting for transfers between devices, scatter_dp(): lax.psum_scatter(total.astype(bf16), 'dp', scatter_dimension=0, tiled=True)  162 us
    reduce_scatter x1, waiting for transfers between devices, per_device(): lax.psum_scatter(key_parts, ALL, scatter_dimension=0, tiled=False)  112 us
    dot_general x15, matrix products, dot(): lax.dot_general(left, right, (dims, ((), ())), preferred_element_type=f32)  107 us
    reduce_scatter x1, waiting for transfers between devices, per_device(): lax.psum_scatter(mm_tn(context_rows, attended_grad).astype(bf16), ALL, sc...  98.7 us
    reduce_scatter x1, waiting for transfers between devices, per_device(): lax.psum_scatter(last, ALL, scatter_dimension=0, tiled=False).astype(f32)  94.8 us
    unnamed x13, waiting for transfers between devices  87.4 us
    all_gather x1, waiting for transfers between devices, per_device(): attn_all = lax.all_gather(attn_shard, ALL, axis=0, tiled=False)  59.3 us
  transfers between devices with their start and end apart: 26, of which 19 were waited for; matrix products, arithmetic and copies ran while one was open for 10% of the time, Pallas kernels for 2%

profile of v1, /device:TPU:0, one launch (start us, length us, event | category | flops | bytes accessed | tf_op | source)
XLA Modules:
  0.0 1224.3 jit_solution(10592876627409439424)
XLA Ops:
  17.4 59.3 %all-gather.19.cloned.1.call-done = bf16[32,37,1536]{2,1,0:T(8,128)(2,1)} async-done(((bf16[1,37,1536]{2,1,0:T(8,128)(2,1)}), bf16[32,37,1536]{2,1,0:T(8,128)(2,1)}) %all-gather.19.cloned.1.call-update) | async-done | bytes 3637264 | tf_op jit(solution)/shard_map/all_gather | solution.py:267
  94.0 13.7 %all_to_all.20 = bf16[4,36,1728]{2,1,0:T(8,128)(2,1)S(1)} all-to-all(bf16[4,36,1728]{2,1,0:T(8,128)(2,1)S(1)} %copy.145), channel_id=1, replica_groups=mesh['dp'=8,'seq'=4] {'seq'}, dimensions={0} | all-to-all | bytes 995328 | tf_op jit(solution)/shard_map/all_to_all | solution.py:280
  112.6 17.2 %all_to_all.21 = bf16[4,36,1728]{2,1,0:T(8,128)(2,1)S(1)} all-to-all(bf16[4,36,1728]{2,1,0:T(8,128)(2,1)S(1)} %copy.147), channel_id=1, replica_groups=mesh['dp'=8,'seq'=4] {'seq'}, dimensions={0} | all-to-all | bytes 995328 | tf_op jit(solution)/shard_map/all_to_all | solution.py:280
  136.5 35.7 %all-gather.9.cloned.1.call-done.kv_ref = bf16[32,2,128,512]{3,2,1,0:T(8,128)(2,1)} async-done(((bf16[1,2,128,512]{3,2,1,0:T(8,128)(2,1)}), bf16[32,2,128,512]{3,2,1,0:T(8,128)(2,1)}) %all-gather.9.cloned.1.call-update) | async-done | bytes 8388624 | tf_op jit(solution)/shard_map/all_gather | solution.py:320
  172.3 21.3 %attend.1 = (f32[2,4,128,256]{3,2,1,0:T(8,128)}, f32[2,1,512]{2,1,0:T(1,128)}) custom-call(s32[2,3]{1,0:T(2,128)} %pad_add_fusion.1.meta_ref, s32[2,4]{1,0:T(2,128)} %copy-done.48, s32[2,16]{1,0:T(2,128)} %deal_ref.3, bf16[2,4,128,256]{3,2,1,0:T(8,128)(2,1)} %fusion.37.q_ref, bf16[32,2,128,512]{3,2,1,0:T(8,128)(2,1)} %all-gather.9.cloned.1.call-done.kv_ref), custom_call_target="tpu_custom_call" | custom-call | flops 2415919104 | bytes 8388608 | tf_op jit(solution)/shard_map/attend/pallas_call | solution.py:179
  195.4 35.5 %all-gather.11.cloned.1.call-done = bf16[1024,1152]{1,0:T(8,128)(2,1)} async-done(((bf16[32,1152]{1,0:T(8,128)(2,1)}), bf16[1024,1152]{1,0:T(8,128)(2,1)}) %all-gather.11.cloned.1.call-update) | async-done | bytes 2359312 | tf_op jit(solution)/shard_map/all_gather | solution.py:275
  238.4 14.3 %collective-permute-done.1 = bf16[256,1152]{1,0:T(8,128)(2,1)} collective-permute-done((bf16[256,1152]{1,0:T(8,128)(2,1)}, bf16[256,1152]{1,0:T(8,128)(2,1)}, u32[]{:S(2)}, u32[]{:S(2)}) %collective-permute-start.1) | collective-permute-done | bytes 589856 | tf_op jit(solution)/shard_map/ppermute | solution.py:61
  252.8 51.5 %all-gather.13.cloned.1.call-done = bf16[1152,1728]{1,0:T(8,128)(2,1)} async-done(((bf16[144,1728]{1,0:T(8,128)(2,1)}), bf16[1152,1728]{1,0:T(8,128)(2,1)}) %all-gather.13.cloned.1.call-update) | async-done | bytes 3981328 | tf_op jit(solution)/shard_map/all_gather | solution.py:78
  304.3 10.5 fusion.68
  314.8 62.6 %all-gather.15.cloned.1.call-done = bf16[1152,1728]{1,0:T(8,128)(2,1)} async-done(((bf16[144,1728]{1,0:T(8,128)(2,1)}), bf16[1152,1728]{1,0:T(8,128)(2,1)}) %all-gather.15.cloned.1.call-update) | async-done | bytes 3981328 | tf_op jit(solution)/shard_map/all_gather | solution.py:78
  377.4 13.3 %multiply_convert_fusion.1 = (bf16[1024,1728]{0,1:T(8,128)(2,1)}, f32[1024,1728]{0,1:T(8,128)}) fusion(f32[1024,1728]{0,1:T(8,128)} %fusion.68, bf16[1152,1728]{1,0:T(8,128)(2,1)} %all-gather.15.cloned.1.call-done, bf16[256,1152]{1,0:T(8,128)(2,1)} %collective-permute-done.2, bf16[256,1152]{1,0:T(8,128)(2,1)} %collective-permute-done.1, ...), kind=kOutput, calls=%fused_computation.13 | convolution fusion | flops 4103995392 | bytes 24035328 | tf_op jit(solution)/shard_map/dot_general | solution.py:44
  390.8 57.4 %all-gather.17.cloned.1.call-done = bf16[1728,1152]{1,0:T(8,128)(2,1)} async-done(((bf16[216,1152]{1,0:T(8,128)(2,1)}), bf16[1728,1152]{1,0:T(8,128)(2,1)}) %all-gather.17.cloned.1.call-update) | async-done | bytes 3981328 | tf_op jit(solution)/shard_map/all_gather | solution.py:78
  463.8 12.2 collective-permute-done.5
  481.9 13.0 %collective-permute-done.7 = bf16[256,1152]{1,0:T(8,128)(2,1)S(1)} collective-permute-done((bf16[256,1152]{1,0:T(8,128)(2,1)S(1)}, bf16[256,1152]{1,0:T(8,128)(2,1)S(1)}, u32[]{:S(2)}, u32[]{:S(2)}) %collective-permute-start.7) | collective-permute-done | bytes 589856 | tf_op jit(solution)/shard_map/ppermute | solution.py:61
  497.0 15.6 %multiply_convert_fusion = (bf16[1024,1728]{0,1:T(8,128)(2,1)}, bf16[1024,1728]{0,1:T(8,128)(2,1)}) fusion(f32[1024,1728]{0,1:T(8,128)} %fusion.68, f32[1024,1728]{0,1:T(8,128)} %get-tuple-element.102, bf16[1728,1152]{1,0:T(8,128)(2,1)S(1)} %copy-done.54, bf16[256,1152]{1,0:T(8,128)(2,1)S(1)} %collective-permute-done.8, ...), kind=kOutput, calls=%fused_computation.12 | convolution fusion | flops 4128768000 | bytes 27574272 | tf_op jit(solution)/shard_map/dot_general | solution.py:44
  512.7 9.4 fusion.80
  533.1 13.9 %collective-permute-done.11 = bf16[256,1152]{1,0:T(8,128)(2,1)S(1)} collective-permute-done((bf16[256,1152]{1,0:T(8,128)(2,1)S(1)}, bf16[256,1152]{1,0:T(8,128)(2,1)S(1)}, u32[]{:S(2)}, u32[]{:S(2)}) %collective-permute-start.11) | collective-permute-done | bytes 589856 | tf_op jit(solution)/shard_map/ppermute | solution.py:61
  556.4 25.0 %attend_back.1 = (f32[2,4,128,256]{3,2,1,0:T(8,128)}, bf16[32,2,128,512]{3,2,1,0:T(8,128)(2,1)}) custom-call(s32[2,3]{1,0:T(2,128)} %pad_add_fusion.1.meta_ref, s32[2,4]{1,0:T(2,128)} %copy-done.48, s32[2,16]{1,0:T(2,128)} %deal_ref.3, bf16[2,4,128,256]{3,2,1,0:T(8,128)(2,1)} %fusion.37.q_ref, bf16[2,4,128,256]{3,2,1,0:T(8,128)(2,1)} %bitcast.197, ...), custom_call_target="tpu_custom_call" | custom-call | flops 6039797760 | bytes 16777216 | tf_op jit(solution)/shard_map/attend_back/pallas_call | solution.py:209
  621.3 112.3 %reduce-scatter.9.cloned.1.call-done = bf16[1,2,128,512]{3,2,1,0:T(8,128)(2,1)} async-done(((bf16[32,2,128,512]{3,2,1,0:T(8,128)(2,1)}), bf16[1,2,128,512]{3,2,1,0:T(8,128)(2,1)}) %reduce-scatter.9.cloned.1.call-update) | async-done | bytes 262160 | tf_op jit(solution)/shard_map/reduce_scatter | solution.py:370
  744.5 76.5 %reduce-scatter.17.cloned.1.call-done = bf16[144,1728]{1,0:T(8,128)(2,1)} async-done(((bf16[1152,1728]{1,0:T(8,128)(2,1)}), bf16[144,1728]{1,0:T(8,128)(2,1)}) %reduce-scatter.17.cloned.1.call-update) | async-done | bytes 497680 | tf_op jit(solution)/shard_map/reduce_scatter | solution.py:82
  826.4 85.7 %reduce-scatter.15.cloned.1.call-done = bf16[144,1728]{1,0:T(8,128)(2,1)} async-done(((bf16[1152,1728]{1,0:T(8,128)(2,1)}), bf16[144,1728]{1,0:T(8,128)(2,1)}) %reduce-scatter.15.cloned.1.call-update) | async-done | bytes 497680 | tf_op jit(solution)/shard_map/reduce_scatter | solution.py:82
  917.9 98.7 %reduce-scatter.13.cloned.1.call-done = bf16[32,1152]{1,0:T(8,128)(2,1)} async-done(((bf16[1024,1152]{1,0:T(8,128)(2,1)}), bf16[32,1152]{1,0:T(8,128)(2,1)}) %reduce-scatter.13.cloned.1.call-update) | async-done | bytes 73744 | tf_op jit(solution)/shard_map/reduce_scatter | solution.py:362
  1018.1 86.0 %reduce-scatter.19.cloned.1.call-done = bf16[216,1152]{1,0:T(8,128)(2,1)} async-done(((bf16[1728,1152]{1,0:T(8,128)(2,1)}), bf16[216,1152]{1,0:T(8,128)(2,1)}) %reduce-scatter.19.cloned.1.call-update) | async-done | bytes 497680
  1118.8 94.8 %reduce-scatter.11.cloned.1.call-done = bf16[1,37,1536]{2,1,0:T(8,128)(2,1)} async-done(((bf16[32,37,1536]{2,1,0:T(8,128)(2,1)}), bf16[1,37,1536]{2,1,0:T(8,128)(2,1)}) %reduce-scatter.11.cloned.1.call-update) | async-done | bytes 113680 | tf_op jit(solution)/shard_map/reduce_scatter | solution.py:397
  (308 shorter events, 172.9 us)
Async XLA Ops:
  7.2 69.5 %all-gather.19.cloned.1.call-start = ((), (), s32[]{:S(2)}) async-start(), calls=%async_computation.20 | async-start | bytes 4055040 | tf_op jit(solution)/shard_map/all_gather | solution.py:267
  12.9 159.3 %all-gather.9.cloned.1.call-start = ((), (), s32[]{:S(2)}) async-start(), calls=%async_computation.10 | async-start | bytes 8650752 | tf_op jit(solution)/shard_map/all_gather | solution.py:320
  90.5 140.4 %all-gather.11.cloned.1.call-start = ((), (), s32[]{:S(2)}) async-start(), calls=%async_computation.11 | async-start | bytes 2433024 | tf_op jit(solution)/shard_map/all_gather | solution.py:275
  91.2 213.1 %all-gather.13.cloned.1.call-start = ((), (), s32[]{:S(2)}) async-start(), calls=%async_computation.12 | async-start | bytes 4644864 | tf_op jit(solution)/shard_map/all_gather | solution.py:78
  108.7 268.7 %all-gather.15.cloned.1.call-start = ((), (), s32[]{:S(2)}) async-start(), calls=%async_computation.13 | async-start | bytes 4644864 | tf_op jit(solution)/shard_map/all_gather | solution.py:78
  130.8 317.4 %all-gather.17.cloned.1.call-start = ((), (), s32[]{:S(2)}) async-start(), calls=%async_computation.14 | async-start | bytes 4478976 | tf_op jit(solution)/shard_map/all_gather | solution.py:78
  131.4 602.2 %reduce-scatter.9.cloned.1.call-start = ((), (), s32[]{:S(2)}) async-start(), calls=%async_computation.15 | async-start | bytes 8650752 | tf_op jit(solution)/shard_map/reduce_scatter | solution.py:370
  237.0 15.8 %collective-permute-start.1 = (bf16[256,1152]{1,0:T(8,128)(2,1)}, bf16[256,1152]{1,0:T(8,128)(2,1)}, u32[]{:S(2)}, u32[]{:S(2)}) collective-permute-start(bf16[256,1152]{1,0:T(8,128)(2,1)} %multiply_convert_fusion.2), channel_id=1, source_target_pairs={{0,2},{1,3},{2,0},{3,1},{4,6},{5,7},{6,4},{7,5},{8,10},{9,11},{10,... | collective-permute-start | bytes 1769480 | tf_op jit(solution)/shard_map/ppermute | solution.py:61
  238.4 65.9 %collective-permute-start = (bf16[256,1152]{1,0:T(8,128)(2,1)}, bf16[256,1152]{1,0:T(8,128)(2,1)}, u32[]{:S(2)}, u32[]{:S(2)}) collective-permute-start(bf16[256,1152]{1,0:T(8,128)(2,1)} %multiply_convert_fusion.2), channel_id=1, source_target_pairs={{0,1},{1,0},{2,3},{3,2},{4,5},{5,4},{6,7},{7,6},{8,9},{9,8},{10,11... | collective-permute-start | bytes 1769480 | tf_op jit(solution)/shard_map/ppermute | solution.py:61
  252.8 51.5 %collective-permute-start.2 = (bf16[256,1152]{1,0:T(8,128)(2,1)}, bf16[256,1152]{1,0:T(8,128)(2,1)}, u32[]{:S(2)}, u32[]{:S(2)}) collective-permute-start(bf16[256,1152]{1,0:T(8,128)(2,1)} %collective-permute-done.1), channel_id=1, source_target_pairs={{0,1},{1,0},{2,3},{3,2},{4,5},{5,4},{6,7},{7,6},{8,9},{9,8},{10,11... | collective-permute-start | bytes 1769480 | tf_op jit(solution)/shard_map/ppermute | solution.py:61
  457.4 6.4 collective-permute-start.3
  460.3 15.7 %collective-permute-start.5 = (bf16[256,1152]{1,0:T(8,128)(2,1)}, bf16[256,1152]{1,0:T(8,128)(2,1)}, u32[]{:S(2)}, u32[]{:S(2)}) collective-permute-start(bf16[256,1152]{1,0:T(8,128)(2,1)} %fusion.9), channel_id=1, source_target_pairs={{0,2},{1,3},{2,0},{3,1},{4,6},{5,7},{6,4},{7,5},{8,10},{9,11},{10,... | collective-permute-start | bytes 1769480 | tf_op jit(solution)/shard_map/ppermute | solution.py:61
  480.5 14.5 %collective-permute-start.7 = (bf16[256,1152]{1,0:T(8,128)(2,1)S(1)}, bf16[256,1152]{1,0:T(8,128)(2,1)S(1)}, u32[]{:S(2)}, u32[]{:S(2)}) collective-permute-start(bf16[256,1152]{1,0:T(8,128)(2,1)S(1)} %get-tuple-element.53), channel_id=1, source_target_pairs={{0,2},{1,3},{2,0},{3,1},{4,6},{5,7},{6,4},{7,5},{8,10},{9,11},{10,... | collective-permute-start | bytes 1769480 | tf_op jit(solution)/shard_map/ppermute | solution.py:61
  481.9 13.0 %collective-permute-start.6 = (bf16[256,1152]{1,0:T(8,128)(2,1)S(1)}, bf16[256,1152]{1,0:T(8,128)(2,1)S(1)}, u32[]{:S(2)}, u32[]{:S(2)}) collective-permute-start(bf16[256,1152]{1,0:T(8,128)(2,1)S(1)} %get-tuple-element.53), channel_id=1, source_target_pairs={{0,1},{1,0},{2,3},{3,2},{4,5},{5,4},{6,7},{7,6},{8,9},{9,8},{10,11... | collective-permute-start | bytes 1769480 | tf_op jit(solution)/shard_map/ppermute | solution.py:61
  529.3 2.1 collective-permute-start.10
  529.5 3.5 collective-permute-start.9
  531.5 15.4 %collective-permute-start.11 = (bf16[256,1152]{1,0:T(8,128)(2,1)S(1)}, bf16[256,1152]{1,0:T(8,128)(2,1)S(1)}, u32[]{:S(2)}, u32[]{:S(2)}) collective-permute-start(bf16[256,1152]{1,0:T(8,128)(2,1)S(1)} %fusion.7), channel_id=1, source_target_pairs={{0,2},{1,3},{2,0},{3,1},{4,6},{5,7},{6,4},{7,5},{8,10},{9,11},{10,... | collective-permute-start | bytes 1769480 | tf_op jit(solution)/shard_map/ppermute | solution.py:61
  581.4 239.5 %reduce-scatter.17.cloned.1.call-start = ((), (), s32[]{:S(2)}) async-start(), calls=%async_computation.19 | async-start | bytes 4644864 | tf_op jit(solution)/shard_map/reduce_scatter | solution.py:82
  590.9 321.2 %reduce-scatter.15.cloned.1.call-start = ((), (), s32[]{:S(2)}) async-start(), calls=%async_computation.18 | async-start | bytes 4644864 | tf_op jit(solution)/shard_map/reduce_scatter | solution.py:82
  600.2 416.3 %reduce-scatter.13.cloned.1.call-start = ((), (), s32[]{:S(2)}) async-start(), calls=%async_computation.17 | async-start | bytes 2433024 | tf_op jit(solution)/shard_map/reduce_scatter | solution.py:362
  603.6 500.6 %reduce-scatter.19.cloned.1.call-start = ((), (), s32[]{:S(2)}) async-start(), calls=%async_computation.21 | async-start | bytes 4478976
  613.1 600.6 %reduce-scatter.11.cloned.1.call-start = ((), (), s32[]{:S(2)}) async-start(), calls=%async_computation.16 | async-start | bytes 4055040 | tf_op jit(solution)/shard_map/reduce_scatter | solution.py:397
  822.9 91.2 %all-to-all-start.3 = ((bf16[4,36,1728]{2,1,0:T(8,128)(2,1)}), bf16[4,36,1728]{2,1,0:T(8,128)(2,1)S(1)}, u32[]{:S(2)}, u32[]{:S(2)}) async-start(bf16[4,36,1728]{2,1,0:T(8,128)(2,1)} %reshape.572), calls=%async_computation.8 | async-start | bytes 1146880 | tf_op jit(solution)/shard_map/all_to_all | solution.py:351
  914.1 196.0 %all-to-all-start.2 = ((bf16[4,36,1728]{2,1,0:T(8,128)(2,1)}), bf16[4,36,1728]{2,1,0:T(8,128)(2,1)S(1)}, u32[]{:S(2)}, u32[]{:S(2)}) async-start(bf16[4,36,1728]{2,1,0:T(8,128)(2,1)} %reshape.571), calls=%async_computation.6 | async-start | bytes 1146880 | tf_op jit(solution)/shard_map/all_to_all | solution.py:351
  (61 other events, 1786.3 us)
Sparse Core Ops, SparseCore 0:
  13.1 63.5 all-gather.18
  90.6 81.6 all-gather.8
  175.2 55.6 all-gather.10
  233.5 70.7 all-gather.12
  306.9 70.4 all-gather.14
  379.5 68.6 all-gather.16
  581.6 152.0 reduce-scatter.8
  737.2 83.7 reduce-scatter.16
  824.6 87.5 reduce-scatter.14
  917.3 99.2 reduce-scatter.12
  1020.2 83.9 reduce-scatter.18
  1109.4 104.1 reduce-scatter.10

commit v2 on v1

v2 whole, which is shorter than its diff:
```python
import functools
import math

import jax
import jax.numpy as jnp
from jax import lax
from jax.experimental import pallas as pl
from jax.experimental.pallas import tpu as pltpu
from jax.sharding import PartitionSpec as P

HEADS = 4
HEAD = 256
MB = 2
STRETCH = 256

eps = 1e-06
rope_base = 1000000.0
masked_score = -1e30
bf16 = jnp.bfloat16
f32 = jnp.float32
ALL = ("dp", "seq")


def norm_scale(values):
    return lax.rsqrt(jnp.mean(values * values, axis=-1, keepdims=True) + eps)


def norm_back(values, scale, weighted):
    return scale * weighted - values * (scale * scale * scale) * jnp.mean(
        weighted * values, axis=-1, keepdims=True
    )


def rotate(values, cosine, sine):
    first, second = jnp.split(values, 2, axis=-1)
    return jnp.concatenate([first * cosine - second * sine, second * cosine + first * sine], axis=-1)


def layout_start(ends, row_ids):
    after = row_ids[:, None] >= ends[None, :]
    return jnp.max(jnp.where(after, ends[None, :], 0), axis=1)


def dot(left, right, dims):
    return lax.dot_general(left, right, (dims, ((), ())), preferred_element_type=f32)


def mm(left, right):
    return dot(left, right, ((1,), (0,)))


def mm_tn(left, right):
    return dot(left, right, ((0,), (0,)))


def mm_nt(left, right):
    return dot(left, right, ((1,), (1,)))


def xor(value, axis, mask):
    return lax.ppermute(value, axis, [(i, i ^ mask) for i in range(lax.axis_size(axis))])


def xor_both(value, dp_mask, seq_mask):
    members = lax.axis_size("seq")
    mask = dp_mask * members + seq_mask
    return lax.ppermute(value, ALL, [(i, i ^ mask) for i in range(lax.axis_size("dp") * members)])


def flips(value, bits):
    for axis, bit in enumerate(bits):
        halves = [lax.slice_in_dim(value, i, i + 1, axis=axis) for i in (1, 0)]
        value = jnp.where(bit == 1, lax.concatenate(halves, axis), value)
    return value


def add16(left, right):
    return (left.astype(f32) + right.astype(f32)).astype(bf16)


def gather_all(piece):
    count = lax.axis_size("dp") // 2
    first = jnp.stack([piece] + [xor(piece, "dp", 2 * k) for k in range(1, count)])
    side = xor(first, "dp", 1)
    across = xor(first, "seq", 2)
    half = count // 2
    both = jnp.concatenate([xor(side[:half], "seq", 2), xor(across[half:], "dp", 1)])
    near = [first, side, across, both]
    return jnp.concatenate(near + [xor(part, "seq", 1) for part in near]).reshape(-1, piece.shape[1])


def all_labels():
    count = lax.axis_size("dp") // 2
    pairs = [(2 * z + y, 2 * x) for x, y in ((0, 0), (0, 1), (1, 0), (1, 1)) for z in range(count)]
    return pairs + [(d, s + 1) for d, s in pairs]


def scatter_all(total, block):
    count = lax.axis_size("dp") // 2
    parts = total.reshape(-1, block, total.shape[1])
    near, far = parts[: 4 * count], parts[4 * count :]
    near = add16(near, xor(far, "seq", 1))
    first, side, across, both = [near[i * count : (i + 1) * count] for i in range(4)]
    half = count // 2
    low, high = xor(both[:half], "seq", 2), xor(both[half:], "dp", 1)
    side = jnp.concatenate([add16(side[:half], low), side[half:]])
    across = jnp.concatenate([across[:half], add16(across[half:], high)])
    first = first.astype(f32) + xor(side, "dp", 1).astype(f32) + xor(across, "seq", 2).astype(f32)
    result = first[0]
    low_first = first.astype(bf16)
    for k in range(1, count):
        result = result + xor(low_first[k], "dp", 2 * k).astype(f32)
    return result


def gather_group(rows):
    half = rows.shape[0] // 2
    across, along = xor(rows, "seq", 2), xor(rows, "dp", 2)
    corner = [xor(across[:half], "dp", 2), xor(along[half:], "seq", 2)]
    near = [rows, across, along, *corner]
    return jnp.concatenate(near + [xor(part, "seq", 1) for part in near], axis=0)


def scatter_group(total):
    parts = total.reshape(2, -1, total.shape[1])
    near = add16(parts[0], xor(parts[1], "seq", 1))
    mine, across, along, corner = jnp.split(near, 4)
    half = mine.shape[0] // 2
    low, high = xor(corner[:half], "dp", 2), xor(corner[half:], "seq", 2)
    across = jnp.concatenate([add16(across[:half], low), across[half:]])
    along = jnp.concatenate([along[:half], add16(along[half:], high)])
    return mine.astype(f32) + xor(across, "seq", 2).astype(f32) + xor(along, "dp", 2).astype(f32)


def place_kernel(sizes, target_ref, *refs):
    pieces, out = refs[: len(sizes)], refs[len(sizes)]
    buffer, arrived, left = refs[len(sizes) + 1 :]
    ins, outs, block = [], [], 0
    for piece, size in zip(pieces, sizes):
        for index in range(size):
            ins.append(pltpu.make_async_copy(piece.at[index], buffer.at[block], arrived.at[block]))
            outs.append(pltpu.make_async_copy(buffer.at[block], out.at[target_ref[block]], left.at[block]))
            ins[-1].start()
            block += 1
    for copy_in, copy_out in zip(ins, outs):
        copy_in.wait()
        copy_out.start()
    for copy_out in outs:
        copy_out.wait()


def place(pieces, targets):
    sizes = [piece.shape[0] for piece in pieces]
    shape = (sum(sizes), *pieces[0].shape[1:])
    anywhere = pl.BlockSpec(memory_space=pl.ANY)
    return pl.pallas_call(
        functools.partial(place_kernel, sizes),
        grid_spec=pltpu.PrefetchScalarGridSpec(
            num_scalar_prefetch=1,
            grid=(1,),
            in_specs=[anywhere] * len(pieces),
            out_specs=anywhere,
            scratch_shapes=[
                pltpu.VMEM(shape, pieces[0].dtype),
                pltpu.SemaphoreType.DMA((shape[0],)),
                pltpu.SemaphoreType.DMA((shape[0],)),
            ],
        ),
        out_shape=jax.ShapeDtypeStruct(shape, pieces[0].dtype),
        name="place",
        cost_estimate=pl.CostEstimate(flops=0, bytes_accessed=4 * math.prod(shape), transcendentals=0),
    )(targets, *pieces)


def query_vectors(meta_ref, ends_ref, unit, rows):
    lanes = lax.broadcasted_iota(jnp.int32, (1, HEADS * rows), 1)
    ids = meta_ref[3 * unit] + lanes % rows
    start = jnp.zeros_like(ids)
    for index in range(ends_ref.shape[0]):
        end = ends_ref[index]
        start = jnp.where(ids >= end, end, start)
    return ids, start


def mask_of(meta_ref, ends_ref, unit, rows, key_stretch):
    ids, start = query_vectors(meta_ref, ends_ref, unit, rows)
    place_in = lax.broadcasted_iota(jnp.int32, (STRETCH, 1), 0)
    near = meta_ref[6] * rows
    place_in = jnp.where(place_in < rows, place_in + near, place_in - near)
    key = key_stretch * STRETCH + place_in
    return (key <= ids) & (key >= start)


def attend_kernel(
    rows, meta_ref, ends_ref, slots_ref, q_ref, near_ref, far_ref, o_ref, lse_ref, top, total, acc
):
    step = pl.program_id(0)

    @pl.when(step == 0)
    def _():
        top[...] = jnp.full_like(top, masked_score)
        total[...] = jnp.zeros_like(total)
        acc[...] = jnp.zeros_like(acc)

    key_stretch = slots_ref[step]
    for unit in range(2):

        @pl.when((key_stretch <= meta_ref[3 * unit + 1]) & (key_stretch >= meta_ref[3 * unit + 2]))
        def _():
            mask = mask_of(meta_ref, ends_ref, unit, rows, key_stretch)
            block = jnp.concatenate([near_ref[...], far_ref[...]], axis=0)
            query = q_ref[unit].reshape(HEADS * rows, HEAD)
            scores = jnp.where(mask, mm_nt(block[:, :HEAD], query), masked_score)
            old = top[unit]
            new = jnp.maximum(old, jnp.max(scores, axis=0, keepdims=True))
            keep = jnp.exp(old - new)
            terms = jnp.exp(scores - new)
            top[unit] = new
            total[unit] = total[unit] * keep + jnp.sum(terms, axis=0, keepdims=True)
            acc[unit] = acc[unit] * keep + mm_tn(block[:, HEAD:], terms.astype(bf16))

    @pl.when(step == pl.num_programs(0) - 1)
    def _():
        for unit in range(2):
            out = acc[unit] * (1.0 / total[unit])
            o_ref[unit] = out.T.reshape(HEADS, rows, HEAD)
            lse_ref[unit] = top[unit] + jnp.log(total[unit])


def attend_back_kernel(
    rows,
    meta_ref,
    ends_ref,
    slots_ref,
    q_ref,
    dc_ref,
    lse_ref,
    delta_ref,
    near_ref,
    far_ref,
    dq_ref,
    dnear_ref,
    dfar_ref,
    acc,
    both,
):
    step = pl.program_id(0)

    @pl.when(step == 0)
    def _():
        acc[...] = jnp.zeros_like(acc)

    key_stretch = slots_ref[step]
    both[...] = jnp.zeros_like(both)
    for unit in range(2):

        @pl.when((key_stretch <= meta_ref[3 * unit + 1]) & (key_stretch >= meta_ref[3 * unit + 2]))
        def _():
            mask = mask_of(meta_ref, ends_ref, unit, rows, key_stretch)
            block = jnp.concatenate([near_ref[...], far_ref[...]], axis=0)
            key, value = block[:, :HEAD], block[:, HEAD:]
            query = q_ref[unit].reshape(HEADS * rows, HEAD)
            grad = dc_ref[unit].reshape(HEADS * rows, HEAD)
            probs = jnp.where(mask, jnp.exp(mm_nt(key, query) - lse_ref[unit]), 0.0)
            score_grad = (probs * (mm_nt(value, grad) - delta_ref[unit])).astype(bf16)
            acc[unit] += mm_tn(key, score_grad)
            both[:, :HEAD] += mm(score_grad, query)
            both[:, HEAD:] += mm(probs.astype(bf16), grad)

    dnear_ref[...] = both[:rows].astype(bf16)
    dfar_ref[...] = both[rows:].astype(bf16)

    @pl.when(step == pl.num_programs(0) - 1)
    def _():
        for unit in range(2):
            dq_ref[unit] = (acc[unit].T * HEAD**-0.5).reshape(HEADS, rows, HEAD)


def attend_specs(query):
    rows = query.shape[2]
    whole = pl.BlockSpec(query.shape, lambda j, *_: (0, 0, 0, 0))
    line = pl.BlockSpec((2, 1, HEADS * rows), lambda j, *_: (0, 0, 0))
    keys = pl.BlockSpec((None, None, rows, 2 * HEAD), lambda j, *_: (j // 2, j % 2, 0, 0))
    return whole, line, keys


def attend(meta, ends, slots, query, near, far):
    rows = query.shape[2]
    wide = HEADS * rows
    whole, line, keys = attend_specs(query)
    return pl.pallas_call(
        functools.partial(attend_kernel, rows),
        grid_spec=pltpu.PrefetchScalarGridSpec(
            num_scalar_prefetch=3,
            grid=(slots.shape[0],),
            in_specs=[whole, keys, keys],
            out_specs=[whole, line],
            scratch_shapes=[
                pltpu.VMEM((2, 1, wide), f32),
                pltpu.VMEM((2, 1, wide), f32),
                pltpu.VMEM((2, HEAD, wide), f32),
            ],
        ),
        out_shape=[
            jax.ShapeDtypeStruct(query.shape, f32),
            jax.ShapeDtypeStruct((2, 1, wide), f32),
        ],
        name="attend",
        cost_estimate=pl.CostEstimate(
            flops=4 * 2 * 9 * STRETCH * wide * HEAD,
            bytes_accessed=4 * near.size,
            transcendentals=2 * 9 * STRETCH * wide,
        ),
    )(meta, ends, slots, query, near, far)


def attend_back(meta, ends, slots, query, grad, lse, delta, near, far):
    rows = query.shape[2]
    wide = HEADS * rows
    whole, line, keys = attend_specs(query)
    return pl.pallas_call(
        functools.partial(attend_back_kernel, rows),
        grid_spec=pltpu.PrefetchScalarGridSpec(
            num_scalar_prefetch=3,
            grid=(slots.shape[0],),
            in_specs=[whole, whole, line, line, keys, keys],
            out_specs=[whole, keys, keys],
            scratch_shapes=[
                pltpu.VMEM((2, HEAD, wide), f32),
                pltpu.VMEM((STRETCH, 2 * HEAD), f32),
            ],
        ),
        out_shape=[
            jax.ShapeDtypeStruct(query.shape, f32),
            jax.ShapeDtypeStruct(near.shape, bf16),
            jax.ShapeDtypeStruct(near.shape, bf16),
        ],
        name="attend_back",
        cost_estimate=pl.CostEstimate(
            flops=10 * 2 * 9 * STRETCH * wide * HEAD,
            bytes_accessed=8 * near.size,
            transcendentals=2 * 9 * STRETCH * wide,
        ),
    )(meta, ends, slots, query, grad, lse, delta, near, far)


def per_device(
    inputs,
    cotangent,
    lengths,
    deal,
    w_query,
    w_key,
    w_value,
    w_out,
    w_gate,
    w_up,
    w_down,
    gain_attn_pre,
    gain_attn_post,
    gain_ffw_pre,
    gain_ffw_post,
    gain_query,
    gain_key,
):
    rows, width = inputs.shape[1], inputs.shape[2]
    groups, members = lax.axis_size("dp"), lax.axis_size("seq")
    devices = groups * members
    total_rows = rows * devices
    dp_id, seq_id = lax.axis_index("dp"), lax.axis_index("seq")
    half_bit, x_bit, y_bit, z_bit = seq_id % 2, seq_id // 2, dp_id % 2, dp_id // 2 % 2
    tops = groups // 4
    count = 2 * rows
    model_rows, out_rows, ff_rows = w_query.shape[0], w_out.shape[0], w_down.shape[0]
    ff_local = 2 * tops * ff_rows
    wide_q = HEADS * HEAD
    gain_sizes = [gain_attn_pre.shape[0]] * 4 + [gain_query.shape[0]] * 2
    gain_total = sum(gain_sizes)
    block_rows = (model_rows + 8) // 8 * 8

    def regroup(array):
        kept = lax.dynamic_index_in_dim(array, y_bit, 0, keepdims=False)
        sent = lax.dynamic_index_in_dim(array, 1 - y_bit, 0, keepdims=False)
        return jnp.concatenate([kept, xor(sent, "dp", 1)], axis=0)

    def ungroup(array):
        kept, sent = array[:rows], array[rows:]
        return flips(jnp.stack([kept, xor(sent, "dp", 1)]), [y_bit])

    rows_in = regroup(inputs).astype(f32)

    gains = jnp.concatenate([gain_attn_pre, gain_attn_post, gain_ffw_pre, gain_ffw_post, gain_query, gain_key])
    gain_line = jnp.pad(gains[None, :], ((0, 0), (0, 2 * HEAD - gain_total)))
    kv_shard = jnp.concatenate([jnp.concatenate([w_key, w_value], axis=1), gain_line], axis=0)
    kv_weight = gather_all(jnp.pad(kv_shard, ((0, block_rows - model_rows - 1), (0, 0))))
    q_weight = gather_all(jnp.pad(w_query, ((0, block_rows - model_rows), (0, 0))))
    out_weight = gather_all(w_out)
    labels = all_labels()
    natural = jnp.stack([(dp_id ^ d) * members + (seq_id ^ s) for d, s in labels])

    def selection(size, block, padded):
        within = jnp.arange(padded, dtype=jnp.int32)
        source = jnp.where(within < block, natural[:, None] * block + within, -1).reshape(-1)
        return (jnp.arange(size, dtype=jnp.int32)[:, None] == source[None, :]).astype(bf16)

    model_pick = selection(width, model_rows, block_rows)
    head_pick = selection(wide_q, out_rows, out_rows)
    device_pick = selection(devices, 1, 1)
    gain_blocks = kv_weight.reshape(devices, block_rows, 2 * HEAD)[:, model_rows, :gain_total]
    gain_all = mm(device_pick, gain_blocks)
    full_gain, at = [], 0
    for size in gain_sizes:
        full_gain.append(gain_all[:, at : at + size].reshape(devices * size))
        at += size
    pre_attention, post_attention, pre_feed, post_feed, query_gain, key_gain = full_gain

    def by_owner(weight):
        split = weight.reshape(model_rows, tops, 2, 2, members, ff_rows)
        return split.transpose(2, 4, 0, 1, 3, 5).reshape(2, 2, 2, model_rows, ff_local)

    group_bits = [z_bit, x_bit, half_bit]

    def exchange(pieces):
        near = flips(pieces, group_bits)
        got = [near[0, 0, 0]]
        for index in range(1, 8):
            i, j, k = index // 4, index // 2 % 2, index % 2
            got.append(xor_both(near[i, j, k], 2 * i, 2 * j + k))
        return flips(jnp.stack(got).reshape(pieces.shape), group_bits)

    def spread(piece):
        tall = [piece] + [xor(piece, "dp", 4 * k) for k in range(1, tops)]
        return tall + [xor(part, "dp", 1) for part in tall]

    halves = jnp.stack([by_owner(w_gate), by_owner(w_up)], axis=3)
    halves = exchange(halves).transpose(3, 0, 1, 2, 4, 5)
    halves = halves.reshape(2, 2, members * model_rows, ff_local)
    top_id = dp_id // 4
    sources = [((top_id ^ k) * 2 + v) * 2 + (y_bit ^ u) for u in range(2) for k in range(tops) for v in range(2)]
    sources = jnp.stack(sources).astype(jnp.int32)
    gate_weight, up_weight = [place(spread(halves[i]), sources).reshape(width, ff_local) for i in range(2)]
    owners = jnp.stack([(top_id ^ k) * 2 + (y_bit ^ u) for u in range(2) for k in range(tops)]).astype(jnp.int32)
    down_weight = place(spread(w_down[None]), owners).reshape(ff_local, width)

    seq_ends = jnp.cumsum(lax.dynamic_index_in_dim(lengths, y_bit, 0, keepdims=False))
    dealt = lax.dynamic_index_in_dim(deal, y_bit, 0, keepdims=False)
    unit_ids = jnp.stack([(dp_id ^ u) * members + seq_id for u in range(2)])
    stretches = dealt[unit_ids * rows // STRETCH]
    first_rows = stretches * STRETCH + unit_ids * rows % STRETCH
    my_rows = (first_rows[:, None] + jnp.arange(rows, dtype=jnp.int32)).reshape(count)
    starts = layout_start(seq_ends, my_rows)
    lows = starts.reshape(2, rows)[:, 0] // STRETCH
    meta = jnp.concatenate([jnp.stack([first_rows, stretches, lows], axis=1).reshape(-1), half_bit[None]])
    layers = groups // 2
    slot_ids = jnp.stack(
        [
            ((dp_id // 2 ^ z) * 2 + (y_bit ^ u)) * (members // 2) + (x_bit ^ x)
            for x in range(2)
            for z in range(layers)
            for u in range(2)
        ]
    )
    slots = dealt[slot_ids]
    positions = my_rows - starts
    valid = (my_rows < total_rows - STRETCH)[:, None]
    freqs = rope_base ** (-2.0 * jnp.arange(HEAD // 2, dtype=f32) / HEAD)
    angle = positions.astype(f32)[:, None, None] * freqs
    cosine, sine = jnp.cos(angle), jnp.sin(angle)

    scale_one = norm_scale(rows_in)
    normed_one = (rows_in * scale_one * pre_attention).astype(bf16)
    picked_one = mm(normed_one, model_pick).astype(bf16)
    kv_raw = mm(picked_one, kv_weight)
    key_raw = kv_raw[:, :HEAD].reshape(count, 1, HEAD)
    key_scale = norm_scale(key_raw)
    key_rot = rotate(key_raw * key_scale * key_gain, cosine, sine).astype(bf16)
    keys_mine = jnp.concatenate([key_rot[:, 0], kv_raw[:, HEAD:].astype(bf16)], axis=1)
    keys_mine = keys_mine.reshape(2, rows, 2 * HEAD)
    column = [keys_mine] + [xor(keys_mine, "dp", 2 * k) for k in range(1, layers)]
    across = [xor(part, "seq", 2) for part in column]
    column, across = jnp.stack(column), jnp.stack(across)
    near_keys = jnp.concatenate([column, across])
    far_keys = jnp.concatenate([xor(column, "seq", 1), xor(across, "seq", 1)])

    query_raw = mm(picked_one, q_weight).reshape(count, HEADS, HEAD)
    query_scale = norm_scale(query_raw)
    query_rot = rotate(query_raw * query_scale * query_gain, cosine, sine).astype(bf16) * HEAD**-0.5

    def to_heads(values):
        return values.reshape(2, rows, HEADS, HEAD).transpose(0, 2, 1, 3)

    def from_heads(values):
        return values.transpose(0, 2, 1, 3).reshape(count, HEADS, HEAD)

    query_heads = to_heads(query_rot.astype(bf16))
    context, lse = attend(meta, seq_ends, slots, query_heads, near_keys, far_keys)
    context_rows = from_heads(context.astype(bf16)).reshape(count, wide_q)
    context_rows = mm(context_rows, head_pick).astype(bf16)
    attended = mm(context_rows, out_weight)
    scale_two = norm_scale(attended)
    hidden_res = rows_in + attended * scale_two * post_attention
    scale_three = norm_scale(hidden_res)
    normed_two = (hidden_res * scale_three * pre_feed).astype(bf16)

    normed_group = gather_group(normed_two)
    gate_raw = mm(normed_group, gate_weight)
    up_raw = mm(normed_group, up_weight)
    hidden_low = (jax.nn.gelu(gate_raw, approximate=True) * up_raw).astype(bf16)
    mixed = scatter_group(mm(hidden_low, down_weight).astype(bf16))
    scale_four = norm_scale(mixed)
    result = hidden_res + mixed * scale_four * post_feed
    output = ungroup(jnp.where(valid, result, 0.0).astype(bf16))

    upstream = jnp.where(valid, regroup(cotangent).astype(f32), 0.0)
    grad_post_feed = jnp.sum(upstream * mixed * scale_four, axis=0)
    mixed_grad = norm_back(mixed, scale_four, post_feed * upstream).astype(bf16)
    mixed_group = gather_group(mixed_grad)
    hidden_grad = mm_nt(mixed_group, down_weight)
    _, gelu_pull = jax.vjp(lambda g, u: jax.nn.gelu(g, approximate=True) * u, gate_raw, up_raw)
    gate_grad, up_grad = gelu_pull(hidden_grad)
    gate_grad, up_grad = gate_grad.astype(bf16), up_grad.astype(bf16)
    normed_two_grad = scatter_group((mm_nt(gate_grad, gate_weight) + mm_nt(up_grad, up_weight)).astype(bf16))

    def collect(total):
        kept = lax.dynamic_index_in_dim(total, y_bit, 2, keepdims=False)
        sent = lax.dynamic_index_in_dim(total, 1 - y_bit, 2, keepdims=False)
        kept = add16(kept, xor(sent, "dp", 1))
        result = lax.dynamic_index_in_dim(kept, top_id, 0, keepdims=False).astype(f32)
        for k in range(1, tops):
            part = lax.dynamic_index_in_dim(kept, top_id ^ k, 0, keepdims=False)
            result = result + xor(part, "dp", 4 * k).astype(f32)
        return result

    def columns_home(total):
        mine = collect(total.astype(bf16).reshape(tops, 2, 2, members * model_rows, ff_local))
        return mine.astype(bf16).reshape(2, 2, 2, model_rows, ff_local)

    grad_down = mm_tn(hidden_low, mixed_group).astype(bf16).reshape(tops, 1, 2, ff_rows, width)
    grad_down = collect(grad_down)[0]
    both_grads = [columns_home(mm_tn(normed_group, grad)) for grad in (gate_grad, up_grad)]
    both_grads = exchange(jnp.stack(both_grads, axis=3))
    both_grads = both_grads.reshape(2, members, 2, model_rows, tops, 2, ff_rows)
    both_grads = both_grads.transpose(2, 3, 4, 0, 5, 1, 6).reshape(2, model_rows, -1).astype(f32)
    grad_pre_feed = jnp.sum(normed_two_grad * hidden_res * scale_three, axis=0)
    hidden_res_grad = upstream + norm_back(hidden_res, scale_three, pre_feed * normed_two_grad)

    grad_post_attention = jnp.sum(hidden_res_grad * attended * scale_two, axis=0)
    attended_grad = norm_back(attended, scale_two, post_attention * hidden_res_grad).astype(bf16)
    grad_out = scatter_all(mm_tn(context_rows, attended_grad).astype(bf16), out_rows)
    context_grad = mm_nt(attended_grad, out_weight).astype(bf16)
    context_grad = to_heads(mm_nt(context_grad, head_pick).astype(bf16))
    delta = jnp.sum(context_grad.astype(f32) * context, axis=-1).reshape(2, 1, HEADS * rows)
    query_grads, near_part, far_part = attend_back(
        meta, seq_ends, slots, query_heads, context_grad, lse, delta, near_keys, far_keys
    )
    near_part = add16(near_part, xor(far_part, "seq", 1)).reshape(2, layers, count, 2 * HEAD)
    near_part = add16(near_part[0], xor(near_part[1], "seq", 2))
    key_grads = near_part[0].astype(f32)
    for k in range(1, layers):
        key_grads = key_grads + xor(near_part[k], "dp", 2 * k).astype(f32)
    query_turned = rotate(from_heads(query_grads), cosine, -sine)
    grad_query_gain = jnp.sum(query_turned * query_raw * query_scale, axis=(0, 1))
    query_grad = norm_back(query_raw, query_scale, query_gain * query_turned)
    query_grad = query_grad.reshape(count, wide_q).astype(bf16)
    grad_query = scatter_all(mm_tn(picked_one, query_grad).astype(bf16), block_rows)
    value_grad = key_grads[:, HEAD:].astype(bf16)
    key_turned = rotate(key_grads[:, None, :HEAD], cosine, -sine)
    grad_key_gain = jnp.sum(key_turned * key_raw * key_scale, axis=(0, 1))
    key_grad = norm_back(key_raw, key_scale, key_gain * key_turned)[:, 0, :].astype(bf16)
    kv_grad = jnp.concatenate([key_grad, value_grad], axis=1)
    normed_one_grad = mm_nt(query_grad, mm(model_pick, q_weight).astype(bf16))
    normed_one_grad += mm_nt(kv_grad, mm(model_pick, kv_weight).astype(bf16))
    grad_pre_attention = jnp.sum(normed_one_grad * rows_in * scale_one, axis=0)
    rows_grad = hidden_res_grad + norm_back(rows_in, scale_one, pre_attention * normed_one_grad)
    input_grad = ungroup(rows_grad.astype(bf16))
    grad_kv = mm_tn(picked_one, kv_grad).reshape(devices, block_rows, 2 * HEAD)
    gain_grads = [
        grad_pre_attention,
        grad_post_attention,
        grad_pre_feed,
        grad_post_feed,
        grad_query_gain,
        grad_key_gain,
    ]
    gain_grads = jnp.concatenate([g.reshape(devices, -1) for g in gain_grads], axis=1)
    gain_grads = mm_tn(device_pick, gain_grads.astype(bf16))
    gain_grads = jnp.pad(
        gain_grads[:, None, :], ((0, 0), (model_rows, block_rows - model_rows - 1), (0, 2 * HEAD - gain_total))
    )
    last = scatter_all((grad_kv + gain_grads).astype(bf16).reshape(devices * block_rows, 2 * HEAD), block_rows)
    gain_out, at = [], 0
    for size in gain_sizes:
        gain_out.append(last[model_rows, at : at + size])
        at += size
    return (
        output,
        input_grad,
        grad_query[:model_rows],
        last[:model_rows, :HEAD],
        last[:model_rows, HEAD:],
        grad_out,
        both_grads[0],
        both_grads[1],
        grad_down,
        *gain_out,
    )


def solution(mesh):
    split = P(None, ALL, None)
    weight, gain = P(ALL, None), P(ALL)
    return jax.shard_map(
        per_device,
        mesh=mesh,
        in_specs=(split, split, P(), P(), *[weight] * 7, *[gain] * 6),
        out_specs=(split, split, *[weight] * 7, *[gain] * 6),
        check_vma=False,
    )
```

time: 1230 us -> 848 us (0.69)
  waiting for transfers between devices: 916 us -> 235 us
  local copies, waits for them, and re-layouts: 53.8 us -> 206 us
  starting transfers between devices: 15.1 us -> 127 us
  other arithmetic: 39.5 us -> 118 us
  blocking collectives: 30.9 us -> 0 us
    reduce_scatter x5 -> x0, waiting for transfers between devices: 468 us -> none  [the longest x2 162 us: scatter_dp(): lax.psum_scatter(total.astype(bf16), 'dp', scatter_dimension=0, tiled=True)]
    all_gather x6 -> x0, waiting for transfers between devices: 302 us -> none  [the longest x3 172 us: gather_dp(): return lax.all_gather(shard, 'dp', axis=0, tiled=True)]
    ppermute x12 -> x132, waiting for transfers between devices: 58.4 us -> 235 us  [the longest x118 228 us: xor(): lax.ppermute(value, axis, [(i, i ^ mask) for i in range(lax.axis_size(axi...]
    ppermute x12 -> x132, starting transfers between devices: 7.01 us -> 127 us  [the longest x118 116 us: xor(): lax.ppermute(value, axis, [(i, i ^ mask) for i in range(lax.axis_size(axi...]
    unnamed x13 -> x0, waiting for transfers between devices: 87.4 us -> none
    unnamed x126 -> x345, local copies, waits for them, and re-layouts: 8.94 us -> 58 us
    slice x6 -> x65, local copies, waits for them, and re-layouts: 2.53 us -> 51.3 us  [the longest x14 13.7 us: flips(): halves = [lax.slice_in_dim(value, i, i + 1, axis=axis) for i in (1, 0)]]
    select_n x1 -> x17, other arithmetic: 0.01 us -> 36 us  [the longest x12 35 us: flips(): value = jnp.where(bit == 1, lax.concatenate(halves, axis), value)]
  transfers between devices with their start and end apart: 26 -> 132, of which waited for: 19 -> 56; matrix products, arithmetic and copies ran while one was open for 10% -> 39% of each run, Pallas kernels for 2% -> 5%
where the time goes in v2:
time: 848 us; the launch traced here: 837 us
  waiting for transfers between devices  235 us (28%)
  local copies, waits for them, and re-layouts  206 us (24%)
  starting transfers between devices  127 us (15%)
  other arithmetic  118 us (14%)
  matrix products  107 us (13%)
  Pallas kernels  40.4 us (5%)
    ppermute x118, waiting for transfers between devices, xor(): lax.ppermute(value, axis, [(i, i ^ mask) for i in range(lax.axis_size(axi...  228 us
    ppermute x118, starting transfers between devices, xor(): lax.ppermute(value, axis, [(i, i ^ mask) for i in range(lax.axis_size(axi...  116 us
    dot_general x22, matrix products, dot(): lax.dot_general(left, right, (dims, ((), ())), preferred_element_type=f32)  107 us
    unnamed x345, local copies, waits for them, and re-layouts  58 us
    select_n x12, other arithmetic, flips(): value = jnp.where(bit == 1, lax.concatenate(halves, axis), value)  35 us
  transfers between devices with their start and end apart: 132, of which 56 were waited for; matrix products, arithmetic and copies ran while one was open for 39% of the time, Pallas kernels for 5%

profile of v2, /device:TPU:0, one launch (start us, length us, event | category | flops | bytes accessed | tf_op | source)
XLA Modules:
  0.0 837.1 jit_solution(2009642475233026741)
XLA Ops:
  177.8 7.3 collective-permute-done.23
  188.2 7.4 collective-permute-done.24
  236.6 14.1 %attend.1 = (f32[2,4,128,256]{3,2,1,0:T(8,128)}, f32[2,1,512]{2,1,0:T(1,128)}) custom-call(s32[7]{0:T(128)} %pad_add_fusion.1.meta_ref, s32[4]{0:T(128)} %bitcast.584, s32[16]{0:T(128)} %gather_fusion.1, bf16[2,4,128,256]{3,2,1,0:T(8,128)(2,1)} %fusion.52.q_ref, bf16[8,2,128,512]{3,2,1,0:T(8,128)(2,1)} %constant_dynamic-update-slice_fusion.24.near_ref, ...), custom_call_target="tpu_custom_call" | custom-call | flops 2415919104 | bytes 4194304 | tf_op jit(solution)/shard_map/attend/pallas_call | solution.py:291
  279.6 7.8 collective-permute-done.60.refs_2_
  287.5 9.4 %collective-permute-done.61.refs_3_ = bf16[2,144,864]{2,1,0:T(8,128)(2,1)} collective-permute-done((bf16[2,144,864]{2,1,0:T(8,128)(2,1)}, bf16[2,144,864]{2,1,0:T(8,128)(2,1)}, u32[]{:S(2)}, u32[]{:S(2)}) %collective-permute-start.61) | collective-permute-done | bytes 497696 | tf_op jit(solution)/shard_map/ppermute | solution.py:61
  316.0 7.0 fusion.127
  323.0 8.7 %multiply_convert_fusion.1 = (bf16[2048,864]{0,1:T(8,128)(2,1)S(1)}, f32[2048,864]{0,1:T(8,128)}) fusion(f32[2048,864]{0,1:T(8,128)S(1)} %fusion.127, bf16[2048,1152]{1,0:T(8,128)(2,1)S(1)} %copy-done.83, bf16[1152,864]{1,0:T(8,128)(2,1)S(1)} %bitcast.512), kind=kOutput, calls=%fused_computation.14 | convolution fusion | flops 4094558208 | bytes 24403968 | tf_op jit(solution)/shard_map/dot_general | solution.py:45
  345.2 7.5 collective-permute-done.69
  361.4 8.1 collective-permute-done.70
  406.6 7.4 convolution_convert_fusion.5
  414.2 13.2 %fusion.6 = (bf16[2048,864]{0,1:T(8,128)(2,1)}, bf16[2048,864]{0,1:T(8,128)(2,1)}) fusion(f32[2048,864]{0,1:T(8,128)S(1)} %bitcast.587, f32[2048,864]{0,1:T(8,128)} %get-tuple-element.206, bf16[2048,1152]{1,0:T(8,128)(2,1)S(1)} %copy-done.84, bf16[864,1152]{1,0:T(8,128)(2,1)S(1)} %bitcast.523), kind=kOutput, calls=%fused_computation.12 | convolution fusion | flops 4119330816 | bytes 27942912 | tf_op jit(solution)/shard_map/dot_general | solution.py:45
  427.4 8.2 convolution_convert_fusion.3
  435.5 8.1 fusion.128
  453.4 9.5 %convolution_convert_fusion.4 = bf16[1152,864]{0,1:T(8,128)(2,1)} fusion(bf16[2048,864]{0,1:T(8,128)(2,1)} %get-tuple-element.56, bf16[2048,1152]{1,0:T(8,128)(2,1)} %constant_dynamic-update-slice_fusion.45), kind=kOutput, calls=%fused_computation.30 | convolution fusion | flops 4077858816 | bytes 10248192 | tf_op jit(solution)/shard_map/dot_general | solution.py:45
  470.2 9.3 %add_convert_fusion = bf16[2048,1152]{1,0:T(8,128)(2,1)S(1)} fusion(f32[2048,1152]{1,0:T(8,128)} %fusion.128, bf16[2048,864]{0,1:T(8,128)(2,1)} %get-tuple-element.56, bf16[1152,864]{1,0:T(8,128)(2,1)} %bitcast.510), kind=kOutput, calls=%fused_computation.4 | convolution fusion | flops 4081582080 | bytes 19685376 | tf_op jit(solution)/shard_map/dot_general | solution.py:45
  482.6 9.3 %collective-permute-done.121 = bf16[2,2,144,864]{3,2,1,0:T(8,128)(2,1)S(1)} collective-permute-done((bf16[2,2,144,864]{3,2,1,0:T(8,128)(2,1)}, bf16[2,2,144,864]{3,2,1,0:T(8,128)(2,1)S(1)}, u32[]{:S(2)}, u32[]{:S(2)}) %collective-permute-start.121) | collective-permute-done | bytes 995360 | tf_op jit(solution)/shard_map/ppermute | solution.py:61
  494.4 19.2 %collective-permute-done.119 = bf16[2,2,144,864]{3,2,1,0:T(8,128)(2,1)S(1)} collective-permute-done((bf16[2,2,144,864]{3,2,1,0:T(8,128)(2,1)S(1)}, bf16[2,2,144,864]{3,2,1,0:T(8,128)(2,1)S(1)}, u32[]{:S(2)}, u32[]{:S(2)}) %collective-permute-start.119) | collective-permute-done | bytes 995360 | tf_op jit(solution)/shard_map/ppermute | solution.py:61
  519.8 30.6 %collective-permute-done.120 = bf16[2,144,864]{2,1,0:T(8,128)(2,1)S(1)} collective-permute-done((bf16[2,144,864]{2,1,0:T(8,128)(2,1)S(1)}, bf16[2,144,864]{2,1,0:T(8,128)(2,1)S(1)}, u32[]{:S(2)}, u32[]{:S(2)}) %collective-permute-start.120) | collective-permute-done | bytes 497696 | tf_op jit(solution)/shard_map/ppermute | solution.py:61
  622.8 6.3 reshape.2113
  650.6 8.2 collective-permute-done.86
  677.5 16.8 %attend_back.1 = (f32[2,4,128,256]{3,2,1,0:T(8,128)}, bf16[8,2,128,512]{3,2,1,0:T(8,128)(2,1)}, bf16[8,2,128,512]{3,2,1,0:T(8,128)(2,1)}) custom-call(s32[7]{0:T(128)} %pad_add_fusion.1.meta_ref, s32[4]{0:T(128)} %bitcast.585, s32[16]{0:T(128)} %gather_fusion.1, bf16[2,4,128,256]{3,2,1,0:T(8,128)(2,1)} %fusion.52.q_ref, bf16[2,4,128,256]{3,2,1,0:T(8,128)(2,1)} %bitcast.547, ...), custom_call_target="tpu_custom_call" | custom-call | flops 6039797760 | bytes 8388608 | tf_op jit(solution)/shard_map/attend_back/pallas_call | solution.py:321
  752.2 13.0 %collective-permute-done.90 = bf16[4,256,512]{2,1,0:T(8,128)(2,1)S(1)} collective-permute-done((bf16[4,256,512]{2,1,0:T(8,128)(2,1)S(1)}, bf16[4,256,512]{2,1,0:T(8,128)(2,1)S(1)}, u32[]{:S(2)}, u32[]{:S(2)}) %collective-permute-start.90) | collective-permute-done | bytes 1048608 | tf_op jit(solution)/shard_map/ppermute | solution.py:61
  780.0 7.1 collective-permute-done.92
  795.1 7.2 fusion.39
  (891 shorter events, 582.7 us)
Async XLA Ops:
  6.2 56.3 %collective-permute-start.1 = (bf16[40,512]{1,0:T(8,128)(2,1)}, bf16[40,512]{1,0:T(8,128)(2,1)S(1)}, u32[]{:S(2)}, u32[]{:S(2)}) collective-permute-start(bf16[40,512]{1,0:T(8,128)(2,1)} %get-tuple-element.177), channel_id=1, source_target_pairs={{0,8},{4,12},{8,0},{12,4},{16,24},{20,28},{24,16},{28,20},{1,9},{5... | collective-permute-start | bytes 122888 | tf_op jit(solution)/shard_map/ppermute | solution.py:61
  9.2 53.9 %collective-permute-start.2 = (bf16[40,512]{1,0:T(8,128)(2,1)}, bf16[40,512]{1,0:T(8,128)(2,1)}, u32[]{:S(2)}, u32[]{:S(2)}) collective-permute-start(bf16[40,512]{1,0:T(8,128)(2,1)} %get-tuple-element.177), channel_id=1, source_target_pairs={{0,16},{4,20},{8,24},{12,28},{16,0},{20,4},{24,8},{28,12},{1,17},{... | collective-permute-start | bytes 122888 | tf_op jit(solution)/shard_map/ppermute | solution.py:61
  11.8 53.3 %collective-permute-start.3 = (bf16[40,512]{1,0:T(8,128)(2,1)}, bf16[40,512]{1,0:T(8,128)(2,1)}, u32[]{:S(2)}, u32[]{:S(2)}) collective-permute-start(bf16[40,512]{1,0:T(8,128)(2,1)} %get-tuple-element.177), channel_id=1, source_target_pairs={{0,24},{4,28},{8,16},{12,20},{16,8},{20,12},{24,0},{28,4},{1,25},{... | collective-permute-start | bytes 122888 | tf_op jit(solution)/shard_map/ppermute | solution.py:61
  13.4 65.5 %collective-permute-start.12 = (bf16[40,1024]{1,0:T(8,128)(2,1)}, bf16[40,1024]{1,0:T(8,128)(2,1)S(1)}, u32[]{:S(2)}, u32[]{:S(2)}) collective-permute-start(bf16[40,1024]{1,0:T(8,128)(2,1)} %get-tuple-element.175), channel_id=1, source_target_pairs={{0,8},{4,12},{8,0},{12,4},{16,24},{20,28},{24,16},{28,20},{1,9},{5... | collective-permute-start | bytes 245768 | tf_op jit(solution)/shard_map/ppermute | solution.py:61
  14.3 65.3 %collective-permute-start.13 = (bf16[40,1024]{1,0:T(8,128)(2,1)}, bf16[40,1024]{1,0:T(8,128)(2,1)}, u32[]{:S(2)}, u32[]{:S(2)}) collective-permute-start(bf16[40,1024]{1,0:T(8,128)(2,1)} %get-tuple-element.175), channel_id=1, source_target_pairs={{0,16},{4,20},{8,24},{12,28},{16,0},{20,4},{24,8},{28,12},{1,17},{... | collective-permute-start | bytes 245768 | tf_op jit(solution)/shard_map/ppermute | solution.py:61
  83.7 150.0 %collective-permute-start.65 = (bf16[1,216,1152]{2,1,0:T(8,128)(2,1)}, bf16[1,216,1152]{2,1,0:T(8,128)(2,1)}, u32[]{:S(2)}, u32[]{:S(2)}) collective-permute-start(bf16[1,216,1152]{2,1,0:T(8,128)(2,1)} %bitcast.167.refs_0_), channel_id=1, source_target_pairs={{0,16},{4,20},{8,24},{12,28},{16,0},{20,4},{24,8},{28,12},{1,17},{... | collective-permute-start | bytes 1493000 | tf_op jit(solution)/shard_map/ppermute | solution.py:61
  86.6 172.5 %collective-permute-start.66 = (bf16[1,216,1152]{2,1,0:T(8,128)(2,1)}, bf16[1,216,1152]{2,1,0:T(8,128)(2,1)}, u32[]{:S(2)}, u32[]{:S(2)}) collective-permute-start(bf16[1,216,1152]{2,1,0:T(8,128)(2,1)} %bitcast.167.refs_0_), channel_id=1, source_target_pairs={{0,4},{4,0},{8,12},{12,8},{16,20},{20,16},{24,28},{28,24},{1,5},{5... | collective-permute-start | bytes 1493000 | tf_op jit(solution)/shard_map/ppermute | solution.py:61
  126.6 37.1 %collective-permute-start.39 = (bf16[4,32,1152]{2,1,0:T(8,128)(2,1)}, bf16[4,32,1152]{2,1,0:T(8,128)(2,1)}, u32[]{:S(2)}, u32[]{:S(2)}) collective-permute-start(bf16[4,32,1152]{2,1,0:T(8,128)(2,1)} %pad_maximum_fusion.20), channel_id=1, source_target_pairs={{0,1},{1,0},{2,3},{3,2},{4,5},{5,4},{6,7},{7,6},{8,9},{9,8},{10,11... | collective-permute-start | bytes 884744 | tf_op jit(solution)/shard_map/ppermute | solution.py:61
  170.0 33.7 %collective-permute-start.20 = (bf16[4,40,1024]{2,1,0:T(8,128)(2,1)}, bf16[4,40,1024]{2,1,0:T(8,128)(2,1)S(1)}, u32[]{:S(2)}, u32[]{:S(2)}) collective-permute-start(bf16[4,40,1024]{2,1,0:T(8,128)(2,1)} %collective-permute-done.15), channel_id=1, source_target_pairs={{0,1},{1,0},{2,3},{3,2},{4,5},{5,4},{6,7},{7,6},{8,9},{9,8},{10,11... | collective-permute-start | bytes 983048 | tf_op jit(solution)/shard_map/ppermute | solution.py:61
  217.8 41.4 %collective-permute-start.62 = (bf16[2,144,864]{2,1,0:T(8,128)(2,1)}, bf16[2,144,864]{2,1,0:T(8,128)(2,1)}, u32[]{:S(2)}, u32[]{:S(2)}) collective-permute-start(bf16[2,144,864]{2,1,0:T(8,128)(2,1)} %copy.829.refs_0_), channel_id=1, source_target_pairs={{0,16},{4,20},{8,24},{12,28},{16,0},{20,4},{24,8},{28,12},{1,17},{... | collective-permute-start | bytes 1493000 | tf_op jit(solution)/shard_map/ppermute | solution.py:61
  259.1 41.0 %collective-permute-start.43 = (bf16[256,1152]{1,0:T(8,128)(2,1)}, bf16[256,1152]{1,0:T(8,128)(2,1)S(1)}, u32[]{:S(2)}, u32[]{:S(2)}) collective-permute-start(bf16[256,1152]{1,0:T(8,128)(2,1)} %get-tuple-element.51), channel_id=1, source_target_pairs={{0,2},{1,3},{2,0},{3,1},{4,6},{5,7},{6,4},{7,5},{8,10},{9,11},{10,... | collective-permute-start | bytes 1769480 | tf_op jit(solution)/shard_map/ppermute | solution.py:61
  259.3 41.7 %collective-permute-start.44 = (bf16[256,1152]{1,0:T(8,128)(2,1)}, bf16[256,1152]{1,0:T(8,128)(2,1)}, u32[]{:S(2)}, u32[]{:S(2)}) collective-permute-start(bf16[256,1152]{1,0:T(8,128)(2,1)} %get-tuple-element.51), channel_id=1, source_target_pairs={{0,8},{4,12},{8,0},{12,4},{16,24},{20,28},{24,16},{28,20},{1,9},{5... | collective-permute-start | bytes 1769480 | tf_op jit(solution)/shard_map/ppermute | solution.py:61
  444.6 71.5 %collective-permute-start.130 = (bf16[2,1,216,1152]{3,2,1,0:T(8,128)(2,1)}, bf16[2,1,216,1152]{3,2,1,0:T(8,128)(2,1)}, u32[]{:S(2)}, u32[]{:S(2)}) collective-permute-start(bf16[2,1,216,1152]{3,2,1,0:T(8,128)(2,1)} %dynamic-slice_bitcast_fusion.2), channel_id=1, source_target_pairs={{0,4},{4,0},{8,12},{12,8},{16,20},{20,16},{24,28},{28,24},{1,5},{5... | collective-permute-start | bytes 2985992 | tf_op jit(solution)/shard_map/ppermute | solution.py:61
  453.2 38.6 %collective-permute-start.121 = (bf16[2,2,144,864]{3,2,1,0:T(8,128)(2,1)}, bf16[2,2,144,864]{3,2,1,0:T(8,128)(2,1)S(1)}, u32[]{:S(2)}, u32[]{:S(2)}) collective-permute-start(bf16[2,2,144,864]{3,2,1,0:T(8,128)(2,1)} %dynamic-slice_bitcast_fusion), channel_id=1, source_target_pairs={{0,4},{4,0},{8,12},{12,8},{16,20},{20,16},{24,28},{28,24},{1,5},{5... | collective-permute-start | bytes 2985992 | tf_op jit(solution)/shard_map/ppermute | solution.py:61
  468.3 45.4 %collective-permute-start.119 = (bf16[2,2,144,864]{3,2,1,0:T(8,128)(2,1)S(1)}, bf16[2,2,144,864]{3,2,1,0:T(8,128)(2,1)S(1)}, u32[]{:S(2)}, u32[]{:S(2)}) collective-permute-start(bf16[2,2,144,864]{3,2,1,0:T(8,128)(2,1)S(1)} %dynamic-slice_bitcast_fusion.1), channel_id=1, source_target_pairs={{0,4},{4,0},{8,12},{12,8},{16,20},{20,16},{24,28},{28,24},{1,5},{5... | collective-permute-start | bytes 2985992 | tf_op jit(solution)/shard_map/ppermute | solution.py:61
  482.6 118.1 %collective-permute-start.84 = (bf16[1024,1152]{1,0:T(8,128)(2,1)}, bf16[1024,1152]{1,0:T(8,128)(2,1)}, u32[]{:S(2)}, u32[]{:S(2)}) collective-permute-start(bf16[1024,1152]{1,0:T(8,128)(2,1)} %slice.683), channel_id=1, source_target_pairs={{0,1},{1,0},{2,3},{3,2},{4,5},{5,4},{6,7},{7,6},{8,9},{9,8},{10,11... | collective-permute-start | bytes 7077896 | tf_op jit(solution)/shard_map/ppermute | solution.py:61
  514.0 36.4 %collective-permute-start.120 = (bf16[2,144,864]{2,1,0:T(8,128)(2,1)S(1)}, bf16[2,144,864]{2,1,0:T(8,128)(2,1)S(1)}, u32[]{:S(2)}, u32[]{:S(2)}) collective-permute-start(bf16[2,144,864]{2,1,0:T(8,128)(2,1)S(1)} %dynamic-slice_bitcast_fusion.4), channel_id=1, source_target_pairs={{0,16},{4,20},{8,24},{12,28},{16,0},{20,4},{24,8},{28,12},{1,17},{... | collective-permute-start | bytes 1493000 | tf_op jit(solution)/shard_map/ppermute | solution.py:61
  518.3 58.0 %collective-permute-start.131 = (bf16[1,216,1152]{2,1,0:T(8,128)(2,1)}, bf16[1,216,1152]{2,1,0:T(8,128)(2,1)}, u32[]{:S(2)}, u32[]{:S(2)}) collective-permute-start(bf16[1,216,1152]{2,1,0:T(8,128)(2,1)} %dynamic-slice_bitcast_fusion.5), channel_id=1, source_target_pairs={{0,16},{4,20},{8,24},{12,28},{16,0},{20,4},{24,8},{28,12},{1,17},{... | collective-permute-start | bytes 1493000 | tf_op jit(solution)/shard_map/ppermute | solution.py:61
  605.5 35.9 %collective-permute-start.85 = (bf16[128,1152]{1,0:T(8,128)(2,1)}, bf16[128,1152]{1,0:T(8,128)(2,1)}, u32[]{:S(2)}, u32[]{:S(2)}) collective-permute-start(bf16[128,1152]{1,0:T(8,128)(2,1)} %get-tuple-element.67), channel_id=1, source_target_pairs={{0,8},{4,12},{8,0},{12,4},{16,24},{20,28},{24,16},{28,20},{1,9},{5... | collective-permute-start | bytes 884744 | tf_op jit(solution)/shard_map/ppermute | solution.py:61
  605.5 35.9 %collective-permute-start.87 = (bf16[128,1152]{1,0:T(8,128)(2,1)}, bf16[128,1152]{1,0:T(8,128)(2,1)}, u32[]{:S(2)}, u32[]{:S(2)}) collective-permute-start(bf16[128,1152]{1,0:T(8,128)(2,1)} %get-tuple-element.68), channel_id=1, source_target_pairs={{0,2},{1,3},{2,0},{3,1},{4,6},{5,7},{6,4},{7,5},{8,10},{9,11},{10,... | collective-permute-start | bytes 884744 | tf_op jit(solution)/shard_map/ppermute | solution.py:61
  677.5 38.0 %collective-permute-start.111 = (bf16[16,32,1152]{2,1,0:T(8,128)(2,1)}, bf16[16,32,1152]{2,1,0:T(8,128)(2,1)}, u32[]{:S(2)}, u32[]{:S(2)}) collective-permute-start(bf16[16,32,1152]{2,1,0:T(8,128)(2,1)} %bitcast.198), channel_id=1, source_target_pairs={{0,1},{1,0},{2,3},{3,2},{4,5},{5,4},{6,7},{7,6},{8,9},{9,8},{10,11... | collective-permute-start | bytes 3538952 | tf_op jit(solution)/shard_map/ppermute | solution.py:61
  730.7 39.8 %collective-permute-start.97 = (bf16[4,40,1024]{2,1,0:T(8,128)(2,1)S(1)}, bf16[4,40,1024]{2,1,0:T(8,128)(2,1)S(1)}, u32[]{:S(2)}, u32[]{:S(2)}) collective-permute-start(bf16[4,40,1024]{2,1,0:T(8,128)(2,1)S(1)} %pad_maximum_fusion.18), channel_id=1, source_target_pairs={{0,4},{4,0},{8,12},{12,8},{16,20},{20,16},{24,28},{28,24},{1,5},{5... | collective-permute-start | bytes 983048 | tf_op jit(solution)/shard_map/ppermute | solution.py:61
  772.3 34.8 %collective-permute-start.100 = (bf16[40,1024]{1,0:T(8,128)(2,1)}, bf16[40,1024]{1,0:T(8,128)(2,1)S(1)}, u32[]{:S(2)}, u32[]{:S(2)}) collective-permute-start(bf16[40,1024]{1,0:T(8,128)(2,1)} %get-tuple-element.153), channel_id=1, source_target_pairs={{0,8},{4,12},{8,0},{12,4},{16,24},{20,28},{24,16},{28,20},{1,9},{5... | collective-permute-start | bytes 245768 | tf_op jit(solution)/shard_map/ppermute | solution.py:61
  772.9 34.2 %collective-permute-start.101 = (bf16[40,1024]{1,0:T(8,128)(2,1)}, bf16[40,1024]{1,0:T(8,128)(2,1)}, u32[]{:S(2)}, u32[]{:S(2)}) collective-permute-start(bf16[40,1024]{1,0:T(8,128)(2,1)} %get-tuple-element.155), channel_id=1, source_target_pairs={{0,16},{4,20},{8,24},{12,28},{16,0},{20,4},{24,8},{28,12},{1,17},{... | collective-permute-start | bytes 245768 | tf_op jit(solution)/shard_map/ppermute | solution.py:61
  (242 other events, 3327.2 us)

commit v3 on v2

v3 whole, which is shorter than its diff:
```python
import functools
import math

import jax
import jax.numpy as jnp
from jax import lax
from jax.experimental import pallas as pl
from jax.experimental.pallas import tpu as pltpu
from jax.sharding import PartitionSpec as P

HEADS = 4
HEAD = 256
MB = 2
STRETCH = 256

eps = 1e-06
rope_base = 1000000.0
masked_score = -1e30
bf16 = jnp.bfloat16
f32 = jnp.float32
ALL = ("dp", "seq")


def norm_scale(values):
    return lax.rsqrt(jnp.mean(values * values, axis=-1, keepdims=True) + eps)


def norm_back(values, scale, weighted):
    return scale * weighted - values * (scale * scale * scale) * jnp.mean(
        weighted * values, axis=-1, keepdims=True
    )


def rotate(values, cosine, sine):
    first, second = jnp.split(values, 2, axis=-1)
    return jnp.concatenate([first * cosine - second * sine, second * cosine + first * sine], axis=-1)


def layout_start(ends, row_ids):
    after = row_ids[:, None] >= ends[None, :]
    return jnp.max(jnp.where(after, ends[None, :], 0), axis=1)


def dot(left, right, dims):
    return lax.dot_general(left, right, (dims, ((), ())), preferred_element_type=f32)


def mm(left, right):
    return dot(left, right, ((1,), (0,)))


def mm_tn(left, right):
    return dot(left, right, ((0,), (0,)))


def mm_nt(left, right):
    return dot(left, right, ((1,), (1,)))


def xor(value, axis, mask):
    return lax.ppermute(value, axis, [(i, i ^ mask) for i in range(lax.axis_size(axis))])


def xor_both(value, dp_mask, seq_mask):
    members = lax.axis_size("seq")
    mask = dp_mask * members + seq_mask
    return lax.ppermute(value, ALL, [(i, i ^ mask) for i in range(lax.axis_size("dp") * members)])


def flips(value, bits):
    for axis, bit in enumerate(bits):
        halves = [lax.slice_in_dim(value, i, i + 1, axis=axis) for i in (1, 0)]
        value = jnp.where(bit == 1, lax.concatenate(halves, axis), value)
    return value


def add16(left, right):
    return (left.astype(f32) + right.astype(f32)).astype(bf16)


def after(value, *others):
    return lax.optimization_barrier((value, *others))[0]


def all_masks():
    rows = [(1 << bit, 0) for bit in range(1, 16) if 1 << bit < lax.axis_size("dp")]
    return rows + [(1, 0), (0, 2), (0, 1)]


def gather_all(piece):
    value = piece[None]
    for dp_mask, seq_mask in all_masks():
        value = jnp.concatenate([value, xor_both(value, dp_mask, seq_mask)])
    return value


def all_labels():
    labels = [(0, 0)]
    for dp_mask, seq_mask in all_masks():
        labels = labels + [(d ^ dp_mask, s ^ seq_mask) for d, s in labels]
    return labels


def scatter_all(total):
    for dp_mask, seq_mask in reversed(all_masks()):
        half = total.shape[0] // 2
        got = xor_both(total[half:], dp_mask, seq_mask)
        total = total[:half].astype(f32) + got.astype(f32)
        total = total if half == 1 else total.astype(bf16)
    return total[0]


def gather_group(rows):
    half = rows.shape[0] // 2
    across, along = xor(rows, "seq", 2), xor(rows, "dp", 2)
    corner = [xor(across[:half], "dp", 2), xor(along[half:], "seq", 2)]
    near = [rows, across, along, *corner]
    far = [rows, jnp.concatenate([across, along]), jnp.concatenate(corner)]
    return jnp.concatenate(near + [xor(part, "seq", 1) for part in far], axis=0)


def scatter_group(total):
    parts = total.reshape(2, -1, total.shape[1])
    near = add16(parts[0], xor(parts[1], "seq", 1))
    mine, across, along, corner = jnp.split(near, 4)
    half = mine.shape[0] // 2
    low, high = xor(corner[:half], "dp", 2), xor(corner[half:], "seq", 2)
    across = jnp.concatenate([add16(across[:half], low), across[half:]])
    along = jnp.concatenate([along[:half], add16(along[half:], high)])
    return mine.astype(f32) + xor(across, "seq", 2).astype(f32) + xor(along, "dp", 2).astype(f32)


def place_kernel(sizes, target_ref, *refs):
    pieces, out = refs[: len(sizes)], refs[len(sizes)]
    buffer, arrived, left = refs[len(sizes) + 1 :]
    ins, outs, block = [], [], 0
    for piece, size in zip(pieces, sizes):
        for index in range(size):
            ins.append(pltpu.make_async_copy(piece.at[index], buffer.at[block], arrived.at[block]))
            outs.append(pltpu.make_async_copy(buffer.at[block], out.at[target_ref[block]], left.at[block]))
            ins[-1].start()
            block += 1
    for copy_in, copy_out in zip(ins, outs):
        copy_in.wait()
        copy_out.start()
    for copy_out in outs:
        copy_out.wait()


def place(pieces, targets):
    sizes = [piece.shape[0] for piece in pieces]
    shape = (sum(sizes), *pieces[0].shape[1:])
    anywhere = pl.BlockSpec(memory_space=pl.ANY)
    return pl.pallas_call(
        functools.partial(place_kernel, sizes),
        grid_spec=pltpu.PrefetchScalarGridSpec(
            num_scalar_prefetch=1,
            grid=(1,),
            in_specs=[anywhere] * len(pieces),
            out_specs=anywhere,
            scratch_shapes=[
                pltpu.VMEM(shape, pieces[0].dtype),
                pltpu.SemaphoreType.DMA((shape[0],)),
                pltpu.SemaphoreType.DMA((shape[0],)),
            ],
        ),
        out_shape=jax.ShapeDtypeStruct(shape, pieces[0].dtype),
        name="place",
        cost_estimate=pl.CostEstimate(flops=0, bytes_accessed=4 * math.prod(shape), transcendentals=0),
    )(targets, *pieces)


def project_kernel(scale, picked_ref, weight_ref, gain_ref, cos_ref, sin_ref, raw_ref, out_ref):
    raw = mm(picked_ref[...], weight_ref[...])
    raw_ref[0] = raw
    turned = rotate(raw * norm_scale(raw) * gain_ref[...], cos_ref[...], sin_ref[...]).astype(bf16)
    out_ref[...] = (turned * scale).astype(bf16).reshape(out_ref.shape)


def project(picked, weight, gain, cosine, sine):
    count, deep = picked.shape
    rows = count // 2
    same = lambda h: (0, 0)
    return pl.pallas_call(
        functools.partial(project_kernel, HEAD**-0.5),
        grid=(HEADS,),
        in_specs=[
            pl.BlockSpec((count, deep), same),
            pl.BlockSpec((deep, HEAD), lambda h: (0, h)),
            pl.BlockSpec((1, HEAD), same),
            pl.BlockSpec((count, HEAD // 2), same),
            pl.BlockSpec((count, HEAD // 2), same),
        ],
        out_specs=[
            pl.BlockSpec((1, count, HEAD), lambda h: (h, 0, 0)),
            pl.BlockSpec((2, 1, rows, HEAD), lambda h: (0, h, 0, 0)),
        ],
        out_shape=[
            jax.ShapeDtypeStruct((HEADS, count, HEAD), f32),
            jax.ShapeDtypeStruct((2, HEADS, rows, HEAD), bf16),
        ],
        name="project",
        cost_estimate=pl.CostEstimate(
            flops=2 * count * deep * HEADS * HEAD, bytes_accessed=2 * deep * HEADS * HEAD, transcendentals=0
        ),
    )(picked, weight, gain, cosine, sine)


def project_keys_kernel(picked_ref, weight_ref, gain_ref, cos_ref, sin_ref, raw_ref, out_ref):
    both = mm(picked_ref[...], weight_ref[...])
    raw = both[:, :HEAD]
    raw_ref[...] = raw
    turned = rotate(raw * norm_scale(raw) * gain_ref[...], cos_ref[...], sin_ref[...])
    both = jnp.concatenate([turned, both[:, HEAD:]], axis=1).astype(bf16)
    out_ref[...] = both.reshape(out_ref.shape)


def project_keys(picked, weight, gain, cosine, sine):
    count, deep = picked.shape
    return pl.pallas_call(
        project_keys_kernel,
        out_shape=[
            jax.ShapeDtypeStruct((count, HEAD), f32),
            jax.ShapeDtypeStruct((2, count // 2, 2 * HEAD), bf16),
        ],
        name="project_keys",
        cost_estimate=pl.CostEstimate(
            flops=4 * count * deep * HEAD, bytes_accessed=4 * deep * HEAD, transcendentals=0
        ),
    )(picked, weight, gain, cosine, sine)


def mask_of(meta_ref, ends_ref, unit, rows, key_stretch):
    lanes = lax.broadcasted_iota(jnp.int32, (1, HEADS * rows), 1)
    ids = meta_ref[3 * unit] + lanes % rows
    start = jnp.zeros_like(ids)
    for index in range(ends_ref.shape[0]):
        end = ends_ref[index]
        start = jnp.where(ids >= end, end, start)
    place_in = lax.broadcasted_iota(jnp.int32, (STRETCH, 1), 0)
    near = meta_ref[6] * rows
    place_in = jnp.where(place_in < rows, place_in + near, place_in - near)
    key = key_stretch * STRETCH + place_in
    return (key <= ids) & (key >= start)


def attend_kernel(
    rows, meta_ref, ends_ref, slots_ref, q_ref, near_ref, far_ref, c_ref, turned_ref, lse_ref, top, total, acc
):
    step = pl.program_id(0)

    @pl.when(step == 0)
    def _():
        top[...] = jnp.full_like(top, masked_score)
        total[...] = jnp.zeros_like(total)
        acc[...] = jnp.zeros_like(acc)

    key_stretch = slots_ref[step]
    for unit in range(2):

        @pl.when((key_stretch <= meta_ref[3 * unit + 1]) & (key_stretch >= meta_ref[3 * unit + 2]))
        def _():
            mask = mask_of(meta_ref, ends_ref, unit, rows, key_stretch)
            block = jnp.concatenate([near_ref[...], far_ref[...]], axis=0)
            query = q_ref[unit].reshape(HEADS * rows, HEAD)
            scores = jnp.where(mask, mm_nt(block[:, :HEAD], query), masked_score)
            old = top[unit]
            new = jnp.maximum(old, jnp.max(scores, axis=0, keepdims=True))
            keep = jnp.exp(old - new)
            terms = jnp.exp(scores - new)
            top[unit] = new
            total[unit] = total[unit] * keep + jnp.sum(terms, axis=0, keepdims=True)
            acc[unit] = acc[unit] * keep + mm_tn(block[:, HEAD:], terms.astype(bf16))

    @pl.when(step == pl.num_programs(0) - 1)
    def _():
        for unit in range(2):
            out = acc[unit] * (1.0 / total[unit])
            turned_ref[unit] = out
            lse_ref[unit] = top[unit] + jnp.log(total[unit])
            out = out.T.astype(bf16)
            for head in range(HEADS):
                c_ref[unit * rows : (unit + 1) * rows, head * HEAD : (head + 1) * HEAD] = out[
                    head * rows : (head + 1) * rows
                ]


def attend_back_kernel(
    rows,
    meta_ref,
    ends_ref,
    slots_ref,
    q_ref,
    dc_ref,
    lse_ref,
    turned_ref,
    raw_ref,
    gain_ref,
    cos_ref,
    sin_ref,
    near_ref,
    far_ref,
    dq_ref,
    dgain_ref,
    dnear_ref,
    dfar_ref,
    grads,
    delta,
    acc,
    both,
):
    step = pl.program_id(0)

    @pl.when(step == 0)
    def _():
        acc[...] = jnp.zeros_like(acc)
        for unit in range(2):
            for head in range(HEADS):
                grads[unit, head * rows : (head + 1) * rows] = dc_ref[
                    unit * rows : (unit + 1) * rows, head * HEAD : (head + 1) * HEAD
                ]
            across = grads[unit].astype(f32).T
            delta[unit] = jnp.sum(across * turned_ref[unit], axis=0, keepdims=True)

    key_stretch = slots_ref[step]
    both[...] = jnp.zeros_like(both)
    for unit in range(2):

        @pl.when((key_stretch <= meta_ref[3 * unit + 1]) & (key_stretch >= meta_ref[3 * unit + 2]))
        def _():
            mask = mask_of(meta_ref, ends_ref, unit, rows, key_stretch)
            block = jnp.concatenate([near_ref[...], far_ref[...]], axis=0)
            key, value = block[:, :HEAD], block[:, HEAD:]
            query = q_ref[unit].reshape(HEADS * rows, HEAD)
            grad = grads[unit]
            probs = jnp.where(mask, jnp.exp(mm_nt(key, query) - lse_ref[unit]), 0.0)
            score_grad = (probs * (mm_nt(value, grad) - delta[unit])).astype(bf16)
            acc[unit] += mm_tn(key, score_grad)
            both[:, :HEAD] += mm(score_grad, query)
            both[:, HEAD:] += mm(probs.astype(bf16), grad)

    dnear_ref[...] = both[:rows].astype(bf16)
    dfar_ref[...] = both[rows:].astype(bf16)

    @pl.when(step == pl.num_programs(0) - 1)
    def _():
        gain = gain_ref[...]
        total = jnp.zeros_like(gain)
        for unit in range(2):
            mine = slice(unit * rows, (unit + 1) * rows)
            grad = acc[unit].T * HEAD**-0.5
            for head in range(HEADS):
                back = rotate(grad[head * rows : (head + 1) * rows], cos_ref[mine], -sin_ref[mine])
                raw = raw_ref[head, mine]
                scale = norm_scale(raw)
                total = total + jnp.sum(back * raw * scale, axis=0, keepdims=True)
                back = norm_back(raw, scale, gain * back)
                dq_ref[mine, head * HEAD : (head + 1) * HEAD] = back.astype(bf16)
        dgain_ref[...] = total


def whole_of(array):
    return pl.BlockSpec(array.shape, lambda *_: (0,) * len(array.shape))


def attend(meta, ends, slots, query, near, far):
    rows = query.shape[2]
    wide = HEADS * rows
    keys = pl.BlockSpec((None, None, rows, 2 * HEAD), lambda j, *_: (j // 2, j % 2, 0, 0))
    outs = [
        jax.ShapeDtypeStruct((2 * rows, HEADS * HEAD), bf16),
        jax.ShapeDtypeStruct((2, HEAD, wide), f32),
        jax.ShapeDtypeStruct((2, 1, wide), f32),
    ]
    return pl.pallas_call(
        functools.partial(attend_kernel, rows),
        grid_spec=pltpu.PrefetchScalarGridSpec(
            num_scalar_prefetch=3,
            grid=(slots.shape[0],),
            in_specs=[whole_of(query), keys, keys],
            out_specs=[whole_of(out) for out in outs],
            scratch_shapes=[
                pltpu.VMEM((2, 1, wide), f32),
                pltpu.VMEM((2, 1, wide), f32),
                pltpu.VMEM((2, HEAD, wide), f32),
            ],
        ),
        out_shape=outs,
        name="attend",
        cost_estimate=pl.CostEstimate(
            flops=4 * 2 * 9 * STRETCH * wide * HEAD,
            bytes_accessed=4 * near.size,
            transcendentals=2 * 9 * STRETCH * wide,
        ),
    )(meta, ends, slots, query, near, far)


def attend_back(meta, ends, slots, query, grad, lse, turned, raw, gain, cosine, sine, near, far):
    rows = query.shape[2]
    wide = HEADS * rows
    keys = pl.BlockSpec((None, None, rows, 2 * HEAD), lambda j, *_: (j // 2, j % 2, 0, 0))
    fixed = [query, grad, lse, turned, raw, gain, cosine, sine]
    outs = [jax.ShapeDtypeStruct(grad.shape, bf16), jax.ShapeDtypeStruct(gain.shape, f32)]
    return pl.pallas_call(
        functools.partial(attend_back_kernel, rows),
        grid_spec=pltpu.PrefetchScalarGridSpec(
            num_scalar_prefetch=3,
            grid=(slots.shape[0],),
            in_specs=[*[whole_of(array) for array in fixed], keys, keys],
            out_specs=[*[whole_of(out) for out in outs], keys, keys],
            scratch_shapes=[
                pltpu.VMEM((2, wide, HEAD), bf16),
                pltpu.VMEM((2, 1, wide), f32),
                pltpu.VMEM((2, HEAD, wide), f32),
                pltpu.VMEM((STRETCH, 2 * HEAD), f32),
            ],
        ),
        out_shape=[*outs, jax.ShapeDtypeStruct(near.shape, bf16), jax.ShapeDtypeStruct(near.shape, bf16)],
        name="attend_back",
        cost_estimate=pl.CostEstimate(
            flops=10 * 2 * 9 * STRETCH * wide * HEAD,
            bytes_accessed=8 * near.size,
            transcendentals=2 * 9 * STRETCH * wide,
        ),
    )(meta, ends, slots, *fixed, near, far)


def blocks_of(tops, low, member, members, ff):
    return [(((hi * 2 + low) * 2 + y) * members + member) * ff for hi in range(tops) for y in range(2)]

def pack_kernel(tops, members, ff, gate_ref, up_ref, out_ref):
    for which, ref in enumerate((gate_ref, up_ref)):
        value = ref[...]
        for low in range(2):
            for member in range(members):
                cuts = [value[:, at : at + ff] for at in blocks_of(tops, low, member, members, ff)]
                out_ref[low, member, which] = jnp.concatenate(cuts, axis=1)

def pack(gate, up, tops, members, ff):
    rows = gate.shape[0]
    return pl.pallas_call(functools.partial(pack_kernel, tops, members, ff),
        out_shape=jax.ShapeDtypeStruct((2, members, 2, rows, 2 * tops * ff), bf16), name="pack")(gate, up)

def unpack_kernel(tops, members, ff, low_ref, in_ref, gate_ref, up_ref):
    for which, ref in enumerate((gate_ref, up_ref)):
        pieces = [None] * (2 * tops * 2 * members)
        for low in range(2):
            for member in range(members):
                value = in_ref[member, low_ref[0] ^ low, which].astype(f32)
                for i, at in enumerate(blocks_of(tops, low, member, members, ff)):
                    pieces[at // ff] = value[:, i * ff : (i + 1) * ff]
        ref[...] = jnp.concatenate(pieces, axis=1)

def unpack(moved, low_bit, tops, members, ff):
    rows = moved.shape[3]
    shape = jax.ShapeDtypeStruct((rows, 4 * tops * members * ff), f32)
    return pl.pallas_call(functools.partial(unpack_kernel, tops, members, ff),
        in_specs=[pl.BlockSpec(memory_space=pltpu.SMEM), pl.BlockSpec(memory_space=pltpu.VMEM)],
        out_shape=[shape, shape], name="unpack")(low_bit[None], moved)

def merge_kernel(in_ref, gate_ref, up_ref):
    for which, ref in enumerate((gate_ref, up_ref)):
        for low in range(2):
            ref[low] = jnp.concatenate([in_ref[m, low, which] for m in range(in_ref.shape[0])], axis=0)

def merge(moved):
    members, _, _, rows, wide = moved.shape
    shape = jax.ShapeDtypeStruct((2, members * rows, wide), bf16)
    return pl.pallas_call(merge_kernel, out_shape=[shape, shape], name="merge")(moved)

def split_kernel(gate_ref, up_ref, out_ref):
    members, rows = out_ref.shape[1], out_ref.shape[3]
    for which, ref in enumerate((gate_ref, up_ref)):
        for low in range(2):
            value = ref[low]
            for m in range(members):
                out_ref[low, m, which] = value[m * rows : (m + 1) * rows]

def split(gate, up, members):
    _, tall, wide = gate.shape
    return pl.pallas_call(split_kernel,
        out_shape=jax.ShapeDtypeStruct((2, members, 2, tall // members, wide), bf16), name="split")(gate, up)


def per_device(
    inputs,
    cotangent,
    lengths,
    deal,
    w_query,
    w_key,
    w_value,
    w_out,
    w_gate,
    w_up,
    w_down,
    gain_attn_pre,
    gain_attn_post,
    gain_ffw_pre,
    gain_ffw_post,
    gain_query,
    gain_key,
):
    rows, width = inputs.shape[1], inputs.shape[2]
    groups, members = lax.axis_size("dp"), lax.axis_size("seq")
    devices = groups * members
    total_rows = rows * devices
    dp_id, seq_id = lax.axis_index("dp"), lax.axis_index("seq")
    half_bit, x_bit, y_bit, z_bit = seq_id % 2, seq_id // 2, dp_id % 2, dp_id // 2 % 2
    tops = groups // 4
    count = 2 * rows
    model_rows, out_rows, ff_rows = w_query.shape[0], w_out.shape[0], w_down.shape[0]
    ff_local = 2 * tops * ff_rows
    wide_q = HEADS * HEAD
    gain_sizes = [gain_attn_pre.shape[0]] * 4 + [gain_query.shape[0]] * 2
    gain_total = sum(gain_sizes)
    block_rows = (model_rows + 8) // 8 * 8

    def regroup(array):
        kept = lax.dynamic_index_in_dim(array, y_bit, 0, keepdims=False)
        sent = lax.dynamic_index_in_dim(array, 1 - y_bit, 0, keepdims=False)
        return jnp.concatenate([kept, xor(sent, "dp", 1)], axis=0)

    def ungroup(array):
        kept, sent = array[:rows], array[rows:]
        return flips(jnp.stack([kept, xor(sent, "dp", 1)]), [y_bit])

    rows_in = regroup(inputs).astype(f32)

    gains = jnp.concatenate([gain_attn_pre, gain_attn_post, gain_ffw_pre, gain_ffw_post, gain_query, gain_key])
    gain_line = jnp.pad(gains[None, :], ((0, 0), (0, 2 * HEAD - gain_total)))
    kv_shard = jnp.concatenate([jnp.concatenate([w_key, w_value], axis=1), gain_line], axis=0)
    kv_blocks = gather_all(jnp.pad(kv_shard, ((0, block_rows - model_rows - 1), (0, 0))))
    kv_weight = kv_blocks.reshape(devices * block_rows, 2 * HEAD)
    q_shard = after(jnp.pad(w_query, ((0, block_rows - model_rows), (0, 0))), kv_weight)
    q_weight = gather_all(q_shard).reshape(devices * block_rows, wide_q)
    out_blocks = gather_all(after(w_out, q_weight))
    labels = all_labels()
    natural = jnp.stack([(dp_id ^ d) * members + (seq_id ^ s) for d, s in labels]).astype(jnp.int32)

    def selection(size, block, padded):
        within = jnp.arange(padded, dtype=jnp.int32)
        source = jnp.where(within < block, natural[:, None] * block + within, -1).reshape(-1)
        return (jnp.arange(size, dtype=jnp.int32)[:, None] == source[None, :]).astype(bf16)

    model_pick = selection(width, model_rows, block_rows)
    relative = jnp.arange(devices, dtype=jnp.int32)
    relative = jnp.sum(jnp.where(natural[:, None] == relative[None, :], relative[:, None], 0), axis=0)
    out_weight = place([out_blocks], natural).reshape(wide_q, width)
    device_pick = selection(devices, 1, 1)
    gain_blocks = kv_blocks[:, model_rows, :gain_total]
    gain_all = mm(device_pick, gain_blocks)
    full_gain, at = [], 0
    for size in gain_sizes:
        full_gain.append(gain_all[:, at : at + size].reshape(devices * size))
        at += size
    pre_attention, post_attention, pre_feed, post_feed, query_gain, key_gain = full_gain

    top_id = dp_id // 4

    def spread(piece):
        tall = [piece] + [xor(piece, "dp", 4 * k) for k in range(1, tops)]
        return tall + [xor(part, "dp", 1) for part in tall]

    def swap_columns(packed):
        kept = lax.dynamic_index_in_dim(packed, z_bit, 0, keepdims=False)
        sent = lax.dynamic_index_in_dim(packed, 1 - z_bit, 0, keepdims=False)
        both = jnp.stack([kept, xor(sent, "dp", 2)], axis=1)
        return lax.all_to_all(both, "seq", split_axis=0, concat_axis=0, tiled=True)

    def feed_weights(w_gate, w_up, w_down):
        owners = [(top_id ^ k) * 2 + (y_bit ^ u) for u in range(2) for k in range(tops)]
        down_weight = place(spread(w_down[None]), jnp.stack(owners).astype(jnp.int32)).reshape(ff_local, width)
        halves = merge(swap_columns(pack(w_gate, w_up, tops, members, ff_rows)))
        sources = [((top_id ^ k) * 2 + (z_bit ^ v)) * 2 + (y_bit ^ u) for u in range(2) for k in range(tops) for v in range(2)]
        sources = jnp.stack(sources).astype(jnp.int32)
        gate_weight, up_weight = [place(spread(half), sources).reshape(width, ff_local) for half in halves]
        return gate_weight, up_weight, down_weight

    seq_ends = jnp.cumsum(lax.dynamic_index_in_dim(lengths, y_bit, 0, keepdims=False))
    dealt = lax.dynamic_index_in_dim(deal, y_bit, 0, keepdims=False)
    unit_ids = jnp.stack([(dp_id ^ u) * members + seq_id for u in range(2)])
    stretches = dealt[unit_ids * rows // STRETCH]
    first_rows = stretches * STRETCH + unit_ids * rows % STRETCH
    my_rows = (first_rows[:, None] + jnp.arange(rows, dtype=jnp.int32)).reshape(count)
    starts = layout_start(seq_ends, my_rows)
    lows = starts.reshape(2, rows)[:, 0] // STRETCH
    meta = jnp.concatenate([jnp.stack([first_rows, stretches, lows], axis=1).reshape(-1), half_bit[None]])
    layers = groups // 2
    slot_ids = jnp.stack(
        [
            ((dp_id // 2 ^ z) * 2 + (y_bit ^ u)) * (members // 2) + (x_bit ^ x)
            for x in range(2)
            for z in range(layers)
            for u in range(2)
        ]
    )
    slots = dealt[slot_ids]
    positions = my_rows - starts
    valid = (my_rows < total_rows - STRETCH)[:, None]
    freqs = rope_base ** (-2.0 * jnp.arange(HEAD // 2, dtype=f32) / HEAD)
    angle = positions.astype(f32)[:, None] * freqs
    cosine, sine = jnp.cos(angle), jnp.sin(angle)

    scale_one = norm_scale(rows_in)
    normed_one = (rows_in * scale_one * pre_attention).astype(bf16)
    picked_one = mm(normed_one, model_pick).astype(bf16)
    key_raw, keys_mine = project_keys(picked_one, kv_weight, key_gain[None], cosine, sine)
    column = [keys_mine] + [xor(keys_mine, "dp", 2 * k) for k in range(1, layers)]
    across = [xor(part, "seq", 2) for part in column]
    column, across = jnp.stack(column), jnp.stack(across)
    near_keys = jnp.concatenate([column, across])
    far_keys = jnp.concatenate([xor(column, "seq", 1), xor(across, "seq", 1)])
    gate_weight, up_weight, down_weight = feed_weights(*lax.optimization_barrier((w_gate, w_up, w_down, keys_mine))[:3])
    query_raw, query_heads = project(picked_one, q_weight, query_gain[None], cosine, sine)
    q_natural = mm(model_pick, q_weight).astype(bf16)
    kv_natural = mm(model_pick, kv_weight).astype(bf16)
    query_heads, q_natural, kv_natural = lax.optimization_barrier((query_heads, q_natural, kv_natural))
    context_rows, turned, lse = attend(meta, seq_ends, slots, query_heads, near_keys, far_keys)
    attended = mm(context_rows, out_weight)
    scale_two = norm_scale(attended)
    hidden_res = rows_in + attended * scale_two * post_attention
    scale_three = norm_scale(hidden_res)
    normed_two = (hidden_res * scale_three * pre_feed).astype(bf16)

    normed_group = gather_group(normed_two)
    gate_raw = mm(normed_group, gate_weight)
    up_raw = mm(normed_group, up_weight)
    hidden_low = (jax.nn.gelu(gate_raw, approximate=True) * up_raw).astype(bf16)
    mixed = scatter_group(mm(hidden_low, down_weight).astype(bf16))
    scale_four = norm_scale(mixed)
    result = hidden_res + mixed * scale_four * post_feed
    output = ungroup(jnp.where(valid, result, 0.0).astype(bf16))

    upstream = jnp.where(valid, regroup(cotangent).astype(f32), 0.0)
    grad_post_feed = jnp.sum(upstream * mixed * scale_four, axis=0)
    mixed_grad = norm_back(mixed, scale_four, post_feed * upstream).astype(bf16)
    mixed_group = gather_group(mixed_grad)
    hidden_grad = mm_nt(mixed_group, down_weight)
    _, gelu_pull = jax.vjp(lambda g, u: jax.nn.gelu(g, approximate=True) * u, gate_raw, up_raw)
    gate_grad, up_grad = gelu_pull(hidden_grad)
    gate_grad, up_grad = gate_grad.astype(bf16), up_grad.astype(bf16)
    partial_grad = (mm_nt(gate_grad, gate_weight) + mm_nt(up_grad, up_weight)).astype(bf16)
    normed_two_grad = scatter_group(partial_grad)
    grad_pre_feed = jnp.sum(normed_two_grad * hidden_res * scale_three, axis=0)
    hidden_res_grad = upstream + norm_back(hidden_res, scale_three, pre_feed * normed_two_grad)

    def halve(total):
        kept = lax.dynamic_index_in_dim(total, y_bit, 2, keepdims=False)
        return kept, xor(lax.dynamic_index_in_dim(total, 1 - y_bit, 2, keepdims=False), "dp", 1)

    def finish(kept, got):
        kept = add16(kept, got)
        mine = lax.dynamic_index_in_dim(kept, top_id, 0, keepdims=False)
        rest = [xor(lax.dynamic_index_in_dim(kept, top_id ^ k, 0, keepdims=False), "dp", 4 * k) for k in range(1, tops)]
        return [mine, *rest]

    def total_of(parts):
        return functools.reduce(jnp.add, [part.astype(f32) for part in parts])

    def column_blocks(total):
        return total.astype(bf16).reshape(tops, 2, 2, members * model_rows, ff_local)

    hidden_low, mixed_group, normed_group, gate_grad, up_grad, _ = lax.optimization_barrier(
        (hidden_low, mixed_group, normed_group, gate_grad, up_grad, partial_grad)
    )
    down_halves = halve(mm_tn(hidden_low, mixed_group).astype(bf16).reshape(tops, 1, 2, ff_rows, width))
    gate_halves = halve(column_blocks(mm_tn(normed_group, gate_grad)))
    up_halves = halve(column_blocks(mm_tn(normed_group, up_grad)))

    grad_post_attention = jnp.sum(hidden_res_grad * attended * scale_two, axis=0)
    attended_grad = norm_back(attended, scale_two, post_attention * hidden_res_grad).astype(bf16)
    context_grad = mm_nt(attended_grad, out_weight).astype(bf16)
    query_grad, grad_query_gain, near_part, far_part = attend_back(
        meta, seq_ends, slots, query_heads, context_grad, lse, turned, query_raw, query_gain[None], cosine, sine, near_keys, far_keys
    )
    halves = lax.optimization_barrier((down_halves, gate_halves, up_halves, context_grad))[:3]
    down_parts, gate_parts, up_parts = [finish(*half) for half in halves]
    far_part = xor(far_part, "seq", 1)
    near_part = add16(near_part, far_part).reshape(2, layers, count, 2 * HEAD)
    near_part = add16(near_part[0], xor(near_part[1], "seq", 2))
    key_grads = near_part[0].astype(f32)
    for k in range(1, layers):
        key_grads = key_grads + xor(near_part[k], "dp", 2 * k).astype(f32)
    attended_low, query_low, _ = lax.optimization_barrier((attended_grad, query_grad, far_part))
    grad_out = mm_tn(context_rows, attended_low).astype(bf16).reshape(devices, out_rows, width)
    grad_query = mm_tn(picked_one, query_low).astype(bf16).reshape(devices, block_rows, wide_q)
    grad_query = scatter_all(grad_query)
    grad_out = scatter_all(place([grad_out], relative))
    down_parts, gate_parts, up_parts, _ = lax.optimization_barrier((down_parts, gate_parts, up_parts, near_part))
    grad_down = total_of(down_parts)[0]
    both_grads = split(total_of(gate_parts).astype(bf16), total_of(up_parts).astype(bf16), members)
    grad_gate, grad_up = unpack(swap_columns(both_grads), z_bit, tops, members, ff_rows)
    value_grad = key_grads[:, HEAD:].astype(bf16)
    key_turned = rotate(key_grads[:, :HEAD], cosine, -sine)
    key_scale = norm_scale(key_raw)
    grad_key_gain = jnp.sum(key_turned * key_raw * key_scale, axis=0)
    key_grad = norm_back(key_raw, key_scale, key_gain * key_turned).astype(bf16)
    kv_grad = jnp.concatenate([key_grad, value_grad], axis=1)
    normed_one_grad = mm_nt(query_grad, q_natural) + mm_nt(kv_grad, kv_natural)
    grad_pre_attention = jnp.sum(normed_one_grad * rows_in * scale_one, axis=0)
    rows_grad = hidden_res_grad + norm_back(rows_in, scale_one, pre_attention * normed_one_grad)
    input_grad = ungroup(rows_grad.astype(bf16))
    grad_kv = mm_tn(picked_one, kv_grad).reshape(devices, block_rows, 2 * HEAD)
    gain_grads = [
        grad_pre_attention,
        grad_post_attention,
        grad_pre_feed,
        grad_post_feed,
        grad_query_gain,
        grad_key_gain,
    ]
    gain_grads = jnp.concatenate([g.reshape(devices, -1) for g in gain_grads], axis=1)
    gain_grads = mm_tn(device_pick, gain_grads.astype(bf16))
    gain_grads = jnp.pad(
        gain_grads[:, None, :], ((0, 0), (model_rows, block_rows - model_rows - 1), (0, 2 * HEAD - gain_total))
    )
    last = scatter_all((grad_kv + gain_grads).astype(bf16))
    gain_out, at = [], 0
    for size in gain_sizes:
        gain_out.append(last[model_rows, at : at + size])
        at += size
    return (
        output,
        input_grad,
        grad_query[:model_rows],
        last[:model_rows, :HEAD],
        last[:model_rows, HEAD:],
        grad_out,
        grad_gate,
        grad_up,
        grad_down,
        *gain_out,
    )


def solution(mesh):
    split = P(None, ALL, None)
    weight, gain = P(ALL, None), P(ALL)
    return jax.shard_map(
        per_device,
        mesh=mesh,
        in_specs=(split, split, P(), P(), *[weight] * 7, *[gain] * 6),
        out_specs=(split, split, *[weight] * 7, *[gain] * 6),
        check_vma=False,
    )
```

time: 848 us -> 687 us (0.81)
  local copies, waits for them, and re-layouts: 206 us -> 104 us
  other arithmetic: 118 us -> 71.2 us
  starting transfers between devices: 127 us -> 93.8 us
  Pallas kernels: 40.4 us -> 67.4 us
  matrix products: 107 us -> 92.8 us
  waiting for transfers between devices: 235 us -> 244 us
    ppermute x14 -> x30, waiting for transfers between devices: 7.38 us -> 93.1 us  [xor_both(): lax.ppermute(value, ALL, [(i, i ^ mask) for i in range(lax.axis_size('dp'...]
    ppermute x118 -> x59, waiting for transfers between devices: 228 us -> 151 us  [xor(): lax.ppermute(value, axis, [(i, i ^ mask) for i in range(lax.axis_size(axi...]
    ppermute x118 -> x59, starting transfers between devices: 116 us -> 61.1 us  [xor(): lax.ppermute(value, axis, [(i, i ^ mask) for i in range(lax.axis_size(axi...]
    slice x52 -> x16, local copies, waits for them, and re-layouts: 45.5 us -> 7.56 us  [the longest x14 7.51 us: scatter_all(): got = xor_both(total[half:], dp_mask, seq_mask)]
    select_n x12 -> x2, other arithmetic: 35 us -> 4.02 us  [flips(): value = jnp.where(bit == 1, lax.concatenate(halves, axis), value)]
    unnamed x345 -> x242, local copies, waits for them, and re-layouts: 58 us -> 31.6 us
    pallas_call x0 -> x6, Pallas kernels: none -> 17.8 us  [the longest x1 4.68 us: project(): pl.pallas_call(functools.partial(project_kernel, HEAD ** (-0.5)), grid=(H...]
    reshape x8 -> x0, local copies, waits for them, and re-layouts: 16.9 us -> none  [the longest x4 5.59 us: by_owner(): split = weight.reshape(model_rows, tops, 2, 2, members, ff_rows)]
  transfers between devices with their start and end apart: 132 -> 91, of which waited for: 56 -> 45; matrix products, arithmetic and copies ran while one was open for 39% -> 28% of each run, Pallas kernels for 5% -> 10%
where the time goes in v3:
time: 687 us; the launch traced here: 676 us
  waiting for transfers between devices  244 us (36%)
  local copies, waits for them, and re-layouts  104 us (15%)
  starting transfers between devices  93.8 us (14%)
  matrix products  92.8 us (14%)
  other arithmetic  71.2 us (10%)
  Pallas kernels  67.4 us (10%)
    ppermute x59, waiting for transfers between devices, xor(): lax.ppermute(value, axis, [(i, i ^ mask) for i in range(lax.axis_size(axi...  151 us
    ppermute x30, waiting for transfers between devices, xor_both(): lax.ppermute(value, ALL, [(i, i ^ mask) for i in range(lax.axis_size('dp'...  93.1 us
    dot_general x21, matrix products, dot(): lax.dot_general(left, right, (dims, ((), ())), preferred_element_type=f32)  92.8 us
    ppermute x59, starting transfers between devices, xor(): lax.ppermute(value, axis, [(i, i ^ mask) for i in range(lax.axis_size(axi...  61.1 us
    unnamed x242, local copies, waits for them, and re-layouts  31.6 us
    ppermute x30, starting transfers between devices, xor_both(): lax.ppermute(value, ALL, [(i, i ^ mask) for i in range(lax.axis_size('dp'...  25.7 us
    pallas_call x1, Pallas kernels, attend_back(): pl.pallas_call(functools.partial(attend_back_kernel, rows), grid_spec=plt...  18.7 us
    pallas_call x5, Pallas kernels, place(): pl.pallas_call(functools.partial(place_kernel, sizes), grid_spec=pltpu.Pr...  16.9 us
  transfers between devices with their start and end apart: 91, of which 45 were waited for; matrix products, arithmetic and copies ran while one was open for 28% of the time, Pallas kernels for 10%

profile of v3, /device:TPU:0, one launch (start us, length us, event | category | flops | bytes accessed | tf_op | source)
XLA Modules:
  0.0 676.1 jit_solution(12489863194973308955)
XLA Ops:
  55.3 12.2 %collective-permute-done.6 = bf16[1,40,1024]{2,1,0:T(8,128)(2,1)S(1)} collective-permute-done((bf16[1,40,1024]{2,1,0:T(8,128)(2,1)S(1)}, bf16[1,40,1024]{2,1,0:T(8,128)(2,1)S(1)}, u32[]{:S(2)}, u32[]{:S(2)}) %collective-permute-start.6) | collective-permute-done | bytes 81952 | tf_op jit(solution)/shard_map/ppermute | solution.py:67
  71.2 7.8 %collective-permute-done.7 = bf16[2,40,1024]{2,1,0:T(8,128)(2,1)S(1)} collective-permute-done((bf16[2,40,1024]{2,1,0:T(8,128)(2,1)S(1)}, bf16[2,40,1024]{2,1,0:T(8,128)(2,1)S(1)}, u32[]{:S(2)}, u32[]{:S(2)}) %collective-permute-start.7) | collective-permute-done | bytes 163872 | tf_op jit(solution)/shard_map/ppermute | solution.py:67
  97.4 7.6 %collective-permute-done.9 = bf16[8,40,1024]{2,1,0:T(8,128)(2,1)} collective-permute-done((bf16[8,40,1024]{2,1,0:T(8,128)(2,1)}, bf16[8,40,1024]{2,1,0:T(8,128)(2,1)}, u32[]{:S(2)}, u32[]{:S(2)}) %collective-permute-start.9) | collective-permute-done | bytes 655392 | tf_op jit(solution)/shard_map/ppermute | solution.py:67
  151.9 7.8 %collective-permute-done.22 = bf16[4,32,1152]{2,1,0:T(8,128)(2,1)S(1)} collective-permute-done((bf16[4,32,1152]{2,1,0:T(8,128)(2,1)S(1)}, bf16[4,32,1152]{2,1,0:T(8,128)(2,1)S(1)}, u32[]{:S(2)}, u32[]{:S(2)}) %collective-permute-start.22) | collective-permute-done | bytes 294944 | tf_op jit(solution)/shard_map/ppermute | solution.py:67
  163.8 10.6 %collective-permute-done.23 = bf16[8,32,1152]{2,1,0:T(8,128)(2,1)S(1)} collective-permute-done((bf16[8,32,1152]{2,1,0:T(8,128)(2,1)S(1)}, bf16[8,32,1152]{2,1,0:T(8,128)(2,1)S(1)}, u32[]{:S(2)}, u32[]{:S(2)}) %collective-permute-start.23) | collective-permute-done | bytes 589856 | tf_op jit(solution)/shard_map/ppermute | solution.py:67
  191.5 14.0 %attend.1 = (bf16[256,1024]{1,0:T(8,128)(2,1)}, f32[2,256,512]{2,1,0:T(8,128)}, f32[2,1,512]{2,1,0:T(1,128)}) custom-call(s32[7]{0:T(128)} %pad_add_fusion.1.meta_ref, s32[4]{0:T(128)} %bitcast.334, s32[16]{0:T(128)} %gather_fusion.1, bf16[2,4,128,256]{3,2,1,0:T(8,128)(2,1)} %get-tuple-element.59.q_ref, ...), custom_call_target="tpu_custom_call" | custom-call | flops 2415919104 | bytes 4194304 | tf_op jit(solution)/shard_map/attend/pallas_call | solution.py:375
  242.7 7.8 %collective-permute-done.37.refs_2_ = bf16[2,144,864]{2,1,0:T(8,128)(2,1)} collective-permute-done((bf16[2,144,864]{2,1,0:T(8,128)(2,1)}, bf16[2,144,864]{2,1,0:T(8,128)(2,1)}, u32[]{:S(2)}, u32[]{:S(2)}) %collective-permute-start.37) | collective-permute-done | bytes 497696 | tf_op jit(solution)/shard_map/ppermute | solution.py:61
  250.5 10.0 %collective-permute-done.38.refs_3_ = bf16[2,144,864]{2,1,0:T(8,128)(2,1)} collective-permute-done((bf16[2,144,864]{2,1,0:T(8,128)(2,1)}, bf16[2,144,864]{2,1,0:T(8,128)(2,1)}, u32[]{:S(2)}, u32[]{:S(2)}) %collective-permute-start.38) | collective-permute-done | bytes 497696 | tf_op jit(solution)/shard_map/ppermute | solution.py:61
  278.1 7.0 %fusion.65 = f32[2048,864]{0,1:T(8,128)S(1)} fusion(bf16[2048,1152]{1,0:T(8,128)(2,1)} %constant_dynamic-update-slice_fusion.43, bf16[1152,864]{1,0:T(8,128)(2,1)S(1)} %bitcast.300), kind=kOutput, calls=%fused_computation.319 | convolution fusion | flops 4076863488 | bytes 13787136 | tf_op jit(solution)/shard_map/dot_general | solution.py:45
  285.1 9.1 %multiply_convert_fusion.1 = (bf16[2048,864]{0,1:T(8,128)(2,1)S(1)}, f32[2048,864]{0,1:T(8,128)}) fusion(f32[2048,864]{0,1:T(8,128)S(1)} %fusion.65, bf16[2048,1152]{1,0:T(8,128)(2,1)S(1)} %copy-done.65, bf16[1152,864]{1,0:T(8,128)(2,1)S(1)} %bitcast.302), kind=kOutput, calls=%fused_computation.14 | convolution fusion | flops 4094558208 | bytes 24403968 | tf_op jit(solution)/shard_map/dot_general | solution.py:45
  325.0 7.2 %collective-permute-done.46 = bf16[256,1152]{1,0:T(8,128)(2,1)S(1)} collective-permute-done((bf16[256,1152]{1,0:T(8,128)(2,1)}, bf16[256,1152]{1,0:T(8,128)(2,1)S(1)}, u32[]{:S(2)}, u32[]{:S(2)}) %collective-permute-start.46) | collective-permute-done | bytes 589856 | tf_op jit(solution)/shard_map/ppermute | solution.py:61
  343.3 10.4 %collective-permute-done.50 = bf16[256,1152]{1,0:T(8,128)(2,1)S(1)} collective-permute-done((bf16[256,1152]{1,0:T(8,128)(2,1)S(1)}, bf16[256,1152]{1,0:T(8,128)(2,1)S(1)}, u32[]{:S(2)}, u32[]{:S(2)}) %collective-permute-start.50) | collective-permute-done | bytes 589856 | tf_op jit(solution)/shard_map/ppermute | solution.py:61
  364.7 14.3 %fusion.6 = (bf16[2048,864]{0,1:T(8,128)(2,1)}, bf16[2048,864]{0,1:T(8,128)(2,1)}) fusion(f32[2048,864]{0,1:T(8,128)S(1)} %bitcast.337, f32[2048,864]{0,1:T(8,128)} %get-tuple-element.227, bf16[2048,1152]{1,0:T(8,128)(2,1)S(1)} %constant_dynamic-update-slice_fusion.51, bf16[864,1152]{1,0:T(8,128)(2,1)S(1)} %bitcast.313), kind=kOutput, calls=%fused_computation.12 | convolution fusion | flops 4119330816 | bytes 27942912 | tf_op jit(solution)/shard_map/dot_general | solution.py:45
  379.0 8.0 %fusion.66 = f32[2048,1152]{1,0:T(8,128)S(1)} fusion(bf16[2048,864]{0,1:T(8,128)(2,1)} %get-tuple-element.84, bf16[1152,864]{1,0:T(8,128)(2,1)S(1)} %bitcast.303), kind=kOutput, calls=%fused_computation.320 | convolution fusion | flops 4076863488 | bytes 14966784 | tf_op jit(solution)/shard_map/dot_general | solution.py:45
  387.0 6.4 add_convert_fusion
  400.9 8.1 %convolution_convert_fusion.5 = bf16[864,1152]{1,0:T(8,128)(2,1)S(1)} fusion(bf16[2048,864]{0,1:T(8,128)(2,1)} %copy-done.94, bf16[2048,1152]{1,0:T(8,128)(2,1)} %copy-done.66), kind=kOutput, calls=%fused_computation.28 | convolution fusion | flops 4077858816 | bytes 10248192 | tf_op jit(solution)/shard_map/dot_general | solution.py:45
  456.3 18.7 %attend_back.1 = (bf16[256,1024]{1,0:T(8,128)(2,1)}, f32[1,256]{1,0:T(1,128)}, bf16[8,2,128,512]{3,2,1,0:T(8,128)(2,1)}, bf16[8,2,128,512]{3,2,1,0:T(8,128)(2,1)}) custom-call(s32[7]{0:T(128)} %pad_add_fusion.1.meta_ref, s32[4]{0:T(128)} %bitcast.335, s32[16]{0:T(128)} %gather_fusion.1, bf16[2,4,128,256]{3,2,1,0:T(8,128)(2,1)} %get-tuple-element.59.q_ref, ...), custom_call_target="tpu_custom_call" | custom-call | flops 6039797760 | bytes 8388608 | tf_op jit(solution)/shard_map/attend_back/pallas_call | solution.py:404
  477.3 13.6 %collective-permute-done.84 = bf16[2,2,144,864]{3,2,1,0:T(8,128)(2,1)} collective-permute-done((bf16[2,2,144,864]{3,2,1,0:T(8,128)(2,1)}, bf16[2,2,144,864]{3,2,1,0:T(8,128)(2,1)}, u32[]{:S(2)}, u32[]{:S(2)}) %collective-permute-start.84) | collective-permute-done | bytes 995360 | tf_op jit(solution)/shard_map/ppermute | solution.py:61
  518.1 9.7 %collective-permute-done.62 = bf16[4,256,512]{2,1,0:T(8,128)(2,1)} collective-permute-done((bf16[4,256,512]{2,1,0:T(8,128)(2,1)}, bf16[4,256,512]{2,1,0:T(8,128)(2,1)}, u32[]{:S(2)}, u32[]{:S(2)}) %collective-permute-start.62) | collective-permute-done | bytes 1048608 | tf_op jit(solution)/shard_map/ppermute | solution.py:61
  530.4 9.2 %collective-permute-done.85 = bf16[1,216,1152]{2,1,0:T(8,128)(2,1)} collective-permute-done((bf16[1,216,1152]{2,1,0:T(8,128)(2,1)}, bf16[1,216,1152]{2,1,0:T(8,128)(2,1)}, u32[]{:S(2)}, u32[]{:S(2)}) %collective-permute-start.85) | collective-permute-done | bytes 497696 | tf_op jit(solution)/shard_map/ppermute | solution.py:61
  539.6 11.1 %collective-permute-done.86 = bf16[2,144,864]{2,1,0:T(8,128)(2,1)} collective-permute-done((bf16[2,144,864]{2,1,0:T(8,128)(2,1)}, bf16[2,144,864]{2,1,0:T(8,128)(2,1)}, u32[]{:S(2)}, u32[]{:S(2)}) %collective-permute-start.86) | collective-permute-done | bytes 497696 | tf_op jit(solution)/shard_map/ppermute | solution.py:61
  550.7 10.8 %collective-permute-done.87 = bf16[2,144,864]{2,1,0:T(8,128)(2,1)} collective-permute-done((bf16[2,144,864]{2,1,0:T(8,128)(2,1)}, bf16[2,144,864]{2,1,0:T(8,128)(2,1)}, u32[]{:S(2)}, u32[]{:S(2)}) %collective-permute-start.87) | collective-permute-done | bytes 497696 | tf_op jit(solution)/shard_map/ppermute | solution.py:61
  579.6 22.3 %collective-permute-done.63 = bf16[256,512]{1,0:T(8,128)(2,1)S(1)} collective-permute-done((bf16[256,512]{1,0:T(8,128)(2,1)S(1)}, bf16[256,512]{1,0:T(8,128)(2,1)S(1)}, u32[]{:S(2)}, u32[]{:S(2)}) %collective-permute-start.63) | collective-permute-done | bytes 262176 | tf_op jit(solution)/shard_map/ppermute | solution.py:61
  659.9 7.9 %collective-permute-done.70 = bf16[2,40,1024]{2,1,0:T(8,128)(2,1)S(1)} collective-permute-done((bf16[2,40,1024]{2,1,0:T(8,128)(2,1)S(1)}, bf16[2,40,1024]{2,1,0:T(8,128)(2,1)S(1)}, u32[]{:S(2)}, u32[]{:S(2)}) %collective-permute-start.70) | collective-permute-done | bytes 163872 | tf_op jit(solution)/shard_map/ppermute | solution.py:67
  (630 shorter events, 421.6 us)
Async XLA Ops:
  44.9 66.4 %collective-permute-start.14 = (bf16[2,128,512]{2,1,0:T(8,128)(2,1)}, bf16[2,128,512]{2,1,0:T(8,128)(2,1)S(1)}, u32[]{:S(2)}, u32[]{:S(2)}) collective-permute-start(bf16[2,128,512]{2,1,0:T(8,128)(2,1)} %get-tuple-element.60), channel_id=1, source_target_pairs={{0,2},{1,3},{2,0},{3,1},{4,6},{5,7},{6,4},{7,5},{8,10},{9,11},{10,... | collective-permute-start | bytes 786440 | tf_op jit(solution)/shard_map/ppermute | solution.py:61
  46.4 48.2 %collective-permute-start.13 = (bf16[2,128,512]{2,1,0:T(8,128)(2,1)}, bf16[2,128,512]{2,1,0:T(8,128)(2,1)}, u32[]{:S(2)}, u32[]{:S(2)}) collective-permute-start(bf16[2,128,512]{2,1,0:T(8,128)(2,1)} %get-tuple-element.60), channel_id=1, source_target_pairs={{0,24},{4,28},{8,16},{12,20},{16,8},{20,12},{24,0},{28,4},{1,25},{... | collective-permute-start | bytes 786440 | tf_op jit(solution)/shard_map/ppermute | solution.py:61
  48.2 59.7 %collective-permute-start.12 = (bf16[2,128,512]{2,1,0:T(8,128)(2,1)}, bf16[2,128,512]{2,1,0:T(8,128)(2,1)}, u32[]{:S(2)}, u32[]{:S(2)}) collective-permute-start(bf16[2,128,512]{2,1,0:T(8,128)(2,1)} %get-tuple-element.60), channel_id=1, source_target_pairs={{0,16},{4,20},{8,24},{12,28},{16,0},{20,4},{24,8},{28,12},{1,17},{... | collective-permute-start | bytes 786440 | tf_op jit(solution)/shard_map/ppermute | solution.py:61
  48.2 44.6 %collective-permute-start.11 = (bf16[2,128,512]{2,1,0:T(8,128)(2,1)}, bf16[2,128,512]{2,1,0:T(8,128)(2,1)S(1)}, u32[]{:S(2)}, u32[]{:S(2)}) collective-permute-start(bf16[2,128,512]{2,1,0:T(8,128)(2,1)} %get-tuple-element.60), channel_id=1, source_target_pairs={{0,8},{4,12},{8,0},{12,4},{16,24},{20,28},{24,16},{28,20},{1,9},{5... | collective-permute-start | bytes 786440 | tf_op jit(solution)/shard_map/ppermute | solution.py:61
  92.8 36.0 %collective-permute-start.39 = (bf16[1,216,1152]{2,1,0:T(8,128)(2,1)}, bf16[1,216,1152]{2,1,0:T(8,128)(2,1)}, u32[]{:S(2)}, u32[]{:S(2)}) collective-permute-start(bf16[1,216,1152]{2,1,0:T(8,128)(2,1)} %bitcast.125.refs_0_), channel_id=1, source_target_pairs={{0,16},{4,20},{8,24},{12,28},{16,0},{20,4},{24,8},{28,12},{1,17},{... | collective-permute-start | bytes 1493000 | tf_op jit(solution)/shard_map/ppermute | solution.py:61
  128.9 90.8 %collective-permute-start.40 = (bf16[1,216,1152]{2,1,0:T(8,128)(2,1)}, bf16[1,216,1152]{2,1,0:T(8,128)(2,1)}, u32[]{:S(2)}, u32[]{:S(2)}) collective-permute-start(bf16[1,216,1152]{2,1,0:T(8,128)(2,1)} %bitcast.125.refs_0_), channel_id=1, source_target_pairs={{0,4},{4,0},{8,12},{12,8},{16,20},{20,16},{24,28},{28,24},{1,5},{5... | collective-permute-start | bytes 1493000 | tf_op jit(solution)/shard_map/ppermute | solution.py:61
  129.4 46.4 %collective-permute-start.18 = (bf16[4,2,128,512]{3,2,1,0:T(8,128)(2,1)}, bf16[4,2,128,512]{3,2,1,0:T(8,128)(2,1)}, u32[]{:S(2)}, u32[]{:S(2)}) collective-permute-start(bf16[4,2,128,512]{3,2,1,0:T(8,128)(2,1)} %pad_maximum_fusion.2), channel_id=1, source_target_pairs={{0,1},{1,0},{2,3},{3,2},{4,5},{5,4},{6,7},{7,6},{8,9},{9,8},{10,11... | collective-permute-start | bytes 3145736 | tf_op jit(solution)/shard_map/ppermute | solution.py:61
  129.5 92.8 %collective-permute-start.41 = (bf16[1,216,1152]{2,1,0:T(8,128)(2,1)}, bf16[1,216,1152]{2,1,0:T(8,128)(2,1)}, u32[]{:S(2)}, u32[]{:S(2)}) collective-permute-start(bf16[1,216,1152]{2,1,0:T(8,128)(2,1)} %collective-permute-done.39.refs_1_), channel_id=1, source_target_pairs={{0,4},{4,0},{8,12},{12,8},{16,20},{20,16},{24,28},{28,24},{1,5},{5... | collective-permute-start | bytes 1493000 | tf_op jit(solution)/shard_map/ppermute | solution.py:61
  133.3 44.9 %collective-permute-start.19 = (bf16[4,2,128,512]{3,2,1,0:T(8,128)(2,1)}, bf16[4,2,128,512]{3,2,1,0:T(8,128)(2,1)}, u32[]{:S(2)}, u32[]{:S(2)}) collective-permute-start(bf16[4,2,128,512]{3,2,1,0:T(8,128)(2,1)} %pad_maximum_fusion.3), channel_id=1, source_target_pairs={{0,1},{1,0},{2,3},{3,2},{4,5},{5,4},{6,7},{7,6},{8,9},{9,8},{10,11... | collective-permute-start | bytes 3145736 | tf_op jit(solution)/shard_map/ppermute | solution.py:61
  174.4 52.2 %collective-permute-start.34 = (bf16[2,144,864]{2,1,0:T(8,128)(2,1)}, bf16[2,144,864]{2,1,0:T(8,128)(2,1)}, u32[]{:S(2)}, u32[]{:S(2)}) collective-permute-start(bf16[2,144,864]{2,1,0:T(8,128)(2,1)} %get-tuple-element.65.refs_0_), channel_id=1, source_target_pairs={{0,4},{4,0},{8,12},{12,8},{16,20},{20,16},{24,28},{28,24},{1,5},{5... | collective-permute-start | bytes 1493000 | tf_op jit(solution)/shard_map/ppermute | solution.py:61
  178.1 46.0 %collective-permute-start.33 = (bf16[2,144,864]{2,1,0:T(8,128)(2,1)}, bf16[2,144,864]{2,1,0:T(8,128)(2,1)}, u32[]{:S(2)}, u32[]{:S(2)}) collective-permute-start(bf16[2,144,864]{2,1,0:T(8,128)(2,1)} %get-tuple-element.65.refs_0_), channel_id=1, source_target_pairs={{0,16},{4,20},{8,24},{12,28},{16,0},{20,4},{24,8},{28,12},{1,17},{... | collective-permute-start | bytes 1493000 | tf_op jit(solution)/shard_map/ppermute | solution.py:61
  219.7 44.1 %collective-permute-start.26 = (bf16[256,1152]{1,0:T(8,128)(2,1)}, bf16[256,1152]{1,0:T(8,128)(2,1)S(1)}, u32[]{:S(2)}, u32[]{:S(2)}) collective-permute-start(bf16[256,1152]{1,0:T(8,128)(2,1)} %get-tuple-element.113), channel_id=1, source_target_pairs={{0,8},{4,12},{8,0},{12,4},{16,24},{20,28},{24,16},{28,20},{1,9},{5... | collective-permute-start | bytes 1769480 | tf_op jit(solution)/shard_map/ppermute | solution.py:61
  222.4 42.0 %collective-permute-start.25 = (bf16[256,1152]{1,0:T(8,128)(2,1)}, bf16[256,1152]{1,0:T(8,128)(2,1)S(1)}, u32[]{:S(2)}, u32[]{:S(2)}) collective-permute-start(bf16[256,1152]{1,0:T(8,128)(2,1)} %get-tuple-element.113), channel_id=1, source_target_pairs={{0,2},{1,3},{2,0},{3,1},{4,6},{5,7},{6,4},{7,5},{8,10},{9,11},{10,... | collective-permute-start | bytes 1769480 | tf_op jit(solution)/shard_map/ppermute | solution.py:61
  399.2 76.1 %collective-permute-start.47 = (bf16[128,1152]{1,0:T(8,128)(2,1)}, bf16[128,1152]{1,0:T(8,128)(2,1)}, u32[]{:S(2)}, u32[]{:S(2)}) collective-permute-start(bf16[128,1152]{1,0:T(8,128)(2,1)} %get-tuple-element.162), channel_id=1, source_target_pairs={{0,4},{4,0},{8,12},{12,8},{16,20},{20,16},{24,28},{28,24},{1,5},{5... | collective-permute-start | bytes 884744 | tf_op jit(solution)/shard_map/ppermute | solution.py:61
  410.5 66.8 %collective-permute-start.82 = (bf16[2,1,216,1152]{3,2,1,0:T(8,128)(2,1)}, bf16[2,1,216,1152]{3,2,1,0:T(8,128)(2,1)}, u32[]{:S(2)}, u32[]{:S(2)}) collective-permute-start(bf16[2,1,216,1152]{3,2,1,0:T(8,128)(2,1)} %get-tuple-element.141), channel_id=1, source_target_pairs={{0,4},{4,0},{8,12},{12,8},{16,20},{20,16},{24,28},{28,24},{1,5},{5... | collective-permute-start | bytes 2985992 | tf_op jit(solution)/shard_map/ppermute | solution.py:61
  445.3 32.0 %collective-permute-start.83 = (bf16[2,2,144,864]{3,2,1,0:T(8,128)(2,1)}, bf16[2,2,144,864]{3,2,1,0:T(8,128)(2,1)}, u32[]{:S(2)}, u32[]{:S(2)}) collective-permute-start(bf16[2,2,144,864]{3,2,1,0:T(8,128)(2,1)} %get-tuple-element.139), channel_id=1, source_target_pairs={{0,4},{4,0},{8,12},{12,8},{16,20},{20,16},{24,28},{28,24},{1,5},{5... | collective-permute-start | bytes 2985992 | tf_op jit(solution)/shard_map/ppermute | solution.py:61
  448.0 42.9 %collective-permute-start.84 = (bf16[2,2,144,864]{3,2,1,0:T(8,128)(2,1)}, bf16[2,2,144,864]{3,2,1,0:T(8,128)(2,1)}, u32[]{:S(2)}, u32[]{:S(2)}) collective-permute-start(bf16[2,2,144,864]{3,2,1,0:T(8,128)(2,1)} %get-tuple-element.137), channel_id=1, source_target_pairs={{0,4},{4,0},{8,12},{12,8},{16,20},{20,16},{24,28},{28,24},{1,5},{5... | collective-permute-start | bytes 2985992 | tf_op jit(solution)/shard_map/ppermute | solution.py:61
  494.6 45.0 %collective-permute-start.85 = (bf16[1,216,1152]{2,1,0:T(8,128)(2,1)}, bf16[1,216,1152]{2,1,0:T(8,128)(2,1)}, u32[]{:S(2)}, u32[]{:S(2)}) collective-permute-start(bf16[1,216,1152]{2,1,0:T(8,128)(2,1)} %get-tuple-element.154), channel_id=1, source_target_pairs={{0,16},{4,20},{8,24},{12,28},{16,0},{20,4},{24,8},{28,12},{1,17},{... | collective-permute-start | bytes 1493000 | tf_op jit(solution)/shard_map/ppermute | solution.py:61
  497.5 53.2 %collective-permute-start.86 = (bf16[2,144,864]{2,1,0:T(8,128)(2,1)}, bf16[2,144,864]{2,1,0:T(8,128)(2,1)}, u32[]{:S(2)}, u32[]{:S(2)}) collective-permute-start(bf16[2,144,864]{2,1,0:T(8,128)(2,1)} %get-tuple-element.152), channel_id=1, source_target_pairs={{0,16},{4,20},{8,24},{12,28},{16,0},{20,4},{24,8},{28,12},{1,17},{... | collective-permute-start | bytes 1493000 | tf_op jit(solution)/shard_map/ppermute | solution.py:61
  507.0 54.5 %collective-permute-start.87 = (bf16[2,144,864]{2,1,0:T(8,128)(2,1)}, bf16[2,144,864]{2,1,0:T(8,128)(2,1)}, u32[]{:S(2)}, u32[]{:S(2)}) collective-permute-start(bf16[2,144,864]{2,1,0:T(8,128)(2,1)} %get-tuple-element.150), channel_id=1, source_target_pairs={{0,16},{4,20},{8,24},{12,28},{16,0},{20,4},{24,8},{28,12},{1,17},{... | collective-permute-start | bytes 1493000 | tf_op jit(solution)/shard_map/ppermute | solution.py:61
  515.9 60.3 %collective-permute-start.77 = (bf16[16,32,1152]{2,1,0:T(8,128)(2,1)}, bf16[16,32,1152]{2,1,0:T(8,128)(2,1)}, u32[]{:S(2)}, u32[]{:S(2)}) collective-permute-start(bf16[16,32,1152]{2,1,0:T(8,128)(2,1)} %slice.410), channel_id=1, source_target_pairs={{0,1},{1,0},{2,3},{3,2},{4,5},{5,4},{6,7},{7,6},{8,9},{9,8},{10,11... | collective-permute-start | bytes 3538952 | tf_op jit(solution)/shard_map/ppermute | solution.py:67
  527.8 86.2 %collective-permute-start.67 = (bf16[16,40,1024]{2,1,0:T(8,128)(2,1)}, bf16[16,40,1024]{2,1,0:T(8,128)(2,1)}, u32[]{:S(2)}, u32[]{:S(2)}) collective-permute-start(bf16[16,40,1024]{2,1,0:T(8,128)(2,1)} %bitcast.140), channel_id=1, source_target_pairs={{0,1},{1,0},{2,3},{3,2},{4,5},{5,4},{6,7},{7,6},{8,9},{9,8},{10,11... | collective-permute-start | bytes 3932168 | tf_op jit(solution)/shard_map/ppermute | solution.py:67
  571.3 47.5 %collective-permute-start.88 = (bf16[4,2,36,864]{3,0,2,1:T(4,128)(2,1)}, bf16[4,2,36,864]{3,0,2,1:T(4,128)(2,1)}, u32[]{:S(2)}, u32[]{:S(2)}) collective-permute-start(bf16[4,2,36,864]{3,0,2,1:T(4,128)(2,1)} %copy.94), channel_id=1, source_target_pairs={{0,8},{4,12},{8,0},{12,4},{16,24},{20,28},{24,16},{28,20},{1,9},{5... | collective-permute-start | bytes 1493000 | tf_op jit(solution)/shard_map/ppermute | solution.py:61
  571.4 30.5 %collective-permute-start.63 = (bf16[256,512]{1,0:T(8,128)(2,1)S(1)}, bf16[256,512]{1,0:T(8,128)(2,1)S(1)}, u32[]{:S(2)}, u32[]{:S(2)}) collective-permute-start(bf16[256,512]{1,0:T(8,128)(2,1)S(1)} %get-tuple-element.147), channel_id=1, source_target_pairs={{0,8},{4,12},{8,0},{12,4},{16,24},{20,28},{24,16},{28,20},{1,9},{5... | collective-permute-start | bytes 786440 | tf_op jit(solution)/shard_map/ppermute | solution.py:61
  (171 other events, 2466.7 us)

commit v4 on v3

--- a/solution.py
+++ b/solution.py
@@ -5,6 +5,7 @@
 import jax.numpy as jnp
 from jax import lax
 from jax.experimental import pallas as pl
+from jax.experimental.layout import Layout, with_layout_constraint
 from jax.experimental.pallas import tpu as pltpu
 from jax.sharding import PartitionSpec as P
 
@@ -527,27 +528,28 @@
 
     rows_in = regroup(inputs).astype(f32)
 
-    gains = jnp.concatenate([gain_attn_pre, gain_attn_post, gain_ffw_pre, gain_ffw_post, gain_query, gain_key])
-    gain_line = jnp.pad(gains[None, :], ((0, 0), (0, 2 * HEAD - gain_total)))
+    gain_line, at = jnp.zeros((1, 2 * HEAD), f32), 0
+    for gain in (gain_attn_pre, gain_attn_post, gain_ffw_pre, gain_ffw_post, gain_query, gain_key):
+        gain_line += jnp.pad(gain.astype(f32)[None, :], ((0, 0), (at, 2 * HEAD - at - gain.shape[0])))
+        at += gain.shape[0]
+    gain_line = gain_line.astype(bf16)
     kv_shard = jnp.concatenate([jnp.concatenate([w_key, w_value], axis=1), gain_line], axis=0)
     kv_blocks = gather_all(jnp.pad(kv_shard, ((0, block_rows - model_rows - 1), (0, 0))))
     kv_weight = kv_blocks.reshape(devices * block_rows, 2 * HEAD)
-    q_shard = after(jnp.pad(w_query, ((0, block_rows - model_rows), (0, 0))), kv_weight)
-    q_weight = gather_all(q_shard).reshape(devices * block_rows, wide_q)
-    out_blocks = gather_all(after(w_out, q_weight))
+    q_shard = jnp.pad(w_query, ((0, block_rows - model_rows), (0, 0)))
+    q_weight = lax.all_gather(q_shard, ALL, axis=0, tiled=True)
+    out_weight = lax.all_gather(w_out, ALL, axis=0, tiled=True)
     labels = all_labels()
     natural = jnp.stack([(dp_id ^ d) * members + (seq_id ^ s) for d, s in labels]).astype(jnp.int32)
 
-    def selection(size, block, padded):
+    def selection(order, size, block, padded):
         within = jnp.arange(padded, dtype=jnp.int32)
-        source = jnp.where(within < block, natural[:, None] * block + within, -1).reshape(-1)
+        source = jnp.where(within < block, order[:, None] * block + within, -1).reshape(-1)
         return (jnp.arange(size, dtype=jnp.int32)[:, None] == source[None, :]).astype(bf16)
 
-    model_pick = selection(width, model_rows, block_rows)
-    relative = jnp.arange(devices, dtype=jnp.int32)
-    relative = jnp.sum(jnp.where(natural[:, None] == relative[None, :], relative[:, None], 0), axis=0)
-    out_weight = place([out_blocks], natural).reshape(wide_q, width)
-    device_pick = selection(devices, 1, 1)
+    model_pick = selection(natural, width, model_rows, block_rows)
+    query_pick = selection(jnp.arange(devices, dtype=jnp.int32), width, model_rows, block_rows)
+    device_pick = selection(natural, devices, 1, 1)
     gain_blocks = kv_blocks[:, model_rows, :gain_total]
     gain_all = mm(device_pick, gain_blocks)
     full_gain, at = [], 0
@@ -558,8 +560,10 @@
 
     top_id = dp_id // 4
 
-    def spread(piece):
-        tall = [piece] + [xor(piece, "dp", 4 * k) for k in range(1, tops)]
+    def from_tops(piece):
+        return [piece] + [xor(piece, "dp", 4 * k) for k in range(1, tops)]
+
+    def both_sides(tall):
         return tall + [xor(part, "dp", 1) for part in tall]
 
     def swap_columns(packed):
@@ -568,14 +572,12 @@
         both = jnp.stack([kept, xor(sent, "dp", 2)], axis=1)
         return lax.all_to_all(both, "seq", split_axis=0, concat_axis=0, tiled=True)
 
-    def feed_weights(w_gate, w_up, w_down):
-        owners = [(top_id ^ k) * 2 + (y_bit ^ u) for u in range(2) for k in range(tops)]
-        down_weight = place(spread(w_down[None]), jnp.stack(owners).astype(jnp.int32)).reshape(ff_local, width)
-        halves = merge(swap_columns(pack(w_gate, w_up, tops, members, ff_rows)))
-        sources = [((top_id ^ k) * 2 + (z_bit ^ v)) * 2 + (y_bit ^ u) for u in range(2) for k in range(tops) for v in range(2)]
-        sources = jnp.stack(sources).astype(jnp.int32)
-        gate_weight, up_weight = [place(spread(half), sources).reshape(width, ff_local) for half in halves]
-        return gate_weight, up_weight, down_weight
+    owners = [(top_id ^ k) * 2 + (y_bit ^ u) for u in range(2) for k in range(tops)]
+    owners = jnp.stack(owners).astype(jnp.int32)
+    sources = [((top_id ^ k) * 2 + (z_bit ^ v)) * 2 + (y_bit ^ u) for u in range(2) for k in range(tops) for v in range(2)]
+    sources = jnp.stack(sources).astype(jnp.int32)
+    down_tall = from_tops(w_down[None])
+    halves = merge(swap_columns(pack(w_gate, w_up, tops, members, ff_rows)))
 
     seq_ends = jnp.cumsum(lax.dynamic_index_in_dim(lengths, y_bit, 0, keepdims=False))
     dealt = lax.dynamic_index_in_dim(deal, y_bit, 0, keepdims=False)
@@ -607,15 +609,22 @@
     picked_one = mm(normed_one, model_pick).astype(bf16)
     key_raw, keys_mine = project_keys(picked_one, kv_weight, key_gain[None], cosine, sine)
     column = [keys_mine] + [xor(keys_mine, "dp", 2 * k) for k in range(1, layers)]
+    halves, column = lax.optimization_barrier((halves, column))
+    gate_tall, up_tall = [from_tops(half) for half in halves]
     across = [xor(part, "seq", 2) for part in column]
+    across, down_pieces = lax.optimization_barrier((across, both_sides(down_tall)))
     column, across = jnp.stack(column), jnp.stack(across)
     near_keys = jnp.concatenate([column, across])
     far_keys = jnp.concatenate([xor(column, "seq", 1), xor(across, "seq", 1)])
-    gate_weight, up_weight, down_weight = feed_weights(*lax.optimization_barrier((w_gate, w_up, w_down, keys_mine))[:3])
-    query_raw, query_heads = project(picked_one, q_weight, query_gain[None], cosine, sine)
-    q_natural = mm(model_pick, q_weight).astype(bf16)
+    picked_query = mm(normed_one, query_pick).astype(bf16)
+    query_raw, query_heads = project(picked_query, q_weight, query_gain[None], cosine, sine)
+    q_natural = mm(query_pick, q_weight).astype(bf16)
     kv_natural = mm(model_pick, kv_weight).astype(bf16)
-    query_heads, q_natural, kv_natural = lax.optimization_barrier((query_heads, q_natural, kv_natural))
+    query_heads, q_natural, kv_natural, gate_tall = lax.optimization_barrier(
+        (query_heads, q_natural, kv_natural, gate_tall)
+    )
+    down_weight = place(down_pieces, owners).reshape(ff_local, width)
+    gate_weight, up_weight = [place(both_sides(tall), sources).reshape(width, ff_local) for tall in (gate_tall, up_tall)]
     context_rows, turned, lse = attend(meta, seq_ends, slots, query_heads, near_keys, far_keys)
     attended = mm(context_rows, out_weight)
     scale_two = norm_scale(attended)
@@ -649,17 +658,19 @@
         kept = lax.dynamic_index_in_dim(total, y_bit, 2, keepdims=False)
         return kept, xor(lax.dynamic_index_in_dim(total, 1 - y_bit, 2, keepdims=False), "dp", 1)
 
-    def finish(kept, got):
+    def by_top(kept, got):
         kept = add16(kept, got)
-        mine = lax.dynamic_index_in_dim(kept, top_id, 0, keepdims=False)
-        rest = [xor(lax.dynamic_index_in_dim(kept, top_id ^ k, 0, keepdims=False), "dp", 4 * k) for k in range(1, tops)]
-        return [mine, *rest]
+        return [lax.dynamic_index_in_dim(kept, top_id ^ k, 0, keepdims=False) for k in range(tops)]
+
+    def send_tops(parts):
+        return [part if k == 0 else xor(part, "dp", 4 * k) for k, part in enumerate(parts)]
 
     def total_of(parts):
         return functools.reduce(jnp.add, [part.astype(f32) for part in parts])
 
     def column_blocks(total):
-        return total.astype(bf16).reshape(tops, 2, 2, members * model_rows, ff_local)
+        total = with_layout_constraint(total.astype(bf16), Layout((0, 1)))
+        return total.reshape(tops, 2, 2, members * model_rows, ff_local)
 
     hidden_low, mixed_group, normed_group, gate_grad, up_grad, _ = lax.optimization_barrier(
         (hidden_low, mixed_group, normed_group, gate_grad, up_grad, partial_grad)
@@ -670,23 +681,29 @@
 
     grad_post_attention = jnp.sum(hidden_res_grad * attended * scale_two, axis=0)
     attended_grad = norm_back(attended, scale_two, post_attention * hidden_res_grad).astype(bf16)
+    out_total = mm_tn(context_rows, attended_grad).astype(bf16)
+    attended_grad, out_total, gate_kept, up_kept = lax.optimization_barrier(
+        (attended_grad, out_total, gate_halves[0], up_halves[0])
+    )
+    gate_halves, up_halves = (gate_kept, gate_halves[1]), (up_kept, up_halves[1])
+    down_parts = send_tops(by_top(*down_halves))
+    grad_out = lax.psum_scatter(out_total, ALL, scatter_dimension=0, tiled=True).astype(f32)
     context_grad = mm_nt(attended_grad, out_weight).astype(bf16)
+    context_grad, gate_tops, down_parts = lax.optimization_barrier((context_grad, by_top(*gate_halves), down_parts))
     query_grad, grad_query_gain, near_part, far_part = attend_back(
         meta, seq_ends, slots, query_heads, context_grad, lse, turned, query_raw, query_gain[None], cosine, sine, near_keys, far_keys
     )
-    halves = lax.optimization_barrier((down_halves, gate_halves, up_halves, context_grad))[:3]
-    down_parts, gate_parts, up_parts = [finish(*half) for half in halves]
+    gate_parts = send_tops(gate_tops)
+    up_parts = send_tops(by_top(*up_halves))
     far_part = xor(far_part, "seq", 1)
     near_part = add16(near_part, far_part).reshape(2, layers, count, 2 * HEAD)
     near_part = add16(near_part[0], xor(near_part[1], "seq", 2))
-    key_grads = near_part[0].astype(f32)
-    for k in range(1, layers):
-        key_grads = key_grads + xor(near_part[k], "dp", 2 * k).astype(f32)
-    attended_low, query_low, _ = lax.optimization_barrier((attended_grad, query_grad, far_part))
-    grad_out = mm_tn(context_rows, attended_low).astype(bf16).reshape(devices, out_rows, width)
+    key_parts = [near_part[k] if k == 0 else xor(near_part[k], "dp", 2 * k) for k in range(layers)]
+    query_low, _ = lax.optimization_barrier((query_grad, far_part))
     grad_query = mm_tn(picked_one, query_low).astype(bf16).reshape(devices, block_rows, wide_q)
     grad_query = scatter_all(grad_query)
-    grad_out = scatter_all(place([grad_out], relative))
+    grad_query, grad_out, key_parts = lax.optimization_barrier((grad_query, grad_out, key_parts))
+    key_grads = functools.reduce(jnp.add, [part.astype(f32) for part in key_parts])
     down_parts, gate_parts, up_parts, _ = lax.optimization_barrier((down_parts, gate_parts, up_parts, near_part))
     grad_down = total_of(down_parts)[0]
     both_grads = split(total_of(gate_parts).astype(bf16), total_of(up_parts).astype(bf16), members)

time: 687 us -> 681 us (level)
  waiting for transfers between devices: 244 us -> 282 us
  local copies, waits for them, and re-layouts: 104 us -> 67.6 us
  other arithmetic: 71.2 us -> 55.8 us
  between operations: 2.78 us -> 15.6 us
  Pallas kernels: 67.4 us -> 59.7 us
    ppermute x59, waiting for transfers between devices: 151 us -> 186 us  [xor(): lax.ppermute(value, axis, [(i, i ^ mask) for i in range(lax.axis_size(axi...]
    ppermute x30 -> x15, waiting for transfers between devices: 93.1 us -> 73.2 us  [xor_both(): lax.ppermute(value, ALL, [(i, i ^ mask) for i in range(lax.axis_size('dp'...]
    reduce_scatter x0 -> x1, waiting for transfers between devices: none -> 12.6 us  [per_device(): lax.psum_scatter(out_total, ALL, scatter_dimension=0, tiled=True)]
    unnamed x242 -> x192, local copies, waits for them, and re-layouts: 31.6 us -> 19.3 us
    all_to_all x2, waiting for transfers between devices: 0.01 us -> 10.5 us  [swap_columns(): return lax.all_to_all(both, 'seq', split_axis=0, concat_axis=0, tiled=True)]
    convert_element_type x2 -> x0, local copies, waits for them, and re-layouts: 8.16 us -> none  [column_blocks(): total.astype(bf16).reshape(tops, 2, 2, members * model_rows, ff_local)]
    ppermute x30 -> x15, starting transfers between devices: 25.7 us -> 17.8 us  [xor_both(): lax.ppermute(value, ALL, [(i, i ^ mask) for i in range(lax.axis_size('dp'...]
    pallas_call x5 -> x3, Pallas kernels: 16.9 us -> 9.53 us  [place(): pl.pallas_call(functools.partial(place_kernel, sizes), grid_spec=pltpu.Pr...]
  transfers between devices with their start and end apart: 91 -> 79, of which waited for: 45 -> 41; matrix products, arithmetic and copies ran while one was open for 28% -> 22% of each run, Pallas kernels for 10% -> 6%
where the time goes in v4:
time: 681 us; the launch traced here: 673 us
  waiting for transfers between devices  282 us (41%)
  matrix products  98.4 us (14%)
  starting transfers between devices  93.5 us (14%)
  local copies, waits for them, and re-layouts  67.6 us (10%)
  Pallas kernels  59.7 us (9%)
  other arithmetic  55.8 us (8%)
  between operations  15.6 us (2%)
    ppermute x59, waiting for transfers between devices, xor(): lax.ppermute(value, axis, [(i, i ^ mask) for i in range(lax.axis_size(axi...  186 us
    dot_general x22, matrix products, dot(): lax.dot_general(left, right, (dims, ((), ())), preferred_element_type=f32)  98.4 us
    ppermute x15, waiting for transfers between devices, xor_both(): lax.ppermute(value, ALL, [(i, i ^ mask) for i in range(lax.axis_size('dp'...  73.2 us
    ppermute x59, starting transfers between devices, xor(): lax.ppermute(value, axis, [(i, i ^ mask) for i in range(lax.axis_size(axi...  67.2 us
    unnamed x192, local copies, waits for them, and re-layouts  19.3 us
    pallas_call x1, Pallas kernels, attend_back(): pl.pallas_call(functools.partial(attend_back_kernel, rows), grid_spec=plt...  18.2 us
    ppermute x15, starting transfers between devices, xor_both(): lax.ppermute(value, ALL, [(i, i ^ mask) for i in range(lax.axis_size('dp'...  17.8 us
  transfers between devices with their start and end apart: 79, of which 41 were waited for; matrix products, arithmetic and copies ran while one was open for 22% of the time, Pallas kernels for 6%

profile of v4, /device:TPU:0, one launch (start us, length us, event | category | flops | bytes accessed | tf_op | source)
XLA Modules:
  0.0 672.9 jit_solution(5815091377293069371)
XLA Ops:
  30.4 10.4 %collective-permute-done.2 = bf16[2,40,512]{2,1,0:T(8,128)(2,1)S(1)} collective-permute-done((bf16[2,40,512]{2,1,0:T(8,128)(2,1)S(1)}, bf16[2,40,512]{2,1,0:T(8,128)(2,1)S(1)}, u32[]{:S(2)}, u32[]{:S(2)}) %collective-permute-start.2) | collective-permute-done | bytes 81952 | tf_op jit(solution)/shard_map/ppermute | solution.py:68
  66.6 10.5 %all-to-all-done = bf16[4,2,2,36,864]{4,2,3,1,0:T(2,128)(2,1)S(1)} async-done(((bf16[4,2,2,36,864]{4,2,3,1,0:T(2,128)(2,1)}), bf16[4,2,2,36,864]{4,2,3,1,0:T(2,128)(2,1)S(1)}, u32[]{:S(2)}, u32[]{:S(2)}) %all-to-all-start) | async-done | bytes 995360 | tf_op jit(solution)/shard_map/all_to_all | solution.py:573
  100.7 14.5 %collective-permute-done.8 = bf16[2,128,512]{2,1,0:T(8,128)(2,1)S(1)} collective-permute-done((bf16[2,128,512]{2,1,0:T(8,128)(2,1)}, bf16[2,128,512]{2,1,0:T(8,128)(2,1)S(1)}, u32[]{:S(2)}, u32[]{:S(2)}) %collective-permute-start.8) | collective-permute-done | bytes 262176 | tf_op jit(solution)/shard_map/ppermute | solution.py:62
  155.4 20.9 %collective-permute-done.10.refs_1_ = bf16[2,144,864]{2,1,0:T(8,128)(2,1)} collective-permute-done((bf16[2,144,864]{2,1,0:T(8,128)(2,1)}, bf16[2,144,864]{2,1,0:T(8,128)(2,1)}, u32[]{:S(2)}, u32[]{:S(2)}) %collective-permute-start.10) | collective-permute-done | bytes 497696 | tf_op jit(solution)/shard_map/ppermute | solution.py:62
  176.2 13.4 %attend.1 = (bf16[256,1024]{1,0:T(8,128)(2,1)}, f32[2,256,512]{2,1,0:T(8,128)}, f32[2,1,512]{2,1,0:T(1,128)}) custom-call(s32[7]{0:T(128)} %pad_add_fusion.1.meta_ref, s32[4]{0:T(128)} %bitcast.329, s32[16]{0:T(128)} %gather_fusion.1, bf16[2,4,128,256]{3,2,1,0:T(8,128)(2,1)} %get-tuple-element.81.q_ref, bf16[8,2,128,512]{3,2,1,0:T(8,128)(2,1)} %copy-done.48, ...), custom_call_target="tpu_custom_call" | custom-call | flops 2415919104 | bytes 4194304 | tf_op jit(solution)/shard_map/attend/pallas_call | solution.py:376
  203.1 8.6 %collective-permute-done.31.refs_3_ = bf16[2,144,864]{2,1,0:T(8,128)(2,1)} collective-permute-done((bf16[2,144,864]{2,1,0:T(8,128)(2,1)}, bf16[2,144,864]{2,1,0:T(8,128)(2,1)}, u32[]{:S(2)}, u32[]{:S(2)}) %collective-permute-start.31) | collective-permute-done | bytes 497696 | tf_op jit(solution)/shard_map/ppermute | solution.py:62
  215.0 7.7 %collective-permute-done.27.refs_2_ = bf16[2,144,864]{2,1,0:T(8,128)(2,1)} collective-permute-done((bf16[2,144,864]{2,1,0:T(8,128)(2,1)}, bf16[2,144,864]{2,1,0:T(8,128)(2,1)}, u32[]{:S(2)}, u32[]{:S(2)}) %collective-permute-start.27) | collective-permute-done | bytes 497696 | tf_op jit(solution)/shard_map/ppermute | solution.py:62
  222.7 9.6 %collective-permute-done.28.refs_3_ = bf16[2,144,864]{2,1,0:T(8,128)(2,1)} collective-permute-done((bf16[2,144,864]{2,1,0:T(8,128)(2,1)}, bf16[2,144,864]{2,1,0:T(8,128)(2,1)}, u32[]{:S(2)}, u32[]{:S(2)}) %collective-permute-start.28) | collective-permute-done | bytes 497696 | tf_op jit(solution)/shard_map/ppermute | solution.py:62
  248.9 7.0 %fusion.70 = f32[2048,864]{0,1:T(8,128)S(1)} fusion(bf16[2048,1152]{1,0:T(8,128)(2,1)} %constant_dynamic-update-slice_fusion.21, bf16[1152,864]{1,0:T(8,128)(2,1)S(1)} %bitcast.284), kind=kOutput, calls=%fused_computation.289 | convolution fusion | flops 4076863488 | bytes 13787136 | tf_op jit(solution)/shard_map/dot_general | solution.py:46
  256.0 8.6 %multiply_convert_fusion.1 = (bf16[2048,864]{0,1:T(8,128)(2,1)S(1)}, f32[2048,864]{0,1:T(8,128)}) fusion(f32[2048,864]{0,1:T(8,128)S(1)} %fusion.70, bf16[2048,1152]{1,0:T(8,128)(2,1)S(1)} %copy-done.45, bf16[1152,864]{1,0:T(8,128)(2,1)S(1)} %bitcast.282), kind=kOutput, calls=%fused_computation.14 | convolution fusion | flops 4094558208 | bytes 24403968 | tf_op jit(solution)/shard_map/dot_general | solution.py:46
  294.4 8.1 %collective-permute-done.36 = bf16[256,1152]{1,0:T(8,128)(2,1)S(1)} collective-permute-done((bf16[256,1152]{1,0:T(8,128)(2,1)}, bf16[256,1152]{1,0:T(8,128)(2,1)S(1)}, u32[]{:S(2)}, u32[]{:S(2)}) %collective-permute-start.36) | collective-permute-done | bytes 589856 | tf_op jit(solution)/shard_map/ppermute | solution.py:62
  314.5 10.4 %collective-permute-done.40 = bf16[256,1152]{1,0:T(8,128)(2,1)S(1)} collective-permute-done((bf16[256,1152]{1,0:T(8,128)(2,1)}, bf16[256,1152]{1,0:T(8,128)(2,1)S(1)}, u32[]{:S(2)}, u32[]{:S(2)}) %collective-permute-start.40) | collective-permute-done | bytes 589856 | tf_op jit(solution)/shard_map/ppermute | solution.py:62
  338.8 14.7 %multiply_convert_fusion = (bf16[2048,864]{0,1:T(8,128)(2,1)}, bf16[2048,864]{0,1:T(8,128)(2,1)S(1)}) fusion(f32[2048,864]{0,1:T(8,128)} %copy-done.75, f32[2048,864]{0,1:T(8,128)} %get-tuple-element.244, bf16[2048,1152]{1,0:T(8,128)(2,1)} %constant_dynamic-update-slice_fusion.29, bf16[864,1152]{1,0:T(8,128)(2,1)S(1)} %bitcast.293), kind=kOutput, calls=%fused_computation.13 | convolution fusion | flops 4119330816 | bytes 27942912 | tf_op jit(solution)/shard_map/dot_general | solution.py:46
  359.3 7.9 %add_convert_fusion = bf16[2048,1152]{1,0:T(8,128)(2,1)S(1)} fusion(f32[2048,1152]{1,0:T(8,128)S(1)} %fusion.71, bf16[2048,864]{0,1:T(8,128)(2,1)} %get-tuple-element.100, bf16[1152,864]{1,0:T(8,128)(2,1)S(1)} %bitcast.283), kind=kOutput, calls=%fused_computation.4 | convolution fusion | flops 4081582080 | bytes 19685376 | tf_op jit(solution)/shard_map/dot_general | solution.py:46
  368.0 7.5 %convolution_convert_fusion.4 = bf16[1152,864]{1,0:T(8,128)(2,1)S(1)} fusion(bf16[2048,1152]{1,0:T(8,128)(2,1)S(1)} %bitcast.315, bf16[2048,864]{0,1:T(8,128)(2,1)} %copy-done.78), kind=kOutput, calls=%fused_computation.29 | convolution fusion | flops 4077858816 | bytes 10248192 | tf_op jit(solution)/shard_map/dot_general | solution.py:46
  383.4 7.2 %convolution_convert_fusion.3 = bf16[1152,864]{1,0:T(8,128)(2,1)S(1)} fusion(bf16[2048,1152]{1,0:T(8,128)(2,1)S(1)} %bitcast.315, bf16[2048,864]{0,1:T(8,128)(2,1)} %get-tuple-element.100), kind=kOutput, calls=%fused_computation.28 | convolution fusion | flops 4077858816 | bytes 10248192 | tf_op jit(solution)/shard_map/dot_general | solution.py:46
  404.0 19.2 %collective-permute-done.52 = bf16[2,1,216,1152]{3,2,0,1:T(8,128)(2,1)S(1)} collective-permute-done((bf16[2,1,216,1152]{3,2,0,1:T(8,128)(2,1)S(1)}, bf16[2,1,216,1152]{3,2,0,1:T(8,128)(2,1)S(1)}, u32[]{:S(2)}, u32[]{:S(2)}) %collective-permute-start.52) | collective-permute-done | bytes 995360 | tf_op jit(solution)/shard_map/ppermute | solution.py:62
  439.2 9.6 %collective-permute-done.53 = bf16[1,216,1152]{2,1,0:T(8,128)(2,1)} collective-permute-done((bf16[1,216,1152]{2,1,0:T(8,128)(2,1)}, bf16[1,216,1152]{2,1,0:T(8,128)(2,1)}, u32[]{:S(2)}, u32[]{:S(2)}) %collective-permute-start.53) | collective-permute-done | bytes 497696 | tf_op jit(solution)/shard_map/ppermute | solution.py:62
  448.9 18.2 %attend_back.1 = (bf16[256,1024]{1,0:T(8,128)(2,1)}, f32[1,256]{1,0:T(1,128)}, bf16[8,2,128,512]{3,2,1,0:T(8,128)(2,1)}, bf16[8,2,128,512]{3,2,1,0:T(8,128)(2,1)}) custom-call(s32[7]{0:T(128)} %pad_add_fusion.1.meta_ref, s32[4]{0:T(128)} %bitcast.330, s32[16]{0:T(128)} %gather_fusion.1, bf16[2,4,128,256]{3,2,1,0:T(8,128)(2,1)} %get-tuple-element.81.q_ref, ...), custom_call_target="tpu_custom_call" | custom-call | flops 6039797760 | bytes 8388608 | tf_op jit(solution)/shard_map/attend_back/pallas_call | solution.py:405
  511.1 9.8 %collective-permute-done.56 = bf16[8,40,1024]{2,1,0:T(8,128)(2,1)S(1)} collective-permute-done((bf16[8,40,1024]{2,1,0:T(8,128)(2,1)S(1)}, bf16[8,40,1024]{2,1,0:T(8,128)(2,1)S(1)}, u32[]{:S(2)}, u32[]{:S(2)}) %collective-permute-start.56) | collective-permute-done | bytes 655392 | tf_op jit(solution)/shard_map/ppermute | solution.py:68
  525.6 14.4 %collective-permute-done.72 = bf16[2,144,864]{2,1,0:T(8,128)(2,1)S(1)} collective-permute-done((bf16[2,144,864]{2,1,0:T(8,128)(2,1)S(1)}, bf16[2,144,864]{2,1,0:T(8,128)(2,1)S(1)}, u32[]{:S(2)}, u32[]{:S(2)}) %collective-permute-start.72) | collective-permute-done | bytes 497696 | tf_op jit(solution)/shard_map/ppermute | solution.py:62
  553.2 23.3 %collective-permute-done.58 = bf16[2,40,1024]{2,1,0:T(8,128)(2,1)S(1)} collective-permute-done((bf16[2,40,1024]{2,1,0:T(8,128)(2,1)S(1)}, bf16[2,40,1024]{2,1,0:T(8,128)(2,1)S(1)}, u32[]{:S(2)}, u32[]{:S(2)}) %collective-permute-start.58) | collective-permute-done | bytes 163872 | tf_op jit(solution)/shard_map/ppermute | solution.py:68
  580.4 12.6 %reduce-scatter.2.cloned.1.call-done = bf16[32,1152]{1,0:T(8,128)(2,1)} async-done(((bf16[1024,1152]{1,0:T(8,128)(2,1)}), bf16[32,1152]{1,0:T(8,128)(2,1)}) %reduce-scatter.2.cloned.1.call-update) | async-done | bytes 73744 | tf_op jit(solution)/shard_map/reduce_scatter | solution.py:690
  625.7 17.3 %collective-permute-done.66 = bf16[8,40,512]{2,0,1:T(8,128)(2,1)S(1)} collective-permute-done((bf16[8,40,512]{2,0,1:T(8,128)(2,1)S(1)}, bf16[8,40,512]{2,0,1:T(8,128)(2,1)S(1)}, u32[]{:S(2)}, u32[]{:S(2)}) %collective-permute-start.66) | collective-permute-done | bytes 327712 | tf_op jit(solution)/shard_map/ppermute | solution.py:68
  (534 shorter events, 366.1 us)
Async XLA Ops:
  7.2 136.6 %all-gather.3.cloned.1.call-start = ((), (), s32[]{:S(2)}) async-start(), calls=%async_computation.3 | async-start | bytes 2703360 | tf_op jit(solution)/shard_map/all_gather | solution.py:540
  8.8 180.8 %all-gather.5.cloned.1.call-start = ((), (), s32[]{:S(2)}) async-start(), calls=%async_computation.4 | async-start | bytes 2433024 | tf_op jit(solution)/shard_map/all_gather | solution.py:541
  8.8 109.5 %collective-permute-start.16 = (bf16[1,216,1152]{2,1,0:T(8,128)(2,1)}, bf16[1,216,1152]{2,1,0:T(8,128)(2,1)}, u32[]{:S(2)}, u32[]{:S(2)}) collective-permute-start(bf16[1,216,1152]{2,1,0:T(8,128)(2,1)} %bitcast.306), channel_id=1, source_target_pairs={{0,4},{4,0},{8,12},{12,8},{16,20},{20,16},{24,28},{28,24},{1,5},{5... | collective-permute-start | bytes 1493000 | tf_op jit(solution)/shard_map/ppermute | solution.py:62
  11.9 53.4 %collective-permute-start.15 = (bf16[1,216,1152]{2,1,0:T(8,128)(2,1)}, bf16[1,216,1152]{2,1,0:T(8,128)(2,1)}, u32[]{:S(2)}, u32[]{:S(2)}) collective-permute-start(bf16[1,216,1152]{2,1,0:T(8,128)(2,1)} %bitcast.307), channel_id=1, source_target_pairs={{0,16},{4,20},{8,24},{12,28},{16,0},{20,4},{24,8},{28,12},{1,17},{... | collective-permute-start | bytes 1493000 | tf_op jit(solution)/shard_map/ppermute | solution.py:62
  16.3 48.2 %collective-permute-start = (bf16[128,1152]{1,0:T(8,128)(2,1)}, bf16[128,1152]{1,0:T(8,128)(2,1)S(1)}, u32[]{:S(2)}, u32[]{:S(2)}) collective-permute-start(bf16[128,1152]{1,0:T(8,128)(2,1)} %get-tuple-element.202), channel_id=1, source_target_pairs={{0,4},{4,0},{8,12},{12,8},{16,20},{20,16},{24,28},{28,24},{1,5},{5... | collective-permute-start | bytes 884744 | tf_op jit(solution)/shard_map/ppermute | solution.py:62
  58.2 534.8 %reduce-scatter.2.cloned.1.call-start = ((), (), s32[]{:S(2)}) async-start(), calls=%async_computation.5 | async-start | bytes 2433024 | tf_op jit(solution)/shard_map/reduce_scatter | solution.py:690
  65.3 54.3 %collective-permute-start.17 = (bf16[1,216,1152]{2,1,0:T(8,128)(2,1)}, bf16[1,216,1152]{2,1,0:T(8,128)(2,1)S(1)}, u32[]{:S(2)}, u32[]{:S(2)}) collective-permute-start(bf16[1,216,1152]{2,1,0:T(8,128)(2,1)} %collective-permute-done.15.refs_1_), channel_id=1, source_target_pairs={{0,4},{4,0},{8,12},{12,8},{16,20},{20,16},{24,28},{28,24},{1,5},{5... | collective-permute-start | bytes 1493000 | tf_op jit(solution)/shard_map/ppermute | solution.py:62
  119.7 79.1 %collective-permute-start.30 = (bf16[2,144,864]{2,1,0:T(8,128)(2,1)}, bf16[2,144,864]{2,1,0:T(8,128)(2,1)}, u32[]{:S(2)}, u32[]{:S(2)}) collective-permute-start(bf16[2,144,864]{2,1,0:T(8,128)(2,1)} %get-tuple-element.93.refs_0_), channel_id=1, source_target_pairs={{0,4},{4,0},{8,12},{12,8},{16,20},{20,16},{24,28},{28,24},{1,5},{5... | collective-permute-start | bytes 1493000 | tf_op jit(solution)/shard_map/ppermute | solution.py:62
  126.5 70.2 %collective-permute-start.29 = (bf16[2,144,864]{2,1,0:T(8,128)(2,1)}, bf16[2,144,864]{2,1,0:T(8,128)(2,1)}, u32[]{:S(2)}, u32[]{:S(2)}) collective-permute-start(bf16[2,144,864]{2,1,0:T(8,128)(2,1)} %get-tuple-element.93.refs_0_), channel_id=1, source_target_pairs={{0,16},{4,20},{8,24},{12,28},{16,0},{20,4},{24,8},{28,12},{1,17},{... | collective-permute-start | bytes 1493000 | tf_op jit(solution)/shard_map/ppermute | solution.py:62
  132.1 44.1 %collective-permute-start.10 = (bf16[2,144,864]{2,1,0:T(8,128)(2,1)}, bf16[2,144,864]{2,1,0:T(8,128)(2,1)}, u32[]{:S(2)}, u32[]{:S(2)}) collective-permute-start(bf16[2,144,864]{2,1,0:T(8,128)(2,1)} %get-tuple-element.91.refs_0_), channel_id=1, source_target_pairs={{0,16},{4,20},{8,24},{12,28},{16,0},{20,4},{24,8},{28,12},{1,17},{... | collective-permute-start | bytes 1493000 | tf_op jit(solution)/shard_map/ppermute | solution.py:62
  195.2 40.4 %collective-permute-start.21 = (bf16[256,1152]{1,0:T(8,128)(2,1)}, bf16[256,1152]{1,0:T(8,128)(2,1)S(1)}, u32[]{:S(2)}, u32[]{:S(2)}) collective-permute-start(bf16[256,1152]{1,0:T(8,128)(2,1)} %get-tuple-element.151), channel_id=1, source_target_pairs={{0,8},{4,12},{8,0},{12,4},{16,24},{20,28},{24,16},{28,20},{1,9},{5... | collective-permute-start | bytes 1769480 | tf_op jit(solution)/shard_map/ppermute | solution.py:62
  195.2 40.8 %collective-permute-start.20 = (bf16[256,1152]{1,0:T(8,128)(2,1)}, bf16[256,1152]{1,0:T(8,128)(2,1)S(1)}, u32[]{:S(2)}, u32[]{:S(2)}) collective-permute-start(bf16[256,1152]{1,0:T(8,128)(2,1)} %get-tuple-element.151), channel_id=1, source_target_pairs={{0,2},{1,3},{2,0},{3,1},{4,6},{5,7},{6,4},{7,5},{8,10},{9,11},{10,... | collective-permute-start | bytes 1769480 | tf_op jit(solution)/shard_map/ppermute | solution.py:62
  198.8 33.6 %collective-permute-start.28 = (bf16[2,144,864]{2,1,0:T(8,128)(2,1)}, bf16[2,144,864]{2,1,0:T(8,128)(2,1)}, u32[]{:S(2)}, u32[]{:S(2)}) collective-permute-start(bf16[2,144,864]{2,1,0:T(8,128)(2,1)} %collective-permute-done.10.refs_1_), channel_id=1, source_target_pairs={{0,4},{4,0},{8,12},{12,8},{16,20},{20,16},{24,28},{28,24},{1,5},{5... | collective-permute-start | bytes 1493000 | tf_op jit(solution)/shard_map/ppermute | solution.py:62
  214.9 30.1 %collective-permute-start.24 = (bf16[256,1152]{1,0:T(8,128)(2,1)}, bf16[256,1152]{1,0:T(8,128)(2,1)}, u32[]{:S(2)}, u32[]{:S(2)}) collective-permute-start(bf16[256,1152]{1,0:T(8,128)(2,1)} %get-tuple-element.151), channel_id=1, source_target_pairs={{0,1},{1,0},{2,3},{3,2},{4,5},{5,4},{6,7},{7,6},{8,9},{9,8},{10,11... | collective-permute-start | bytes 1769480 | tf_op jit(solution)/shard_map/ppermute | solution.py:62
  377.1 57.7 %collective-permute-start.51 = (bf16[2,2,144,864]{3,2,1,0:T(8,128)(2,1)}, bf16[2,2,144,864]{3,2,1,0:T(8,128)(2,1)}, u32[]{:S(2)}, u32[]{:S(2)}) collective-permute-start(bf16[2,2,144,864]{3,2,1,0:T(8,128)(2,1)} %get-tuple-element.179), channel_id=1, source_target_pairs={{0,4},{4,0},{8,12},{12,8},{16,20},{20,16},{24,28},{28,24},{1,5},{5... | collective-permute-start | bytes 2985992 | tf_op jit(solution)/shard_map/ppermute | solution.py:62
  393.3 29.9 %collective-permute-start.52 = (bf16[2,1,216,1152]{3,2,0,1:T(8,128)(2,1)S(1)}, bf16[2,1,216,1152]{3,2,0,1:T(8,128)(2,1)S(1)}, u32[]{:S(2)}, u32[]{:S(2)}) collective-permute-start(bf16[2,1,216,1152]{3,2,0,1:T(8,128)(2,1)S(1)} %dynamic-slice_bitcast_fusion.4), channel_id=1, source_target_pairs={{0,4},{4,0},{8,12},{12,8},{16,20},{20,16},{24,28},{28,24},{1,5},{5... | collective-permute-start | bytes 2985992 | tf_op jit(solution)/shard_map/ppermute | solution.py:62
  484.1 124.9 %collective-permute-start.37 = (bf16[128,1152]{1,0:T(8,128)(2,1)}, bf16[128,1152]{1,0:T(8,128)(2,1)}, u32[]{:S(2)}, u32[]{:S(2)}) collective-permute-start(bf16[128,1152]{1,0:T(8,128)(2,1)} %get-tuple-element.199), channel_id=1, source_target_pairs={{0,4},{4,0},{8,12},{12,8},{16,20},{20,16},{24,28},{28,24},{1,5},{5... | collective-permute-start | bytes 884744 | tf_op jit(solution)/shard_map/ppermute | solution.py:62
  487.1 38.5 %collective-permute-start.70 = (bf16[2,144,864]{2,1,0:T(8,128)(2,1)}, bf16[2,144,864]{2,1,0:T(8,128)(2,1)S(1)}, u32[]{:S(2)}, u32[]{:S(2)}) collective-permute-start(bf16[2,144,864]{2,1,0:T(8,128)(2,1)} %get-tuple-element.127), channel_id=1, source_target_pairs={{0,16},{4,20},{8,24},{12,28},{16,0},{20,4},{24,8},{28,12},{1,17},{... | collective-permute-start | bytes 1493000 | tf_op jit(solution)/shard_map/ppermute | solution.py:62
  504.1 35.9 %collective-permute-start.72 = (bf16[2,144,864]{2,1,0:T(8,128)(2,1)S(1)}, bf16[2,144,864]{2,1,0:T(8,128)(2,1)S(1)}, u32[]{:S(2)}, u32[]{:S(2)}) collective-permute-start(bf16[2,144,864]{2,1,0:T(8,128)(2,1)S(1)} %get-tuple-element.189), channel_id=1, source_target_pairs={{0,16},{4,20},{8,24},{12,28},{16,0},{20,4},{24,8},{28,12},{1,17},{... | collective-permute-start | bytes 1493000 | tf_op jit(solution)/shard_map/ppermute | solution.py:62
  540.0 56.6 %collective-permute-start.63 = (bf16[256,512]{1,0:T(8,128)(2,1)}, bf16[256,512]{1,0:T(8,128)(2,1)}, u32[]{:S(2)}, u32[]{:S(2)}) collective-permute-start(bf16[256,512]{1,0:T(8,128)(2,1)} %get-tuple-element.185), channel_id=1, source_target_pairs={{0,24},{4,28},{8,16},{12,20},{16,8},{20,12},{24,0},{28,4},{1,25},{... | collective-permute-start | bytes 786440 | tf_op jit(solution)/shard_map/ppermute | solution.py:62
  545.9 50.6 %collective-permute-start.62 = (bf16[256,512]{1,0:T(8,128)(2,1)}, bf16[256,512]{1,0:T(8,128)(2,1)}, u32[]{:S(2)}, u32[]{:S(2)}) collective-permute-start(bf16[256,512]{1,0:T(8,128)(2,1)} %get-tuple-element.186), channel_id=1, source_target_pairs={{0,16},{4,20},{8,24},{12,28},{16,0},{20,4},{24,8},{28,12},{1,17},{... | collective-permute-start | bytes 786440 | tf_op jit(solution)/shard_map/ppermute | solution.py:62
  545.9 50.6 %collective-permute-start.61 = (bf16[256,512]{1,0:T(8,128)(2,1)}, bf16[256,512]{1,0:T(8,128)(2,1)}, u32[]{:S(2)}, u32[]{:S(2)}) collective-permute-start(bf16[256,512]{1,0:T(8,128)(2,1)} %get-tuple-element.187), channel_id=1, source_target_pairs={{0,8},{4,12},{8,0},{12,4},{16,24},{20,28},{24,16},{28,20},{1,9},{5... | collective-permute-start | bytes 786440 | tf_op jit(solution)/shard_map/ppermute | solution.py:62
  547.5 29.0 %collective-permute-start.58 = (bf16[2,40,1024]{2,1,0:T(8,128)(2,1)S(1)}, bf16[2,40,1024]{2,1,0:T(8,128)(2,1)S(1)}, u32[]{:S(2)}, u32[]{:S(2)}) collective-permute-start(bf16[2,40,1024]{2,1,0:T(8,128)(2,1)S(1)} %slice.339), channel_id=1, source_target_pairs={{0,16},{1,17},{2,18},{3,19},{4,20},{5,21},{6,22},{7,23},{8,24},{9,... | collective-permute-start | bytes 491528 | tf_op jit(solution)/shard_map/ppermute | solution.py:68
  617.4 36.9 %all-to-all-start.1 = ((bf16[4,2,2,36,864]{4,2,3,1,0:T(2,128)(2,1)}), bf16[4,2,2,36,864]{4,2,3,1,0:T(2,128)(2,1)}, u32[]{:S(2)}, u32[]{:S(2)}) async-start(bf16[4,2,2,36,864]{4,2,3,1,0:T(2,128)(2,1)} %copy.82), calls=%async_computation.2 | async-start | bytes 2064384 | tf_op jit(solution)/shard_map/all_to_all | solution.py:573
  (138 other events, 1894.2 us)
Sparse Core Ops, SparseCore 0:
  11.4 72.8 all-gather.2
  87.2 90.7 all-gather.4
  477.0 115.8 reduce-scatter.1

commit v5 on v4

--- a/solution.py
+++ b/solution.py
@@ -79,8 +79,8 @@
     return (left.astype(f32) + right.astype(f32)).astype(bf16)
 
 
-def after(value, *others):
-    return lax.optimization_barrier((value, *others))[0]
+def together(*values):
+    return lax.optimization_barrier(values)
 
 
 def all_masks():
@@ -88,11 +88,8 @@
     return rows + [(1, 0), (0, 2), (0, 1)]
 
 
-def gather_all(piece):
-    value = piece[None]
-    for dp_mask, seq_mask in all_masks():
-        value = jnp.concatenate([value, xor_both(value, dp_mask, seq_mask)])
-    return value
+def gather_step(value, dp_mask, seq_mask):
+    return jnp.concatenate([value, xor_both(value, dp_mask, seq_mask)])
 
 
 def all_labels():
@@ -102,12 +99,16 @@
     return labels
 
 
-def scatter_all(total):
-    for dp_mask, seq_mask in reversed(all_masks()):
-        half = total.shape[0] // 2
-        got = xor_both(total[half:], dp_mask, seq_mask)
-        total = total[:half].astype(f32) + got.astype(f32)
-        total = total if half == 1 else total.astype(bf16)
+def scatter_step(total, dp_mask, seq_mask):
+    half = total.shape[0] // 2
+    got = xor_both(total[half:], dp_mask, seq_mask)
+    total = total[:half].astype(f32) + got.astype(f32)
+    return total if half == 1 else total.astype(bf16)
+
+
+def scatter_rest(total):
+    for masks in list(reversed(all_masks()))[1:]:
+        total = scatter_step(total, *masks)
     return total[0]
 
 
@@ -220,6 +221,18 @@
     count, deep = picked.shape
     return pl.pallas_call(
         project_keys_kernel,
+        grid=(1,),
+        in_specs=[
+            whole_of(picked),
+            pl.BlockSpec((deep, 2 * HEAD), lambda i: (0, HEADS // 2)),
+            whole_of(gain),
+            whole_of(cosine),
+            whole_of(sine),
+        ],
+        out_specs=[
+            pl.BlockSpec((count, HEAD), lambda i: (0, 0)),
+            pl.BlockSpec((2, count // 2, 2 * HEAD), lambda i: (0, 0, 0)),
+        ],
         out_shape=[
             jax.ShapeDtypeStruct((count, HEAD), f32),
             jax.ShapeDtypeStruct((2, count // 2, 2 * HEAD), bf16),
@@ -528,17 +541,33 @@
 
     rows_in = regroup(inputs).astype(f32)
 
-    gain_line, at = jnp.zeros((1, 2 * HEAD), f32), 0
+    def column_exchange(packed):
+        kept = lax.dynamic_index_in_dim(packed, z_bit, 0, keepdims=False)
+        sent = lax.dynamic_index_in_dim(packed, 1 - z_bit, 0, keepdims=False)
+        return jnp.stack([kept, xor(sent, "dp", 2)], axis=1)
+
+    def swap_members(parts):
+        return lax.all_to_all(parts, "seq", split_axis=0, concat_axis=0, tiled=True)
+
+    gain_line, at = jnp.zeros((1, wide_q + 2 * HEAD), f32), 0
     for gain in (gain_attn_pre, gain_attn_post, gain_ffw_pre, gain_ffw_post, gain_query, gain_key):
-        gain_line += jnp.pad(gain.astype(f32)[None, :], ((0, 0), (at, 2 * HEAD - at - gain.shape[0])))
+        gain_line += jnp.pad(gain.astype(f32)[None, :], ((0, 0), (at, gain_line.shape[1] - at - gain.shape[0])))
         at += gain.shape[0]
-    gain_line = gain_line.astype(bf16)
-    kv_shard = jnp.concatenate([jnp.concatenate([w_key, w_value], axis=1), gain_line], axis=0)
-    kv_blocks = gather_all(jnp.pad(kv_shard, ((0, block_rows - model_rows - 1), (0, 0))))
-    kv_weight = kv_blocks.reshape(devices * block_rows, 2 * HEAD)
-    q_shard = jnp.pad(w_query, ((0, block_rows - model_rows), (0, 0)))
-    q_weight = lax.all_gather(q_shard, ALL, axis=0, tiled=True)
-    out_weight = lax.all_gather(w_out, ALL, axis=0, tiled=True)
+    shard = jnp.concatenate([w_query, w_key, w_value], axis=1)
+    shard = jnp.concatenate([shard, gain_line.astype(bf16)], axis=0)
+    blocks = jnp.pad(shard, ((0, block_rows - model_rows - 1), (0, 0)))[None]
+    packed = pack(w_gate, w_up, tops, members, ff_rows)
+    *row_masks, y_mask, x_mask, core_mask = all_masks()
+    for masks in row_masks:
+        blocks = gather_step(blocks, *masks)
+    blocks, packed, down_piece = together(blocks, packed, w_down[None])
+    column_parts = column_exchange(packed)
+    blocks = gather_step(gather_step(blocks, *y_mask), *x_mask)
+    blocks, column_parts = together(blocks, column_parts)
+    blocks = gather_step(blocks, *core_mask)
+    blocks, late_out = together(blocks, w_out)
+    qkv_weight = blocks.reshape(devices * block_rows, wide_q + 2 * HEAD)
+    out_weight = lax.all_gather(late_out, ALL, axis=0, tiled=True)
     labels = all_labels()
     natural = jnp.stack([(dp_id ^ d) * members + (seq_id ^ s) for d, s in labels]).astype(jnp.int32)
 
@@ -548,9 +577,8 @@
         return (jnp.arange(size, dtype=jnp.int32)[:, None] == source[None, :]).astype(bf16)
 
     model_pick = selection(natural, width, model_rows, block_rows)
-    query_pick = selection(jnp.arange(devices, dtype=jnp.int32), width, model_rows, block_rows)
     device_pick = selection(natural, devices, 1, 1)
-    gain_blocks = kv_blocks[:, model_rows, :gain_total]
+    gain_blocks = blocks[:, model_rows, :gain_total]
     gain_all = mm(device_pick, gain_blocks)
     full_gain, at = [], 0
     for size in gain_sizes:
@@ -566,18 +594,12 @@
     def both_sides(tall):
         return tall + [xor(part, "dp", 1) for part in tall]
 
-    def swap_columns(packed):
-        kept = lax.dynamic_index_in_dim(packed, z_bit, 0, keepdims=False)
-        sent = lax.dynamic_index_in_dim(packed, 1 - z_bit, 0, keepdims=False)
-        both = jnp.stack([kept, xor(sent, "dp", 2)], axis=1)
-        return lax.all_to_all(both, "seq", split_axis=0, concat_axis=0, tiled=True)
-
     owners = [(top_id ^ k) * 2 + (y_bit ^ u) for u in range(2) for k in range(tops)]
     owners = jnp.stack(owners).astype(jnp.int32)
     sources = [((top_id ^ k) * 2 + (z_bit ^ v)) * 2 + (y_bit ^ u) for u in range(2) for k in range(tops) for v in range(2)]
     sources = jnp.stack(sources).astype(jnp.int32)
-    down_tall = from_tops(w_down[None])
-    halves = merge(swap_columns(pack(w_gate, w_up, tops, members, ff_rows)))
+    down_tall = from_tops(down_piece)
+    halves = swap_members(column_parts)
 
     seq_ends = jnp.cumsum(lax.dynamic_index_in_dim(lengths, y_bit, 0, keepdims=False))
     dealt = lax.dynamic_index_in_dim(deal, y_bit, 0, keepdims=False)
@@ -607,25 +629,27 @@
     scale_one = norm_scale(rows_in)
     normed_one = (rows_in * scale_one * pre_attention).astype(bf16)
     picked_one = mm(normed_one, model_pick).astype(bf16)
-    key_raw, keys_mine = project_keys(picked_one, kv_weight, key_gain[None], cosine, sine)
+    key_raw, keys_mine = project_keys(picked_one, qkv_weight, key_gain[None], cosine, sine)
+    key_raw, down_tall, halves = together(key_raw, down_tall, halves)
+    halves = merge(halves)
     column = [keys_mine] + [xor(keys_mine, "dp", 2 * k) for k in range(1, layers)]
-    halves, column = lax.optimization_barrier((halves, column))
+    halves, others = together(halves, column[1:])
+    column = [column[0], *others]
     gate_tall, up_tall = [from_tops(half) for half in halves]
     across = [xor(part, "seq", 2) for part in column]
     across, down_pieces = lax.optimization_barrier((across, both_sides(down_tall)))
     column, across = jnp.stack(column), jnp.stack(across)
     near_keys = jnp.concatenate([column, across])
     far_keys = jnp.concatenate([xor(column, "seq", 1), xor(across, "seq", 1)])
-    picked_query = mm(normed_one, query_pick).astype(bf16)
-    query_raw, query_heads = project(picked_query, q_weight, query_gain[None], cosine, sine)
-    q_natural = mm(query_pick, q_weight).astype(bf16)
-    kv_natural = mm(model_pick, kv_weight).astype(bf16)
-    query_heads, q_natural, kv_natural, gate_tall = lax.optimization_barrier(
-        (query_heads, q_natural, kv_natural, gate_tall)
-    )
+    query_raw, query_heads = project(picked_one, qkv_weight, query_gain[None], cosine, sine)
+    natural_weight = mm(model_pick, qkv_weight).astype(bf16)
+    query_heads, natural_weight, gate_tall = lax.optimization_barrier((query_heads, natural_weight, gate_tall))
+    gate_pieces = both_sides(gate_tall)
+    context_rows, turned, lse = attend(meta, seq_ends, slots, query_heads, near_keys, far_keys)
+    context_rows, gate_pieces, up_tall = together(context_rows, gate_pieces, up_tall)
+    up_pieces = both_sides(up_tall)
     down_weight = place(down_pieces, owners).reshape(ff_local, width)
-    gate_weight, up_weight = [place(both_sides(tall), sources).reshape(width, ff_local) for tall in (gate_tall, up_tall)]
-    context_rows, turned, lse = attend(meta, seq_ends, slots, query_heads, near_keys, far_keys)
+    gate_weight, up_weight = [place(pieces, sources).reshape(width, ff_local) for pieces in (gate_pieces, up_pieces)]
     attended = mm(context_rows, out_weight)
     scale_two = norm_scale(attended)
     hidden_res = rows_in + attended * scale_two * post_attention
@@ -650,6 +674,9 @@
     gate_grad, up_grad = gelu_pull(hidden_grad)
     gate_grad, up_grad = gate_grad.astype(bf16), up_grad.astype(bf16)
     partial_grad = (mm_nt(gate_grad, gate_weight) + mm_nt(up_grad, up_weight)).astype(bf16)
+    hidden_low, mixed_group, normed_group, gate_grad, up_grad, partial_grad = together(
+        hidden_low, mixed_group, normed_group, gate_grad, up_grad, partial_grad
+    )
     normed_two_grad = scatter_group(partial_grad)
     grad_pre_feed = jnp.sum(normed_two_grad * hidden_res * scale_three, axis=0)
     hidden_res_grad = upstream + norm_back(hidden_res, scale_three, pre_feed * normed_two_grad)
@@ -672,12 +699,12 @@
         total = with_layout_constraint(total.astype(bf16), Layout((0, 1)))
         return total.reshape(tops, 2, 2, members * model_rows, ff_local)
 
-    hidden_low, mixed_group, normed_group, gate_grad, up_grad, _ = lax.optimization_barrier(
-        (hidden_low, mixed_group, normed_group, gate_grad, up_grad, partial_grad)
-    )
     down_halves = halve(mm_tn(hidden_low, mixed_group).astype(bf16).reshape(tops, 1, 2, ff_rows, width))
+    down_kept, gate_grad = together(down_halves[0], gate_grad)
     gate_halves = halve(column_blocks(mm_tn(normed_group, gate_grad)))
+    gate_kept, down_got, up_grad = together(gate_halves[0], down_halves[1], up_grad)
     up_halves = halve(column_blocks(mm_tn(normed_group, up_grad)))
+    down_halves, gate_halves = (down_kept, down_got), (gate_kept, gate_halves[1])
 
     grad_post_attention = jnp.sum(hidden_res_grad * attended * scale_two, axis=0)
     attended_grad = norm_back(attended, scale_two, post_attention * hidden_res_grad).astype(bf16)
@@ -689,32 +716,33 @@
     down_parts = send_tops(by_top(*down_halves))
     grad_out = lax.psum_scatter(out_total, ALL, scatter_dimension=0, tiled=True).astype(f32)
     context_grad = mm_nt(attended_grad, out_weight).astype(bf16)
-    context_grad, gate_tops, down_parts = lax.optimization_barrier((context_grad, by_top(*gate_halves), down_parts))
     query_grad, grad_query_gain, near_part, far_part = attend_back(
         meta, seq_ends, slots, query_heads, context_grad, lse, turned, query_raw, query_gain[None], cosine, sine, near_keys, far_keys
     )
-    gate_parts = send_tops(gate_tops)
-    up_parts = send_tops(by_top(*up_halves))
+    far_part, near_part, gate_halves, up_halves, down_parts = lax.optimization_barrier(
+        (far_part, near_part, gate_halves, up_halves, down_parts)
+    )
+    gate_parts, up_parts = [send_tops(by_top(*half)) for half in (gate_halves, up_halves)]
     far_part = xor(far_part, "seq", 1)
+    query_low, far_part = together(query_grad, far_part)
     near_part = add16(near_part, far_part).reshape(2, layers, count, 2 * HEAD)
     near_part = add16(near_part[0], xor(near_part[1], "seq", 2))
+    grad_query = mm_tn(picked_one, query_low).astype(bf16).reshape(devices, block_rows, wide_q)
+    grad_query, near_part = together(scatter_step(grad_query, *core_mask), near_part)
+    grad_query = scatter_rest(grad_query)
     key_parts = [near_part[k] if k == 0 else xor(near_part[k], "dp", 2 * k) for k in range(layers)]
-    query_low, _ = lax.optimization_barrier((query_grad, far_part))
-    grad_query = mm_tn(picked_one, query_low).astype(bf16).reshape(devices, block_rows, wide_q)
-    grad_query = scatter_all(grad_query)
-    grad_query, grad_out, key_parts = lax.optimization_barrier((grad_query, grad_out, key_parts))
     key_grads = functools.reduce(jnp.add, [part.astype(f32) for part in key_parts])
-    down_parts, gate_parts, up_parts, _ = lax.optimization_barrier((down_parts, gate_parts, up_parts, near_part))
-    grad_down = total_of(down_parts)[0]
-    both_grads = split(total_of(gate_parts).astype(bf16), total_of(up_parts).astype(bf16), members)
-    grad_gate, grad_up = unpack(swap_columns(both_grads), z_bit, tops, members, ff_rows)
     value_grad = key_grads[:, HEAD:].astype(bf16)
     key_turned = rotate(key_grads[:, :HEAD], cosine, -sine)
     key_scale = norm_scale(key_raw)
     grad_key_gain = jnp.sum(key_turned * key_raw * key_scale, axis=0)
     key_grad = norm_back(key_raw, key_scale, key_gain * key_turned).astype(bf16)
     kv_grad = jnp.concatenate([key_grad, value_grad], axis=1)
-    normed_one_grad = mm_nt(query_grad, q_natural) + mm_nt(kv_grad, kv_natural)
+    down_parts, gate_parts, up_parts, kv_grad = together(down_parts, gate_parts, up_parts, kv_grad)
+    grad_down = total_of(down_parts)[0]
+    both_grads = split(total_of(gate_parts).astype(bf16), total_of(up_parts).astype(bf16), members)
+    grad_gate, grad_up = unpack(swap_members(column_exchange(both_grads)), z_bit, tops, members, ff_rows)
+    normed_one_grad = mm_nt(query_grad, natural_weight[:, :wide_q]) + mm_nt(kv_grad, natural_weight[:, wide_q:])
     grad_pre_attention = jnp.sum(normed_one_grad * rows_in * scale_one, axis=0)
     rows_grad = hidden_res_grad + norm_back(rows_in, scale_one, pre_attention * normed_one_grad)
     input_grad = ungroup(rows_grad.astype(bf16))
@@ -732,7 +760,7 @@
     gain_grads = jnp.pad(
         gain_grads[:, None, :], ((0, 0), (model_rows, block_rows - model_rows - 1), (0, 2 * HEAD - gain_total))
     )
-    last = scatter_all((grad_kv + gain_grads).astype(bf16))
+    last = scatter_rest(scatter_step((grad_kv + gain_grads).astype(bf16), *core_mask))
     gain_out, at = [], 0
     for size in gain_sizes:
         gain_out.append(last[model_rows, at : at + size])

time: 681 us -> 671 us (0.985)
  other arithmetic: 55.8 us -> 70 us
  waiting for transfers between devices: 282 us -> 272 us
  local copies, waits for them, and re-layouts: 67.6 us -> 57.7 us
    reduce_scatter x1, waiting for transfers between devices: 12.6 us -> 82.9 us  [per_device(): lax.psum_scatter(out_total, ALL, scatter_dimension=0, tiled=True)]
    ppermute x15, waiting for transfers between devices: 73.2 us -> 37.6 us  [xor_both(): lax.ppermute(value, ALL, [(i, i ^ mask) for i in range(lax.axis_size('dp'...]
    ppermute x59, waiting for transfers between devices: 186 us -> 152 us  [xor(): lax.ppermute(value, axis, [(i, i ^ mask) for i in range(lax.axis_size(axi...]
    all_to_all x2, waiting for transfers between devices: 10.5 us -> 0.01 us  [swap_members(): return lax.all_to_all(parts, 'seq', split_axis=0, concat_axis=0, tiled=True)]
    dot_general x22 -> x20, matrix products: 98.4 us -> 91.8 us  [dot(): lax.dot_general(left, right, (dims, ((), ())), preferred_element_type=f32)]
    unnamed x192 -> x190, local copies, waits for them, and re-layouts: 19.3 us -> 13.5 us
  transfers between devices with their start and end apart: 79 -> 78, of which waited for: 41 -> 34; matrix products, arithmetic and copies ran while one was open for 22% -> 22% of each run, Pallas kernels for 6% -> 8%
where the time goes in v5:
time: 671 us; the launch traced here: 661 us
  waiting for transfers between devices  272 us (41%)
  starting transfers between devices  98.7 us (15%)
  matrix products  91.8 us (14%)
  other arithmetic  70 us (10%)
  local copies, waits for them, and re-layouts  57.7 us (9%)
  Pallas kernels  54.3 us (8%)
  between operations  16 us (2%)
    ppermute x59, waiting for transfers between devices, xor(): lax.ppermute(value, axis, [(i, i ^ mask) for i in range(lax.axis_size(axi...  152 us
    dot_general x20, matrix products, dot(): lax.dot_general(left, right, (dims, ((), ())), preferred_element_type=f32)  91.8 us
    reduce_scatter x1, waiting for transfers between devices, per_device(): lax.psum_scatter(out_total, ALL, scatter_dimension=0, tiled=True)  82.9 us
    ppermute x59, starting transfers between devices, xor(): lax.ppermute(value, axis, [(i, i ^ mask) for i in range(lax.axis_size(axi...  73.8 us
    ppermute x15, waiting for transfers between devices, xor_both(): lax.ppermute(value, ALL, [(i, i ^ mask) for i in range(lax.axis_size('dp'...  37.6 us
    ppermute x15, starting transfers between devices, xor_both(): lax.ppermute(value, ALL, [(i, i ^ mask) for i in range(lax.axis_size('dp'...  17 us
    pallas_call x1, Pallas kernels, attend_back(): pl.pallas_call(functools.partial(attend_back_kernel, rows), grid_spec=plt...  15.4 us
    unnamed x190, local copies, waits for them, and re-layouts  13.5 us
  transfers between devices with their start and end apart: 78, of which 34 were waited for; matrix products, arithmetic and copies ran while one was open for 22% of the time, Pallas kernels for 8%

profile of v5, /device:TPU:0, one launch (start us, length us, event | category | flops | bytes accessed | tf_op | source)
XLA Modules:
  0.0 660.9 jit_solution(5862982737477596688)
XLA Ops:
  21.1 7.8 %collective-permute-done.2 = bf16[2,40,1536]{2,1,0:T(8,128)(2,1)S(1)} collective-permute-done((bf16[2,40,1536]{2,1,0:T(8,128)(2,1)S(1)}, bf16[2,40,1536]{2,1,0:T(8,128)(2,1)S(1)}, u32[]{:S(2)}, u32[]{:S(2)}) %collective-permute-start.2) | collective-permute-done | bytes 245792 | tf_op jit(solution)/shard_map/ppermute | solution.py:68
  31.8 11.3 %collective-permute-done.3 = bf16[4,40,1536]{2,1,0:T(8,128)(2,1)S(1)} collective-permute-done((bf16[4,40,1536]{2,1,0:T(8,128)(2,1)S(1)}, bf16[4,40,1536]{2,1,0:T(8,128)(2,1)S(1)}, u32[]{:S(2)}, u32[]{:S(2)}) %collective-permute-start.3) | collective-permute-done | bytes 491552 | tf_op jit(solution)/shard_map/ppermute | solution.py:68
  48.3 9.1 %collective-permute-done.5 = bf16[4,2,36,864]{3,0,2,1:T(4,128)(2,1)S(1)} collective-permute-done((bf16[4,2,36,864]{3,0,2,1:T(4,128)(2,1)S(1)}, bf16[4,2,36,864]{3,0,2,1:T(4,128)(2,1)S(1)}, u32[]{:S(2)}, u32[]{:S(2)}) %collective-permute-start.5) | collective-permute-done | bytes 497696 | tf_op jit(solution)/shard_map/ppermute | solution.py:62
  101.5 8.5 %convolution_convert_fusion = bf16[1152,1536]{1,0:T(8,128)(2,1)} fusion(bf16[1280,1536]{1,0:T(8,128)(2,1)} %bitcast.278, s32[1280]{0:T(1024)S(1)} %select_n.192), kind=kOutput, calls=%fused_computation.5 | convolution fusion | flops 4533092352 | bytes 7476224 | tf_op jit(solution)/shard_map/dot_general | solution.py:46
  124.9 7.8 %collective-permute-done.17.refs_3_ = bf16[1,216,1152]{2,1,0:T(8,128)(2,1)S(1)} collective-permute-done((bf16[1,216,1152]{2,1,0:T(8,128)(2,1)}, bf16[1,216,1152]{2,1,0:T(8,128)(2,1)S(1)}, u32[]{:S(2)}, u32[]{:S(2)}) %collective-permute-start.17) | collective-permute-done | bytes 497696 | tf_op jit(solution)/shard_map/ppermute | solution.py:62
  141.8 24.8 %collective-permute-done.11.refs_1_ = bf16[2,144,864]{2,1,0:T(8,128)(2,1)} collective-permute-done((bf16[2,144,864]{2,1,0:T(8,128)(2,1)}, bf16[2,144,864]{2,1,0:T(8,128)(2,1)}, u32[]{:S(2)}, u32[]{:S(2)}) %collective-permute-start.11) | collective-permute-done | bytes 497696 | tf_op jit(solution)/shard_map/ppermute | solution.py:62
  170.2 11.7 %attend.1 = (bf16[256,1024]{1,0:T(8,128)(2,1)}, f32[2,256,512]{2,1,0:T(8,128)}, f32[2,1,512]{2,1,0:T(1,128)}) custom-call(s32[7]{0:T(128)} %pad_add_fusion.1.meta_ref, s32[4]{0:T(128)} %bitcast.325, s32[16]{0:T(128)} %gather_fusion.1, bf16[2,4,128,256]{3,2,1,0:T(8,128)(2,1)} %get-tuple-element.112.q_ref, bf16[8,2,128,512]{3,2,1,0:T(8,128)(2,1)} %copy-done.48, ...), custom_call_target="tpu_custom_call" | custom-call | flops 2415919104 | bytes 4194304 | tf_op jit(solution)/shard_map/attend/pallas_call | solution.py:389
  181.8 8.9 %collective-permute-done.21.refs_3_ = bf16[2,144,864]{2,1,0:T(8,128)(2,1)} collective-permute-done((bf16[2,144,864]{2,1,0:T(8,128)(2,1)}, bf16[2,144,864]{2,1,0:T(8,128)(2,1)}, u32[]{:S(2)}, u32[]{:S(2)}) %collective-permute-start.21) | collective-permute-done | bytes 497696 | tf_op jit(solution)/shard_map/ppermute | solution.py:62
  213.0 8.8 %collective-permute-done.31.refs_3_ = bf16[2,144,864]{2,1,0:T(8,128)(2,1)} collective-permute-done((bf16[2,144,864]{2,1,0:T(8,128)(2,1)}, bf16[2,144,864]{2,1,0:T(8,128)(2,1)}, u32[]{:S(2)}, u32[]{:S(2)}) %collective-permute-start.31) | collective-permute-done | bytes 497696 | tf_op jit(solution)/shard_map/ppermute | solution.py:62
  239.2 7.0 %fusion.65 = f32[2048,864]{0,1:T(8,128)S(1)} fusion(bf16[2048,1152]{1,0:T(8,128)(2,1)} %constant_dynamic-update-slice_fusion.10, bf16[1152,864]{1,0:T(8,128)(2,1)S(1)} %bitcast.282), kind=kOutput, calls=%fused_computation.275 | convolution fusion | flops 4076863488 | bytes 13787136 | tf_op jit(solution)/shard_map/dot_general | solution.py:46
  246.2 9.1 %multiply_convert_fusion.1 = (bf16[2048,864]{0,1:T(8,128)(2,1)S(1)}, f32[2048,864]{0,1:T(8,128)}) fusion(f32[2048,864]{0,1:T(8,128)S(1)} %fusion.65, bf16[2048,1152]{1,0:T(8,128)(2,1)S(1)} %copy-done.45, bf16[1152,864]{1,0:T(8,128)(2,1)S(1)} %bitcast.284), kind=kOutput, calls=%fused_computation.15 | convolution fusion | flops 4094558208 | bytes 24403968 | tf_op jit(solution)/shard_map/dot_general | solution.py:46
  255.3 5.9 convolution_convert_fusion.1
  286.3 7.1 %collective-permute-done.36 = bf16[256,1152]{1,0:T(8,128)(2,1)S(1)} collective-permute-done((bf16[256,1152]{1,0:T(8,128)(2,1)}, bf16[256,1152]{1,0:T(8,128)(2,1)S(1)}, u32[]{:S(2)}, u32[]{:S(2)}) %collective-permute-start.36) | collective-permute-done | bytes 589856 | tf_op jit(solution)/shard_map/ppermute | solution.py:62
  305.4 10.6 %collective-permute-done.40 = bf16[256,1152]{1,0:T(8,128)(2,1)S(1)} collective-permute-done((bf16[256,1152]{1,0:T(8,128)(2,1)}, bf16[256,1152]{1,0:T(8,128)(2,1)S(1)}, u32[]{:S(2)}, u32[]{:S(2)}) %collective-permute-start.40) | collective-permute-done | bytes 589856 | tf_op jit(solution)/shard_map/ppermute | solution.py:62
  329.2 13.4 %multiply_convert_fusion = (bf16[2048,864]{0,1:T(8,128)(2,1)S(1)}, bf16[2048,864]{0,1:T(8,128)(2,1)S(1)}) fusion(f32[2048,864]{0,1:T(8,128)} %copy-done.73, f32[2048,864]{0,1:T(8,128)} %get-tuple-element.281, bf16[2048,1152]{1,0:T(8,128)(2,1)} %constant_dynamic-update-slice_fusion.18, bf16[864,1152]{1,0:T(8,128)(2,1)S(1)} %bitcast.293), kind=kOutput, calls=%fused_computation.14 | convolution fusion | flops 4119330816 | bytes 27942912 | tf_op jit(solution)/shard_map/dot_general | solution.py:46
  342.7 8.0 %fusion.66 = f32[2048,1152]{1,0:T(8,128)} fusion(bf16[2048,864]{0,1:T(8,128)(2,1)S(1)} %get-tuple-element.143, bf16[1152,864]{1,0:T(8,128)(2,1)S(1)} %bitcast.283), kind=kOutput, calls=%fused_computation.276 | convolution fusion | flops 4076863488 | bytes 14966784 | tf_op jit(solution)/shard_map/dot_general | solution.py:46
  350.7 8.3 %add_convert_fusion = bf16[2048,1152]{1,0:T(8,128)(2,1)S(1)} fusion(f32[2048,1152]{1,0:T(8,128)} %fusion.66, bf16[2048,864]{0,1:T(8,128)(2,1)S(1)} %get-tuple-element.146, bf16[1152,864]{1,0:T(8,128)(2,1)S(1)} %bitcast.285), kind=kOutput, calls=%fused_computation.4 | convolution fusion | flops 4081582080 | bytes 19685376 | tf_op jit(solution)/shard_map/dot_general | solution.py:46
  375.6 14.7 %collective-permute-done.51 = bf16[2,1,216,1152]{3,2,1,0:T(8,128)(2,1)S(1)} collective-permute-done((bf16[2,1,216,1152]{3,2,1,0:T(8,128)(2,1)S(1)}, bf16[2,1,216,1152]{3,2,1,0:T(8,128)(2,1)S(1)}, u32[]{:S(2)}, u32[]{:S(2)}) %collective-permute-start.51) | collective-permute-done | bytes 995360 | tf_op jit(solution)/shard_map/ppermute | solution.py:62
  407.0 12.5 %collective-permute-done.50 = bf16[256,1152]{1,0:T(8,128)(2,1)S(1)} collective-permute-done((bf16[256,1152]{1,0:T(8,128)(2,1)S(1)}, bf16[256,1152]{1,0:T(8,128)(2,1)S(1)}, u32[]{:S(2)}, u32[]{:S(2)}) %collective-permute-start.50) | collective-permute-done | bytes 589856 | tf_op jit(solution)/shard_map/ppermute | solution.py:62
  429.3 15.4 %attend_back.1 = (bf16[256,1024]{1,0:T(8,128)(2,1)}, f32[1,256]{1,0:T(1,128)}, bf16[8,2,128,512]{3,2,1,0:T(8,128)(2,1)}, bf16[8,2,128,512]{3,2,1,0:T(8,128)(2,1)}) custom-call(s32[7]{0:T(128)} %pad_add_fusion.1.meta_ref, s32[4]{0:T(128)} %bitcast.326, s32[16]{0:T(128)} %gather_fusion.1, bf16[2,4,128,256]{3,2,1,0:T(8,128)(2,1)} %get-tuple-element.112.q_ref, ...), custom_call_target="tpu_custom_call" | custom-call | flops 6039797760 | bytes 8388608 | tf_op jit(solution)/shard_map/attend_back/pallas_call | solution.py:418
  470.9 9.9 %collective-permute-done.59 = bf16[4,256,512]{2,1,0:T(8,128)(2,1)} collective-permute-done((bf16[4,256,512]{2,1,0:T(8,128)(2,1)}, bf16[4,256,512]{2,1,0:T(8,128)(2,1)}, u32[]{:S(2)}, u32[]{:S(2)}) %collective-permute-start.59) | collective-permute-done | bytes 1048608 | tf_op jit(solution)/shard_map/ppermute | solution.py:62
  487.0 8.0 %collective-permute-start.62 = (bf16[256,512]{1,0:T(8,128)(2,1)}, bf16[256,512]{1,0:T(8,128)(2,1)}, u32[]{:S(2)}, u32[]{:S(2)}) collective-permute-start(bf16[256,512]{1,0:T(8,128)(2,1)} %get-tuple-element.232), channel_id=1, source_target_pairs={{0,24},{4,28},{8,16},{12,20},{16,8},{20,12},{24,0},{28,4},{1,25},{... | collective-permute-start | bytes 786440 | tf_op jit(solution)/shard_map/ppermute | solution.py:62
  500.6 82.9 %reduce-scatter.2.cloned.1.call-done = bf16[32,1152]{1,0:T(8,128)(2,1)} async-done(((bf16[1024,1152]{1,0:T(8,128)(2,1)}), bf16[32,1152]{1,0:T(8,128)(2,1)}) %reduce-scatter.2.cloned.1.call-update) | async-done | bytes 73744 | tf_op jit(solution)/shard_map/reduce_scatter | solution.py:717
  633.6 6.9 %collective-permute-done.66 = bf16[2,40,1024]{2,1,0:T(8,128)(2,1)S(1)} collective-permute-done((bf16[2,40,1024]{2,1,0:T(8,128)(2,1)S(1)}, bf16[2,40,1024]{2,1,0:T(8,128)(2,1)S(1)}, u32[]{:S(2)}, u32[]{:S(2)}) %collective-permute-start.66) | collective-permute-done | bytes 163872 | tf_op jit(solution)/shard_map/ppermute | solution.py:68
  (526 shorter events, 326.7 us)
Async XLA Ops:
  31.2 39.0 %collective-permute-start = (bf16[128,1152]{1,0:T(8,128)(2,1)}, bf16[128,1152]{1,0:T(8,128)(2,1)S(1)}, u32[]{:S(2)}, u32[]{:S(2)}) collective-permute-start(bf16[128,1152]{1,0:T(8,128)(2,1)} %get-tuple-element.247), channel_id=1, source_target_pairs={{0,4},{4,0},{8,12},{12,8},{16,20},{20,16},{24,28},{28,24},{1,5},{5... | collective-permute-start | bytes 884744 | tf_op jit(solution)/shard_map/ppermute | solution.py:62
  70.9 29.0 %collective-permute-start.7 = (bf16[1,216,1152]{2,1,0:T(8,128)(2,1)}, bf16[1,216,1152]{2,1,0:T(8,128)(2,1)}, u32[]{:S(2)}, u32[]{:S(2)}) collective-permute-start(bf16[1,216,1152]{2,1,0:T(8,128)(2,1)} %bitcast.303), channel_id=1, source_target_pairs={{0,16},{4,20},{8,24},{12,28},{16,0},{20,4},{24,8},{28,12},{1,17},{... | collective-permute-start | bytes 1493000 | tf_op jit(solution)/shard_map/ppermute | solution.py:62
  73.8 26.1 %all-to-all-start = ((bf16[4,2,2,36,864]{4,2,3,1,0:T(2,128)(2,1)}), bf16[4,2,2,36,864]{4,2,3,1,0:T(2,128)(2,1)}, u32[]{:S(2)}, u32[]{:S(2)}) async-start(bf16[4,2,2,36,864]{4,2,3,1,0:T(2,128)(2,1)} %copy.75), calls=%async_computation | async-start | bytes 2064384 | tf_op jit(solution)/shard_map/all_to_all | solution.py:550
  78.1 112.7 %all-gather.2.cloned.1.call-start = ((), (), s32[]{:S(2)}) async-start(), calls=%async_computation.3 | async-start | bytes 2433024 | tf_op jit(solution)/shard_map/all_gather | solution.py:570
  82.0 501.5 %reduce-scatter.2.cloned.1.call-start = ((), (), s32[]{:S(2)}) async-start(), calls=%async_computation.4 | async-start | bytes 2433024 | tf_op jit(solution)/shard_map/reduce_scatter | solution.py:717
  89.9 34.3 %collective-permute-start.12 = (bf16[2,128,512]{2,1,0:T(8,128)(2,1)}, bf16[2,128,512]{2,1,0:T(8,128)(2,1)S(1)}, u32[]{:S(2)}, u32[]{:S(2)}) collective-permute-start(bf16[2,128,512]{2,1,0:T(8,128)(2,1)} %get-tuple-element.110), channel_id=1, source_target_pairs={{0,2},{1,3},{2,0},{3,1},{4,6},{5,7},{6,4},{7,5},{8,10},{9,11},{10,... | collective-permute-start | bytes 786440 | tf_op jit(solution)/shard_map/ppermute | solution.py:62
  91.8 27.6 %collective-permute-start.10 = (bf16[2,128,512]{2,1,0:T(8,128)(2,1)}, bf16[2,128,512]{2,1,0:T(8,128)(2,1)S(1)}, u32[]{:S(2)}, u32[]{:S(2)}) collective-permute-start(bf16[2,128,512]{2,1,0:T(8,128)(2,1)} %get-tuple-element.110), channel_id=1, source_target_pairs={{0,24},{4,28},{8,16},{12,20},{16,8},{20,12},{24,0},{28,4},{1,25},{... | collective-permute-start | bytes 786440 | tf_op jit(solution)/shard_map/ppermute | solution.py:62
  124.8 41.9 %collective-permute-start.11 = (bf16[2,144,864]{2,1,0:T(8,128)(2,1)}, bf16[2,144,864]{2,1,0:T(8,128)(2,1)}, u32[]{:S(2)}, u32[]{:S(2)}) collective-permute-start(bf16[2,144,864]{2,1,0:T(8,128)(2,1)} %get-tuple-element.128.refs_0_), channel_id=1, source_target_pairs={{0,16},{4,20},{8,24},{12,28},{16,0},{20,4},{24,8},{28,12},{1,17},{... | collective-permute-start | bytes 1493000 | tf_op jit(solution)/shard_map/ppermute | solution.py:62
  132.6 49.2 %collective-permute-start.22 = (bf16[2,144,864]{2,1,0:T(8,128)(2,1)}, bf16[2,144,864]{2,1,0:T(8,128)(2,1)}, u32[]{:S(2)}, u32[]{:S(2)}) collective-permute-start(bf16[2,144,864]{2,1,0:T(8,128)(2,1)} %get-tuple-element.132.refs_0_), channel_id=1, source_target_pairs={{0,16},{4,20},{8,24},{12,28},{16,0},{20,4},{24,8},{28,12},{1,17},{... | collective-permute-start | bytes 1493000 | tf_op jit(solution)/shard_map/ppermute | solution.py:62
  134.5 34.2 %collective-permute-start.18 = (bf16[4,2,128,512]{3,2,1,0:T(8,128)(2,1)S(1)}, bf16[4,2,128,512]{3,2,1,0:T(8,128)(2,1)S(1)}, u32[]{:S(2)}, u32[]{:S(2)}) collective-permute-start(bf16[4,2,128,512]{3,2,1,0:T(8,128)(2,1)S(1)} %pad_maximum_fusion.4), channel_id=1, source_target_pairs={{0,1},{1,0},{2,3},{3,2},{4,5},{5,4},{6,7},{7,6},{8,9},{9,8},{10,11... | collective-permute-start | bytes 3145736 | tf_op jit(solution)/shard_map/ppermute | solution.py:62
  141.6 27.2 %collective-permute-start.19 = (bf16[4,2,128,512]{3,2,1,0:T(8,128)(2,1)S(1)}, bf16[4,2,128,512]{3,2,1,0:T(8,128)(2,1)S(1)}, u32[]{:S(2)}, u32[]{:S(2)}) collective-permute-start(bf16[4,2,128,512]{3,2,1,0:T(8,128)(2,1)S(1)} %pad_maximum_fusion.5), channel_id=1, source_target_pairs={{0,1},{1,0},{2,3},{3,2},{4,5},{5,4},{6,7},{7,6},{8,9},{9,8},{10,11... | collective-permute-start | bytes 3145736 | tf_op jit(solution)/shard_map/ppermute | solution.py:62
  196.3 28.8 %collective-permute-start.24 = (bf16[256,1152]{1,0:T(8,128)(2,1)}, bf16[256,1152]{1,0:T(8,128)(2,1)S(1)}, u32[]{:S(2)}, u32[]{:S(2)}) collective-permute-start(bf16[256,1152]{1,0:T(8,128)(2,1)} %get-tuple-element.197), channel_id=1, source_target_pairs={{0,8},{4,12},{8,0},{12,4},{16,24},{20,28},{24,16},{28,20},{1,9},{5... | collective-permute-start | bytes 1769480 | tf_op jit(solution)/shard_map/ppermute | solution.py:62
  196.3 29.2 %collective-permute-start.23 = (bf16[256,1152]{1,0:T(8,128)(2,1)}, bf16[256,1152]{1,0:T(8,128)(2,1)S(1)}, u32[]{:S(2)}, u32[]{:S(2)}) collective-permute-start(bf16[256,1152]{1,0:T(8,128)(2,1)} %get-tuple-element.197), channel_id=1, source_target_pairs={{0,2},{1,3},{2,0},{3,1},{4,6},{5,7},{6,4},{7,5},{8,10},{9,11},{10,... | collective-permute-start | bytes 1769480 | tf_op jit(solution)/shard_map/ppermute | solution.py:62
  359.3 31.1 %collective-permute-start.46 = (bf16[1024,1152]{1,0:T(8,128)(2,1)S(1)}, bf16[1024,1152]{1,0:T(8,128)(2,1)S(1)}, u32[]{:S(2)}, u32[]{:S(2)}) collective-permute-start(bf16[1024,1152]{1,0:T(8,128)(2,1)S(1)} %slice.262), channel_id=1, source_target_pairs={{0,1},{1,0},{2,3},{3,2},{4,5},{5,4},{6,7},{7,6},{8,9},{9,8},{10,11... | collective-permute-start | bytes 7077896 | tf_op jit(solution)/shard_map/ppermute | solution.py:62
  374.0 70.6 %collective-permute-start.52 = (bf16[2,2,144,864]{3,2,1,0:T(8,128)(2,1)}, bf16[2,2,144,864]{3,2,1,0:T(8,128)(2,1)}, u32[]{:S(2)}, u32[]{:S(2)}) collective-permute-start(bf16[2,2,144,864]{3,2,1,0:T(8,128)(2,1)} %get-tuple-element.223), channel_id=1, source_target_pairs={{0,4},{4,0},{8,12},{12,8},{16,20},{20,16},{24,28},{28,24},{1,5},{5... | collective-permute-start | bytes 2985992 | tf_op jit(solution)/shard_map/ppermute | solution.py:62
  403.6 41.0 %collective-permute-start.54 = (bf16[1,216,1152]{2,1,0:T(8,128)(2,1)}, bf16[1,216,1152]{2,1,0:T(8,128)(2,1)}, u32[]{:S(2)}, u32[]{:S(2)}) collective-permute-start(bf16[1,216,1152]{2,1,0:T(8,128)(2,1)} %get-tuple-element.238), channel_id=1, source_target_pairs={{0,16},{4,20},{8,24},{12,28},{16,0},{20,4},{24,8},{28,12},{1,17},{... | collective-permute-start | bytes 1493000 | tf_op jit(solution)/shard_map/ppermute | solution.py:62
  405.3 39.4 %collective-permute-start.53 = (bf16[2,2,144,864]{3,2,1,0:T(8,128)(2,1)}, bf16[2,2,144,864]{3,2,1,0:T(8,128)(2,1)}, u32[]{:S(2)}, u32[]{:S(2)}) collective-permute-start(bf16[2,2,144,864]{3,2,1,0:T(8,128)(2,1)} %get-tuple-element.221), channel_id=1, source_target_pairs={{0,4},{4,0},{8,12},{12,8},{16,20},{20,16},{24,28},{28,24},{1,5},{5... | collective-permute-start | bytes 2985992 | tf_op jit(solution)/shard_map/ppermute | solution.py:62
  453.7 27.1 %collective-permute-start.59 = (bf16[4,256,512]{2,1,0:T(8,128)(2,1)}, bf16[4,256,512]{2,1,0:T(8,128)(2,1)}, u32[]{:S(2)}, u32[]{:S(2)}) collective-permute-start(bf16[4,256,512]{2,1,0:T(8,128)(2,1)} %bitcast.151), channel_id=1, source_target_pairs={{0,2},{1,3},{2,0},{3,1},{4,6},{5,7},{6,4},{7,5},{8,10},{9,11},{10,... | collective-permute-start | bytes 3145736 | tf_op jit(solution)/shard_map/ppermute | solution.py:62
  467.4 123.4 %collective-permute-start.55 = (bf16[2,144,864]{2,1,0:T(8,128)(2,1)}, bf16[2,144,864]{2,1,0:T(8,128)(2,1)}, u32[]{:S(2)}, u32[]{:S(2)}) collective-permute-start(bf16[2,144,864]{2,1,0:T(8,128)(2,1)} %get-tuple-element.236), channel_id=1, source_target_pairs={{0,16},{4,20},{8,24},{12,28},{16,0},{20,4},{24,8},{28,12},{1,17},{... | collective-permute-start | bytes 1493000 | tf_op jit(solution)/shard_map/ppermute | solution.py:62
  486.6 99.3 %collective-permute-start.60 = (bf16[256,512]{1,0:T(8,128)(2,1)}, bf16[256,512]{1,0:T(8,128)(2,1)}, u32[]{:S(2)}, u32[]{:S(2)}) collective-permute-start(bf16[256,512]{1,0:T(8,128)(2,1)} %get-tuple-element.231), channel_id=1, source_target_pairs={{0,8},{4,12},{8,0},{12,4},{16,24},{20,28},{24,16},{28,20},{1,9},{5... | collective-permute-start | bytes 786440 | tf_op jit(solution)/shard_map/ppermute | solution.py:62
  487.0 100.4 %collective-permute-start.62 = (bf16[256,512]{1,0:T(8,128)(2,1)}, bf16[256,512]{1,0:T(8,128)(2,1)}, u32[]{:S(2)}, u32[]{:S(2)}) collective-permute-start(bf16[256,512]{1,0:T(8,128)(2,1)} %get-tuple-element.232), channel_id=1, source_target_pairs={{0,24},{4,28},{8,16},{12,20},{16,8},{20,12},{24,0},{28,4},{1,25},{... | collective-permute-start | bytes 786440 | tf_op jit(solution)/shard_map/ppermute | solution.py:62
  495.0 92.4 %collective-permute-start.61 = (bf16[256,512]{1,0:T(8,128)(2,1)}, bf16[256,512]{1,0:T(8,128)(2,1)}, u32[]{:S(2)}, u32[]{:S(2)}) collective-permute-start(bf16[256,512]{1,0:T(8,128)(2,1)} %get-tuple-element.233), channel_id=1, source_target_pairs={{0,16},{4,20},{8,24},{12,28},{16,0},{20,4},{24,8},{28,12},{1,17},{... | collective-permute-start | bytes 786440 | tf_op jit(solution)/shard_map/ppermute | solution.py:62
  498.2 92.7 %collective-permute-start.56 = (bf16[2,144,864]{2,1,0:T(8,128)(2,1)}, bf16[2,144,864]{2,1,0:T(8,128)(2,1)}, u32[]{:S(2)}, u32[]{:S(2)}) collective-permute-start(bf16[2,144,864]{2,1,0:T(8,128)(2,1)} %get-tuple-element.234), channel_id=1, source_target_pairs={{0,16},{4,20},{8,24},{12,28},{16,0},{20,4},{24,8},{28,12},{1,17},{... | collective-permute-start | bytes 1493000 | tf_op jit(solution)/shard_map/ppermute | solution.py:62
  585.9 30.9 %collective-permute-start.64 = (bf16[8,40,1024]{2,1,0:T(8,128)(2,1)}, bf16[8,40,1024]{2,1,0:T(8,128)(2,1)}, u32[]{:S(2)}, u32[]{:S(2)}) collective-permute-start(bf16[8,40,1024]{2,1,0:T(8,128)(2,1)} %slice.284), channel_id=1, source_target_pairs={{0,2},{1,3},{2,0},{3,1},{4,6},{5,7},{6,4},{7,5},{8,10},{9,11},{10,... | collective-permute-start | bytes 1966088 | tf_op jit(solution)/shard_map/ppermute | solution.py:68
  (138 other events, 1875.6 us)
Sparse Core Ops, SparseCore 0:
  82.1 99.2 all-gather.1
  448.7 134.7 reduce-scatter.1

commit v6 on v5

--- a/solution.py
+++ b/solution.py
@@ -539,7 +539,6 @@
         kept, sent = array[:rows], array[rows:]
         return flips(jnp.stack([kept, xor(sent, "dp", 1)]), [y_bit])
 
-    rows_in = regroup(inputs).astype(f32)
 
     def column_exchange(packed):
         kept = lax.dynamic_index_in_dim(packed, z_bit, 0, keepdims=False)
@@ -560,7 +559,8 @@
     *row_masks, y_mask, x_mask, core_mask = all_masks()
     for masks in row_masks:
         blocks = gather_step(blocks, *masks)
-    blocks, packed, down_piece = together(blocks, packed, w_down[None])
+    blocks, packed, down_piece, rows_low = together(blocks, packed, w_down[None], regroup(inputs))
+    rows_in = rows_low.astype(f32)
     column_parts = column_exchange(packed)
     blocks = gather_step(gather_step(blocks, *y_mask), *x_mask)
     blocks, column_parts = together(blocks, column_parts)
@@ -635,15 +635,15 @@
     column = [keys_mine] + [xor(keys_mine, "dp", 2 * k) for k in range(1, layers)]
     halves, others = together(halves, column[1:])
     column = [column[0], *others]
-    gate_tall, up_tall = [from_tops(half) for half in halves]
+    gate_tall, up_half = together(from_tops(halves[0]), halves[1])
+    up_tall = from_tops(up_half)
     across = [xor(part, "seq", 2) for part in column]
     across, down_pieces = lax.optimization_barrier((across, both_sides(down_tall)))
     column, across = jnp.stack(column), jnp.stack(across)
     near_keys = jnp.concatenate([column, across])
     far_keys = jnp.concatenate([xor(column, "seq", 1), xor(across, "seq", 1)])
     query_raw, query_heads = project(picked_one, qkv_weight, query_gain[None], cosine, sine)
-    natural_weight = mm(model_pick, qkv_weight).astype(bf16)
-    query_heads, natural_weight, gate_tall = lax.optimization_barrier((query_heads, natural_weight, gate_tall))
+    query_heads, gate_tall = together(query_heads, gate_tall)
     gate_pieces = both_sides(gate_tall)
     context_rows, turned, lse = attend(meta, seq_ends, slots, query_heads, near_keys, far_keys)
     context_rows, gate_pieces, up_tall = together(context_rows, gate_pieces, up_tall)
@@ -661,6 +661,7 @@
     up_raw = mm(normed_group, up_weight)
     hidden_low = (jax.nn.gelu(gate_raw, approximate=True) * up_raw).astype(bf16)
     mixed = scatter_group(mm(hidden_low, down_weight).astype(bf16))
+    natural_weight, mixed = together(mm(model_pick, qkv_weight).astype(bf16), mixed)
     scale_four = norm_scale(mixed)
     result = hidden_res + mixed * scale_four * post_feed
     output = ungroup(jnp.where(valid, result, 0.0).astype(bf16))
@@ -714,7 +715,7 @@
     )
     gate_halves, up_halves = (gate_kept, gate_halves[1]), (up_kept, up_halves[1])
     down_parts = send_tops(by_top(*down_halves))
-    grad_out = lax.psum_scatter(out_total, ALL, scatter_dimension=0, tiled=True).astype(f32)
+    grad_out = lax.psum_scatter(out_total, ALL, scatter_dimension=0, tiled=True)
     context_grad = mm_nt(attended_grad, out_weight).astype(bf16)
     query_grad, grad_query_gain, near_part, far_part = attend_back(
         meta, seq_ends, slots, query_heads, context_grad, lse, turned, query_raw, query_gain[None], cosine, sine, near_keys, far_keys
@@ -728,9 +729,10 @@
     near_part = add16(near_part, far_part).reshape(2, layers, count, 2 * HEAD)
     near_part = add16(near_part[0], xor(near_part[1], "seq", 2))
     grad_query = mm_tn(picked_one, query_low).astype(bf16).reshape(devices, block_rows, wide_q)
-    grad_query, near_part = together(scatter_step(grad_query, *core_mask), near_part)
+    grad_query, near_part, gate_parts = together(scatter_step(grad_query, *core_mask), near_part, gate_parts)
     grad_query = scatter_rest(grad_query)
     key_parts = [near_part[k] if k == 0 else xor(near_part[k], "dp", 2 * k) for k in range(layers)]
+    key_parts, up_parts = together(key_parts, up_parts)
     key_grads = functools.reduce(jnp.add, [part.astype(f32) for part in key_parts])
     value_grad = key_grads[:, HEAD:].astype(bf16)
     key_turned = rotate(key_grads[:, :HEAD], cosine, -sine)
@@ -738,14 +740,14 @@
     grad_key_gain = jnp.sum(key_turned * key_raw * key_scale, axis=0)
     key_grad = norm_back(key_raw, key_scale, key_gain * key_turned).astype(bf16)
     kv_grad = jnp.concatenate([key_grad, value_grad], axis=1)
-    down_parts, gate_parts, up_parts, kv_grad = together(down_parts, gate_parts, up_parts, kv_grad)
+    normed_one_grad = mm_nt(query_grad, natural_weight[:, :wide_q]) + mm_nt(kv_grad, natural_weight[:, wide_q:])
+    grad_pre_attention = jnp.sum(normed_one_grad * rows_in * scale_one, axis=0)
+    rows_grad = hidden_res_grad + norm_back(rows_in, scale_one, pre_attention * normed_one_grad)
+    rows_low, down_parts, gate_parts, up_parts = together(rows_grad.astype(bf16), down_parts, gate_parts, up_parts)
     grad_down = total_of(down_parts)[0]
     both_grads = split(total_of(gate_parts).astype(bf16), total_of(up_parts).astype(bf16), members)
     grad_gate, grad_up = unpack(swap_members(column_exchange(both_grads)), z_bit, tops, members, ff_rows)
-    normed_one_grad = mm_nt(query_grad, natural_weight[:, :wide_q]) + mm_nt(kv_grad, natural_weight[:, wide_q:])
-    grad_pre_attention = jnp.sum(normed_one_grad * rows_in * scale_one, axis=0)
-    rows_grad = hidden_res_grad + norm_back(rows_in, scale_one, pre_attention * normed_one_grad)
-    input_grad = ungroup(rows_grad.astype(bf16))
+    input_grad = ungroup(rows_low)
     grad_kv = mm_tn(picked_one, kv_grad).reshape(devices, block_rows, 2 * HEAD)
     gain_grads = [
         grad_pre_attention,
@@ -761,6 +763,8 @@
         gain_grads[:, None, :], ((0, 0), (model_rows, block_rows - model_rows - 1), (0, 2 * HEAD - gain_total))
     )
     last = scatter_rest(scatter_step((grad_kv + gain_grads).astype(bf16), *core_mask))
+    last, grad_out = together(last, grad_out)
+    grad_out = grad_out.astype(f32)
     gain_out, at = [], 0
     for size in gain_sizes:
         gain_out.append(last[model_rows, at : at + size])

time: 671 us -> 630 us (0.939)
  starting transfers between devices: 98.7 us -> 77 us
  waiting for transfers between devices: 272 us -> 256 us
    reduce_scatter x1, waiting for transfers between devices: 82.9 us -> 0.02 us  [per_device(): grad_out = lax.psum_scatter(out_total, ALL, scatter_dimension=0, tiled=True)]
    ppermute x59, waiting for transfers between devices: 152 us -> 216 us  [xor(): lax.ppermute(value, axis, [(i, i ^ mask) for i in range(lax.axis_size(axi...]
    ppermute x59, starting transfers between devices: 73.8 us -> 50.7 us  [xor(): lax.ppermute(value, axis, [(i, i ^ mask) for i in range(lax.axis_size(axi...]
    unnamed x190 -> x206, local copies, waits for them, and re-layouts: 13.5 us -> 17.6 us
  transfers between devices with their start and end apart: 78 -> 78, of which waited for: 34 -> 39; matrix products, arithmetic and copies ran while one was open for 22% -> 20% of each run, Pallas kernels for 8% -> 9%
where the time goes in v6:
time: 630 us; the launch traced here: 619 us
  waiting for transfers between devices  256 us (41%)
  matrix products  89.3 us (14%)
  starting transfers between devices  77 us (12%)
  other arithmetic  63.8 us (10%)
  local copies, waits for them, and re-layouts  59.1 us (9%)
  Pallas kernels  57.3 us (9%)
  between operations  15.9 us (3%)
    ppermute x59, waiting for transfers between devices, xor(): lax.ppermute(value, axis, [(i, i ^ mask) for i in range(lax.axis_size(axi...  216 us
    dot_general x20, matrix products, dot(): lax.dot_general(left, right, (dims, ((), ())), preferred_element_type=f32)  89.3 us
    ppermute x59, starting transfers between devices, xor(): lax.ppermute(value, axis, [(i, i ^ mask) for i in range(lax.axis_size(axi...  50.7 us
    ppermute x15, waiting for transfers between devices, xor_both(): lax.ppermute(value, ALL, [(i, i ^ mask) for i in range(lax.axis_size('dp'...  40.5 us
    ppermute x15, starting transfers between devices, xor_both(): lax.ppermute(value, ALL, [(i, i ^ mask) for i in range(lax.axis_size('dp'...  19.2 us
    unnamed x206, local copies, waits for them, and re-layouts  17.6 us
    pallas_call x1, Pallas kernels, attend_back(): pl.pallas_call(functools.partial(attend_back_kernel, rows), grid_spec=plt...  17.1 us
    pallas_call x1, Pallas kernels, attend(): pl.pallas_call(functools.partial(attend_kernel, rows), grid_spec=pltpu.Pr...  12.7 us
  transfers between devices with their start and end apart: 78, of which 39 were waited for; matrix products, arithmetic and copies ran while one was open for 20% of the time, Pallas kernels for 9%

profile of v6, /device:TPU:0, one launch (start us, length us, event | category | flops | bytes accessed | tf_op | source)
XLA Modules:
  0.0 618.9 jit_solution(17943675965051469697)
XLA Ops:
  21.8 9.0 %collective-permute-done.1 = bf16[2,40,1536]{2,1,0:T(8,128)(2,1)S(1)} collective-permute-done((bf16[2,40,1536]{2,1,0:T(8,128)(2,1)S(1)}, bf16[2,40,1536]{2,1,0:T(8,128)(2,1)S(1)}, u32[]{:S(2)}, u32[]{:S(2)}) %collective-permute-start.1) | collective-permute-done | bytes 245792 | tf_op jit(solution)/shard_map/ppermute | solution.py:68
  31.5 12.7 %collective-permute-done.3 = bf16[4,40,1536]{2,1,0:T(8,128)(2,1)S(1)} collective-permute-done((bf16[4,40,1536]{2,1,0:T(8,128)(2,1)S(1)}, bf16[4,40,1536]{2,1,0:T(8,128)(2,1)S(1)}, u32[]{:S(2)}, u32[]{:S(2)}) %collective-permute-start.3) | collective-permute-done | bytes 491552 | tf_op jit(solution)/shard_map/ppermute | solution.py:68
  47.9 11.7 %collective-permute-done.5 = bf16[4,2,36,864]{3,0,2,1:T(4,128)(2,1)S(1)} collective-permute-done((bf16[4,2,36,864]{3,0,2,1:T(4,128)(2,1)S(1)}, bf16[4,2,36,864]{3,0,2,1:T(4,128)(2,1)S(1)}, u32[]{:S(2)}, u32[]{:S(2)}) %collective-permute-start.5) | collective-permute-done | bytes 497696 | tf_op jit(solution)/shard_map/ppermute | solution.py:62
  102.2 15.0 %collective-permute-done.7.refs_1_ = bf16[1,216,1152]{2,1,0:T(8,128)(2,1)S(1)} collective-permute-done((bf16[1,216,1152]{2,1,0:T(8,128)(2,1)}, bf16[1,216,1152]{2,1,0:T(8,128)(2,1)S(1)}, u32[]{:S(2)}, u32[]{:S(2)}) %collective-permute-start.7) | collective-permute-done | bytes 497696 | tf_op jit(solution)/shard_map/ppermute | solution.py:62
  135.4 10.2 %collective-permute-done.17.refs_3_ = bf16[1,216,1152]{2,1,0:T(8,128)(2,1)} collective-permute-done((bf16[1,216,1152]{2,1,0:T(8,128)(2,1)}, bf16[1,216,1152]{2,1,0:T(8,128)(2,1)}, u32[]{:S(2)}, u32[]{:S(2)}) %collective-permute-start.17) | collective-permute-done | bytes 497696 | tf_op jit(solution)/shard_map/ppermute | solution.py:62
  154.8 9.0 %collective-permute-done.11.refs_1_ = bf16[2,144,864]{2,1,0:T(8,128)(2,1)} collective-permute-done((bf16[2,144,864]{2,1,0:T(8,128)(2,1)S(1)}, bf16[2,144,864]{2,1,0:T(8,128)(2,1)}, u32[]{:S(2)}, u32[]{:S(2)}) %collective-permute-start.11) | collective-permute-done | bytes 497696 | tf_op jit(solution)/shard_map/ppermute | solution.py:62
  167.3 12.7 %attend.1 = (bf16[256,1024]{1,0:T(8,128)(2,1)}, f32[2,256,512]{2,1,0:T(8,128)}, f32[2,1,512]{2,1,0:T(1,128)}) custom-call(s32[7]{0:T(128)} %pad_add_fusion.1.meta_ref, s32[4]{0:T(128)} %bitcast.320, s32[16]{0:T(128)} %gather_fusion.1, bf16[2,4,128,256]{3,2,1,0:T(8,128)(2,1)} %get-tuple-element.131.q_ref, bf16[8,2,128,512]{3,2,1,0:T(8,128)(2,1)} %copy-done.54, ...), custom_call_target="tpu_custom_call" | custom-call | flops 2415919104 | bytes 4194304 | tf_op jit(solution)/shard_map/attend/pallas_call | solution.py:389
  180.0 8.9 %collective-permute-done.22.refs_1_ = bf16[2,144,864]{2,1,0:T(8,128)(2,1)} collective-permute-done((bf16[2,144,864]{2,1,0:T(8,128)(2,1)}, bf16[2,144,864]{2,1,0:T(8,128)(2,1)}, u32[]{:S(2)}, u32[]{:S(2)}) %collective-permute-start.22) | collective-permute-done | bytes 497696 | tf_op jit(solution)/shard_map/ppermute | solution.py:62
  211.8 8.4 %collective-permute-done.31.refs_3_ = bf16[2,144,864]{2,1,0:T(8,128)(2,1)} collective-permute-done((bf16[2,144,864]{2,1,0:T(8,128)(2,1)}, bf16[2,144,864]{2,1,0:T(8,128)(2,1)}, u32[]{:S(2)}, u32[]{:S(2)}) %collective-permute-start.31) | collective-permute-done | bytes 497696 | tf_op jit(solution)/shard_map/ppermute | solution.py:62
  238.7 7.0 %fusion.66 = f32[2048,864]{0,1:T(8,128)S(1)} fusion(bf16[2048,1152]{1,0:T(8,128)(2,1)} %constant_dynamic-update-slice_fusion.10, bf16[1152,864]{1,0:T(8,128)(2,1)S(1)} %bitcast.279), kind=kOutput, calls=%fused_computation.277 | convolution fusion | flops 4076863488 | bytes 13787136 | tf_op jit(solution)/shard_map/dot_general | solution.py:46
  245.7 8.7 %multiply_convert_fusion.1 = (bf16[2048,864]{0,1:T(8,128)(2,1)S(1)}, f32[2048,864]{0,1:T(8,128)}) fusion(f32[2048,864]{0,1:T(8,128)S(1)} %fusion.66, bf16[2048,1152]{1,0:T(8,128)(2,1)S(1)} %copy-done.51, bf16[1152,864]{1,0:T(8,128)(2,1)S(1)} %bitcast.281), kind=kOutput, calls=%fused_computation.15 | convolution fusion | flops 4094558208 | bytes 24403968 | tf_op jit(solution)/shard_map/dot_general | solution.py:46
  288.4 6.9 %collective-permute-done.36 = bf16[256,1152]{1,0:T(8,128)(2,1)S(1)} collective-permute-done((bf16[256,1152]{1,0:T(8,128)(2,1)S(1)}, bf16[256,1152]{1,0:T(8,128)(2,1)S(1)}, u32[]{:S(2)}, u32[]{:S(2)}) %collective-permute-start.36) | collective-permute-done | bytes 589856 | tf_op jit(solution)/shard_map/ppermute | solution.py:62
  302.8 11.4 %collective-permute-done.40 = bf16[256,1152]{1,0:T(8,128)(2,1)S(1)} collective-permute-done((bf16[256,1152]{1,0:T(8,128)(2,1)}, bf16[256,1152]{1,0:T(8,128)(2,1)S(1)}, u32[]{:S(2)}, u32[]{:S(2)}) %collective-permute-start.40) | collective-permute-done | bytes 589856 | tf_op jit(solution)/shard_map/ppermute | solution.py:62
  328.0 13.3 %multiply_convert_fusion = (bf16[2048,864]{0,1:T(8,128)(2,1)S(1)}, bf16[2048,864]{0,1:T(8,128)(2,1)S(1)}) fusion(f32[2048,864]{0,1:T(8,128)} %copy-done.81, f32[2048,864]{0,1:T(8,128)} %get-tuple-element.312, bf16[2048,1152]{1,0:T(8,128)(2,1)} %constant_dynamic-update-slice_fusion.18, bf16[864,1152]{1,0:T(8,128)(2,1)S(1)} %bitcast.290), kind=kOutput, calls=%fused_computation.14 | convolution fusion | flops 4119330816 | bytes 27942912 | tf_op jit(solution)/shard_map/dot_general | solution.py:46
  341.3 8.2 %fusion.67 = f32[2048,1152]{1,0:T(8,128)} fusion(bf16[2048,864]{0,1:T(8,128)(2,1)S(1)} %get-tuple-element.163, bf16[1152,864]{1,0:T(8,128)(2,1)S(1)} %bitcast.280), kind=kOutput, calls=%fused_computation.278 | convolution fusion | flops 4076863488 | bytes 14966784 | tf_op jit(solution)/shard_map/dot_general | solution.py:46
  349.6 8.3 %add_convert_fusion = bf16[2048,1152]{1,0:T(8,128)(2,1)S(1)} fusion(f32[2048,1152]{1,0:T(8,128)} %fusion.67, bf16[2048,864]{0,1:T(8,128)(2,1)S(1)} %get-tuple-element.166, bf16[1152,864]{1,0:T(8,128)(2,1)S(1)} %bitcast.282), kind=kOutput, calls=%fused_computation.4 | convolution fusion | flops 4081582080 | bytes 19685376 | tf_op jit(solution)/shard_map/dot_general | solution.py:46
  373.3 15.9 %collective-permute-done.51 = bf16[2,1,216,1152]{3,2,1,0:T(8,128)(2,1)S(1)} collective-permute-done((bf16[2,1,216,1152]{3,2,1,0:T(8,128)(2,1)S(1)}, bf16[2,1,216,1152]{3,2,1,0:T(8,128)(2,1)S(1)}, u32[]{:S(2)}, u32[]{:S(2)}) %collective-permute-start.51) | collective-permute-done | bytes 995360 | tf_op jit(solution)/shard_map/ppermute | solution.py:62
  405.4 14.9 %collective-permute-done.50 = bf16[256,1152]{1,0:T(8,128)(2,1)S(1)} collective-permute-done((bf16[256,1152]{1,0:T(8,128)(2,1)S(1)}, bf16[256,1152]{1,0:T(8,128)(2,1)S(1)}, u32[]{:S(2)}, u32[]{:S(2)}) %collective-permute-start.50) | collective-permute-done | bytes 589856 | tf_op jit(solution)/shard_map/ppermute | solution.py:62
  429.0 17.1 %attend_back.1 = (bf16[256,1024]{1,0:T(8,128)(2,1)}, f32[1,256]{1,0:T(1,128)}, bf16[8,2,128,512]{3,2,1,0:T(8,128)(2,1)}, bf16[8,2,128,512]{3,2,1,0:T(8,128)(2,1)}) custom-call(s32[7]{0:T(128)} %pad_add_fusion.1.meta_ref, s32[4]{0:T(128)} %bitcast.321, s32[16]{0:T(128)} %gather_fusion.1, bf16[2,4,128,256]{3,2,1,0:T(8,128)(2,1)} %get-tuple-element.131.q_ref, ...), custom_call_target="tpu_custom_call" | custom-call | flops 6039797760 | bytes 8388608 | tf_op jit(solution)/shard_map/attend_back/pallas_call | solution.py:418
  469.4 11.4 %collective-permute-done.57 = bf16[4,256,512]{2,1,0:T(8,128)(2,1)} collective-permute-done((bf16[4,256,512]{2,1,0:T(8,128)(2,1)}, bf16[4,256,512]{2,1,0:T(8,128)(2,1)}, u32[]{:S(2)}, u32[]{:S(2)}) %collective-permute-start.57) | collective-permute-done | bytes 1048608 | tf_op jit(solution)/shard_map/ppermute | solution.py:62
  485.3 14.5 %collective-permute-done.58 = bf16[2,144,864]{2,1,0:T(8,128)(2,1)S(1)} collective-permute-done((bf16[2,144,864]{2,1,0:T(8,128)(2,1)S(1)}, bf16[2,144,864]{2,1,0:T(8,128)(2,1)S(1)}, u32[]{:S(2)}, u32[]{:S(2)}) %collective-permute-start.58) | collective-permute-done | bytes 497696 | tf_op jit(solution)/shard_map/ppermute | solution.py:62
  511.3 10.9 %collective-permute-done.62 = bf16[2,144,864]{2,1,0:T(8,128)(2,1)} collective-permute-done((bf16[2,144,864]{2,1,0:T(8,128)(2,1)}, bf16[2,144,864]{2,1,0:T(8,128)(2,1)}, u32[]{:S(2)}, u32[]{:S(2)}) %collective-permute-start.62) | collective-permute-done | bytes 497696 | tf_op jit(solution)/shard_map/ppermute | solution.py:62
  522.3 11.2 %collective-permute-done.60 = bf16[256,512]{1,0:T(8,128)(2,1)} collective-permute-done((bf16[256,512]{1,0:T(8,128)(2,1)}, bf16[256,512]{1,0:T(8,128)(2,1)}, u32[]{:S(2)}, u32[]{:S(2)}) %collective-permute-start.60) | collective-permute-done | bytes 262176 | tf_op jit(solution)/shard_map/ppermute | solution.py:62
  564.6 9.8 %collective-permute-done.73 = bf16[4,2,36,864]{3,0,2,1:T(4,128)(2,1)S(1)} collective-permute-done((bf16[4,2,36,864]{3,0,2,1:T(4,128)(2,1)S(1)}, bf16[4,2,36,864]{3,0,2,1:T(4,128)(2,1)S(1)}, u32[]{:S(2)}, u32[]{:S(2)}) %collective-permute-start.73) | collective-permute-done | bytes 497696 | tf_op jit(solution)/shard_map/ppermute | solution.py:62
  (543 shorter events, 335.9 us)
Async XLA Ops:
  7.2 181.6 %all-gather.2.cloned.1.call-start = ((), (), s32[]{:S(2)}) async-start(), calls=%async_computation.3 | async-start | bytes 2433024 | tf_op jit(solution)/shard_map/all_gather | solution.py:570
  81.2 36.0 %collective-permute-start.7 = (bf16[1,216,1152]{2,1,0:T(8,128)(2,1)}, bf16[1,216,1152]{2,1,0:T(8,128)(2,1)S(1)}, u32[]{:S(2)}, u32[]{:S(2)}) collective-permute-start(bf16[1,216,1152]{2,1,0:T(8,128)(2,1)} %bitcast.14.refs_0_), channel_id=1, source_target_pairs={{0,16},{4,20},{8,24},{12,28},{16,0},{20,4},{24,8},{28,12},{1,17},{... | collective-permute-start | bytes 1493000 | tf_op jit(solution)/shard_map/ppermute | solution.py:62
  83.7 33.6 %all-to-all-start = ((bf16[4,2,2,36,864]{4,2,3,1,0:T(2,128)(2,1)}), bf16[4,2,2,36,864]{4,2,3,1,0:T(2,128)(2,1)S(1)}, u32[]{:S(2)}, u32[]{:S(2)}) async-start(bf16[4,2,2,36,864]{4,2,3,1,0:T(2,128)(2,1)} %copy.75), calls=%async_computation | async-start | bytes 2064384 | tf_op jit(solution)/shard_map/all_to_all | solution.py:549
  87.2 521.2 %reduce-scatter.2.cloned.1.call-start = ((), (), s32[]{:S(2)}) async-start(), calls=%async_computation.4 | async-start | bytes 2433024 | tf_op jit(solution)/shard_map/reduce_scatter | solution.py:718
  95.0 38.6 %collective-permute-start.12 = (bf16[2,128,512]{2,1,0:T(8,128)(2,1)}, bf16[2,128,512]{2,1,0:T(8,128)(2,1)S(1)}, u32[]{:S(2)}, u32[]{:S(2)}) collective-permute-start(bf16[2,128,512]{2,1,0:T(8,128)(2,1)} %get-tuple-element.126), channel_id=1, source_target_pairs={{0,2},{1,3},{2,0},{3,1},{4,6},{5,7},{6,4},{7,5},{8,10},{9,11},{10,... | collective-permute-start | bytes 786440 | tf_op jit(solution)/shard_map/ppermute | solution.py:62
  97.0 29.2 %collective-permute-start.10 = (bf16[2,128,512]{2,1,0:T(8,128)(2,1)}, bf16[2,128,512]{2,1,0:T(8,128)(2,1)S(1)}, u32[]{:S(2)}, u32[]{:S(2)}) collective-permute-start(bf16[2,128,512]{2,1,0:T(8,128)(2,1)} %get-tuple-element.126), channel_id=1, source_target_pairs={{0,24},{4,28},{8,16},{12,20},{16,8},{20,12},{24,0},{28,4},{1,25},{... | collective-permute-start | bytes 786440 | tf_op jit(solution)/shard_map/ppermute | solution.py:62
  97.5 34.0 %collective-permute-start.9 = (bf16[2,128,512]{2,1,0:T(8,128)(2,1)}, bf16[2,128,512]{2,1,0:T(8,128)(2,1)S(1)}, u32[]{:S(2)}, u32[]{:S(2)}) collective-permute-start(bf16[2,128,512]{2,1,0:T(8,128)(2,1)} %get-tuple-element.126), channel_id=1, source_target_pairs={{0,16},{4,20},{8,24},{12,28},{16,0},{20,4},{24,8},{28,12},{1,17},{... | collective-permute-start | bytes 786440 | tf_op jit(solution)/shard_map/ppermute | solution.py:62
  99.9 31.6 %collective-permute-start.8 = (bf16[2,128,512]{2,1,0:T(8,128)(2,1)}, bf16[2,128,512]{2,1,0:T(8,128)(2,1)S(1)}, u32[]{:S(2)}, u32[]{:S(2)}) collective-permute-start(bf16[2,128,512]{2,1,0:T(8,128)(2,1)} %get-tuple-element.126), channel_id=1, source_target_pairs={{0,8},{4,12},{8,0},{12,4},{16,24},{20,28},{24,16},{28,20},{1,9},{5... | collective-permute-start | bytes 786440 | tf_op jit(solution)/shard_map/ppermute | solution.py:62
  135.3 28.4 %collective-permute-start.11 = (bf16[2,144,864]{2,1,0:T(8,128)(2,1)S(1)}, bf16[2,144,864]{2,1,0:T(8,128)(2,1)}, u32[]{:S(2)}, u32[]{:S(2)}) collective-permute-start(bf16[2,144,864]{2,1,0:T(8,128)(2,1)S(1)} %copy-done.42), channel_id=1, source_target_pairs={{0,16},{4,20},{8,24},{12,28},{16,0},{20,4},{24,8},{28,12},{1,17},{... | collective-permute-start | bytes 1493000 | tf_op jit(solution)/shard_map/ppermute | solution.py:62
  163.7 25.1 %collective-permute-start.22 = (bf16[2,144,864]{2,1,0:T(8,128)(2,1)}, bf16[2,144,864]{2,1,0:T(8,128)(2,1)}, u32[]{:S(2)}, u32[]{:S(2)}) collective-permute-start(bf16[2,144,864]{2,1,0:T(8,128)(2,1)} %get-tuple-element.151.refs_0_), channel_id=1, source_target_pairs={{0,16},{4,20},{8,24},{12,28},{16,0},{20,4},{24,8},{28,12},{1,17},{... | collective-permute-start | bytes 1493000 | tf_op jit(solution)/shard_map/ppermute | solution.py:62
  194.4 29.1 %collective-permute-start.24 = (bf16[256,1152]{1,0:T(8,128)(2,1)}, bf16[256,1152]{1,0:T(8,128)(2,1)S(1)}, u32[]{:S(2)}, u32[]{:S(2)}) collective-permute-start(bf16[256,1152]{1,0:T(8,128)(2,1)} %get-tuple-element.227), channel_id=1, source_target_pairs={{0,8},{4,12},{8,0},{12,4},{16,24},{20,28},{24,16},{28,20},{1,9},{5... | collective-permute-start | bytes 1769480 | tf_op jit(solution)/shard_map/ppermute | solution.py:62
  196.2 28.7 %collective-permute-start.23 = (bf16[256,1152]{1,0:T(8,128)(2,1)}, bf16[256,1152]{1,0:T(8,128)(2,1)S(1)}, u32[]{:S(2)}, u32[]{:S(2)}) collective-permute-start(bf16[256,1152]{1,0:T(8,128)(2,1)} %get-tuple-element.227), channel_id=1, source_target_pairs={{0,2},{1,3},{2,0},{3,1},{4,6},{5,7},{6,4},{7,5},{8,10},{9,11},{10,... | collective-permute-start | bytes 1769480 | tf_op jit(solution)/shard_map/ppermute | solution.py:62
  271.4 25.8 %collective-permute-start.38 = (bf16[128,1152]{1,0:T(8,128)(2,1)}, bf16[128,1152]{1,0:T(8,128)(2,1)S(1)}, u32[]{:S(2)}, u32[]{:S(2)}) collective-permute-start(bf16[128,1152]{1,0:T(8,128)(2,1)} %get-tuple-element.274), channel_id=1, source_target_pairs={{0,4},{4,0},{8,12},{12,8},{16,20},{20,16},{24,28},{28,24},{1,5},{5... | collective-permute-start | bytes 884744 | tf_op jit(solution)/shard_map/ppermute | solution.py:62
  358.1 31.1 %collective-permute-start.46 = (bf16[1024,1152]{1,0:T(8,128)(2,1)S(1)}, bf16[1024,1152]{1,0:T(8,128)(2,1)S(1)}, u32[]{:S(2)}, u32[]{:S(2)}) collective-permute-start(bf16[1024,1152]{1,0:T(8,128)(2,1)S(1)} %slice.262), channel_id=1, source_target_pairs={{0,1},{1,0},{2,3},{3,2},{4,5},{5,4},{6,7},{7,6},{8,9},{9,8},{10,11... | collective-permute-start | bytes 7077896 | tf_op jit(solution)/shard_map/ppermute | solution.py:62
  372.8 73.4 %collective-permute-start.52 = (bf16[2,2,144,864]{3,2,1,0:T(8,128)(2,1)}, bf16[2,2,144,864]{3,2,1,0:T(8,128)(2,1)}, u32[]{:S(2)}, u32[]{:S(2)}) collective-permute-start(bf16[2,2,144,864]{3,2,1,0:T(8,128)(2,1)} %get-tuple-element.252), channel_id=1, source_target_pairs={{0,4},{4,0},{8,12},{12,8},{16,20},{20,16},{24,28},{28,24},{1,5},{5... | collective-permute-start | bytes 2985992 | tf_op jit(solution)/shard_map/ppermute | solution.py:62
  401.4 44.8 %collective-permute-start.54 = (bf16[1,216,1152]{2,1,0:T(8,128)(2,1)}, bf16[1,216,1152]{2,1,0:T(8,128)(2,1)}, u32[]{:S(2)}, u32[]{:S(2)}) collective-permute-start(bf16[1,216,1152]{2,1,0:T(8,128)(2,1)} %get-tuple-element.269), channel_id=1, source_target_pairs={{0,16},{4,20},{8,24},{12,28},{16,0},{20,4},{24,8},{28,12},{1,17},{... | collective-permute-start | bytes 1493000 | tf_op jit(solution)/shard_map/ppermute | solution.py:62
  404.5 41.7 %collective-permute-start.53 = (bf16[2,2,144,864]{3,2,1,0:T(8,128)(2,1)}, bf16[2,2,144,864]{3,2,1,0:T(8,128)(2,1)}, u32[]{:S(2)}, u32[]{:S(2)}) collective-permute-start(bf16[2,2,144,864]{3,2,1,0:T(8,128)(2,1)} %get-tuple-element.250), channel_id=1, source_target_pairs={{0,4},{4,0},{8,12},{12,8},{16,20},{20,16},{24,28},{28,24},{1,5},{5... | collective-permute-start | bytes 2985992 | tf_op jit(solution)/shard_map/ppermute | solution.py:62
  455.3 25.5 %collective-permute-start.57 = (bf16[4,256,512]{2,1,0:T(8,128)(2,1)}, bf16[4,256,512]{2,1,0:T(8,128)(2,1)}, u32[]{:S(2)}, u32[]{:S(2)}) collective-permute-start(bf16[4,256,512]{2,1,0:T(8,128)(2,1)} %bitcast.147), channel_id=1, source_target_pairs={{0,2},{1,3},{2,0},{3,1},{4,6},{5,7},{6,4},{7,5},{8,10},{9,11},{10,... | collective-permute-start | bytes 3145736 | tf_op jit(solution)/shard_map/ppermute | solution.py:62
  458.8 46.4 %collective-permute-start.37 = (bf16[128,1152]{1,0:T(8,128)(2,1)}, bf16[128,1152]{1,0:T(8,128)(2,1)S(1)}, u32[]{:S(2)}, u32[]{:S(2)}) collective-permute-start(bf16[128,1152]{1,0:T(8,128)(2,1)} %get-tuple-element.275), channel_id=1, source_target_pairs={{0,4},{4,0},{8,12},{12,8},{16,20},{20,16},{24,28},{28,24},{1,5},{5... | collective-permute-start | bytes 884744 | tf_op jit(solution)/shard_map/ppermute | solution.py:62
  463.9 35.9 %collective-permute-start.58 = (bf16[2,144,864]{2,1,0:T(8,128)(2,1)S(1)}, bf16[2,144,864]{2,1,0:T(8,128)(2,1)S(1)}, u32[]{:S(2)}, u32[]{:S(2)}) collective-permute-start(bf16[2,144,864]{2,1,0:T(8,128)(2,1)S(1)} %get-tuple-element.267), channel_id=1, source_target_pairs={{0,16},{4,20},{8,24},{12,28},{16,0},{20,4},{24,8},{28,12},{1,17},{... | collective-permute-start | bytes 1493000 | tf_op jit(solution)/shard_map/ppermute | solution.py:62
  466.6 55.7 %collective-permute-start.62 = (bf16[2,144,864]{2,1,0:T(8,128)(2,1)}, bf16[2,144,864]{2,1,0:T(8,128)(2,1)}, u32[]{:S(2)}, u32[]{:S(2)}) collective-permute-start(bf16[2,144,864]{2,1,0:T(8,128)(2,1)} %get-tuple-element.265), channel_id=1, source_target_pairs={{0,16},{4,20},{8,24},{12,28},{16,0},{20,4},{24,8},{28,12},{1,17},{... | collective-permute-start | bytes 1493000 | tf_op jit(solution)/shard_map/ppermute | solution.py:62
  503.1 30.3 %collective-permute-start.60 = (bf16[256,512]{1,0:T(8,128)(2,1)}, bf16[256,512]{1,0:T(8,128)(2,1)}, u32[]{:S(2)}, u32[]{:S(2)}) collective-permute-start(bf16[256,512]{1,0:T(8,128)(2,1)} %get-tuple-element.262), channel_id=1, source_target_pairs={{0,16},{4,20},{8,24},{12,28},{16,0},{20,4},{24,8},{28,12},{1,17},{... | collective-permute-start | bytes 786440 | tf_op jit(solution)/shard_map/ppermute | solution.py:62
  503.1 30.3 %collective-permute-start.59 = (bf16[256,512]{1,0:T(8,128)(2,1)}, bf16[256,512]{1,0:T(8,128)(2,1)}, u32[]{:S(2)}, u32[]{:S(2)}) collective-permute-start(bf16[256,512]{1,0:T(8,128)(2,1)} %get-tuple-element.263), channel_id=1, source_target_pairs={{0,8},{4,12},{8,0},{12,4},{16,24},{20,28},{24,16},{28,20},{1,9},{5... | collective-permute-start | bytes 786440 | tf_op jit(solution)/shard_map/ppermute | solution.py:62
  509.3 53.1 %collective-permute-start.64 = (bf16[8,40,1024]{2,1,0:T(8,128)(2,1)}, bf16[8,40,1024]{2,1,0:T(8,128)(2,1)}, u32[]{:S(2)}, u32[]{:S(2)}) collective-permute-start(bf16[8,40,1024]{2,1,0:T(8,128)(2,1)} %slice.284), channel_id=1, source_target_pairs={{0,2},{1,3},{2,0},{3,1},{4,6},{5,7},{6,4},{7,5},{8,10},{9,11},{10,... | collective-permute-start | bytes 1966088 | tf_op jit(solution)/shard_map/ppermute | solution.py:68
  (146 other events, 1751.1 us)
Sparse Core Ops, SparseCore 0:
  77.9 78.3 all-gather.1
  507.8 100.3 reduce-scatter.1

commit v7 on v6

--- a/solution.py
+++ b/solution.py
@@ -104,12 +104,6 @@
     got = xor_both(total[half:], dp_mask, seq_mask)
     total = total[:half].astype(f32) + got.astype(f32)
     return total if half == 1 else total.astype(bf16)
-
-
-def scatter_rest(total):
-    for masks in list(reversed(all_masks()))[1:]:
-        total = scatter_step(total, *masks)
-    return total[0]
 
 
 def gather_group(rows):
@@ -224,7 +218,7 @@
         grid=(1,),
         in_specs=[
             whole_of(picked),
-            pl.BlockSpec((deep, 2 * HEAD), lambda i: (0, HEADS // 2)),
+            whole_of(weight),
             whole_of(gain),
             whole_of(cosine),
             whole_of(sine),
@@ -548,26 +542,26 @@
     def swap_members(parts):
         return lax.all_to_all(parts, "seq", split_axis=0, concat_axis=0, tiled=True)
 
-    gain_line, at = jnp.zeros((1, wide_q + 2 * HEAD), f32), 0
+    gain_line, at = jnp.zeros((1, 2 * HEAD), f32), 0
     for gain in (gain_attn_pre, gain_attn_post, gain_ffw_pre, gain_ffw_post, gain_query, gain_key):
         gain_line += jnp.pad(gain.astype(f32)[None, :], ((0, 0), (at, gain_line.shape[1] - at - gain.shape[0])))
         at += gain.shape[0]
-    shard = jnp.concatenate([w_query, w_key, w_value], axis=1)
-    shard = jnp.concatenate([shard, gain_line.astype(bf16)], axis=0)
+    shard = jnp.concatenate([jnp.concatenate([w_key, w_value], axis=1), gain_line.astype(bf16)], axis=0)
     blocks = jnp.pad(shard, ((0, block_rows - model_rows - 1), (0, 0)))[None]
+    q_blocks = jnp.pad(w_query, ((0, block_rows - model_rows), (0, 0)))[None]
     packed = pack(w_gate, w_up, tops, members, ff_rows)
-    *row_masks, y_mask, x_mask, core_mask = all_masks()
-    for masks in row_masks:
-        blocks = gather_step(blocks, *masks)
+    first_mask, *more_masks, x_mask, core_mask = all_masks()
+    blocks = gather_step(blocks, *first_mask)
+    last_mask = first_mask
+    for masks in [*more_masks, x_mask]:
+        blocks, q_blocks = together(gather_step(blocks, *masks), gather_step(q_blocks, *last_mask))
+        last_mask = masks
     blocks, packed, down_piece, rows_low = together(blocks, packed, w_down[None], regroup(inputs))
     rows_in = rows_low.astype(f32)
     column_parts = column_exchange(packed)
-    blocks = gather_step(gather_step(blocks, *y_mask), *x_mask)
-    blocks, column_parts = together(blocks, column_parts)
+    q_blocks = gather_step(q_blocks, *x_mask)
     blocks = gather_step(blocks, *core_mask)
-    blocks, late_out = together(blocks, w_out)
-    qkv_weight = blocks.reshape(devices * block_rows, wide_q + 2 * HEAD)
-    out_weight = lax.all_gather(late_out, ALL, axis=0, tiled=True)
+    kv_weight = blocks.reshape(devices * block_rows, 2 * HEAD)
     labels = all_labels()
     natural = jnp.stack([(dp_id ^ d) * members + (seq_id ^ s) for d, s in labels]).astype(jnp.int32)
 
@@ -578,6 +572,7 @@
 
     model_pick = selection(natural, width, model_rows, block_rows)
     device_pick = selection(natural, devices, 1, 1)
+    out_pick = selection(natural, wide_q, out_rows, out_rows)
     gain_blocks = blocks[:, model_rows, :gain_total]
     gain_all = mm(device_pick, gain_blocks)
     full_gain, at = [], 0
@@ -598,8 +593,8 @@
     owners = jnp.stack(owners).astype(jnp.int32)
     sources = [((top_id ^ k) * 2 + (z_bit ^ v)) * 2 + (y_bit ^ u) for u in range(2) for k in range(tops) for v in range(2)]
     sources = jnp.stack(sources).astype(jnp.int32)
+
     down_tall = from_tops(down_piece)
-    halves = swap_members(column_parts)
 
     seq_ends = jnp.cumsum(lax.dynamic_index_in_dim(lengths, y_bit, 0, keepdims=False))
     dealt = lax.dynamic_index_in_dim(deal, y_bit, 0, keepdims=False)
@@ -629,24 +624,27 @@
     scale_one = norm_scale(rows_in)
     normed_one = (rows_in * scale_one * pre_attention).astype(bf16)
     picked_one = mm(normed_one, model_pick).astype(bf16)
-    key_raw, keys_mine = project_keys(picked_one, qkv_weight, key_gain[None], cosine, sine)
-    key_raw, down_tall, halves = together(key_raw, down_tall, halves)
-    halves = merge(halves)
+    key_raw, keys_mine = project_keys(picked_one, kv_weight, key_gain[None], cosine, sine)
     column = [keys_mine] + [xor(keys_mine, "dp", 2 * k) for k in range(1, layers)]
-    halves, others = together(halves, column[1:])
+    column[1], down_tall, column_parts, late_out = together(column[1], down_tall, column_parts, w_out)
+    out_weight = lax.all_gather(late_out, ALL, axis=0, tiled=True)
+    halves = merge(swap_members(column_parts))
+    halves, others, q_blocks = together(halves, column[1:], q_blocks)
+    q_weight = gather_step(q_blocks, *core_mask).reshape(devices * block_rows, wide_q)
     column = [column[0], *others]
     gate_tall, up_half = together(from_tops(halves[0]), halves[1])
     up_tall = from_tops(up_half)
     across = [xor(part, "seq", 2) for part in column]
-    across, down_pieces = lax.optimization_barrier((across, both_sides(down_tall)))
+    down_pieces = both_sides(down_tall)
     column, across = jnp.stack(column), jnp.stack(across)
     near_keys = jnp.concatenate([column, across])
     far_keys = jnp.concatenate([xor(column, "seq", 1), xor(across, "seq", 1)])
-    query_raw, query_heads = project(picked_one, qkv_weight, query_gain[None], cosine, sine)
+    query_raw, query_heads = project(picked_one, q_weight, query_gain[None], cosine, sine)
     query_heads, gate_tall = together(query_heads, gate_tall)
     gate_pieces = both_sides(gate_tall)
     context_rows, turned, lse = attend(meta, seq_ends, slots, query_heads, near_keys, far_keys)
-    context_rows, gate_pieces, up_tall = together(context_rows, gate_pieces, up_tall)
+    context_rows, gate_pieces, up_tall, down_pieces = together(context_rows, gate_pieces, up_tall, down_pieces)
+    picked_context = mm(context_rows, out_pick).astype(bf16)
     up_pieces = both_sides(up_tall)
     down_weight = place(down_pieces, owners).reshape(ff_local, width)
     gate_weight, up_weight = [place(pieces, sources).reshape(width, ff_local) for pieces in (gate_pieces, up_pieces)]
@@ -661,7 +659,8 @@
     up_raw = mm(normed_group, up_weight)
     hidden_low = (jax.nn.gelu(gate_raw, approximate=True) * up_raw).astype(bf16)
     mixed = scatter_group(mm(hidden_low, down_weight).astype(bf16))
-    natural_weight, mixed = together(mm(model_pick, qkv_weight).astype(bf16), mixed)
+    q_natural, kv_natural = mm(model_pick, q_weight).astype(bf16), mm(model_pick, kv_weight).astype(bf16)
+    q_natural, kv_natural, picked_context, mixed = together(q_natural, kv_natural, picked_context, mixed)
     scale_four = norm_scale(mixed)
     result = hidden_res + mixed * scale_four * post_feed
     output = ungroup(jnp.where(valid, result, 0.0).astype(bf16))
@@ -709,29 +708,34 @@
 
     grad_post_attention = jnp.sum(hidden_res_grad * attended * scale_two, axis=0)
     attended_grad = norm_back(attended, scale_two, post_attention * hidden_res_grad).astype(bf16)
-    out_total = mm_tn(context_rows, attended_grad).astype(bf16)
+    out_total = mm_tn(picked_context, attended_grad).astype(bf16).reshape(devices, out_rows, width)
     attended_grad, out_total, gate_kept, up_kept = lax.optimization_barrier(
         (attended_grad, out_total, gate_halves[0], up_halves[0])
     )
     gate_halves, up_halves = (gate_kept, gate_halves[1]), (up_kept, up_halves[1])
     down_parts = send_tops(by_top(*down_halves))
-    grad_out = lax.psum_scatter(out_total, ALL, scatter_dimension=0, tiled=True)
     context_grad = mm_nt(attended_grad, out_weight).astype(bf16)
+    out_total, context_grad, gate_halves = together(scatter_step(out_total, *core_mask), context_grad, gate_halves)
+    gate_parts = send_tops(by_top(*gate_halves))
+    out_total = scatter_step(out_total, *x_mask)
     query_grad, grad_query_gain, near_part, far_part = attend_back(
         meta, seq_ends, slots, query_heads, context_grad, lse, turned, query_raw, query_gain[None], cosine, sine, near_keys, far_keys
     )
-    far_part, near_part, gate_halves, up_halves, down_parts = lax.optimization_barrier(
-        (far_part, near_part, gate_halves, up_halves, down_parts)
-    )
-    gate_parts, up_parts = [send_tops(by_top(*half)) for half in (gate_halves, up_halves)]
+    far_part, near_part, up_halves, down_parts, out_total = together(far_part, near_part, up_halves, down_parts, out_total)
     far_part = xor(far_part, "seq", 1)
-    query_low, far_part = together(query_grad, far_part)
+    query_low, far_part, up_tops = together(query_grad, far_part, by_top(*up_halves))
+    up_parts = send_tops(up_tops)
+    for masks in reversed([first_mask, *more_masks]):
+        out_total = scatter_step(out_total, *masks)
     near_part = add16(near_part, far_part).reshape(2, layers, count, 2 * HEAD)
     near_part = add16(near_part[0], xor(near_part[1], "seq", 2))
     grad_query = mm_tn(picked_one, query_low).astype(bf16).reshape(devices, block_rows, wide_q)
     grad_query, near_part, gate_parts = together(scatter_step(grad_query, *core_mask), near_part, gate_parts)
-    grad_query = scatter_rest(grad_query)
+    for masks in reversed([first_mask, *more_masks, x_mask]):
+        grad_query = scatter_step(grad_query, *masks)
+    grad_query = grad_query[0]
     key_parts = [near_part[k] if k == 0 else xor(near_part[k], "dp", 2 * k) for k in range(layers)]
+    grad_out = out_total[0]
     key_parts, up_parts = together(key_parts, up_parts)
     key_grads = functools.reduce(jnp.add, [part.astype(f32) for part in key_parts])
     value_grad = key_grads[:, HEAD:].astype(bf16)
@@ -740,13 +744,12 @@
     grad_key_gain = jnp.sum(key_turned * key_raw * key_scale, axis=0)
     key_grad = norm_back(key_raw, key_scale, key_gain * key_turned).astype(bf16)
     kv_grad = jnp.concatenate([key_grad, value_grad], axis=1)
-    normed_one_grad = mm_nt(query_grad, natural_weight[:, :wide_q]) + mm_nt(kv_grad, natural_weight[:, wide_q:])
+    normed_one_grad = mm_nt(query_grad, q_natural) + mm_nt(kv_grad, kv_natural)
     grad_pre_attention = jnp.sum(normed_one_grad * rows_in * scale_one, axis=0)
     rows_grad = hidden_res_grad + norm_back(rows_in, scale_one, pre_attention * normed_one_grad)
     rows_low, down_parts, gate_parts, up_parts = together(rows_grad.astype(bf16), down_parts, gate_parts, up_parts)
     grad_down = total_of(down_parts)[0]
     both_grads = split(total_of(gate_parts).astype(bf16), total_of(up_parts).astype(bf16), members)
-    grad_gate, grad_up = unpack(swap_members(column_exchange(both_grads)), z_bit, tops, members, ff_rows)
     input_grad = ungroup(rows_low)
     grad_kv = mm_tn(picked_one, kv_grad).reshape(devices, block_rows, 2 * HEAD)
     gain_grads = [
@@ -762,9 +765,13 @@
     gain_grads = jnp.pad(
         gain_grads[:, None, :], ((0, 0), (model_rows, block_rows - model_rows - 1), (0, 2 * HEAD - gain_total))
     )
-    last = scatter_rest(scatter_step((grad_kv + gain_grads).astype(bf16), *core_mask))
-    last, grad_out = together(last, grad_out)
-    grad_out = grad_out.astype(f32)
+    last = scatter_step((grad_kv + gain_grads).astype(bf16), *core_mask)
+    last, column_parts = together(scatter_step(last, *x_mask), column_exchange(both_grads))
+    for masks in reversed(more_masks):
+        last = scatter_step(last, *masks)
+    last, column_parts = together(last, swap_members(column_parts))
+    grad_gate, grad_up = unpack(column_parts, z_bit, tops, members, ff_rows)
+    last = scatter_step(last, *first_mask)[0]
     gain_out, at = [], 0
     for size in gain_sizes:
         gain_out.append(last[model_rows, at : at + size])

time: 630 us -> 652 us (1.035)
  starting transfers between devices: 77 us -> 88.6 us
  local copies, waits for them, and re-layouts: 59.1 us -> 67.4 us
  waiting for transfers between devices: 256 us -> 264 us
    all_to_all x2, waiting for transfers between devices: 0.01 us -> 8.53 us  [swap_members(): return lax.all_to_all(parts, 'seq', split_axis=0, concat_axis=0, tiled=True)]
    ppermute x59, waiting for transfers between devices: 216 us -> 209 us  [xor(): lax.ppermute(value, axis, [(i, i ^ mask) for i in range(lax.axis_size(axi...]
    ppermute x15 -> x25, starting transfers between devices: 19.2 us -> 26 us  [xor_both(): lax.ppermute(value, ALL, [(i, i ^ mask) for i in range(lax.axis_size('dp'...]
    ppermute x15 -> x25, waiting for transfers between devices: 40.5 us -> 46.1 us  [xor_both(): lax.ppermute(value, ALL, [(i, i ^ mask) for i in range(lax.axis_size('dp'...]
    unnamed x206 -> x229, local copies, waits for them, and re-layouts: 17.6 us -> 21.4 us
    dot_general x20 -> x22, matrix products: 89.3 us -> 87.2 us  [dot(): lax.dot_general(left, right, (dims, ((), ())), preferred_element_type=f32)]
  transfers between devices with their start and end apart: 78 -> 87, of which waited for: 39 -> 43; matrix products, arithmetic and copies ran while one was open for 20% -> 21% of each run, Pallas kernels for 9% -> 9%
where the time goes in v7:
time: 652 us; the launch traced here: 643 us
  waiting for transfers between devices  264 us (40%)
  starting transfers between devices  88.6 us (14%)
  matrix products  87.2 us (13%)
  local copies, waits for them, and re-layouts  67.4 us (10%)
  other arithmetic  61.7 us (9%)
  Pallas kernels  58.3 us (9%)
  between operations  16.1 us (2%)
    ppermute x59, waiting for transfers between devices, xor(): lax.ppermute(value, axis, [(i, i ^ mask) for i in range(lax.axis_size(axi...  209 us
    dot_general x22, matrix products, dot(): lax.dot_general(left, right, (dims, ((), ())), preferred_element_type=f32)  87.2 us
    ppermute x59, starting transfers between devices, xor(): lax.ppermute(value, axis, [(i, i ^ mask) for i in range(lax.axis_size(axi...  55 us
    ppermute x25, waiting for transfers between devices, xor_both(): lax.ppermute(value, ALL, [(i, i ^ mask) for i in range(lax.axis_size('dp'...  46.1 us
    ppermute x25, starting transfers between devices, xor_both(): lax.ppermute(value, ALL, [(i, i ^ mask) for i in range(lax.axis_size('dp'...  26 us
    unnamed x229, local copies, waits for them, and re-layouts  21.4 us
    pallas_call x1, Pallas kernels, attend_back(): pl.pallas_call(functools.partial(attend_back_kernel, rows), grid_spec=plt...  17.6 us
    convert_element_type x9, other arithmetic, add16(): return (left.astype(f32) + right.astype(f32)).astype(bf16)  13.7 us
  transfers between devices with their start and end apart: 87, of which 43 were waited for; matrix products, arithmetic and copies ran while one was open for 21% of the time, Pallas kernels for 9%

profile of v7, /device:TPU:0, one launch (start us, length us, event | category | flops | bytes accessed | tf_op | source)
XLA Modules:
  0.0 643.0 jit_solution(13786741767348766231)
XLA Ops:
  58.7 12.5 %collective-permute-done.11 = bf16[4,2,36,864]{3,0,2,1:T(4,128)(2,1)} collective-permute-done((bf16[4,2,36,864]{3,0,2,1:T(4,128)(2,1)}, bf16[4,2,36,864]{3,0,2,1:T(4,128)(2,1)}, u32[]{:S(2)}, u32[]{:S(2)}) %collective-permute-start.11) | collective-permute-done | bytes 497696 | tf_op jit(solution)/shard_map/ppermute | solution.py:62
  97.8 8.0 %all-to-all-done = bf16[4,2,2,36,864]{4,2,3,1,0:T(2,128)(2,1)S(1)} async-done(((bf16[4,2,2,36,864]{4,2,3,1,0:T(2,128)(2,1)}), bf16[4,2,2,36,864]{4,2,3,1,0:T(2,128)(2,1)S(1)}, u32[]{:S(2)}, u32[]{:S(2)}) %all-to-all-start) | async-done | bytes 995360 | tf_op jit(solution)/shard_map/all_to_all | solution.py:543
  127.7 6.4 collective-permute-done.20
  140.0 14.3 %collective-permute-done.16.refs_1_ = bf16[2,144,864]{2,1,0:T(8,128)(2,1)} collective-permute-done((bf16[2,144,864]{2,1,0:T(8,128)(2,1)S(1)}, bf16[2,144,864]{2,1,0:T(8,128)(2,1)}, u32[]{:S(2)}, u32[]{:S(2)}) %collective-permute-start.16) | collective-permute-done | bytes 497696 | tf_op jit(solution)/shard_map/ppermute | solution.py:62
  167.3 13.4 %attend.1 = (bf16[256,1024]{1,0:T(8,128)(2,1)}, f32[2,256,512]{2,1,0:T(8,128)}, f32[2,1,512]{2,1,0:T(1,128)}) custom-call(s32[7]{0:T(128)} %pad_add_fusion.1.meta_ref, s32[4]{0:T(128)} %bitcast.328, s32[16]{0:T(128)} %gather_fusion.1, bf16[2,4,128,256]{3,2,1,0:T(8,128)(2,1)} %get-tuple-element.144.q_ref, ...), custom_call_target="tpu_custom_call" | custom-call | flops 2415919104 | bytes 4194304 | tf_op jit(solution)/shard_map/attend/pallas_call | solution.py:383
  180.8 9.2 %collective-permute-done.24.refs_3_ = bf16[2,144,864]{2,1,0:T(8,128)(2,1)} collective-permute-done((bf16[2,144,864]{2,1,0:T(8,128)(2,1)}, bf16[2,144,864]{2,1,0:T(8,128)(2,1)}, u32[]{:S(2)}, u32[]{:S(2)}) %collective-permute-start.24) | collective-permute-done | bytes 497696 | tf_op jit(solution)/shard_map/ppermute | solution.py:62
  211.8 9.0 %collective-permute-done.36.refs_3_ = bf16[2,144,864]{2,1,0:T(8,128)(2,1)} collective-permute-done((bf16[2,144,864]{2,1,0:T(8,128)(2,1)}, bf16[2,144,864]{2,1,0:T(8,128)(2,1)}, u32[]{:S(2)}, u32[]{:S(2)}) %collective-permute-start.36) | collective-permute-done | bytes 497696 | tf_op jit(solution)/shard_map/ppermute | solution.py:62
  238.7 7.0 %fusion.69 = f32[2048,864]{0,1:T(8,128)S(1)} fusion(bf16[2048,1152]{1,0:T(8,128)(2,1)} %constant_dynamic-update-slice_fusion.12, bf16[1152,864]{1,0:T(8,128)(2,1)S(1)} %bitcast.292), kind=kOutput, calls=%fused_computation.295 | convolution fusion | flops 4076863488 | bytes 13787136 | tf_op jit(solution)/shard_map/dot_general | solution.py:46
  245.7 8.9 %multiply_convert_fusion.1 = (bf16[2048,864]{0,1:T(8,128)(2,1)S(1)}, f32[2048,864]{0,1:T(8,128)}) fusion(f32[2048,864]{0,1:T(8,128)S(1)} %fusion.69, bf16[2048,1152]{1,0:T(8,128)(2,1)S(1)} %copy-done.59, bf16[1152,864]{1,0:T(8,128)(2,1)S(1)} %bitcast.294), kind=kOutput, calls=%fused_computation.14 | convolution fusion | flops 4094558208 | bytes 24403968 | tf_op jit(solution)/shard_map/dot_general | solution.py:46
  254.6 5.9 convolution_convert_fusion
  291.1 6.8 %collective-permute-done.41 = bf16[256,1152]{1,0:T(8,128)(2,1)S(1)} collective-permute-done((bf16[256,1152]{1,0:T(8,128)(2,1)S(1)}, bf16[256,1152]{1,0:T(8,128)(2,1)S(1)}, u32[]{:S(2)}, u32[]{:S(2)}) %collective-permute-start.41) | collective-permute-done | bytes 589856 | tf_op jit(solution)/shard_map/ppermute | solution.py:62
  304.0 10.8 %collective-permute-done.45 = bf16[256,1152]{1,0:T(8,128)(2,1)S(1)} collective-permute-done((bf16[256,1152]{1,0:T(8,128)(2,1)S(1)}, bf16[256,1152]{1,0:T(8,128)(2,1)S(1)}, u32[]{:S(2)}, u32[]{:S(2)}) %collective-permute-start.45) | collective-permute-done | bytes 589856 | tf_op jit(solution)/shard_map/ppermute | solution.py:62
  325.7 12.5 %multiply_convert_fusion = (bf16[2048,864]{0,1:T(8,128)(2,1)}, bf16[2048,864]{0,1:T(8,128)(2,1)S(1)}) fusion(f32[2048,864]{0,1:T(8,128)S(1)} %bitcast.331, f32[2048,864]{0,1:T(8,128)} %get-tuple-element.332, bf16[2048,1152]{1,0:T(8,128)(2,1)S(1)} %constant_dynamic-update-slice_fusion.20, bf16[864,1152]{1,0:T(8,128)(2,1)S(1)} %bitcast.303), kind=kOutput, calls=%fused_computation.13 | convolution fusion | flops 4119330816 | bytes 27942912 | tf_op jit(solution)/shard_map/dot_general | solution.py:46
  338.1 8.0 %fusion.70 = f32[2048,1152]{1,0:T(8,128)} fusion(bf16[2048,864]{0,1:T(8,128)(2,1)S(1)} %get-tuple-element.173, bf16[1152,864]{1,0:T(8,128)(2,1)S(1)} %bitcast.293), kind=kOutput, calls=%fused_computation.296 | convolution fusion | flops 4076863488 | bytes 14966784 | tf_op jit(solution)/shard_map/dot_general | solution.py:46
  346.1 8.2 %add_convert_fusion = bf16[2048,1152]{1,0:T(8,128)(2,1)S(1)} fusion(f32[2048,1152]{1,0:T(8,128)} %fusion.70, bf16[2048,864]{0,1:T(8,128)(2,1)S(1)} %copy-done.98, bf16[1152,864]{1,0:T(8,128)(2,1)S(1)} %bitcast.295), kind=kOutput, calls=%fused_computation.4 | convolution fusion | flops 4081582080 | bytes 19685376 | tf_op jit(solution)/shard_map/dot_general | solution.py:46
  372.4 14.3 %collective-permute-done.56 = bf16[2,1,216,1152]{3,2,1,0:T(8,128)(2,1)S(1)} collective-permute-done((bf16[2,1,216,1152]{3,2,1,0:T(8,128)(2,1)S(1)}, bf16[2,1,216,1152]{3,2,1,0:T(8,128)(2,1)S(1)}, u32[]{:S(2)}, u32[]{:S(2)}) %collective-permute-start.56) | collective-permute-done | bytes 995360 | tf_op jit(solution)/shard_map/ppermute | solution.py:62
  413.3 19.6 %collective-permute-done.58 = bf16[2,2,144,864]{3,2,1,0:T(8,128)(2,1)S(1)} collective-permute-done((bf16[2,2,144,864]{3,2,1,0:T(8,128)(2,1)}, bf16[2,2,144,864]{3,2,1,0:T(8,128)(2,1)S(1)}, u32[]{:S(2)}, u32[]{:S(2)}) %collective-permute-start.58) | collective-permute-done | bytes 995360 | tf_op jit(solution)/shard_map/ppermute | solution.py:62
  438.1 17.6 %attend_back.1 = (bf16[256,1024]{1,0:T(8,128)(2,1)}, f32[1,256]{1,0:T(1,128)}, bf16[8,2,128,512]{3,2,1,0:T(8,128)(2,1)}, bf16[8,2,128,512]{3,2,1,0:T(8,128)(2,1)}) custom-call(s32[7]{0:T(128)} %pad_add_fusion.1.meta_ref, s32[4]{0:T(128)} %bitcast.329, s32[16]{0:T(128)} %gather_fusion.1, bf16[2,4,128,256]{3,2,1,0:T(8,128)(2,1)} %get-tuple-element.144.q_ref, ...), custom_call_target="tpu_custom_call" | custom-call | flops 6039797760 | bytes 8388608 | tf_op jit(solution)/shard_map/attend_back/pallas_call | solution.py:412
  465.7 7.2 %collective-permute-done.42 = bf16[128,1152]{1,0:T(8,128)(2,1)S(1)} collective-permute-done((bf16[128,1152]{1,0:T(8,128)(2,1)S(1)}, bf16[128,1152]{1,0:T(8,128)(2,1)S(1)}, u32[]{:S(2)}, u32[]{:S(2)}) %collective-permute-start.42) | collective-permute-done | bytes 294944 | tf_op jit(solution)/shard_map/ppermute | solution.py:62
  492.9 16.9 %collective-permute-done.82 = bf16[2,32,1152]{2,1,0:T(8,128)(2,1)} collective-permute-done((bf16[2,32,1152]{2,1,0:T(8,128)(2,1)}, bf16[2,32,1152]{2,1,0:T(8,128)(2,1)}, u32[]{:S(2)}, u32[]{:S(2)}) %collective-permute-start.82) | collective-permute-done | bytes 147488 | tf_op jit(solution)/shard_map/ppermute | solution.py:68
  517.1 14.8 %collective-permute-done.65 = bf16[2,144,864]{2,1,0:T(8,128)(2,1)S(1)} collective-permute-done((bf16[2,144,864]{2,1,0:T(8,128)(2,1)S(1)}, bf16[2,144,864]{2,1,0:T(8,128)(2,1)S(1)}, u32[]{:S(2)}, u32[]{:S(2)}) %collective-permute-start.65) | collective-permute-done | bytes 497696 | tf_op jit(solution)/shard_map/ppermute | solution.py:62
  539.5 14.7 %collective-permute-done.69 = bf16[2,144,864]{2,1,0:T(8,128)(2,1)S(1)} collective-permute-done((bf16[2,144,864]{2,1,0:T(8,128)(2,1)S(1)}, bf16[2,144,864]{2,1,0:T(8,128)(2,1)S(1)}, u32[]{:S(2)}, u32[]{:S(2)}) %collective-permute-start.69) | collective-permute-done | bytes 497696 | tf_op jit(solution)/shard_map/ppermute | solution.py:62
  554.2 10.8 %collective-permute-done.67 = bf16[256,512]{1,0:T(8,128)(2,1)S(1)} collective-permute-done((bf16[256,512]{1,0:T(8,128)(2,1)S(1)}, bf16[256,512]{1,0:T(8,128)(2,1)S(1)}, u32[]{:S(2)}, u32[]{:S(2)}) %collective-permute-start.67) | collective-permute-done | bytes 262176 | tf_op jit(solution)/shard_map/ppermute | solution.py:62
  588.2 11.0 %collective-permute-done.77 = bf16[4,2,36,864]{3,0,2,1:T(4,128)(2,1)S(1)} collective-permute-done((bf16[4,2,36,864]{3,0,2,1:T(4,128)(2,1)S(1)}, bf16[4,2,36,864]{3,0,2,1:T(4,128)(2,1)S(1)}, u32[]{:S(2)}, u32[]{:S(2)}) %collective-permute-start.77) | collective-permute-done | bytes 497696 | tf_op jit(solution)/shard_map/ppermute | solution.py:62
  (603 shorter events, 359.1 us)
Async XLA Ops:
  7.2 182.8 %all-gather.2.cloned.1.call-start = ((), (), s32[]{:S(2)}) async-start(), calls=%async_computation.2 | async-start | bytes 2433024 | tf_op jit(solution)/shard_map/all_gather | solution.py:630
  43.4 30.8 %collective-permute-start.10 = (bf16[1,216,1152]{2,1,0:T(8,128)(2,1)}, bf16[1,216,1152]{2,1,0:T(8,128)(2,1)}, u32[]{:S(2)}, u32[]{:S(2)}) collective-permute-start(bf16[1,216,1152]{2,1,0:T(8,128)(2,1)} %bitcast.15.refs_0_), channel_id=1, source_target_pairs={{0,16},{4,20},{8,24},{12,28},{16,0},{20,4},{24,8},{28,12},{1,17},{... | collective-permute-start | bytes 1493000 | tf_op jit(solution)/shard_map/ppermute | solution.py:62
  45.4 25.8 %collective-permute-start.11 = (bf16[4,2,36,864]{3,0,2,1:T(4,128)(2,1)}, bf16[4,2,36,864]{3,0,2,1:T(4,128)(2,1)}, u32[]{:S(2)}, u32[]{:S(2)}) collective-permute-start(bf16[4,2,36,864]{3,0,2,1:T(4,128)(2,1)} %copy.73), channel_id=1, source_target_pairs={{0,8},{4,12},{8,0},{12,4},{16,24},{20,28},{24,16},{28,20},{1,9},{5... | collective-permute-start | bytes 1493000 | tf_op jit(solution)/shard_map/ppermute | solution.py:62
  79.0 26.8 %all-to-all-start = ((bf16[4,2,2,36,864]{4,2,3,1,0:T(2,128)(2,1)}), bf16[4,2,2,36,864]{4,2,3,1,0:T(2,128)(2,1)S(1)}, u32[]{:S(2)}, u32[]{:S(2)}) async-start(bf16[4,2,2,36,864]{4,2,3,1,0:T(2,128)(2,1)} %copy.75), calls=%async_computation | async-start | bytes 2064384 | tf_op jit(solution)/shard_map/all_to_all | solution.py:543
  84.8 35.8 %collective-permute-start.17 = (bf16[2,128,512]{2,1,0:T(8,128)(2,1)S(1)}, bf16[2,128,512]{2,1,0:T(8,128)(2,1)}, u32[]{:S(2)}, u32[]{:S(2)}) collective-permute-start(bf16[2,128,512]{2,1,0:T(8,128)(2,1)S(1)} %copy-done.42), channel_id=1, source_target_pairs={{0,2},{1,3},{2,0},{3,1},{4,6},{5,7},{6,4},{7,5},{8,10},{9,11},{10,... | collective-permute-start | bytes 786440 | tf_op jit(solution)/shard_map/ppermute | solution.py:62
  115.3 39.4 %collective-permute-start.15 = (bf16[16,40,1024]{2,1,0:T(8,128)(2,1)S(1)}, bf16[16,40,1024]{2,1,0:T(8,128)(2,1)S(1)}, u32[]{:S(2)}, u32[]{:S(2)}) collective-permute-start(bf16[16,40,1024]{2,1,0:T(8,128)(2,1)S(1)} %pad_maximum_fusion.1), channel_id=1, source_target_pairs={{0,1},{1,0},{2,3},{3,2},{4,5},{5,4},{6,7},{7,6},{8,9},{9,8},{10,11... | collective-permute-start | bytes 3932168 | tf_op jit(solution)/shard_map/ppermute | solution.py:68
  120.6 60.2 %collective-permute-start.26 = (bf16[1,216,1152]{2,1,0:T(8,128)(2,1)}, bf16[1,216,1152]{2,1,0:T(8,128)(2,1)}, u32[]{:S(2)}, u32[]{:S(2)}) collective-permute-start(bf16[1,216,1152]{2,1,0:T(8,128)(2,1)} %bitcast.15.refs_0_), channel_id=1, source_target_pairs={{0,4},{4,0},{8,12},{12,8},{16,20},{20,16},{24,28},{28,24},{1,5},{5... | collective-permute-start | bytes 1493000 | tf_op jit(solution)/shard_map/ppermute | solution.py:62
  122.1 32.1 %collective-permute-start.16 = (bf16[2,144,864]{2,1,0:T(8,128)(2,1)S(1)}, bf16[2,144,864]{2,1,0:T(8,128)(2,1)}, u32[]{:S(2)}, u32[]{:S(2)}) collective-permute-start(bf16[2,144,864]{2,1,0:T(8,128)(2,1)S(1)} %copy-done.49), channel_id=1, source_target_pairs={{0,16},{4,20},{8,24},{12,28},{16,0},{20,4},{24,8},{28,12},{1,17},{... | collective-permute-start | bytes 1493000 | tf_op jit(solution)/shard_map/ppermute | solution.py:62
  127.7 33.6 %collective-permute-start.21 = (bf16[4,2,128,512]{3,2,1,0:T(8,128)(2,1)S(1)}, bf16[4,2,128,512]{3,2,1,0:T(8,128)(2,1)}, u32[]{:S(2)}, u32[]{:S(2)}) collective-permute-start(bf16[4,2,128,512]{3,2,1,0:T(8,128)(2,1)S(1)} %pad_maximum_fusion.4), channel_id=1, source_target_pairs={{0,1},{1,0},{2,3},{3,2},{4,5},{5,4},{6,7},{7,6},{8,9},{9,8},{10,11... | collective-permute-start | bytes 3145736 | tf_op jit(solution)/shard_map/ppermute | solution.py:62
  136.1 26.7 %collective-permute-start.22 = (bf16[4,2,128,512]{3,2,1,0:T(8,128)(2,1)}, bf16[4,2,128,512]{3,2,1,0:T(8,128)(2,1)}, u32[]{:S(2)}, u32[]{:S(2)}) collective-permute-start(bf16[4,2,128,512]{3,2,1,0:T(8,128)(2,1)} %pad_maximum_fusion.5), channel_id=1, source_target_pairs={{0,1},{1,0},{2,3},{3,2},{4,5},{5,4},{6,7},{7,6},{8,9},{9,8},{10,11... | collective-permute-start | bytes 3145736 | tf_op jit(solution)/shard_map/ppermute | solution.py:62
  154.2 26.6 %collective-permute-start.27 = (bf16[1,216,1152]{2,1,0:T(8,128)(2,1)}, bf16[1,216,1152]{2,1,0:T(8,128)(2,1)}, u32[]{:S(2)}, u32[]{:S(2)}) collective-permute-start(bf16[1,216,1152]{2,1,0:T(8,128)(2,1)} %collective-permute-done.10.refs_1_), channel_id=1, source_target_pairs={{0,4},{4,0},{8,12},{12,8},{16,20},{20,16},{24,28},{28,24},{1,5},{5... | collective-permute-start | bytes 1493000 | tf_op jit(solution)/shard_map/ppermute | solution.py:62
  154.7 26.1 %collective-permute-start.25 = (bf16[2,144,864]{2,1,0:T(8,128)(2,1)}, bf16[2,144,864]{2,1,0:T(8,128)(2,1)}, u32[]{:S(2)}, u32[]{:S(2)}) collective-permute-start(bf16[2,144,864]{2,1,0:T(8,128)(2,1)} %get-tuple-element.160.refs_0_), channel_id=1, source_target_pairs={{0,16},{4,20},{8,24},{12,28},{16,0},{20,4},{24,8},{28,12},{1,17},{... | collective-permute-start | bytes 1493000 | tf_op jit(solution)/shard_map/ppermute | solution.py:62
  162.8 27.2 %collective-permute-start.24 = (bf16[2,144,864]{2,1,0:T(8,128)(2,1)}, bf16[2,144,864]{2,1,0:T(8,128)(2,1)}, u32[]{:S(2)}, u32[]{:S(2)}) collective-permute-start(bf16[2,144,864]{2,1,0:T(8,128)(2,1)} %collective-permute-done.16.refs_1_), channel_id=1, source_target_pairs={{0,4},{4,0},{8,12},{12,8},{16,20},{20,16},{24,28},{28,24},{1,5},{5... | collective-permute-start | bytes 1493000 | tf_op jit(solution)/shard_map/ppermute | solution.py:62
  195.5 28.6 %collective-permute-start.29 = (bf16[256,1152]{1,0:T(8,128)(2,1)}, bf16[256,1152]{1,0:T(8,128)(2,1)S(1)}, u32[]{:S(2)}, u32[]{:S(2)}) collective-permute-start(bf16[256,1152]{1,0:T(8,128)(2,1)} %get-tuple-element.245), channel_id=1, source_target_pairs={{0,8},{4,12},{8,0},{12,4},{16,24},{20,28},{24,16},{28,20},{1,9},{5... | collective-permute-start | bytes 1769480 | tf_op jit(solution)/shard_map/ppermute | solution.py:62
  195.5 29.4 %collective-permute-start.28 = (bf16[256,1152]{1,0:T(8,128)(2,1)}, bf16[256,1152]{1,0:T(8,128)(2,1)S(1)}, u32[]{:S(2)}, u32[]{:S(2)}) collective-permute-start(bf16[256,1152]{1,0:T(8,128)(2,1)} %get-tuple-element.245), channel_id=1, source_target_pairs={{0,2},{1,3},{2,0},{3,1},{4,6},{5,7},{6,4},{7,5},{8,10},{9,11},{10,... | collective-permute-start | bytes 1769480 | tf_op jit(solution)/shard_map/ppermute | solution.py:62
  264.9 33.8 %collective-permute-start.43 = (bf16[128,1152]{1,0:T(8,128)(2,1)S(1)}, bf16[128,1152]{1,0:T(8,128)(2,1)S(1)}, u32[]{:S(2)}, u32[]{:S(2)}) collective-permute-start(bf16[128,1152]{1,0:T(8,128)(2,1)S(1)} %get-tuple-element.292), channel_id=1, source_target_pairs={{0,4},{4,0},{8,12},{12,8},{16,20},{20,16},{24,28},{28,24},{1,5},{5... | collective-permute-start | bytes 884744 | tf_op jit(solution)/shard_map/ppermute | solution.py:62
  484.1 29.6 %collective-permute-start.64 = (bf16[4,256,512]{2,1,0:T(8,128)(2,1)}, bf16[4,256,512]{2,1,0:T(8,128)(2,1)}, u32[]{:S(2)}, u32[]{:S(2)}) collective-permute-start(bf16[4,256,512]{2,1,0:T(8,128)(2,1)} %bitcast.152), channel_id=1, source_target_pairs={{0,2},{1,3},{2,0},{3,1},{4,6},{5,7},{6,4},{7,5},{8,10},{9,11},{10,... | collective-permute-start | bytes 3145736 | tf_op jit(solution)/shard_map/ppermute | solution.py:62
  486.9 28.3 %collective-permute-start.63 = (bf16[16,40,1024]{2,1,0:T(8,128)(2,1)}, bf16[16,40,1024]{2,1,0:T(8,128)(2,1)}, u32[]{:S(2)}, u32[]{:S(2)}) collective-permute-start(bf16[16,40,1024]{2,1,0:T(8,128)(2,1)} %bitcast.150), channel_id=1, source_target_pairs={{0,1},{1,0},{2,3},{3,2},{4,5},{5,4},{6,7},{7,6},{8,9},{9,8},{10,11... | collective-permute-start | bytes 3932168 | tf_op jit(solution)/shard_map/ppermute | solution.py:68
  491.8 40.1 %collective-permute-start.65 = (bf16[2,144,864]{2,1,0:T(8,128)(2,1)S(1)}, bf16[2,144,864]{2,1,0:T(8,128)(2,1)S(1)}, u32[]{:S(2)}, u32[]{:S(2)}) collective-permute-start(bf16[2,144,864]{2,1,0:T(8,128)(2,1)S(1)} %get-tuple-element.283), channel_id=1, source_target_pairs={{0,16},{4,20},{8,24},{12,28},{16,0},{20,4},{24,8},{28,12},{1,17},{... | collective-permute-start | bytes 1493000 | tf_op jit(solution)/shard_map/ppermute | solution.py:62
  510.8 25.7 %collective-permute-start.83 = (bf16[1,32,1152]{2,1,0:T(8,128)(2,1)S(1)}, bf16[1,32,1152]{2,1,0:T(8,128)(2,1)S(1)}, u32[]{:S(2)}, u32[]{:S(2)}) collective-permute-start(bf16[1,32,1152]{2,1,0:T(8,128)(2,1)S(1)} %slice.398), channel_id=1, source_target_pairs={{0,8},{1,9},{2,10},{3,11},{4,12},{5,13},{6,14},{7,15},{8,0},{9,1},... | collective-permute-start | bytes 221192 | tf_op jit(solution)/shard_map/ppermute | solution.py:68
  510.9 43.3 %collective-permute-start.69 = (bf16[2,144,864]{2,1,0:T(8,128)(2,1)S(1)}, bf16[2,144,864]{2,1,0:T(8,128)(2,1)S(1)}, u32[]{:S(2)}, u32[]{:S(2)}) collective-permute-start(bf16[2,144,864]{2,1,0:T(8,128)(2,1)S(1)} %copy-done.48), channel_id=1, source_target_pairs={{0,16},{4,20},{8,24},{12,28},{16,0},{20,4},{24,8},{28,12},{1,17},{... | collective-permute-start | bytes 1493000 | tf_op jit(solution)/shard_map/ppermute | solution.py:62
  534.4 30.6 %collective-permute-start.67 = (bf16[256,512]{1,0:T(8,128)(2,1)S(1)}, bf16[256,512]{1,0:T(8,128)(2,1)S(1)}, u32[]{:S(2)}, u32[]{:S(2)}) collective-permute-start(bf16[256,512]{1,0:T(8,128)(2,1)S(1)} %get-tuple-element.280), channel_id=1, source_target_pairs={{0,16},{4,20},{8,24},{12,28},{16,0},{20,4},{24,8},{28,12},{1,17},{... | collective-permute-start | bytes 786440 | tf_op jit(solution)/shard_map/ppermute | solution.py:62
  534.4 30.6 %collective-permute-start.66 = (bf16[256,512]{1,0:T(8,128)(2,1)S(1)}, bf16[256,512]{1,0:T(8,128)(2,1)S(1)}, u32[]{:S(2)}, u32[]{:S(2)}) collective-permute-start(bf16[256,512]{1,0:T(8,128)(2,1)S(1)} %get-tuple-element.281), channel_id=1, source_target_pairs={{0,8},{4,12},{8,0},{12,4},{16,24},{20,28},{24,16},{28,20},{1,9},{5... | collective-permute-start | bytes 786440 | tf_op jit(solution)/shard_map/ppermute | solution.py:62
  538.1 48.0 %collective-permute-start.71 = (bf16[8,40,1024]{2,1,0:T(8,128)(2,1)}, bf16[8,40,1024]{2,1,0:T(8,128)(2,1)}, u32[]{:S(2)}, u32[]{:S(2)}) collective-permute-start(bf16[8,40,1024]{2,1,0:T(8,128)(2,1)} %slice.310), channel_id=1, source_target_pairs={{0,2},{1,3},{2,0},{3,1},{4,6},{5,7},{6,4},{7,5},{8,10},{9,11},{10,... | collective-permute-start | bytes 1966088 | tf_op jit(solution)/shard_map/ppermute | solution.py:68
  (166 other events, 1941.6 us)
Sparse Core Ops, SparseCore 0:
  76.4 79.5 all-gather.1

commit v8 on v7

--- a/solution.py
+++ b/solution.py
@@ -558,7 +558,6 @@
         last_mask = masks
     blocks, packed, down_piece, rows_low = together(blocks, packed, w_down[None], regroup(inputs))
     rows_in = rows_low.astype(f32)
-    column_parts = column_exchange(packed)
     q_blocks = gather_step(q_blocks, *x_mask)
     blocks = gather_step(blocks, *core_mask)
     kv_weight = blocks.reshape(devices * block_rows, 2 * HEAD)
@@ -572,7 +571,7 @@
 
     model_pick = selection(natural, width, model_rows, block_rows)
     device_pick = selection(natural, devices, 1, 1)
-    out_pick = selection(natural, wide_q, out_rows, out_rows)
+    out_pick = selection(natural, wide_q, out_rows, block_rows)
     gain_blocks = blocks[:, model_rows, :gain_total]
     gain_all = mm(device_pick, gain_blocks)
     full_gain, at = [], 0
@@ -626,12 +625,13 @@
     picked_one = mm(normed_one, model_pick).astype(bf16)
     key_raw, keys_mine = project_keys(picked_one, kv_weight, key_gain[None], cosine, sine)
     column = [keys_mine] + [xor(keys_mine, "dp", 2 * k) for k in range(1, layers)]
-    column[1], down_tall, column_parts, late_out = together(column[1], down_tall, column_parts, w_out)
+    key_raw, packed = together(key_raw, packed)
+    column_parts = column_exchange(packed)
+    others, down_tall, column_parts, late_out, q_blocks = together(column[1:], down_tall, column_parts, w_out, q_blocks)
+    column = [column[0], *others]
     out_weight = lax.all_gather(late_out, ALL, axis=0, tiled=True)
     halves = merge(swap_members(column_parts))
-    halves, others, q_blocks = together(halves, column[1:], q_blocks)
     q_weight = gather_step(q_blocks, *core_mask).reshape(devices * block_rows, wide_q)
-    column = [column[0], *others]
     gate_tall, up_half = together(from_tops(halves[0]), halves[1])
     up_tall = from_tops(up_half)
     across = [xor(part, "seq", 2) for part in column]
@@ -663,7 +663,7 @@
     q_natural, kv_natural, picked_context, mixed = together(q_natural, kv_natural, picked_context, mixed)
     scale_four = norm_scale(mixed)
     result = hidden_res + mixed * scale_four * post_feed
-    output = ungroup(jnp.where(valid, result, 0.0).astype(bf16))
+    result = jnp.where(valid, result, 0.0).astype(bf16)
 
     upstream = jnp.where(valid, regroup(cotangent).astype(f32), 0.0)
     grad_post_feed = jnp.sum(upstream * mixed * scale_four, axis=0)
@@ -708,34 +708,29 @@
 
     grad_post_attention = jnp.sum(hidden_res_grad * attended * scale_two, axis=0)
     attended_grad = norm_back(attended, scale_two, post_attention * hidden_res_grad).astype(bf16)
-    out_total = mm_tn(picked_context, attended_grad).astype(bf16).reshape(devices, out_rows, width)
+    out_total = mm_tn(picked_context, attended_grad).astype(bf16)
     attended_grad, out_total, gate_kept, up_kept = lax.optimization_barrier(
         (attended_grad, out_total, gate_halves[0], up_halves[0])
     )
     gate_halves, up_halves = (gate_kept, gate_halves[1]), (up_kept, up_halves[1])
     down_parts = send_tops(by_top(*down_halves))
     context_grad = mm_nt(attended_grad, out_weight).astype(bf16)
-    out_total, context_grad, gate_halves = together(scatter_step(out_total, *core_mask), context_grad, gate_halves)
-    gate_parts = send_tops(by_top(*gate_halves))
-    out_total = scatter_step(out_total, *x_mask)
     query_grad, grad_query_gain, near_part, far_part = attend_back(
         meta, seq_ends, slots, query_heads, context_grad, lse, turned, query_raw, query_gain[None], cosine, sine, near_keys, far_keys
     )
-    far_part, near_part, up_halves, down_parts, out_total = together(far_part, near_part, up_halves, down_parts, out_total)
+    far_part, near_part, gate_halves, up_halves, down_parts = together(
+        far_part, near_part, gate_halves, up_halves, down_parts
+    )
     far_part = xor(far_part, "seq", 1)
-    query_low, far_part, up_tops = together(query_grad, far_part, by_top(*up_halves))
-    up_parts = send_tops(up_tops)
-    for masks in reversed([first_mask, *more_masks]):
-        out_total = scatter_step(out_total, *masks)
+    query_low, far_part, gate_tops, up_tops = together(query_grad, far_part, by_top(*gate_halves), by_top(*up_halves))
+    gate_parts, up_parts = send_tops(gate_tops), send_tops(up_tops)
     near_part = add16(near_part, far_part).reshape(2, layers, count, 2 * HEAD)
     near_part = add16(near_part[0], xor(near_part[1], "seq", 2))
-    grad_query = mm_tn(picked_one, query_low).astype(bf16).reshape(devices, block_rows, wide_q)
+    grad_query = jnp.concatenate([mm_tn(picked_one, query_low).astype(bf16), out_total], axis=1)
+    grad_query = grad_query.reshape(devices, block_rows, wide_q + width)
     grad_query, near_part, gate_parts = together(scatter_step(grad_query, *core_mask), near_part, gate_parts)
-    for masks in reversed([first_mask, *more_masks, x_mask]):
-        grad_query = scatter_step(grad_query, *masks)
-    grad_query = grad_query[0]
+    grad_query = scatter_step(grad_query, *x_mask)
     key_parts = [near_part[k] if k == 0 else xor(near_part[k], "dp", 2 * k) for k in range(layers)]
-    grad_out = out_total[0]
     key_parts, up_parts = together(key_parts, up_parts)
     key_grads = functools.reduce(jnp.add, [part.astype(f32) for part in key_parts])
     value_grad = key_grads[:, HEAD:].astype(bf16)
@@ -747,7 +742,10 @@
     normed_one_grad = mm_nt(query_grad, q_natural) + mm_nt(kv_grad, kv_natural)
     grad_pre_attention = jnp.sum(normed_one_grad * rows_in * scale_one, axis=0)
     rows_grad = hidden_res_grad + norm_back(rows_in, scale_one, pre_attention * normed_one_grad)
-    rows_low, down_parts, gate_parts, up_parts = together(rows_grad.astype(bf16), down_parts, gate_parts, up_parts)
+    rows_low, result, down_parts, gate_parts, up_parts = together(
+        rows_grad.astype(bf16), result, down_parts, gate_parts, up_parts
+    )
+    output = ungroup(result)
     grad_down = total_of(down_parts)[0]
     both_grads = split(total_of(gate_parts).astype(bf16), total_of(up_parts).astype(bf16), members)
     input_grad = ungroup(rows_low)
@@ -765,13 +763,19 @@
     gain_grads = jnp.pad(
         gain_grads[:, None, :], ((0, 0), (model_rows, block_rows - model_rows - 1), (0, 2 * HEAD - gain_total))
     )
-    last = scatter_step((grad_kv + gain_grads).astype(bf16), *core_mask)
-    last, column_parts = together(scatter_step(last, *x_mask), column_exchange(both_grads))
-    for masks in reversed(more_masks):
-        last = scatter_step(last, *masks)
-    last, column_parts = together(last, swap_members(column_parts))
+    last, grad_query = together(scatter_step((grad_kv + gain_grads).astype(bf16), *core_mask), grad_query)
+    rest = [*reversed(more_masks), first_mask]
+    last, grad_query, column_parts = together(
+        scatter_step(last, *x_mask), scatter_step(grad_query, *rest[0]), column_exchange(both_grads)
+    )
+    column_parts = swap_members(column_parts)
+    for masks, ahead in zip(rest[:-1], rest[1:]):
+        last, grad_query, column_parts = together(
+            scatter_step(last, *masks), scatter_step(grad_query, *ahead), column_parts
+        )
     grad_gate, grad_up = unpack(column_parts, z_bit, tops, members, ff_rows)
     last = scatter_step(last, *first_mask)[0]
+    grad_query, grad_out = grad_query[0, :model_rows, :wide_q], grad_query[0, :out_rows, wide_q:]
     gain_out, at = [], 0
     for size in gain_sizes:
         gain_out.append(last[model_rows, at : at + size])
@@ -779,7 +783,7 @@
     return (
         output,
         input_grad,
-        grad_query[:model_rows],
+        grad_query,
         last[:model_rows, :HEAD],
         last[:model_rows, HEAD:],
         grad_out,

time: 652 us -> 663 us (1.017)
  local copies, waits for them, and re-layouts: 67.4 us -> 77.2 us
    ppermute x59, waiting for transfers between devices: 209 us -> 221 us  [xor(): lax.ppermute(value, axis, [(i, i ^ mask) for i in range(lax.axis_size(axi...]
    ppermute x25 -> x20, waiting for transfers between devices: 46.1 us -> 35.6 us  [xor_both(): lax.ppermute(value, ALL, [(i, i ^ mask) for i in range(lax.axis_size('dp'...]
    unnamed x229 -> x211, local copies, waits for them, and re-layouts: 21.4 us -> 30.6 us
    ppermute x25 -> x20, starting transfers between devices: 26 us -> 22.1 us  [xor_both(): lax.ppermute(value, ALL, [(i, i ^ mask) for i in range(lax.axis_size('dp'...]
  transfers between devices with their start and end apart: 87 -> 82, of which waited for: 43 -> 39; matrix products, arithmetic and copies ran while one was open for 21% -> 22% of each run, Pallas kernels for 9% -> 9%
where the time goes in v8:
time: 663 us; the launch traced here: 654 us
  waiting for transfers between devices  263 us (40%)
  starting transfers between devices  90.1 us (14%)
  matrix products  87.5 us (13%)
  local copies, waits for them, and re-layouts  77.2 us (12%)
  other arithmetic  61.7 us (9%)
  Pallas kernels  58.5 us (9%)
  between operations  15.9 us (2%)
    ppermute x59, waiting for transfers between devices, xor(): lax.ppermute(value, axis, [(i, i ^ mask) for i in range(lax.axis_size(axi...  221 us
    dot_general x22, matrix products, dot(): lax.dot_general(left, right, (dims, ((), ())), preferred_element_type=f32)  87.5 us
    ppermute x59, starting transfers between devices, xor(): lax.ppermute(value, axis, [(i, i ^ mask) for i in range(lax.axis_size(axi...  60.7 us
    ppermute x20, waiting for transfers between devices, xor_both(): lax.ppermute(value, ALL, [(i, i ^ mask) for i in range(lax.axis_size('dp'...  35.6 us
    unnamed x211, local copies, waits for them, and re-layouts  30.6 us
    ppermute x20, starting transfers between devices, xor_both(): lax.ppermute(value, ALL, [(i, i ^ mask) for i in range(lax.axis_size('dp'...  22.1 us
    pallas_call x1, Pallas kernels, attend_back(): pl.pallas_call(functools.partial(attend_back_kernel, rows), grid_spec=plt...  17.4 us
    pallas_call x1, Pallas kernels, attend(): pl.pallas_call(functools.partial(attend_kernel, rows), grid_spec=pltpu.Pr...  13.5 us
  transfers between devices with their start and end apart: 82, of which 39 were waited for; matrix products, arithmetic and copies ran while one was open for 22% of the time, Pallas kernels for 9%

profile of v8, /device:TPU:0, one launch (start us, length us, event | category | flops | bytes accessed | tf_op | source)
XLA Modules:
  0.0 653.7 jit_solution(2734703011773016939)
XLA Ops:
  62.6 14.1 %collective-permute-done.14 = bf16[4,2,36,864]{3,0,2,1:T(4,128)(2,1)S(1)} collective-permute-done((bf16[4,2,36,864]{3,0,2,1:T(4,128)(2,1)S(1)}, bf16[4,2,36,864]{3,0,2,1:T(4,128)(2,1)S(1)}, u32[]{:S(2)}, u32[]{:S(2)}) %collective-permute-start.14) | collective-permute-done | bytes 497696 | tf_op jit(solution)/shard_map/ppermute | solution.py:62
  78.6 12.4 %collective-permute-done.13.refs_1_ = bf16[1,216,1152]{2,1,0:T(8,128)(2,1)} collective-permute-done((bf16[1,216,1152]{2,1,0:T(8,128)(2,1)}, bf16[1,216,1152]{2,1,0:T(8,128)(2,1)}, u32[]{:S(2)}, u32[]{:S(2)}) %collective-permute-start.13) | collective-permute-done | bytes 497696 | tf_op jit(solution)/shard_map/ppermute | solution.py:62
  91.0 10.4 %collective-permute-done.11 = bf16[2,128,512]{2,1,0:T(8,128)(2,1)S(1)} collective-permute-done((bf16[2,128,512]{2,1,0:T(8,128)(2,1)S(1)}, bf16[2,128,512]{2,1,0:T(8,128)(2,1)S(1)}, u32[]{:S(2)}, u32[]{:S(2)}) %collective-permute-start.11) | collective-permute-done | bytes 262176 | tf_op jit(solution)/shard_map/ppermute | solution.py:62
  124.7 10.7 %collective-permute-done.19 = bf16[2,128,512]{2,1,0:T(8,128)(2,1)S(1)} collective-permute-done((bf16[2,128,512]{2,1,0:T(8,128)(2,1)}, bf16[2,128,512]{2,1,0:T(8,128)(2,1)S(1)}, u32[]{:S(2)}, u32[]{:S(2)}) %collective-permute-start.19) | collective-permute-done | bytes 262176 | tf_op jit(solution)/shard_map/ppermute | solution.py:62
  155.6 24.7 %collective-permute-done.17.refs_1_ = bf16[2,144,864]{2,1,0:T(8,128)(2,1)} collective-permute-done((bf16[2,144,864]{2,1,0:T(8,128)(2,1)}, bf16[2,144,864]{2,1,0:T(8,128)(2,1)}, u32[]{:S(2)}, u32[]{:S(2)}) %collective-permute-start.17) | collective-permute-done | bytes 497696 | tf_op jit(solution)/shard_map/ppermute | solution.py:62
  195.7 13.5 %attend.1 = (bf16[256,1024]{1,0:T(8,128)(2,1)}, f32[2,256,512]{2,1,0:T(8,128)}, f32[2,1,512]{2,1,0:T(1,128)}) custom-call(s32[7]{0:T(128)} %pad_add_fusion.1.meta_ref, s32[4]{0:T(128)} %bitcast.326, s32[16]{0:T(128)} %gather_fusion.1, bf16[2,4,128,256]{3,2,1,0:T(8,128)(2,1)} %get-tuple-element.149.q_ref, ...), custom_call_target="tpu_custom_call" | custom-call | flops 2415919104 | bytes 4194304 | tf_op jit(solution)/shard_map/attend/pallas_call | solution.py:383
  209.2 6.9 %collective-permute-done.25.refs_3_ = bf16[2,144,864]{2,1,0:T(8,128)(2,1)} collective-permute-done((bf16[2,144,864]{2,1,0:T(8,128)(2,1)}, bf16[2,144,864]{2,1,0:T(8,128)(2,1)}, u32[]{:S(2)}, u32[]{:S(2)}) %collective-permute-start.25) | collective-permute-done | bytes 497696 | tf_op jit(solution)/shard_map/ppermute | solution.py:62
  237.8 9.0 %collective-permute-done.37.refs_3_ = bf16[2,144,864]{2,1,0:T(8,128)(2,1)} collective-permute-done((bf16[2,144,864]{2,1,0:T(8,128)(2,1)}, bf16[2,144,864]{2,1,0:T(8,128)(2,1)}, u32[]{:S(2)}, u32[]{:S(2)}) %collective-permute-start.37) | collective-permute-done | bytes 497696 | tf_op jit(solution)/shard_map/ppermute | solution.py:62
  264.8 7.0 %fusion.68 = f32[2048,864]{0,1:T(8,128)S(1)} fusion(bf16[2048,1152]{1,0:T(8,128)(2,1)} %constant_dynamic-update-slice_fusion.12, bf16[1152,864]{1,0:T(8,128)(2,1)S(1)} %bitcast.289), kind=kOutput, calls=%fused_computation.294 | convolution fusion | flops 4076863488 | bytes 13787136 | tf_op jit(solution)/shard_map/dot_general | solution.py:46
  271.9 9.0 %multiply_convert_fusion.1 = (bf16[2048,864]{0,1:T(8,128)(2,1)S(1)}, f32[2048,864]{0,1:T(8,128)}) fusion(f32[2048,864]{0,1:T(8,128)S(1)} %fusion.68, bf16[2048,1152]{1,0:T(8,128)(2,1)S(1)} %copy-done.57, bf16[1152,864]{1,0:T(8,128)(2,1)S(1)} %bitcast.291), kind=kOutput, calls=%fused_computation.15 | convolution fusion | flops 4094558208 | bytes 24403968 | tf_op jit(solution)/shard_map/dot_general | solution.py:46
  317.2 6.1 collective-permute-done.42
  330.1 11.1 %collective-permute-done.44 = bf16[256,1152]{1,0:T(8,128)(2,1)S(1)} collective-permute-done((bf16[256,1152]{1,0:T(8,128)(2,1)}, bf16[256,1152]{1,0:T(8,128)(2,1)S(1)}, u32[]{:S(2)}, u32[]{:S(2)}) %collective-permute-start.44) | collective-permute-done | bytes 589856 | tf_op jit(solution)/shard_map/ppermute | solution.py:62
  355.4 13.3 %multiply_convert_fusion = (bf16[2048,864]{0,1:T(8,128)(2,1)S(1)}, bf16[2048,864]{0,1:T(8,128)(2,1)S(1)}) fusion(f32[2048,864]{0,1:T(8,128)} %copy-done.83, f32[2048,864]{0,1:T(8,128)} %get-tuple-element.342, bf16[2048,1152]{1,0:T(8,128)(2,1)} %constant_dynamic-update-slice_fusion.20, bf16[864,1152]{1,0:T(8,128)(2,1)S(1)} %bitcast.300), kind=kOutput, calls=%fused_computation.14 | convolution fusion | flops 4119330816 | bytes 27942912 | tf_op jit(solution)/shard_map/dot_general | solution.py:46
  368.8 8.0 %fusion.69 = f32[2048,1152]{1,0:T(8,128)} fusion(bf16[2048,864]{0,1:T(8,128)(2,1)S(1)} %get-tuple-element.178, bf16[1152,864]{1,0:T(8,128)(2,1)S(1)} %bitcast.290), kind=kOutput, calls=%fused_computation.295 | convolution fusion | flops 4076863488 | bytes 14966784 | tf_op jit(solution)/shard_map/dot_general | solution.py:46
  376.8 8.3 %add_convert_fusion = bf16[2048,1152]{1,0:T(8,128)(2,1)S(1)} fusion(f32[2048,1152]{1,0:T(8,128)} %fusion.69, bf16[2048,864]{0,1:T(8,128)(2,1)S(1)} %get-tuple-element.181, bf16[1152,864]{1,0:T(8,128)(2,1)S(1)} %bitcast.292), kind=kOutput, calls=%fused_computation.4 | convolution fusion | flops 4081582080 | bytes 19685376 | tf_op jit(solution)/shard_map/dot_general | solution.py:46
  401.1 15.1 %collective-permute-done.55 = bf16[2,1,216,1152]{3,2,1,0:T(8,128)(2,1)S(1)} collective-permute-done((bf16[2,1,216,1152]{3,2,1,0:T(8,128)(2,1)S(1)}, bf16[2,1,216,1152]{3,2,1,0:T(8,128)(2,1)S(1)}, u32[]{:S(2)}, u32[]{:S(2)}) %collective-permute-start.55) | collective-permute-done | bytes 995360 | tf_op jit(solution)/shard_map/ppermute | solution.py:62
  432.8 13.7 %collective-permute-done.54 = bf16[256,1152]{1,0:T(8,128)(2,1)S(1)} collective-permute-done((bf16[256,1152]{1,0:T(8,128)(2,1)S(1)}, bf16[256,1152]{1,0:T(8,128)(2,1)S(1)}, u32[]{:S(2)}, u32[]{:S(2)}) %collective-permute-start.54) | collective-permute-done | bytes 589856 | tf_op jit(solution)/shard_map/ppermute | solution.py:62
  454.0 17.4 %attend_back.1 = (bf16[256,1024]{1,0:T(8,128)(2,1)}, f32[1,256]{1,0:T(1,128)}, bf16[8,2,128,512]{3,2,1,0:T(8,128)(2,1)}, bf16[8,2,128,512]{3,2,1,0:T(8,128)(2,1)}) custom-call(s32[7]{0:T(128)} %pad_add_fusion.1.meta_ref, s32[4]{0:T(128)} %bitcast.327, s32[16]{0:T(128)} %gather_fusion.1, bf16[2,4,128,256]{3,2,1,0:T(8,128)(2,1)} %get-tuple-element.149.q_ref, ...), custom_call_target="tpu_custom_call" | custom-call | flops 6039797760 | bytes 8388608 | tf_op jit(solution)/shard_map/attend_back/pallas_call | solution.py:412
  489.0 20.5 %collective-permute-done.61 = bf16[4,256,512]{2,1,0:T(8,128)(2,1)} collective-permute-done((bf16[4,256,512]{2,1,0:T(8,128)(2,1)}, bf16[4,256,512]{2,1,0:T(8,128)(2,1)}, u32[]{:S(2)}, u32[]{:S(2)}) %collective-permute-start.61) | collective-permute-done | bytes 1048608 | tf_op jit(solution)/shard_map/ppermute | solution.py:62
  515.5 8.4 %collective-permute-done.62 = bf16[2,144,864]{2,1,0:T(8,128)(2,1)S(1)} collective-permute-done((bf16[2,144,864]{2,1,0:T(8,128)(2,1)}, bf16[2,144,864]{2,1,0:T(8,128)(2,1)S(1)}, u32[]{:S(2)}, u32[]{:S(2)}) %collective-permute-start.62) | collective-permute-done | bytes 497696 | tf_op jit(solution)/shard_map/ppermute | solution.py:62
  532.9 13.5 %collective-permute-done.66 = bf16[2,144,864]{2,1,0:T(8,128)(2,1)} collective-permute-done((bf16[2,144,864]{2,1,0:T(8,128)(2,1)}, bf16[2,144,864]{2,1,0:T(8,128)(2,1)}, u32[]{:S(2)}, u32[]{:S(2)}) %collective-permute-start.66) | collective-permute-done | bytes 497696 | tf_op jit(solution)/shard_map/ppermute | solution.py:62
  546.4 10.0 %collective-permute-done.64 = bf16[256,512]{1,0:T(8,128)(2,1)S(1)} collective-permute-done((bf16[256,512]{1,0:T(8,128)(2,1)S(1)}, bf16[256,512]{1,0:T(8,128)(2,1)S(1)}, u32[]{:S(2)}, u32[]{:S(2)}) %collective-permute-start.64) | collective-permute-done | bytes 262176 | tf_op jit(solution)/shard_map/ppermute | solution.py:62
  594.3 9.3 %collective-permute-done.72 = bf16[4,40,2176]{2,1,0:T(8,128)(2,1)S(1)} collective-permute-done((bf16[4,40,2176]{2,1,0:T(8,128)(2,1)S(1)}, bf16[4,40,2176]{2,1,0:T(8,128)(2,1)S(1)}, u32[]{:S(2)}, u32[]{:S(2)}) %collective-permute-start.72) | collective-permute-done | bytes 696352 | tf_op jit(solution)/shard_map/ppermute | solution.py:68
  615.7 8.0 %collective-permute-done.75 = bf16[2,40,2176]{2,1,0:T(8,128)(2,1)S(1)} collective-permute-done((bf16[2,40,2176]{2,1,0:T(8,128)(2,1)}, bf16[2,40,2176]{2,1,0:T(8,128)(2,1)S(1)}, u32[]{:S(2)}, u32[]{:S(2)}) %collective-permute-start.75) | collective-permute-done | bytes 348192 | tf_op jit(solution)/shard_map/ppermute | solution.py:68
  (567 shorter events, 357.5 us)
Async XLA Ops:
  7.2 208.9 %all-gather.2.cloned.1.call-start = ((), (), s32[]{:S(2)}) async-start(), calls=%async_computation.2 | async-start | bytes 2433024 | tf_op jit(solution)/shard_map/all_gather | solution.py:632
  52.5 38.5 %collective-permute-start.13 = (bf16[1,216,1152]{2,1,0:T(8,128)(2,1)}, bf16[1,216,1152]{2,1,0:T(8,128)(2,1)}, u32[]{:S(2)}, u32[]{:S(2)}) collective-permute-start(bf16[1,216,1152]{2,1,0:T(8,128)(2,1)} %bitcast.17.refs_0_), channel_id=1, source_target_pairs={{0,16},{4,20},{8,24},{12,28},{16,0},{20,4},{24,8},{28,12},{1,17},{... | collective-permute-start | bytes 1493000 | tf_op jit(solution)/shard_map/ppermute | solution.py:62
  56.5 34.5 %collective-permute-start.12 = (bf16[2,128,512]{2,1,0:T(8,128)(2,1)S(1)}, bf16[2,128,512]{2,1,0:T(8,128)(2,1)S(1)}, u32[]{:S(2)}, u32[]{:S(2)}) collective-permute-start(bf16[2,128,512]{2,1,0:T(8,128)(2,1)S(1)} %copy-done.36), channel_id=1, source_target_pairs={{0,24},{4,28},{8,16},{12,20},{16,8},{20,12},{24,0},{28,4},{1,25},{... | collective-permute-start | bytes 786440 | tf_op jit(solution)/shard_map/ppermute | solution.py:62
  56.5 44.9 %collective-permute-start.11 = (bf16[2,128,512]{2,1,0:T(8,128)(2,1)S(1)}, bf16[2,128,512]{2,1,0:T(8,128)(2,1)S(1)}, u32[]{:S(2)}, u32[]{:S(2)}) collective-permute-start(bf16[2,128,512]{2,1,0:T(8,128)(2,1)S(1)} %copy-done.36), channel_id=1, source_target_pairs={{0,16},{4,20},{8,24},{12,28},{16,0},{20,4},{24,8},{28,12},{1,17},{... | collective-permute-start | bytes 786440 | tf_op jit(solution)/shard_map/ppermute | solution.py:62
  60.1 42.0 %collective-permute-start.10 = (bf16[2,128,512]{2,1,0:T(8,128)(2,1)S(1)}, bf16[2,128,512]{2,1,0:T(8,128)(2,1)}, u32[]{:S(2)}, u32[]{:S(2)}) collective-permute-start(bf16[2,128,512]{2,1,0:T(8,128)(2,1)S(1)} %copy-done.36), channel_id=1, source_target_pairs={{0,8},{4,12},{8,0},{12,4},{16,24},{20,28},{24,16},{28,20},{1,9},{5... | collective-permute-start | bytes 786440 | tf_op jit(solution)/shard_map/ppermute | solution.py:62
  109.1 40.8 %all-to-all-start = ((bf16[4,2,2,36,864]{4,2,3,1,0:T(2,128)(2,1)}), bf16[4,2,2,36,864]{4,2,3,1,0:T(2,128)(2,1)S(1)}, u32[]{:S(2)}, u32[]{:S(2)}) async-start(bf16[4,2,2,36,864]{4,2,3,1,0:T(2,128)(2,1)} %copy.80), calls=%async_computation | async-start | bytes 2064384 | tf_op jit(solution)/shard_map/all_to_all | solution.py:543
  115.0 31.0 %collective-permute-start.21 = (bf16[2,128,512]{2,1,0:T(8,128)(2,1)S(1)}, bf16[2,128,512]{2,1,0:T(8,128)(2,1)S(1)}, u32[]{:S(2)}, u32[]{:S(2)}) collective-permute-start(bf16[2,128,512]{2,1,0:T(8,128)(2,1)S(1)} %collective-permute-done.12), channel_id=1, source_target_pairs={{0,2},{1,3},{2,0},{3,1},{4,6},{5,7},{6,4},{7,5},{8,10},{9,11},{10,... | collective-permute-start | bytes 786440 | tf_op jit(solution)/shard_map/ppermute | solution.py:62
  117.0 64.8 %collective-permute-start.16 = (bf16[16,40,1024]{2,1,0:T(8,128)(2,1)S(1)}, bf16[16,40,1024]{2,1,0:T(8,128)(2,1)}, u32[]{:S(2)}, u32[]{:S(2)}) collective-permute-start(bf16[16,40,1024]{2,1,0:T(8,128)(2,1)S(1)} %pad_maximum_fusion.2), channel_id=1, source_target_pairs={{0,1},{1,0},{2,3},{3,2},{4,5},{5,4},{6,7},{7,6},{8,9},{9,8},{10,11... | collective-permute-start | bytes 3932168 | tf_op jit(solution)/shard_map/ppermute | solution.py:68
  123.1 86.0 %collective-permute-start.27 = (bf16[1,216,1152]{2,1,0:T(8,128)(2,1)}, bf16[1,216,1152]{2,1,0:T(8,128)(2,1)}, u32[]{:S(2)}, u32[]{:S(2)}) collective-permute-start(bf16[1,216,1152]{2,1,0:T(8,128)(2,1)} %bitcast.17.refs_0_), channel_id=1, source_target_pairs={{0,4},{4,0},{8,12},{12,8},{16,20},{20,16},{24,28},{28,24},{1,5},{5... | collective-permute-start | bytes 1493000 | tf_op jit(solution)/shard_map/ppermute | solution.py:62
  135.4 54.2 %collective-permute-start.22 = (bf16[4,2,128,512]{3,2,1,0:T(8,128)(2,1)}, bf16[4,2,128,512]{3,2,1,0:T(8,128)(2,1)}, u32[]{:S(2)}, u32[]{:S(2)}) collective-permute-start(bf16[4,2,128,512]{3,2,1,0:T(8,128)(2,1)} %pad_maximum_fusion.5), channel_id=1, source_target_pairs={{0,1},{1,0},{2,3},{3,2},{4,5},{5,4},{6,7},{7,6},{8,9},{9,8},{10,11... | collective-permute-start | bytes 3145736 | tf_op jit(solution)/shard_map/ppermute | solution.py:62
  148.2 41.9 %collective-permute-start.23 = (bf16[4,2,128,512]{3,2,1,0:T(8,128)(2,1)}, bf16[4,2,128,512]{3,2,1,0:T(8,128)(2,1)}, u32[]{:S(2)}, u32[]{:S(2)}) collective-permute-start(bf16[4,2,128,512]{3,2,1,0:T(8,128)(2,1)} %pad_maximum_fusion.6), channel_id=1, source_target_pairs={{0,1},{1,0},{2,3},{3,2},{4,5},{5,4},{6,7},{7,6},{8,9},{9,8},{10,11... | collective-permute-start | bytes 3145736 | tf_op jit(solution)/shard_map/ppermute | solution.py:62
  290.9 33.2 %collective-permute-start = (bf16[128,1152]{1,0:T(8,128)(2,1)}, bf16[128,1152]{1,0:T(8,128)(2,1)S(1)}, u32[]{:S(2)}, u32[]{:S(2)}) collective-permute-start(bf16[128,1152]{1,0:T(8,128)(2,1)} %get-tuple-element.306), channel_id=1, source_target_pairs={{0,4},{4,0},{8,12},{12,8},{16,20},{20,16},{24,28},{28,24},{1,5},{5... | collective-permute-start | bytes 884744 | tf_op jit(solution)/shard_map/ppermute | solution.py:62
  385.3 30.9 %collective-permute-start.50 = (bf16[1024,1152]{1,0:T(8,128)(2,1)S(1)}, bf16[1024,1152]{1,0:T(8,128)(2,1)S(1)}, u32[]{:S(2)}, u32[]{:S(2)}) collective-permute-start(bf16[1024,1152]{1,0:T(8,128)(2,1)S(1)} %slice.254), channel_id=1, source_target_pairs={{0,1},{1,0},{2,3},{3,2},{4,5},{5,4},{6,7},{7,6},{8,9},{9,8},{10,11... | collective-permute-start | bytes 7077896 | tf_op jit(solution)/shard_map/ppermute | solution.py:62
  399.7 71.7 %collective-permute-start.56 = (bf16[2,2,144,864]{3,2,1,0:T(8,128)(2,1)}, bf16[2,2,144,864]{3,2,1,0:T(8,128)(2,1)}, u32[]{:S(2)}, u32[]{:S(2)}) collective-permute-start(bf16[2,2,144,864]{3,2,1,0:T(8,128)(2,1)} %get-tuple-element.282), channel_id=1, source_target_pairs={{0,4},{4,0},{8,12},{12,8},{16,20},{20,16},{24,28},{28,24},{1,5},{5... | collective-permute-start | bytes 2985992 | tf_op jit(solution)/shard_map/ppermute | solution.py:62
  428.9 42.6 %collective-permute-start.58 = (bf16[1,216,1152]{2,1,0:T(8,128)(2,1)}, bf16[1,216,1152]{2,1,0:T(8,128)(2,1)}, u32[]{:S(2)}, u32[]{:S(2)}) collective-permute-start(bf16[1,216,1152]{2,1,0:T(8,128)(2,1)} %get-tuple-element.299), channel_id=1, source_target_pairs={{0,16},{4,20},{8,24},{12,28},{16,0},{20,4},{24,8},{28,12},{1,17},{... | collective-permute-start | bytes 1493000 | tf_op jit(solution)/shard_map/ppermute | solution.py:62
  431.4 40.1 %collective-permute-start.57 = (bf16[2,2,144,864]{3,2,1,0:T(8,128)(2,1)}, bf16[2,2,144,864]{3,2,1,0:T(8,128)(2,1)}, u32[]{:S(2)}, u32[]{:S(2)}) collective-permute-start(bf16[2,2,144,864]{3,2,1,0:T(8,128)(2,1)} %get-tuple-element.280), channel_id=1, source_target_pairs={{0,4},{4,0},{8,12},{12,8},{16,20},{20,16},{24,28},{28,24},{1,5},{5... | collective-permute-start | bytes 2985992 | tf_op jit(solution)/shard_map/ppermute | solution.py:62
  481.1 30.3 %collective-permute-start.60 = (bf16[16,40,2176]{2,1,0:T(8,128)(2,1)}, bf16[16,40,2176]{2,1,0:T(8,128)(2,1)}, u32[]{:S(2)}, u32[]{:S(2)}) collective-permute-start(bf16[16,40,2176]{2,1,0:T(8,128)(2,1)} %bitcast.149), channel_id=1, source_target_pairs={{0,1},{1,0},{2,3},{3,2},{4,5},{5,4},{6,7},{7,6},{8,9},{9,8},{10,11... | collective-permute-start | bytes 8355848 | tf_op jit(solution)/shard_map/ppermute | solution.py:68
  486.0 37.9 %collective-permute-start.62 = (bf16[2,144,864]{2,1,0:T(8,128)(2,1)}, bf16[2,144,864]{2,1,0:T(8,128)(2,1)S(1)}, u32[]{:S(2)}, u32[]{:S(2)}) collective-permute-start(bf16[2,144,864]{2,1,0:T(8,128)(2,1)} %get-tuple-element.205), channel_id=1, source_target_pairs={{0,16},{4,20},{8,24},{12,28},{16,0},{20,4},{24,8},{28,12},{1,17},{... | collective-permute-start | bytes 1493000 | tf_op jit(solution)/shard_map/ppermute | solution.py:62
  486.1 60.3 %collective-permute-start.66 = (bf16[2,144,864]{2,1,0:T(8,128)(2,1)}, bf16[2,144,864]{2,1,0:T(8,128)(2,1)}, u32[]{:S(2)}, u32[]{:S(2)}) collective-permute-start(bf16[2,144,864]{2,1,0:T(8,128)(2,1)} %get-tuple-element.208), channel_id=1, source_target_pairs={{0,16},{4,20},{8,24},{12,28},{16,0},{20,4},{24,8},{28,12},{1,17},{... | collective-permute-start | bytes 1493000 | tf_op jit(solution)/shard_map/ppermute | solution.py:62
  524.8 31.5 %collective-permute-start.64 = (bf16[256,512]{1,0:T(8,128)(2,1)S(1)}, bf16[256,512]{1,0:T(8,128)(2,1)S(1)}, u32[]{:S(2)}, u32[]{:S(2)}) collective-permute-start(bf16[256,512]{1,0:T(8,128)(2,1)S(1)} %get-tuple-element.292), channel_id=1, source_target_pairs={{0,16},{4,20},{8,24},{12,28},{16,0},{20,4},{24,8},{28,12},{1,17},{... | collective-permute-start | bytes 786440 | tf_op jit(solution)/shard_map/ppermute | solution.py:62
  524.8 31.5 %collective-permute-start.63 = (bf16[256,512]{1,0:T(8,128)(2,1)S(1)}, bf16[256,512]{1,0:T(8,128)(2,1)S(1)}, u32[]{:S(2)}, u32[]{:S(2)}) collective-permute-start(bf16[256,512]{1,0:T(8,128)(2,1)S(1)} %get-tuple-element.293), channel_id=1, source_target_pairs={{0,8},{4,12},{8,0},{12,4},{16,24},{20,28},{24,16},{28,20},{1,9},{5... | collective-permute-start | bytes 786440 | tf_op jit(solution)/shard_map/ppermute | solution.py:62
  532.8 46.9 %collective-permute-start.70 = (bf16[8,40,2176]{2,1,0:T(8,128)(2,1)}, bf16[8,40,2176]{2,1,0:T(8,128)(2,1)}, u32[]{:S(2)}, u32[]{:S(2)}) collective-permute-start(bf16[8,40,2176]{2,1,0:T(8,128)(2,1)} %slice.278), channel_id=1, source_target_pairs={{0,2},{1,3},{2,0},{3,1},{4,6},{5,7},{6,4},{7,5},{8,10},{9,11},{10,... | collective-permute-start | bytes 4177928 | tf_op jit(solution)/shard_map/ppermute | solution.py:68
  565.4 43.0 %collective-permute-start.67 = (bf16[128,1152]{1,0:T(8,128)(2,1)}, bf16[128,1152]{1,0:T(8,128)(2,1)}, u32[]{:S(2)}, u32[]{:S(2)}) collective-permute-start(bf16[128,1152]{1,0:T(8,128)(2,1)} %get-tuple-element.303), channel_id=1, source_target_pairs={{0,4},{4,0},{8,12},{12,8},{16,20},{20,16},{24,28},{28,24},{1,5},{5... | collective-permute-start | bytes 884744 | tf_op jit(solution)/shard_map/ppermute | solution.py:62
  579.4 50.6 %collective-permute-start.68 = (bf16[128,1152]{1,0:T(8,128)(2,1)}, bf16[128,1152]{1,0:T(8,128)(2,1)}, u32[]{:S(2)}, u32[]{:S(2)}) collective-permute-start(bf16[128,1152]{1,0:T(8,128)(2,1)} %get-tuple-element.301), channel_id=1, source_target_pairs={{0,4},{4,0},{8,12},{12,8},{16,20},{20,16},{24,28},{28,24},{1,5},{5... | collective-permute-start | bytes 884744 | tf_op jit(solution)/shard_map/ppermute | solution.py:62
  (152 other events, 1770.6 us)
Sparse Core Ops, SparseCore 0:
  102.2 69.1 all-gather.1

commit v9 on v6

--- a/solution.py
+++ b/solution.py
@@ -224,7 +224,7 @@
         grid=(1,),
         in_specs=[
             whole_of(picked),
-            pl.BlockSpec((deep, 2 * HEAD), lambda i: (0, HEADS // 2)),
+            whole_of(weight),
             whole_of(gain),
             whole_of(cosine),
             whole_of(sine),
@@ -548,26 +548,33 @@
     def swap_members(parts):
         return lax.all_to_all(parts, "seq", split_axis=0, concat_axis=0, tiled=True)
 
-    gain_line, at = jnp.zeros((1, wide_q + 2 * HEAD), f32), 0
+    top_id = dp_id // 4
+
+    def from_tops(piece):
+        return [piece] + [xor(piece, "dp", 4 * k) for k in range(1, tops)]
+
+    def both_sides(tall):
+        return tall + [xor(part, "dp", 1) for part in tall]
+
+    gain_line, at = jnp.zeros((1, 2 * HEAD), f32), 0
     for gain in (gain_attn_pre, gain_attn_post, gain_ffw_pre, gain_ffw_post, gain_query, gain_key):
         gain_line += jnp.pad(gain.astype(f32)[None, :], ((0, 0), (at, gain_line.shape[1] - at - gain.shape[0])))
         at += gain.shape[0]
-    shard = jnp.concatenate([w_query, w_key, w_value], axis=1)
-    shard = jnp.concatenate([shard, gain_line.astype(bf16)], axis=0)
+    shard = jnp.concatenate([jnp.concatenate([w_key, w_value], axis=1), gain_line.astype(bf16)], axis=0)
     blocks = jnp.pad(shard, ((0, block_rows - model_rows - 1), (0, 0)))[None]
+    q_blocks = jnp.pad(w_query, ((0, block_rows - model_rows), (0, 0)))[None]
     packed = pack(w_gate, w_up, tops, members, ff_rows)
-    *row_masks, y_mask, x_mask, core_mask = all_masks()
-    for masks in row_masks:
-        blocks = gather_step(blocks, *masks)
-    blocks, packed, down_piece, rows_low = together(blocks, packed, w_down[None], regroup(inputs))
+    first_mask, *more_masks, x_mask, core_mask = all_masks()
+    blocks = gather_step(blocks, *first_mask)
+    last_mask = first_mask
+    for masks in [*more_masks, x_mask]:
+        blocks, q_blocks = together(gather_step(blocks, *masks), gather_step(q_blocks, *last_mask))
+        last_mask = masks
+    blocks, packed, down_tall, rows_low = together(blocks, packed, from_tops(w_down[None]), regroup(inputs))
     rows_in = rows_low.astype(f32)
-    column_parts = column_exchange(packed)
-    blocks = gather_step(gather_step(blocks, *y_mask), *x_mask)
-    blocks, column_parts = together(blocks, column_parts)
+    q_blocks = gather_step(q_blocks, *x_mask)
     blocks = gather_step(blocks, *core_mask)
-    blocks, late_out = together(blocks, w_out)
-    qkv_weight = blocks.reshape(devices * block_rows, wide_q + 2 * HEAD)
-    out_weight = lax.all_gather(late_out, ALL, axis=0, tiled=True)
+    kv_weight = blocks.reshape(devices * block_rows, 2 * HEAD)
     labels = all_labels()
     natural = jnp.stack([(dp_id ^ d) * members + (seq_id ^ s) for d, s in labels]).astype(jnp.int32)
 
@@ -586,20 +593,11 @@
         at += size
     pre_attention, post_attention, pre_feed, post_feed, query_gain, key_gain = full_gain
 
-    top_id = dp_id // 4
-
-    def from_tops(piece):
-        return [piece] + [xor(piece, "dp", 4 * k) for k in range(1, tops)]
-
-    def both_sides(tall):
-        return tall + [xor(part, "dp", 1) for part in tall]
 
     owners = [(top_id ^ k) * 2 + (y_bit ^ u) for u in range(2) for k in range(tops)]
     owners = jnp.stack(owners).astype(jnp.int32)
     sources = [((top_id ^ k) * 2 + (z_bit ^ v)) * 2 + (y_bit ^ u) for u in range(2) for k in range(tops) for v in range(2)]
     sources = jnp.stack(sources).astype(jnp.int32)
-    down_tall = from_tops(down_piece)
-    halves = swap_members(column_parts)
 
     seq_ends = jnp.cumsum(lax.dynamic_index_in_dim(lengths, y_bit, 0, keepdims=False))
     dealt = lax.dynamic_index_in_dim(deal, y_bit, 0, keepdims=False)
@@ -629,39 +627,41 @@
     scale_one = norm_scale(rows_in)
     normed_one = (rows_in * scale_one * pre_attention).astype(bf16)
     picked_one = mm(normed_one, model_pick).astype(bf16)
-    key_raw, keys_mine = project_keys(picked_one, qkv_weight, key_gain[None], cosine, sine)
-    key_raw, down_tall, halves = together(key_raw, down_tall, halves)
-    halves = merge(halves)
+    key_raw, keys_mine = project_keys(picked_one, kv_weight, key_gain[None], cosine, sine)
     column = [keys_mine] + [xor(keys_mine, "dp", 2 * k) for k in range(1, layers)]
-    halves, others = together(halves, column[1:])
+    key_raw, packed = together(key_raw, packed)
+    column_parts = column_exchange(packed)
+    others, down_pieces, column_parts, late_out, q_blocks = together(
+        column[1:], both_sides(down_tall), column_parts, w_out, q_blocks
+    )
     column = [column[0], *others]
-    gate_tall, up_half = together(from_tops(halves[0]), halves[1])
-    up_tall = from_tops(up_half)
+    out_weight = lax.all_gather(late_out, ALL, axis=0, tiled=True)
+    halves = merge(swap_members(column_parts))
+    q_weight = gather_step(q_blocks, *core_mask).reshape(devices * block_rows, wide_q)
+    gate_tall, up_tall = from_tops(halves[0]), from_tops(halves[1])
     across = [xor(part, "seq", 2) for part in column]
-    across, down_pieces = lax.optimization_barrier((across, both_sides(down_tall)))
     column, across = jnp.stack(column), jnp.stack(across)
     near_keys = jnp.concatenate([column, across])
     far_keys = jnp.concatenate([xor(column, "seq", 1), xor(across, "seq", 1)])
-    query_raw, query_heads = project(picked_one, qkv_weight, query_gain[None], cosine, sine)
-    query_heads, gate_tall = together(query_heads, gate_tall)
-    gate_pieces = both_sides(gate_tall)
+    query_raw, query_heads = project(picked_one, q_weight, query_gain[None], cosine, sine)
     context_rows, turned, lse = attend(meta, seq_ends, slots, query_heads, near_keys, far_keys)
-    context_rows, gate_pieces, up_tall = together(context_rows, gate_pieces, up_tall)
-    up_pieces = both_sides(up_tall)
+    context_rows, gate_tall, up_tall = together(context_rows, gate_tall, up_tall)
+    gate_pieces, up_pieces = both_sides(gate_tall), both_sides(up_tall)
     down_weight = place(down_pieces, owners).reshape(ff_local, width)
-    gate_weight, up_weight = [place(pieces, sources).reshape(width, ff_local) for pieces in (gate_pieces, up_pieces)]
     attended = mm(context_rows, out_weight)
     scale_two = norm_scale(attended)
     hidden_res = rows_in + attended * scale_two * post_attention
     scale_three = norm_scale(hidden_res)
     normed_two = (hidden_res * scale_three * pre_feed).astype(bf16)
 
-    normed_group = gather_group(normed_two)
+    normed_group, up_pieces = together(gather_group(normed_two), up_pieces)
+    gate_weight, up_weight = [place(pieces, sources).reshape(width, ff_local) for pieces in (gate_pieces, up_pieces)]
     gate_raw = mm(normed_group, gate_weight)
     up_raw = mm(normed_group, up_weight)
     hidden_low = (jax.nn.gelu(gate_raw, approximate=True) * up_raw).astype(bf16)
     mixed = scatter_group(mm(hidden_low, down_weight).astype(bf16))
-    natural_weight, mixed = together(mm(model_pick, qkv_weight).astype(bf16), mixed)
+    q_natural, kv_natural = mm(model_pick, q_weight).astype(bf16), mm(model_pick, kv_weight).astype(bf16)
+    q_natural, kv_natural, mixed = together(q_natural, kv_natural, mixed)
     scale_four = norm_scale(mixed)
     result = hidden_res + mixed * scale_four * post_feed
     output = ungroup(jnp.where(valid, result, 0.0).astype(bf16))
@@ -740,7 +740,7 @@
     grad_key_gain = jnp.sum(key_turned * key_raw * key_scale, axis=0)
     key_grad = norm_back(key_raw, key_scale, key_gain * key_turned).astype(bf16)
     kv_grad = jnp.concatenate([key_grad, value_grad], axis=1)
-    normed_one_grad = mm_nt(query_grad, natural_weight[:, :wide_q]) + mm_nt(kv_grad, natural_weight[:, wide_q:])
+    normed_one_grad = mm_nt(query_grad, q_natural) + mm_nt(kv_grad, kv_natural)
     grad_pre_attention = jnp.sum(normed_one_grad * rows_in * scale_one, axis=0)
     rows_grad = hidden_res_grad + norm_back(rows_in, scale_one, pre_attention * normed_one_grad)
     rows_low, down_parts, gate_parts, up_parts = together(rows_grad.astype(bf16), down_parts, gate_parts, up_parts)

time: 630 us -> 663 us (1.052)
  waiting for transfers between devices: 256 us -> 268 us
  local copies, waits for them, and re-layouts: 59.1 us -> 70.1 us
  matrix products: 89.3 us -> 99 us
    unnamed x206 -> x197, local copies, waits for them, and re-layouts: 17.6 us -> 28 us
    dot_general x20 -> x21, matrix products: 89.3 us -> 99 us  [dot(): lax.dot_general(left, right, (dims, ((), ())), preferred_element_type=f32)]
    ppermute x15 -> x20, waiting for transfers between devices: 40.5 us -> 48.5 us  [xor_both(): lax.ppermute(value, ALL, [(i, i ^ mask) for i in range(lax.axis_size('dp'...]
    ppermute x15 -> x20, starting transfers between devices: 19.2 us -> 14.1 us  [xor_both(): lax.ppermute(value, ALL, [(i, i ^ mask) for i in range(lax.axis_size('dp'...]
  transfers between devices with their start and end apart: 78 -> 83, of which waited for: 39 -> 43; matrix products, arithmetic and copies ran while one was open for 20% -> 22% of each run, Pallas kernels for 9% -> 9%
where the time goes in v9:
time: 663 us; the launch traced here: 653 us
  waiting for transfers between devices  268 us (40%)
  matrix products  99 us (15%)
  starting transfers between devices  75 us (11%)
  local copies, waits for them, and re-layouts  70.1 us (11%)
  other arithmetic  62.3 us (9%)
  Pallas kernels  62.3 us (9%)
  between operations  15.8 us (2%)
    ppermute x59, waiting for transfers between devices, xor(): lax.ppermute(value, axis, [(i, i ^ mask) for i in range(lax.axis_size(axi...  216 us
    dot_general x21, matrix products, dot(): lax.dot_general(left, right, (dims, ((), ())), preferred_element_type=f32)  99 us
    ppermute x59, starting transfers between devices, xor(): lax.ppermute(value, axis, [(i, i ^ mask) for i in range(lax.axis_size(axi...  53.6 us
    ppermute x20, waiting for transfers between devices, xor_both(): lax.ppermute(value, ALL, [(i, i ^ mask) for i in range(lax.axis_size('dp'...  48.5 us
    unnamed x197, local copies, waits for them, and re-layouts  28 us
    pallas_call x1, Pallas kernels, attend_back(): pl.pallas_call(functools.partial(attend_back_kernel, rows), grid_spec=plt...  19.3 us
    pallas_call x1, Pallas kernels, attend(): pl.pallas_call(functools.partial(attend_kernel, rows), grid_spec=pltpu.Pr...  15.2 us
    ppermute x20, starting transfers between devices, xor_both(): lax.ppermute(value, ALL, [(i, i ^ mask) for i in range(lax.axis_size('dp'...  14.1 us
  transfers between devices with their start and end apart: 83, of which 43 were waited for; matrix products, arithmetic and copies ran while one was open for 22% of the time, Pallas kernels for 9%

profile of v9, /device:TPU:0, one launch (start us, length us, event | category | flops | bytes accessed | tf_op | source)
XLA Modules:
  0.0 652.9 jit_solution(17232606309431282803)
XLA Ops:
  21.1 20.0 %collective-permute-done.1 = bf16[2,40,512]{2,1,0:T(8,128)(2,1)S(1)} collective-permute-done((bf16[2,40,512]{2,1,0:T(8,128)(2,1)S(1)}, bf16[2,40,512]{2,1,0:T(8,128)(2,1)S(1)}, u32[]{:S(2)}, u32[]{:S(2)}) %collective-permute-start.1) | collective-permute-done | bytes 81952 | tf_op jit(solution)/shard_map/ppermute | solution.py:68
  79.5 14.4 %collective-permute-done.15 = bf16[4,2,36,864]{3,0,2,1:T(4,128)(2,1)S(1)} collective-permute-done((bf16[4,2,36,864]{3,0,2,1:T(4,128)(2,1)S(1)}, bf16[4,2,36,864]{3,0,2,1:T(4,128)(2,1)S(1)}, u32[]{:S(2)}, u32[]{:S(2)}) %collective-permute-start.15) | collective-permute-done | bytes 497696 | tf_op jit(solution)/shard_map/ppermute | solution.py:62
  127.1 9.8 %collective-permute-done.19 = bf16[2,128,512]{2,1,0:T(8,128)(2,1)S(1)} collective-permute-done((bf16[2,128,512]{2,1,0:T(8,128)(2,1)}, bf16[2,128,512]{2,1,0:T(8,128)(2,1)S(1)}, u32[]{:S(2)}, u32[]{:S(2)}) %collective-permute-start.19) | collective-permute-done | bytes 262176 | tf_op jit(solution)/shard_map/ppermute | solution.py:62
  171.1 15.2 %attend.1 = (bf16[256,1024]{1,0:T(8,128)(2,1)}, f32[2,256,512]{2,1,0:T(8,128)}, f32[2,1,512]{2,1,0:T(1,128)}) custom-call(s32[7]{0:T(128)} %pad_add_fusion.1.meta_ref, s32[4]{0:T(128)} %bitcast.328, s32[16]{0:T(128)} %gather_fusion.1, bf16[2,4,128,256]{3,2,1,0:T(8,128)(2,1)} %get-tuple-element.125.q_ref, ...), custom_call_target="tpu_custom_call" | custom-call | flops 2415919104 | bytes 4194304 | tf_op jit(solution)/shard_map/attend/pallas_call | solution.py:389
  186.3 7.0 %collective-permute-done.24.refs_1_ = bf16[2,144,864]{2,1,0:T(8,128)(2,1)} collective-permute-done((bf16[2,144,864]{2,1,0:T(8,128)(2,1)}, bf16[2,144,864]{2,1,0:T(8,128)(2,1)}, u32[]{:S(2)}, u32[]{:S(2)}) %collective-permute-start.24) | collective-permute-done | bytes 497696 | tf_op jit(solution)/shard_map/ppermute | solution.py:62
  193.4 10.7 %collective-permute-done.25.refs_1_ = bf16[2,144,864]{2,1,0:T(8,128)(2,1)S(1)} collective-permute-done((bf16[2,144,864]{2,1,0:T(8,128)(2,1)}, bf16[2,144,864]{2,1,0:T(8,128)(2,1)S(1)}, u32[]{:S(2)}, u32[]{:S(2)}) %collective-permute-start.25) | collective-permute-done | bytes 497696 | tf_op jit(solution)/shard_map/ppermute | solution.py:62
  217.6 7.9 %collective-permute-done.35.refs_2_ = bf16[2,144,864]{2,1,0:T(8,128)(2,1)} collective-permute-done((bf16[2,144,864]{2,1,0:T(8,128)(2,1)}, bf16[2,144,864]{2,1,0:T(8,128)(2,1)}, u32[]{:S(2)}, u32[]{:S(2)}) %collective-permute-start.35) | collective-permute-done | bytes 497696 | tf_op jit(solution)/shard_map/ppermute | solution.py:62
  226.1 10.5 %collective-permute-done.36.refs_3_ = bf16[2,144,864]{2,1,0:T(8,128)(2,1)} collective-permute-done((bf16[2,144,864]{2,1,0:T(8,128)(2,1)}, bf16[2,144,864]{2,1,0:T(8,128)(2,1)}, u32[]{:S(2)}, u32[]{:S(2)}) %collective-permute-start.36) | collective-permute-done | bytes 497696 | tf_op jit(solution)/shard_map/ppermute | solution.py:62
  257.5 10.1 %fusion.67 = f32[2048,864]{0,1:T(8,128)} fusion(bf16[2048,1152]{1,0:T(8,128)(2,1)} %constant_dynamic-update-slice_fusion.12, bf16[1152,864]{1,0:T(8,128)(2,1)S(1)} %bitcast.286), kind=kOutput, calls=%fused_computation.284 | convolution fusion | flops 4076863488 | bytes 13787136 | tf_op jit(solution)/shard_map/dot_general | solution.py:46
  270.9 12.4 %multiply_convert_fusion.1 = (bf16[2048,864]{0,1:T(8,128)(2,1)S(1)}, f32[2048,864]{0,1:T(8,128)}) fusion(f32[2048,864]{0,1:T(8,128)} %fusion.67, bf16[2048,1152]{1,0:T(8,128)(2,1)} %constant_dynamic-update-slice_fusion.12, bf16[1152,864]{1,0:T(8,128)(2,1)} %bitcast.288), kind=kOutput, calls=%fused_computation.14 | convolution fusion | flops 4094558208 | bytes 24403968 | tf_op jit(solution)/shard_map/dot_general | solution.py:46
  316.9 8.2 %collective-permute-done.41 = bf16[256,1152]{1,0:T(8,128)(2,1)S(1)} collective-permute-done((bf16[256,1152]{1,0:T(8,128)(2,1)S(1)}, bf16[256,1152]{1,0:T(8,128)(2,1)S(1)}, u32[]{:S(2)}, u32[]{:S(2)}) %collective-permute-start.41) | collective-permute-done | bytes 589856 | tf_op jit(solution)/shard_map/ppermute | solution.py:62
  331.7 11.2 %collective-permute-done.45 = bf16[256,1152]{1,0:T(8,128)(2,1)S(1)} collective-permute-done((bf16[256,1152]{1,0:T(8,128)(2,1)}, bf16[256,1152]{1,0:T(8,128)(2,1)S(1)}, u32[]{:S(2)}, u32[]{:S(2)}) %collective-permute-start.45) | collective-permute-done | bytes 589856 | tf_op jit(solution)/shard_map/ppermute | solution.py:62
  356.3 14.3 %multiply_convert_fusion = (bf16[2048,864]{0,1:T(8,128)(2,1)S(1)}, bf16[2048,864]{0,1:T(8,128)(2,1)}) fusion(f32[2048,864]{0,1:T(8,128)} %fusion.67, f32[2048,864]{0,1:T(8,128)} %get-tuple-element.304, bf16[2048,1152]{1,0:T(8,128)(2,1)} %constant_dynamic-update-slice_fusion.20, bf16[864,1152]{1,0:T(8,128)(2,1)S(1)} %bitcast.297), kind=kOutput, calls=%fused_computation.13 | convolution fusion | flops 4119330816 | bytes 27942912 | tf_op jit(solution)/shard_map/dot_general | solution.py:46
  370.7 8.0 %fusion.68 = f32[2048,1152]{1,0:T(8,128)} fusion(bf16[2048,864]{0,1:T(8,128)(2,1)S(1)} %get-tuple-element.157, bf16[1152,864]{1,0:T(8,128)(2,1)S(1)} %bitcast.289), kind=kOutput, calls=%fused_computation.285 | convolution fusion | flops 4076863488 | bytes 14966784 | tf_op jit(solution)/shard_map/dot_general | solution.py:46
  378.7 10.1 %add_convert_fusion = bf16[2048,1152]{1,0:T(8,128)(2,1)S(1)} fusion(f32[2048,1152]{1,0:T(8,128)} %fusion.68, bf16[2048,864]{0,1:T(8,128)(2,1)} %get-tuple-element.154, bf16[1152,864]{1,0:T(8,128)(2,1)S(1)} %bitcast.287), kind=kOutput, calls=%fused_computation.4 | convolution fusion | flops 4081582080 | bytes 19685376 | tf_op jit(solution)/shard_map/dot_general | solution.py:46
  404.2 15.9 %collective-permute-done.56 = bf16[2,1,216,1152]{3,2,1,0:T(8,128)(2,1)S(1)} collective-permute-done((bf16[2,1,216,1152]{3,2,1,0:T(8,128)(2,1)S(1)}, bf16[2,1,216,1152]{3,2,1,0:T(8,128)(2,1)S(1)}, u32[]{:S(2)}, u32[]{:S(2)}) %collective-permute-start.56) | collective-permute-done | bytes 995360 | tf_op jit(solution)/shard_map/ppermute | solution.py:62
  436.3 14.4 %collective-permute-done.55 = bf16[256,1152]{1,0:T(8,128)(2,1)S(1)} collective-permute-done((bf16[256,1152]{1,0:T(8,128)(2,1)S(1)}, bf16[256,1152]{1,0:T(8,128)(2,1)S(1)}, u32[]{:S(2)}, u32[]{:S(2)}) %collective-permute-start.55) | collective-permute-done | bytes 589856 | tf_op jit(solution)/shard_map/ppermute | solution.py:62
  459.6 19.3 %attend_back.1 = (bf16[256,1024]{1,0:T(8,128)(2,1)}, f32[1,256]{1,0:T(1,128)}, bf16[8,2,128,512]{3,2,1,0:T(8,128)(2,1)}, bf16[8,2,128,512]{3,2,1,0:T(8,128)(2,1)}) custom-call(s32[7]{0:T(128)} %pad_add_fusion.1.meta_ref, s32[4]{0:T(128)} %bitcast.329, s32[16]{0:T(128)} %gather_fusion.1, bf16[2,4,128,256]{3,2,1,0:T(8,128)(2,1)} %get-tuple-element.125.q_ref, ...), custom_call_target="tpu_custom_call" | custom-call | flops 6039797760 | bytes 8388608 | tf_op jit(solution)/shard_map/attend_back/pallas_call | solution.py:418
  502.1 11.4 %collective-permute-done.62 = bf16[4,256,512]{2,1,0:T(8,128)(2,1)} collective-permute-done((bf16[4,256,512]{2,1,0:T(8,128)(2,1)}, bf16[4,256,512]{2,1,0:T(8,128)(2,1)}, u32[]{:S(2)}, u32[]{:S(2)}) %collective-permute-start.62) | collective-permute-done | bytes 1048608 | tf_op jit(solution)/shard_map/ppermute | solution.py:62
  518.0 14.9 %collective-permute-done.63 = bf16[2,144,864]{2,1,0:T(8,128)(2,1)S(1)} collective-permute-done((bf16[2,144,864]{2,1,0:T(8,128)(2,1)S(1)}, bf16[2,144,864]{2,1,0:T(8,128)(2,1)S(1)}, u32[]{:S(2)}, u32[]{:S(2)}) %collective-permute-start.63) | collective-permute-done | bytes 497696 | tf_op jit(solution)/shard_map/ppermute | solution.py:62
  542.5 12.9 %collective-permute-done.67 = bf16[2,144,864]{2,1,0:T(8,128)(2,1)} collective-permute-done((bf16[2,144,864]{2,1,0:T(8,128)(2,1)}, bf16[2,144,864]{2,1,0:T(8,128)(2,1)}, u32[]{:S(2)}, u32[]{:S(2)}) %collective-permute-start.67) | collective-permute-done | bytes 497696 | tf_op jit(solution)/shard_map/ppermute | solution.py:62
  555.4 11.2 %collective-permute-done.65 = bf16[256,512]{1,0:T(8,128)(2,1)} collective-permute-done((bf16[256,512]{1,0:T(8,128)(2,1)}, bf16[256,512]{1,0:T(8,128)(2,1)}, u32[]{:S(2)}, u32[]{:S(2)}) %collective-permute-start.65) | collective-permute-done | bytes 262176 | tf_op jit(solution)/shard_map/ppermute | solution.py:62
  594.1 11.4 %collective-permute-done.78 = bf16[4,2,36,864]{3,0,2,1:T(4,128)(2,1)S(1)} collective-permute-done((bf16[4,2,36,864]{3,0,2,1:T(4,128)(2,1)S(1)}, bf16[4,2,36,864]{3,0,2,1:T(4,128)(2,1)S(1)}, u32[]{:S(2)}, u32[]{:S(2)}) %collective-permute-start.78) | collective-permute-done | bytes 497696 | tf_op jit(solution)/shard_map/ppermute | solution.py:62
  619.5 7.0 %collective-permute-done.71 = bf16[2,40,1024]{2,1,0:T(8,128)(2,1)S(1)} collective-permute-done((bf16[2,40,1024]{2,1,0:T(8,128)(2,1)S(1)}, bf16[2,40,1024]{2,1,0:T(8,128)(2,1)S(1)}, u32[]{:S(2)}, u32[]{:S(2)}) %collective-permute-start.71) | collective-permute-done | bytes 163872 | tf_op jit(solution)/shard_map/ppermute | solution.py:68
  (551 shorter events, 348.8 us)
Async XLA Ops:
  7.2 196.8 %all-gather.2.cloned.1.call-start = ((), (), s32[]{:S(2)}) async-start(), calls=%async_computation.3 | async-start | bytes 2433024 | tf_op jit(solution)/shard_map/all_gather | solution.py:638
  12.9 48.0 %collective-permute-start.7 = (bf16[1,216,1152]{2,1,0:T(8,128)(2,1)}, bf16[1,216,1152]{2,1,0:T(8,128)(2,1)S(1)}, u32[]{:S(2)}, u32[]{:S(2)}) collective-permute-start(bf16[1,216,1152]{2,1,0:T(8,128)(2,1)} %bitcast.305), channel_id=1, source_target_pairs={{0,16},{4,20},{8,24},{12,28},{16,0},{20,4},{24,8},{28,12},{1,17},{... | collective-permute-start | bytes 1493000 | tf_op jit(solution)/shard_map/ppermute | solution.py:62
  17.0 37.3 %collective-permute-start.8 = (bf16[128,1152]{1,0:T(8,128)(2,1)S(1)}, bf16[128,1152]{1,0:T(8,128)(2,1)S(1)}, u32[]{:S(2)}, u32[]{:S(2)}) collective-permute-start(bf16[128,1152]{1,0:T(8,128)(2,1)S(1)} %get-tuple-element.270), channel_id=1, source_target_pairs={{0,4},{4,0},{8,12},{12,8},{16,20},{20,16},{24,28},{28,24},{1,5},{5... | collective-permute-start | bytes 884744 | tf_op jit(solution)/shard_map/ppermute | solution.py:62
  110.9 41.0 %all-to-all-start = ((bf16[4,2,2,36,864]{4,2,3,1,0:T(2,128)(2,1)}), bf16[4,2,2,36,864]{4,2,3,1,0:T(2,128)(2,1)S(1)}, u32[]{:S(2)}, u32[]{:S(2)}) async-start(bf16[4,2,2,36,864]{4,2,3,1,0:T(2,128)(2,1)} %copy.75), calls=%async_computation | async-start | bytes 2064384 | tf_op jit(solution)/shard_map/all_to_all | solution.py:549
  114.4 528.0 %reduce-scatter.2.cloned.1.call-start = ((), (), s32[]{:S(2)}) async-start(), calls=%async_computation.4 | async-start | bytes 2433024 | tf_op jit(solution)/shard_map/reduce_scatter | solution.py:718
  116.8 30.8 %collective-permute-start.21 = (bf16[2,128,512]{2,1,0:T(8,128)(2,1)S(1)}, bf16[2,128,512]{2,1,0:T(8,128)(2,1)S(1)}, u32[]{:S(2)}, u32[]{:S(2)}) collective-permute-start(bf16[2,128,512]{2,1,0:T(8,128)(2,1)S(1)} %collective-permute-done.12), channel_id=1, source_target_pairs={{0,2},{1,3},{2,0},{3,1},{4,6},{5,7},{6,4},{7,5},{8,10},{9,11},{10,... | collective-permute-start | bytes 786440 | tf_op jit(solution)/shard_map/ppermute | solution.py:62
  118.7 41.8 %collective-permute-start.17 = (bf16[16,40,1024]{2,1,0:T(8,128)(2,1)S(1)}, bf16[16,40,1024]{2,1,0:T(8,128)(2,1)}, u32[]{:S(2)}, u32[]{:S(2)}) collective-permute-start(bf16[16,40,1024]{2,1,0:T(8,128)(2,1)S(1)} %pad_maximum_fusion.1), channel_id=1, source_target_pairs={{0,1},{1,0},{2,3},{3,2},{4,5},{5,4},{6,7},{7,6},{8,9},{9,8},{10,11... | collective-permute-start | bytes 3932168 | tf_op jit(solution)/shard_map/ppermute | solution.py:68
  124.9 33.3 %collective-permute-start.22 = (bf16[4,2,128,512]{3,2,1,0:T(8,128)(2,1)}, bf16[4,2,128,512]{3,2,1,0:T(8,128)(2,1)}, u32[]{:S(2)}, u32[]{:S(2)}) collective-permute-start(bf16[4,2,128,512]{3,2,1,0:T(8,128)(2,1)} %pad_maximum_fusion.4), channel_id=1, source_target_pairs={{0,1},{1,0},{2,3},{3,2},{4,5},{5,4},{6,7},{7,6},{8,9},{9,8},{10,11... | collective-permute-start | bytes 3145736 | tf_op jit(solution)/shard_map/ppermute | solution.py:62
  155.3 38.1 %collective-permute-start.24 = (bf16[2,144,864]{2,1,0:T(8,128)(2,1)}, bf16[2,144,864]{2,1,0:T(8,128)(2,1)}, u32[]{:S(2)}, u32[]{:S(2)}) collective-permute-start(bf16[2,144,864]{2,1,0:T(8,128)(2,1)} %get-tuple-element.138.refs_0_), channel_id=1, source_target_pairs={{0,16},{4,20},{8,24},{12,28},{16,0},{20,4},{24,8},{28,12},{1,17},{... | collective-permute-start | bytes 1493000 | tf_op jit(solution)/shard_map/ppermute | solution.py:62
  156.1 47.9 %collective-permute-start.25 = (bf16[2,144,864]{2,1,0:T(8,128)(2,1)}, bf16[2,144,864]{2,1,0:T(8,128)(2,1)S(1)}, u32[]{:S(2)}, u32[]{:S(2)}) collective-permute-start(bf16[2,144,864]{2,1,0:T(8,128)(2,1)} %get-tuple-element.140.refs_0_), channel_id=1, source_target_pairs={{0,16},{4,20},{8,24},{12,28},{16,0},{20,4},{24,8},{28,12},{1,17},{... | collective-permute-start | bytes 1493000 | tf_op jit(solution)/shard_map/ppermute | solution.py:62
  209.7 31.3 %collective-permute-start.26 = (bf16[256,1152]{1,0:T(8,128)(2,1)}, bf16[256,1152]{1,0:T(8,128)(2,1)S(1)}, u32[]{:S(2)}, u32[]{:S(2)}) collective-permute-start(bf16[256,1152]{1,0:T(8,128)(2,1)} %get-tuple-element.219), channel_id=1, source_target_pairs={{0,2},{1,3},{2,0},{3,1},{4,6},{5,7},{6,4},{7,5},{8,10},{9,11},{10,... | collective-permute-start | bytes 1769480 | tf_op jit(solution)/shard_map/ppermute | solution.py:62
  216.9 35.5 %collective-permute-start.33 = (bf16[2,144,864]{2,1,0:T(8,128)(2,1)}, bf16[2,144,864]{2,1,0:T(8,128)(2,1)}, u32[]{:S(2)}, u32[]{:S(2)}) collective-permute-start(bf16[2,144,864]{2,1,0:T(8,128)(2,1)} %get-tuple-element.140.refs_0_), channel_id=1, source_target_pairs={{0,4},{4,0},{8,12},{12,8},{16,20},{20,16},{24,28},{28,24},{1,5},{5... | collective-permute-start | bytes 1493000 | tf_op jit(solution)/shard_map/ppermute | solution.py:62
  225.5 32.0 %collective-permute-start.34 = (bf16[2,144,864]{2,1,0:T(8,128)(2,1)}, bf16[2,144,864]{2,1,0:T(8,128)(2,1)}, u32[]{:S(2)}, u32[]{:S(2)}) collective-permute-start(bf16[2,144,864]{2,1,0:T(8,128)(2,1)} %copy-done.40), channel_id=1, source_target_pairs={{0,4},{4,0},{8,12},{12,8},{16,20},{20,16},{24,28},{28,24},{1,5},{5... | collective-permute-start | bytes 1493000 | tf_op jit(solution)/shard_map/ppermute | solution.py:62
  292.2 33.7 %collective-permute-start.43 = (bf16[128,1152]{1,0:T(8,128)(2,1)S(1)}, bf16[128,1152]{1,0:T(8,128)(2,1)S(1)}, u32[]{:S(2)}, u32[]{:S(2)}) collective-permute-start(bf16[128,1152]{1,0:T(8,128)(2,1)S(1)} %get-tuple-element.266), channel_id=1, source_target_pairs={{0,4},{4,0},{8,12},{12,8},{16,20},{20,16},{24,28},{28,24},{1,5},{5... | collective-permute-start | bytes 884744 | tf_op jit(solution)/shard_map/ppermute | solution.py:62
  389.0 31.1 %collective-permute-start.51 = (bf16[1024,1152]{1,0:T(8,128)(2,1)S(1)}, bf16[1024,1152]{1,0:T(8,128)(2,1)S(1)}, u32[]{:S(2)}, u32[]{:S(2)}) collective-permute-start(bf16[1024,1152]{1,0:T(8,128)(2,1)S(1)} %slice.256), channel_id=1, source_target_pairs={{0,1},{1,0},{2,3},{3,2},{4,5},{5,4},{6,7},{7,6},{8,9},{9,8},{10,11... | collective-permute-start | bytes 7077896 | tf_op jit(solution)/shard_map/ppermute | solution.py:62
  403.6 75.3 %collective-permute-start.57 = (bf16[2,2,144,864]{3,2,1,0:T(8,128)(2,1)}, bf16[2,2,144,864]{3,2,1,0:T(8,128)(2,1)}, u32[]{:S(2)}, u32[]{:S(2)}) collective-permute-start(bf16[2,2,144,864]{3,2,1,0:T(8,128)(2,1)} %get-tuple-element.244), channel_id=1, source_target_pairs={{0,4},{4,0},{8,12},{12,8},{16,20},{20,16},{24,28},{28,24},{1,5},{5... | collective-permute-start | bytes 2985992 | tf_op jit(solution)/shard_map/ppermute | solution.py:62
  432.4 46.5 %collective-permute-start.59 = (bf16[1,216,1152]{2,1,0:T(8,128)(2,1)}, bf16[1,216,1152]{2,1,0:T(8,128)(2,1)}, u32[]{:S(2)}, u32[]{:S(2)}) collective-permute-start(bf16[1,216,1152]{2,1,0:T(8,128)(2,1)} %get-tuple-element.261), channel_id=1, source_target_pairs={{0,16},{4,20},{8,24},{12,28},{16,0},{20,4},{24,8},{28,12},{1,17},{... | collective-permute-start | bytes 1493000 | tf_op jit(solution)/shard_map/ppermute | solution.py:62
  435.5 43.5 %collective-permute-start.58 = (bf16[2,2,144,864]{3,2,1,0:T(8,128)(2,1)}, bf16[2,2,144,864]{3,2,1,0:T(8,128)(2,1)}, u32[]{:S(2)}, u32[]{:S(2)}) collective-permute-start(bf16[2,2,144,864]{3,2,1,0:T(8,128)(2,1)} %get-tuple-element.242), channel_id=1, source_target_pairs={{0,4},{4,0},{8,12},{12,8},{16,20},{20,16},{24,28},{28,24},{1,5},{5... | collective-permute-start | bytes 2985992 | tf_op jit(solution)/shard_map/ppermute | solution.py:62
  491.3 47.1 %collective-permute-start.42 = (bf16[128,1152]{1,0:T(8,128)(2,1)}, bf16[128,1152]{1,0:T(8,128)(2,1)S(1)}, u32[]{:S(2)}, u32[]{:S(2)}) collective-permute-start(bf16[128,1152]{1,0:T(8,128)(2,1)} %get-tuple-element.267), channel_id=1, source_target_pairs={{0,4},{4,0},{8,12},{12,8},{16,20},{20,16},{24,28},{28,24},{1,5},{5... | collective-permute-start | bytes 884744 | tf_op jit(solution)/shard_map/ppermute | solution.py:62
  496.6 36.3 %collective-permute-start.63 = (bf16[2,144,864]{2,1,0:T(8,128)(2,1)S(1)}, bf16[2,144,864]{2,1,0:T(8,128)(2,1)S(1)}, u32[]{:S(2)}, u32[]{:S(2)}) collective-permute-start(bf16[2,144,864]{2,1,0:T(8,128)(2,1)S(1)} %get-tuple-element.259), channel_id=1, source_target_pairs={{0,16},{4,20},{8,24},{12,28},{16,0},{20,4},{24,8},{28,12},{1,17},{... | collective-permute-start | bytes 1493000 | tf_op jit(solution)/shard_map/ppermute | solution.py:62
  501.7 53.7 %collective-permute-start.67 = (bf16[2,144,864]{2,1,0:T(8,128)(2,1)}, bf16[2,144,864]{2,1,0:T(8,128)(2,1)}, u32[]{:S(2)}, u32[]{:S(2)}) collective-permute-start(bf16[2,144,864]{2,1,0:T(8,128)(2,1)} %get-tuple-element.257), channel_id=1, source_target_pairs={{0,16},{4,20},{8,24},{12,28},{16,0},{20,4},{24,8},{28,12},{1,17},{... | collective-permute-start | bytes 1493000 | tf_op jit(solution)/shard_map/ppermute | solution.py:62
  534.7 31.9 %collective-permute-start.65 = (bf16[256,512]{1,0:T(8,128)(2,1)}, bf16[256,512]{1,0:T(8,128)(2,1)}, u32[]{:S(2)}, u32[]{:S(2)}) collective-permute-start(bf16[256,512]{1,0:T(8,128)(2,1)} %get-tuple-element.254), channel_id=1, source_target_pairs={{0,16},{4,20},{8,24},{12,28},{16,0},{20,4},{24,8},{28,12},{1,17},{... | collective-permute-start | bytes 786440 | tf_op jit(solution)/shard_map/ppermute | solution.py:62
  534.7 31.9 %collective-permute-start.64 = (bf16[256,512]{1,0:T(8,128)(2,1)}, bf16[256,512]{1,0:T(8,128)(2,1)}, u32[]{:S(2)}, u32[]{:S(2)}) collective-permute-start(bf16[256,512]{1,0:T(8,128)(2,1)} %get-tuple-element.255), channel_id=1, source_target_pairs={{0,8},{4,12},{8,0},{12,4},{16,24},{20,28},{24,16},{28,20},{1,9},{5... | collective-permute-start | bytes 786440 | tf_op jit(solution)/shard_map/ppermute | solution.py:62
  542.5 48.5 %collective-permute-start.69 = (bf16[8,40,1024]{2,1,0:T(8,128)(2,1)}, bf16[8,40,1024]{2,1,0:T(8,128)(2,1)}, u32[]{:S(2)}, u32[]{:S(2)}) collective-permute-start(bf16[8,40,1024]{2,1,0:T(8,128)(2,1)} %slice.276), channel_id=1, source_target_pairs={{0,2},{1,3},{2,0},{3,1},{4,6},{5,7},{6,4},{7,5},{8,10},{9,11},{10,... | collective-permute-start | bytes 1966088 | tf_op jit(solution)/shard_map/ppermute | solution.py:68
  (146 other events, 1935.9 us)
Sparse Core Ops, SparseCore 0:
  104.0 80.0 all-gather.1
  540.9 101.4 reduce-scatter.1

commit v10 on v6

--- a/solution.py
+++ b/solution.py
@@ -559,11 +559,9 @@
     *row_masks, y_mask, x_mask, core_mask = all_masks()
     for masks in row_masks:
         blocks = gather_step(blocks, *masks)
-    blocks, packed, down_piece, rows_low = together(blocks, packed, w_down[None], regroup(inputs))
+    blocks, rows_low = together(blocks, regroup(inputs))
     rows_in = rows_low.astype(f32)
-    column_parts = column_exchange(packed)
     blocks = gather_step(gather_step(blocks, *y_mask), *x_mask)
-    blocks, column_parts = together(blocks, column_parts)
     blocks = gather_step(blocks, *core_mask)
     blocks, late_out = together(blocks, w_out)
     qkv_weight = blocks.reshape(devices * block_rows, wide_q + 2 * HEAD)
@@ -598,8 +596,6 @@
     owners = jnp.stack(owners).astype(jnp.int32)
     sources = [((top_id ^ k) * 2 + (z_bit ^ v)) * 2 + (y_bit ^ u) for u in range(2) for k in range(tops) for v in range(2)]
     sources = jnp.stack(sources).astype(jnp.int32)
-    down_tall = from_tops(down_piece)
-    halves = swap_members(column_parts)
 
     seq_ends = jnp.cumsum(lax.dynamic_index_in_dim(lengths, y_bit, 0, keepdims=False))
     dealt = lax.dynamic_index_in_dim(deal, y_bit, 0, keepdims=False)
@@ -630,33 +626,33 @@
     normed_one = (rows_in * scale_one * pre_attention).astype(bf16)
     picked_one = mm(normed_one, model_pick).astype(bf16)
     key_raw, keys_mine = project_keys(picked_one, qkv_weight, key_gain[None], cosine, sine)
-    key_raw, down_tall, halves = together(key_raw, down_tall, halves)
-    halves = merge(halves)
+    key_raw, packed = together(key_raw, packed)
     column = [keys_mine] + [xor(keys_mine, "dp", 2 * k) for k in range(1, layers)]
-    halves, others = together(halves, column[1:])
+    others, column_parts, down_piece = together(column[1:], column_exchange(packed), w_down[None])
     column = [column[0], *others]
-    gate_tall, up_half = together(from_tops(halves[0]), halves[1])
-    up_tall = from_tops(up_half)
+    down_tall = from_tops(down_piece)
+    halves = merge(swap_members(column_parts))
+    gate_tall, up_tall = from_tops(halves[0]), from_tops(halves[1])
     across = [xor(part, "seq", 2) for part in column]
-    across, down_pieces = lax.optimization_barrier((across, both_sides(down_tall)))
+    down_pieces = both_sides(down_tall)
     column, across = jnp.stack(column), jnp.stack(across)
     near_keys = jnp.concatenate([column, across])
     far_keys = jnp.concatenate([xor(column, "seq", 1), xor(across, "seq", 1)])
     query_raw, query_heads = project(picked_one, qkv_weight, query_gain[None], cosine, sine)
-    query_heads, gate_tall = together(query_heads, gate_tall)
+    context_rows, turned, lse = attend(meta, seq_ends, slots, query_heads, near_keys, far_keys)
+    context_rows, gate_tall = together(context_rows, gate_tall)
     gate_pieces = both_sides(gate_tall)
-    context_rows, turned, lse = attend(meta, seq_ends, slots, query_heads, near_keys, far_keys)
-    context_rows, gate_pieces, up_tall = together(context_rows, gate_pieces, up_tall)
-    up_pieces = both_sides(up_tall)
     down_weight = place(down_pieces, owners).reshape(ff_local, width)
-    gate_weight, up_weight = [place(pieces, sources).reshape(width, ff_local) for pieces in (gate_pieces, up_pieces)]
     attended = mm(context_rows, out_weight)
     scale_two = norm_scale(attended)
     hidden_res = rows_in + attended * scale_two * post_attention
     scale_three = norm_scale(hidden_res)
     normed_two = (hidden_res * scale_three * pre_feed).astype(bf16)
 
-    normed_group = gather_group(normed_two)
+    normed_two, up_tall = together(normed_two, up_tall)
+    up_pieces = both_sides(up_tall)
+    normed_group, gate_pieces, up_pieces = together(gather_group(normed_two), gate_pieces, up_pieces)
+    gate_weight, up_weight = [place(pieces, sources).reshape(width, ff_local) for pieces in (gate_pieces, up_pieces)]
     gate_raw = mm(normed_group, gate_weight)
     up_raw = mm(normed_group, up_weight)
     hidden_low = (jax.nn.gelu(gate_raw, approximate=True) * up_raw).astype(bf16)

time: 630 us -> 677 us (1.075)
  waiting for transfers between devices: 256 us -> 277 us
  starting transfers between devices: 77 us -> 90.6 us
  local copies, waits for them, and re-layouts: 59.1 us -> 66.6 us
  matrix products: 89.3 us -> 96.6 us
    ppermute x59, starting transfers between devices: 50.7 us -> 66.9 us  [xor(): lax.ppermute(value, axis, [(i, i ^ mask) for i in range(lax.axis_size(axi...]
    ppermute x59, waiting for transfers between devices: 216 us -> 226 us  [xor(): lax.ppermute(value, axis, [(i, i ^ mask) for i in range(lax.axis_size(axi...]
    ppermute x15, waiting for transfers between devices: 40.5 us -> 48.9 us  [xor_both(): lax.ppermute(value, ALL, [(i, i ^ mask) for i in range(lax.axis_size('dp'...]
    dot_general x20, matrix products: 89.3 us -> 96.6 us  [dot(): lax.dot_general(left, right, (dims, ((), ())), preferred_element_type=f32)]
    unnamed x206 -> x209, local copies, waits for them, and re-layouts: 17.6 us -> 22.2 us
  transfers between devices with their start and end apart: 78 -> 78, of which waited for: 39 -> 42; matrix products, arithmetic and copies ran while one was open for 20% -> 21% of each run, Pallas kernels for 9% -> 7%
where the time goes in v10:
time: 677 us; the launch traced here: 667 us
  waiting for transfers between devices  277 us (41%)
  matrix products  96.6 us (14%)
  starting transfers between devices  90.6 us (13%)
  local copies, waits for them, and re-layouts  66.6 us (10%)
  other arithmetic  64.2 us (9%)
  Pallas kernels  56.1 us (8%)
  between operations  15.8 us (2%)
    ppermute x59, waiting for transfers between devices, xor(): lax.ppermute(value, axis, [(i, i ^ mask) for i in range(lax.axis_size(axi...  226 us
    dot_general x20, matrix products, dot(): lax.dot_general(left, right, (dims, ((), ())), preferred_element_type=f32)  96.6 us
    ppermute x59, starting transfers between devices, xor(): lax.ppermute(value, axis, [(i, i ^ mask) for i in range(lax.axis_size(axi...  66.9 us
    ppermute x15, waiting for transfers between devices, xor_both(): lax.ppermute(value, ALL, [(i, i ^ mask) for i in range(lax.axis_size('dp'...  48.9 us
    unnamed x209, local copies, waits for them, and re-layouts  22.2 us
    ppermute x15, starting transfers between devices, xor_both(): lax.ppermute(value, ALL, [(i, i ^ mask) for i in range(lax.axis_size('dp'...  16.4 us
    pallas_call x1, Pallas kernels, attend_back(): pl.pallas_call(functools.partial(attend_back_kernel, rows), grid_spec=plt...  16.4 us
  transfers between devices with their start and end apart: 78, of which 42 were waited for; matrix products, arithmetic and copies ran while one was open for 21% of the time, Pallas kernels for 7%

profile of v10, /device:TPU:0, one launch (start us, length us, event | category | flops | bytes accessed | tf_op | source)
XLA Modules:
  0.0 666.8 jit_solution(16177859313361677139)
XLA Ops:
  21.8 7.0 %collective-permute-done.1 = bf16[2,40,1536]{2,1,0:T(8,128)(2,1)S(1)} collective-permute-done((bf16[2,40,1536]{2,1,0:T(8,128)(2,1)S(1)}, bf16[2,40,1536]{2,1,0:T(8,128)(2,1)S(1)}, u32[]{:S(2)}, u32[]{:S(2)}) %collective-permute-start.1) | collective-permute-done | bytes 245792 | tf_op jit(solution)/shard_map/ppermute | solution.py:68
  30.4 10.8 %collective-permute-done.3 = bf16[4,40,1536]{2,1,0:T(8,128)(2,1)S(1)} collective-permute-done((bf16[4,40,1536]{2,1,0:T(8,128)(2,1)S(1)}, bf16[4,40,1536]{2,1,0:T(8,128)(2,1)S(1)}, u32[]{:S(2)}, u32[]{:S(2)}) %collective-permute-start.3) | collective-permute-done | bytes 491552 | tf_op jit(solution)/shard_map/ppermute | solution.py:68
  44.5 19.8 %collective-permute-done.4 = bf16[8,40,1536]{2,1,0:T(8,128)(2,1)S(1)} collective-permute-done((bf16[8,40,1536]{2,1,0:T(8,128)(2,1)}, bf16[8,40,1536]{2,1,0:T(8,128)(2,1)S(1)}, u32[]{:S(2)}, u32[]{:S(2)}) %collective-permute-start.4) | collective-permute-done | bytes 983072 | tf_op jit(solution)/shard_map/ppermute | solution.py:68
  101.0 9.9 %collective-permute-done.9 = bf16[4,2,36,864]{3,0,2,1:T(4,128)(2,1)} collective-permute-done((bf16[4,2,36,864]{3,0,2,1:T(4,128)(2,1)}, bf16[4,2,36,864]{3,0,2,1:T(4,128)(2,1)}, u32[]{:S(2)}, u32[]{:S(2)}) %collective-permute-start.9) | collective-permute-done | bytes 497696 | tf_op jit(solution)/shard_map/ppermute | solution.py:62
  140.6 9.8 %collective-permute-done.11 = bf16[2,128,512]{2,1,0:T(8,128)(2,1)S(1)} collective-permute-done((bf16[2,128,512]{2,1,0:T(8,128)(2,1)}, bf16[2,128,512]{2,1,0:T(8,128)(2,1)S(1)}, u32[]{:S(2)}, u32[]{:S(2)}) %collective-permute-start.11) | collective-permute-done | bytes 262176 | tf_op jit(solution)/shard_map/ppermute | solution.py:62
  177.7 12.2 %attend.1 = (bf16[256,1024]{1,0:T(8,128)(2,1)}, f32[2,256,512]{2,1,0:T(8,128)}, f32[2,1,512]{2,1,0:T(1,128)}) custom-call(s32[7]{0:T(128)} %pad_add_fusion.1.meta_ref, s32[4]{0:T(128)} %bitcast.320, s32[16]{0:T(128)} %gather_fusion.1, bf16[2,4,128,256]{3,2,1,0:T(8,128)(2,1)} %get-tuple-element.105.q_ref, ...), custom_call_target="tpu_custom_call" | custom-call | flops 2415919104 | bytes 4194304 | tf_op jit(solution)/shard_map/attend/pallas_call | solution.py:389
  189.9 18.7 %collective-permute-done.16.refs_1_ = bf16[2,144,864]{2,1,0:T(8,128)(2,1)S(1)} collective-permute-done((bf16[2,144,864]{2,1,0:T(8,128)(2,1)}, bf16[2,144,864]{2,1,0:T(8,128)(2,1)S(1)}, u32[]{:S(2)}, u32[]{:S(2)}) %collective-permute-start.16) | collective-permute-done | bytes 497696 | tf_op jit(solution)/shard_map/ppermute | solution.py:62
  227.5 6.9 %collective-permute-done.19 = bf16[256,1152]{1,0:T(8,128)(2,1)S(1)} collective-permute-done((bf16[256,1152]{1,0:T(8,128)(2,1)}, bf16[256,1152]{1,0:T(8,128)(2,1)S(1)}, u32[]{:S(2)}, u32[]{:S(2)}) %collective-permute-start.19) | collective-permute-done | bytes 589856 | tf_op jit(solution)/shard_map/ppermute | solution.py:62
  249.7 11.1 %collective-permute-done.27.refs_2_ = bf16[2,144,864]{2,1,0:T(8,128)(2,1)S(1)} collective-permute-done((bf16[2,144,864]{2,1,0:T(8,128)(2,1)S(1)}, bf16[2,144,864]{2,1,0:T(8,128)(2,1)S(1)}, u32[]{:S(2)}, u32[]{:S(2)}) %collective-permute-start.27) | collective-permute-done | bytes 497696 | tf_op jit(solution)/shard_map/ppermute | solution.py:62
  260.8 9.7 %collective-permute-done.28.refs_3_ = bf16[2,144,864]{2,1,0:T(8,128)(2,1)S(1)} collective-permute-done((bf16[2,144,864]{2,1,0:T(8,128)(2,1)}, bf16[2,144,864]{2,1,0:T(8,128)(2,1)S(1)}, u32[]{:S(2)}, u32[]{:S(2)}) %collective-permute-start.28) | collective-permute-done | bytes 497696 | tf_op jit(solution)/shard_map/ppermute | solution.py:62
  273.7 10.8 %fusion.66 = f32[2048,864]{0,1:T(8,128)} fusion(bf16[2048,1152]{1,0:T(8,128)(2,1)} %copy-done.54, bf16[1152,864]{1,0:T(8,128)(2,1)} %bitcast.279), kind=kOutput, calls=%fused_computation.277 | convolution fusion | flops 4076863488 | bytes 13787136 | tf_op jit(solution)/shard_map/dot_general | solution.py:46
  287.7 12.4 %multiply_convert_fusion.1 = (bf16[2048,864]{0,1:T(8,128)(2,1)S(1)}, f32[2048,864]{0,1:T(8,128)}) fusion(f32[2048,864]{0,1:T(8,128)} %fusion.66, bf16[2048,1152]{1,0:T(8,128)(2,1)} %copy-done.54, bf16[1152,864]{1,0:T(8,128)(2,1)} %bitcast.281), kind=kOutput, calls=%fused_computation.15 | convolution fusion | flops 4094558208 | bytes 24403968 | tf_op jit(solution)/shard_map/dot_general | solution.py:46
  348.6 10.3 %collective-permute-done.40 = bf16[256,1152]{1,0:T(8,128)(2,1)S(1)} collective-permute-done((bf16[256,1152]{1,0:T(8,128)(2,1)}, bf16[256,1152]{1,0:T(8,128)(2,1)S(1)}, u32[]{:S(2)}, u32[]{:S(2)}) %collective-permute-start.40) | collective-permute-done | bytes 589856 | tf_op jit(solution)/shard_map/ppermute | solution.py:62
  372.7 13.3 %multiply_convert_fusion = (bf16[2048,864]{0,1:T(8,128)(2,1)S(1)}, bf16[2048,864]{0,1:T(8,128)(2,1)S(1)}) fusion(f32[2048,864]{0,1:T(8,128)} %fusion.66, f32[2048,864]{0,1:T(8,128)} %get-tuple-element.286, bf16[2048,1152]{1,0:T(8,128)(2,1)} %constant_dynamic-update-slice_fusion.18, bf16[864,1152]{1,0:T(8,128)(2,1)S(1)} %bitcast.290), kind=kOutput, calls=%fused_computation.14 | convolution fusion | flops 4119330816 | bytes 27942912 | tf_op jit(solution)/shard_map/dot_general | solution.py:46
  386.0 8.0 %fusion.67 = f32[2048,1152]{1,0:T(8,128)} fusion(bf16[2048,864]{0,1:T(8,128)(2,1)S(1)} %get-tuple-element.139, bf16[1152,864]{1,0:T(8,128)(2,1)S(1)} %bitcast.280), kind=kOutput, calls=%fused_computation.278 | convolution fusion | flops 4076863488 | bytes 14966784 | tf_op jit(solution)/shard_map/dot_general | solution.py:46
  394.0 8.3 %add_convert_fusion = bf16[2048,1152]{1,0:T(8,128)(2,1)S(1)} fusion(f32[2048,1152]{1,0:T(8,128)} %fusion.67, bf16[2048,864]{0,1:T(8,128)(2,1)S(1)} %get-tuple-element.142, bf16[1152,864]{1,0:T(8,128)(2,1)S(1)} %bitcast.282), kind=kOutput, calls=%fused_computation.4 | convolution fusion | flops 4081582080 | bytes 19685376 | tf_op jit(solution)/shard_map/dot_general | solution.py:46
  417.6 16.1 %collective-permute-done.51 = bf16[2,1,216,1152]{3,2,1,0:T(8,128)(2,1)S(1)} collective-permute-done((bf16[2,1,216,1152]{3,2,1,0:T(8,128)(2,1)S(1)}, bf16[2,1,216,1152]{3,2,1,0:T(8,128)(2,1)S(1)}, u32[]{:S(2)}, u32[]{:S(2)}) %collective-permute-start.51) | collective-permute-done | bytes 995360 | tf_op jit(solution)/shard_map/ppermute | solution.py:62
  451.5 13.8 %collective-permute-done.50 = bf16[256,1152]{1,0:T(8,128)(2,1)S(1)} collective-permute-done((bf16[256,1152]{1,0:T(8,128)(2,1)S(1)}, bf16[256,1152]{1,0:T(8,128)(2,1)S(1)}, u32[]{:S(2)}, u32[]{:S(2)}) %collective-permute-start.50) | collective-permute-done | bytes 589856 | tf_op jit(solution)/shard_map/ppermute | solution.py:62
  474.1 16.4 %attend_back.1 = (bf16[256,1024]{1,0:T(8,128)(2,1)}, f32[1,256]{1,0:T(1,128)}, bf16[8,2,128,512]{3,2,1,0:T(8,128)(2,1)}, bf16[8,2,128,512]{3,2,1,0:T(8,128)(2,1)}) custom-call(s32[7]{0:T(128)} %pad_add_fusion.1.meta_ref, s32[4]{0:T(128)} %bitcast.321, s32[16]{0:T(128)} %gather_fusion.1, bf16[2,4,128,256]{3,2,1,0:T(8,128)(2,1)} %get-tuple-element.105.q_ref, ...), custom_call_target="tpu_custom_call" | custom-call | flops 6039797760 | bytes 8388608 | tf_op jit(solution)/shard_map/attend_back/pallas_call | solution.py:418
  516.4 9.7 %collective-permute-done.57 = bf16[4,256,512]{2,1,0:T(8,128)(2,1)} collective-permute-done((bf16[4,256,512]{2,1,0:T(8,128)(2,1)}, bf16[4,256,512]{2,1,0:T(8,128)(2,1)}, u32[]{:S(2)}, u32[]{:S(2)}) %collective-permute-start.57) | collective-permute-done | bytes 1048608 | tf_op jit(solution)/shard_map/ppermute | solution.py:62
  530.6 15.8 %collective-permute-done.58 = bf16[2,144,864]{2,1,0:T(8,128)(2,1)S(1)} collective-permute-done((bf16[2,144,864]{2,1,0:T(8,128)(2,1)S(1)}, bf16[2,144,864]{2,1,0:T(8,128)(2,1)S(1)}, u32[]{:S(2)}, u32[]{:S(2)}) %collective-permute-start.58) | collective-permute-done | bytes 497696 | tf_op jit(solution)/shard_map/ppermute | solution.py:62
  555.9 12.9 %collective-permute-done.62 = bf16[2,144,864]{2,1,0:T(8,128)(2,1)} collective-permute-done((bf16[2,144,864]{2,1,0:T(8,128)(2,1)}, bf16[2,144,864]{2,1,0:T(8,128)(2,1)}, u32[]{:S(2)}, u32[]{:S(2)}) %collective-permute-start.62) | collective-permute-done | bytes 497696 | tf_op jit(solution)/shard_map/ppermute | solution.py:62
  568.8 11.2 %collective-permute-done.60 = bf16[256,512]{1,0:T(8,128)(2,1)} collective-permute-done((bf16[256,512]{1,0:T(8,128)(2,1)}, bf16[256,512]{1,0:T(8,128)(2,1)}, u32[]{:S(2)}, u32[]{:S(2)}) %collective-permute-start.60) | collective-permute-done | bytes 262176 | tf_op jit(solution)/shard_map/ppermute | solution.py:62
  611.0 10.5 %collective-permute-done.73 = bf16[4,2,36,864]{3,0,2,1:T(4,128)(2,1)S(1)} collective-permute-done((bf16[4,2,36,864]{3,0,2,1:T(4,128)(2,1)S(1)}, bf16[4,2,36,864]{3,0,2,1:T(4,128)(2,1)S(1)}, u32[]{:S(2)}, u32[]{:S(2)}) %collective-permute-start.73) | collective-permute-done | bytes 497696 | tf_op jit(solution)/shard_map/ppermute | solution.py:62
  (546 shorter events, 365.5 us)
Async XLA Ops:
  7.2 201.4 %all-gather.2.cloned.1.call-start = ((), (), s32[]{:S(2)}) async-start(), calls=%async_computation.3 | async-start | bytes 2433024 | tf_op jit(solution)/shard_map/all_gather | solution.py:568
  84.3 26.7 %collective-permute-start.9 = (bf16[4,2,36,864]{3,0,2,1:T(4,128)(2,1)}, bf16[4,2,36,864]{3,0,2,1:T(4,128)(2,1)}, u32[]{:S(2)}, u32[]{:S(2)}) collective-permute-start(bf16[4,2,36,864]{3,0,2,1:T(4,128)(2,1)} %copy.73), channel_id=1, source_target_pairs={{0,8},{4,12},{8,0},{12,4},{16,24},{20,28},{24,16},{28,20},{1,9},{5... | collective-permute-start | bytes 1493000 | tf_op jit(solution)/shard_map/ppermute | solution.py:62
  88.4 48.5 %collective-permute-start.10 = (bf16[2,128,512]{2,1,0:T(8,128)(2,1)S(1)}, bf16[2,128,512]{2,1,0:T(8,128)(2,1)S(1)}, u32[]{:S(2)}, u32[]{:S(2)}) collective-permute-start(bf16[2,128,512]{2,1,0:T(8,128)(2,1)S(1)} %copy-done.32), channel_id=1, source_target_pairs={{0,2},{1,3},{2,0},{3,1},{4,6},{5,7},{6,4},{7,5},{8,10},{9,11},{10,... | collective-permute-start | bytes 786440 | tf_op jit(solution)/shard_map/ppermute | solution.py:62
  92.7 27.4 %collective-permute-start.7 = (bf16[2,128,512]{2,1,0:T(8,128)(2,1)S(1)}, bf16[2,128,512]{2,1,0:T(8,128)(2,1)S(1)}, u32[]{:S(2)}, u32[]{:S(2)}) collective-permute-start(bf16[2,128,512]{2,1,0:T(8,128)(2,1)S(1)} %copy-done.32), channel_id=1, source_target_pairs={{0,16},{4,20},{8,24},{12,28},{16,0},{20,4},{24,8},{28,12},{1,17},{... | collective-permute-start | bytes 786440 | tf_op jit(solution)/shard_map/ppermute | solution.py:62
  93.3 27.3 %collective-permute-start.6 = (bf16[2,128,512]{2,1,0:T(8,128)(2,1)S(1)}, bf16[2,128,512]{2,1,0:T(8,128)(2,1)S(1)}, u32[]{:S(2)}, u32[]{:S(2)}) collective-permute-start(bf16[2,128,512]{2,1,0:T(8,128)(2,1)S(1)} %copy-done.32), channel_id=1, source_target_pairs={{0,8},{4,12},{8,0},{12,4},{16,24},{20,28},{24,16},{28,20},{1,9},{5... | collective-permute-start | bytes 786440 | tf_op jit(solution)/shard_map/ppermute | solution.py:62
  122.2 44.4 %all-to-all-start = ((bf16[4,2,2,36,864]{4,2,3,1,0:T(2,128)(2,1)}), bf16[4,2,2,36,864]{4,2,3,1,0:T(2,128)(2,1)S(1)}, u32[]{:S(2)}, u32[]{:S(2)}) async-start(bf16[4,2,2,36,864]{4,2,3,1,0:T(2,128)(2,1)} %copy.75), calls=%async_computation | async-start | bytes 2064384 | tf_op jit(solution)/shard_map/all_to_all | solution.py:549
  125.8 530.6 %reduce-scatter.2.cloned.1.call-start = ((), (), s32[]{:S(2)}) async-start(), calls=%async_computation.4 | async-start | bytes 2433024 | tf_op jit(solution)/shard_map/reduce_scatter | solution.py:714
  128.0 28.0 %collective-permute-start.12 = (bf16[2,128,512]{2,1,0:T(8,128)(2,1)}, bf16[2,128,512]{2,1,0:T(8,128)(2,1)S(1)}, u32[]{:S(2)}, u32[]{:S(2)}) collective-permute-start(bf16[2,128,512]{2,1,0:T(8,128)(2,1)} %copy-done.35), channel_id=1, source_target_pairs={{0,2},{1,3},{2,0},{3,1},{4,6},{5,7},{6,4},{7,5},{8,10},{9,11},{10,... | collective-permute-start | bytes 786440 | tf_op jit(solution)/shard_map/ppermute | solution.py:62
  128.1 32.9 %collective-permute-start.13 = (bf16[2,128,512]{2,1,0:T(8,128)(2,1)}, bf16[2,128,512]{2,1,0:T(8,128)(2,1)S(1)}, u32[]{:S(2)}, u32[]{:S(2)}) collective-permute-start(bf16[2,128,512]{2,1,0:T(8,128)(2,1)} %copy-done.33), channel_id=1, source_target_pairs={{0,2},{1,3},{2,0},{3,1},{4,6},{5,7},{6,4},{7,5},{8,10},{9,11},{10,... | collective-permute-start | bytes 786440 | tf_op jit(solution)/shard_map/ppermute | solution.py:62
  130.1 91.2 %collective-permute-start.30 = (bf16[1,216,1152]{2,1,0:T(8,128)(2,1)}, bf16[1,216,1152]{2,1,0:T(8,128)(2,1)}, u32[]{:S(2)}, u32[]{:S(2)}) collective-permute-start(bf16[1,216,1152]{2,1,0:T(8,128)(2,1)} %bitcast.106.refs_0_), channel_id=1, source_target_pairs={{0,4},{4,0},{8,12},{12,8},{16,20},{20,16},{24,28},{28,24},{1,5},{5... | collective-permute-start | bytes 1493000 | tf_op jit(solution)/shard_map/ppermute | solution.py:62
  136.9 28.1 %collective-permute-start.29 = (bf16[1,216,1152]{2,1,0:T(8,128)(2,1)}, bf16[1,216,1152]{2,1,0:T(8,128)(2,1)}, u32[]{:S(2)}, u32[]{:S(2)}) collective-permute-start(bf16[1,216,1152]{2,1,0:T(8,128)(2,1)} %bitcast.106.refs_0_), channel_id=1, source_target_pairs={{0,16},{4,20},{8,24},{12,28},{16,0},{20,4},{24,8},{28,12},{1,17},{... | collective-permute-start | bytes 1493000 | tf_op jit(solution)/shard_map/ppermute | solution.py:62
  165.1 56.2 %collective-permute-start.31 = (bf16[1,216,1152]{2,1,0:T(8,128)(2,1)}, bf16[1,216,1152]{2,1,0:T(8,128)(2,1)}, u32[]{:S(2)}, u32[]{:S(2)}) collective-permute-start(bf16[1,216,1152]{2,1,0:T(8,128)(2,1)} %collective-permute-done.29.refs_1_), channel_id=1, source_target_pairs={{0,4},{4,0},{8,12},{12,8},{16,20},{20,16},{24,28},{28,24},{1,5},{5... | collective-permute-start | bytes 1493000 | tf_op jit(solution)/shard_map/ppermute | solution.py:62
  170.0 38.6 %collective-permute-start.16 = (bf16[2,144,864]{2,1,0:T(8,128)(2,1)}, bf16[2,144,864]{2,1,0:T(8,128)(2,1)S(1)}, u32[]{:S(2)}, u32[]{:S(2)}) collective-permute-start(bf16[2,144,864]{2,1,0:T(8,128)(2,1)} %get-tuple-element.124.refs_0_), channel_id=1, source_target_pairs={{0,16},{4,20},{8,24},{12,28},{16,0},{20,4},{24,8},{28,12},{1,17},{... | collective-permute-start | bytes 1493000 | tf_op jit(solution)/shard_map/ppermute | solution.py:62
  173.7 45.6 %collective-permute-start.17 = (bf16[2,144,864]{2,1,0:T(8,128)(2,1)}, bf16[2,144,864]{2,1,0:T(8,128)(2,1)}, u32[]{:S(2)}, u32[]{:S(2)}) collective-permute-start(bf16[2,144,864]{2,1,0:T(8,128)(2,1)} %get-tuple-element.128.refs_0_), channel_id=1, source_target_pairs={{0,16},{4,20},{8,24},{12,28},{16,0},{20,4},{24,8},{28,12},{1,17},{... | collective-permute-start | bytes 1493000 | tf_op jit(solution)/shard_map/ppermute | solution.py:62
  402.6 31.1 %collective-permute-start.46 = (bf16[1024,1152]{1,0:T(8,128)(2,1)S(1)}, bf16[1024,1152]{1,0:T(8,128)(2,1)S(1)}, u32[]{:S(2)}, u32[]{:S(2)}) collective-permute-start(bf16[1024,1152]{1,0:T(8,128)(2,1)S(1)} %slice.262), channel_id=1, source_target_pairs={{0,1},{1,0},{2,3},{3,2},{4,5},{5,4},{6,7},{7,6},{8,9},{9,8},{10,11... | collective-permute-start | bytes 7077896 | tf_op jit(solution)/shard_map/ppermute | solution.py:62
  417.2 73.3 %collective-permute-start.52 = (bf16[2,2,144,864]{3,2,1,0:T(8,128)(2,1)}, bf16[2,2,144,864]{3,2,1,0:T(8,128)(2,1)}, u32[]{:S(2)}, u32[]{:S(2)}) collective-permute-start(bf16[2,2,144,864]{3,2,1,0:T(8,128)(2,1)} %get-tuple-element.226), channel_id=1, source_target_pairs={{0,4},{4,0},{8,12},{12,8},{16,20},{20,16},{24,28},{28,24},{1,5},{5... | collective-permute-start | bytes 2985992 | tf_op jit(solution)/shard_map/ppermute | solution.py:62
  446.8 43.7 %collective-permute-start.54 = (bf16[1,216,1152]{2,1,0:T(8,128)(2,1)}, bf16[1,216,1152]{2,1,0:T(8,128)(2,1)}, u32[]{:S(2)}, u32[]{:S(2)}) collective-permute-start(bf16[1,216,1152]{2,1,0:T(8,128)(2,1)} %get-tuple-element.243), channel_id=1, source_target_pairs={{0,16},{4,20},{8,24},{12,28},{16,0},{20,4},{24,8},{28,12},{1,17},{... | collective-permute-start | bytes 1493000 | tf_op jit(solution)/shard_map/ppermute | solution.py:62
  450.9 39.6 %collective-permute-start.53 = (bf16[2,2,144,864]{3,2,1,0:T(8,128)(2,1)}, bf16[2,2,144,864]{3,2,1,0:T(8,128)(2,1)}, u32[]{:S(2)}, u32[]{:S(2)}) collective-permute-start(bf16[2,2,144,864]{3,2,1,0:T(8,128)(2,1)} %get-tuple-element.224), channel_id=1, source_target_pairs={{0,4},{4,0},{8,12},{12,8},{16,20},{20,16},{24,28},{28,24},{1,5},{5... | collective-permute-start | bytes 2985992 | tf_op jit(solution)/shard_map/ppermute | solution.py:62
  505.5 46.4 %collective-permute-start.37 = (bf16[128,1152]{1,0:T(8,128)(2,1)}, bf16[128,1152]{1,0:T(8,128)(2,1)S(1)}, u32[]{:S(2)}, u32[]{:S(2)}) collective-permute-start(bf16[128,1152]{1,0:T(8,128)(2,1)} %get-tuple-element.249), channel_id=1, source_target_pairs={{0,4},{4,0},{8,12},{12,8},{16,20},{20,16},{24,28},{28,24},{1,5},{5... | collective-permute-start | bytes 884744 | tf_op jit(solution)/shard_map/ppermute | solution.py:62
  510.9 35.5 %collective-permute-start.58 = (bf16[2,144,864]{2,1,0:T(8,128)(2,1)S(1)}, bf16[2,144,864]{2,1,0:T(8,128)(2,1)S(1)}, u32[]{:S(2)}, u32[]{:S(2)}) collective-permute-start(bf16[2,144,864]{2,1,0:T(8,128)(2,1)S(1)} %get-tuple-element.241), channel_id=1, source_target_pairs={{0,16},{4,20},{8,24},{12,28},{16,0},{20,4},{24,8},{28,12},{1,17},{... | collective-permute-start | bytes 1493000 | tf_op jit(solution)/shard_map/ppermute | solution.py:62
  513.6 55.3 %collective-permute-start.62 = (bf16[2,144,864]{2,1,0:T(8,128)(2,1)}, bf16[2,144,864]{2,1,0:T(8,128)(2,1)}, u32[]{:S(2)}, u32[]{:S(2)}) collective-permute-start(bf16[2,144,864]{2,1,0:T(8,128)(2,1)} %get-tuple-element.239), channel_id=1, source_target_pairs={{0,16},{4,20},{8,24},{12,28},{16,0},{20,4},{24,8},{28,12},{1,17},{... | collective-permute-start | bytes 1493000 | tf_op jit(solution)/shard_map/ppermute | solution.py:62
  550.2 29.9 %collective-permute-start.60 = (bf16[256,512]{1,0:T(8,128)(2,1)}, bf16[256,512]{1,0:T(8,128)(2,1)}, u32[]{:S(2)}, u32[]{:S(2)}) collective-permute-start(bf16[256,512]{1,0:T(8,128)(2,1)} %get-tuple-element.236), channel_id=1, source_target_pairs={{0,16},{4,20},{8,24},{12,28},{16,0},{20,4},{24,8},{28,12},{1,17},{... | collective-permute-start | bytes 786440 | tf_op jit(solution)/shard_map/ppermute | solution.py:62
  550.2 29.9 %collective-permute-start.59 = (bf16[256,512]{1,0:T(8,128)(2,1)}, bf16[256,512]{1,0:T(8,128)(2,1)}, u32[]{:S(2)}, u32[]{:S(2)}) collective-permute-start(bf16[256,512]{1,0:T(8,128)(2,1)} %get-tuple-element.237), channel_id=1, source_target_pairs={{0,8},{4,12},{8,0},{12,4},{16,24},{20,28},{24,16},{28,20},{1,9},{5... | collective-permute-start | bytes 786440 | tf_op jit(solution)/shard_map/ppermute | solution.py:62
  555.9 53.3 %collective-permute-start.64 = (bf16[8,40,1024]{2,1,0:T(8,128)(2,1)}, bf16[8,40,1024]{2,1,0:T(8,128)(2,1)}, u32[]{:S(2)}, u32[]{:S(2)}) collective-permute-start(bf16[8,40,1024]{2,1,0:T(8,128)(2,1)} %slice.284), channel_id=1, source_target_pairs={{0,2},{1,3},{2,0},{3,1},{4,6},{5,7},{6,4},{7,5},{8,10},{9,11},{10,... | collective-permute-start | bytes 1966088 | tf_op jit(solution)/shard_map/ppermute | solution.py:68
  (147 other events, 1823.5 us)
Sparse Core Ops, SparseCore 0:
  74.6 82.7 all-gather.1
  554.4 101.9 reduce-scatter.1
